TPU v7x, 256 devices: a whole 4x4x8 slice. The times are simulated.
256 devices in a mesh: rows: 16 (over z_hi, x), cent: 16 (over z_lo, y, core).
Axes of the slice: x: 4, y: 4, z: 8 (z_hi: 4, z_lo: 2; z = z_hi * 2 + z_lo), core: 2. Of those that a mesh axis runs over, the one named last changes fastest.
Arguments:
- emb_values: bfloat16 [32768, 1024], P(('cent', 'rows')), may hold values from -6 to 6
- emb_scales: bfloat16 [32768, 8], P(('cent', 'rows')), may hold values from 0.125 to 8, as said below
- coarse_ids: int32 [16, 2048], P(None, 'rows'), may hold values from 0 to 32767, as said below
- centroids: bfloat16 [32768, 1024], P('cent'), may hold values from -6 to 6
- codes_one: int32 [16, 32768], P('rows', 'cent'), may hold values from 0 to 255
- codes_two: int32 [16, 32768], P('rows', 'cent'), may hold values from 0 to 255
- codebook_init: float32 [16, 256, 64], P('rows'), may hold values from -6 to 6
Outputs:
- coarse_gap: float32 [32768], P(('cent', 'rows'))
- codebook_one: float32 [16, 256, 64], P('rows')
- codebook_two: float32 [16, 256, 64], P('rows')
- distortion: float32 [16, 32768], P('rows', 'cent')
Inputs may be any that keep to these rules, and one draw needn't show every extreme that they name: `coarse_ids`: in each aligned block of 128 rows of the flattened ids (the rows of one device), at most 16 ids fall in any one aligned range of 2048 centroids, and exactly 16 fall in some range. `emb_scales`: every scale is a power of two.
All inputs are finite; a program needn't handle non-finite values.
Results may differ from a plain program's by a relative error of at most 0.0003.
Values may be sent and summed in bfloat16 or wider, within the bound.
No kernel may reach another device: no remote copies, remote signals or barrier semaphores. Data moves between devices by JAX's collectives and lax.ppermute only.
A program may use at most 64 MiB of HBM per device.

v0:
```python
import functools

import jax
import jax.numpy as jnp
from jax import lax
from jax.experimental import pallas as pl
from jax.experimental.pallas import tpu as pltpu
from jax.sharding import PartitionSpec as P


bf16 = jnp.bfloat16
f32 = jnp.float32
prior_weight = 8.0
VM = pl.BlockSpec(memory_space=pltpu.VMEM)
LIMIT = pltpu.CompilerParams(vmem_limit_bytes=16 << 20)


def on_chip(x):
    return pltpu.with_memory_space_constraint(x, pltpu.VMEM)


STATS = 136
PAY = 144


def quantize_kernel(values_ref, scales_t_ref, q_ref, squares_ref):
    scales = scales_t_ref[...].astype(f32).T
    squares = None
    for b in range(scales.shape[1]):
        lanes = slice(128 * b, 128 * b + 128)
        q = (values_ref[:, lanes].astype(f32) * scales[:, b : b + 1]).astype(bf16)
        q_ref[:, lanes] = q
        wide = q.astype(f32)
        squares = wide * wide if squares is None else squares + wide * wide
    squares_ref[...] = jnp.sum(squares.T, axis=0, keepdims=True)


def quantize(values, scales):
    rows, width = values.shape
    return pl.pallas_call(
        quantize_kernel,
        out_shape=(
            pltpu.VMEM((rows, width), bf16),
            pltpu.VMEM((1, rows), f32),
        ),
        in_specs=[VM, VM],
        out_specs=(VM, VM),
        cost_estimate=pl.CostEstimate(flops=rows * width * 3, bytes_accessed=rows * width * 4, transcendentals=0),
        compiler_params=LIMIT,
        name="quantize",
    )(values, scales.T)


def gather_kernel(slots, ids_ref, cents_ref, out_ref, onehot_ref):
    count = cents_ref.shape[0]
    groups, rows = ids_ref.shape

    local = ids_ref[...] - lax.axis_index("cent") * count
    mine = (local >= 0) & (local < count)
    before = lax.broadcasted_iota(jnp.int32, (rows, rows), 0) <= lax.broadcasted_iota(
        jnp.int32, (rows, rows), 1
    )
    rank = jnp.dot(
        mine.astype(f32).astype(bf16), before.astype(f32).astype(bf16), preferred_element_type=f32
    )
    slot = jnp.where(mine, rank - 1.0, -1.0)
    local = local.astype(f32)
    spread_slot = jnp.concatenate(
        [jnp.broadcast_to(slot[g : g + 1], (slots, rows)) for g in range(groups)], axis=0
    )
    spread_local = jnp.concatenate(
        [jnp.broadcast_to(local[g : g + 1], (slots, rows)) for g in range(groups)], axis=0
    )
    number = lax.rem(lax.broadcasted_iota(jnp.int32, (groups * slots, rows), 0), slots).astype(f32)
    chosen = jnp.sum(jnp.where(spread_slot == number, spread_local + 1.0, 0.0), axis=1, keepdims=True)
    chosen = chosen.astype(jnp.int32) - 1
    for j in range(count // 256):
        at = lax.broadcasted_iota(jnp.int32, (groups * slots, 256), 1) + 256 * j
        onehot_ref[:, 256 * j : 256 * j + 256] = (at == chosen).astype(f32).astype(bf16)
    for j in range(cents_ref.shape[1] // 256):
        lanes = slice(256 * j, 256 * j + 256)
        out_ref[:, lanes] = jnp.dot(
            onehot_ref[...], cents_ref[:, lanes], preferred_element_type=f32
        ).astype(bf16)


def gather(ids, cents, slots):
    groups, _ = ids.shape
    count, width = cents.shape
    return pl.pallas_call(
        functools.partial(gather_kernel, slots),
        out_shape=pltpu.VMEM((groups * slots, width), bf16),
        in_specs=[VM, VM],
        out_specs=VM,
        scratch_shapes=[pltpu.VMEM((groups * slots, count), bf16)],
        cost_estimate=pl.CostEstimate(
            flops=2 * groups * slots * count * width, bytes_accessed=count * width * 2, transcendentals=0
        ),
        compiler_params=LIMIT,
        name="gather",
    )(ids, on_chip(cents))


def residual_kernel(count, slots, ids_ref, fetched_ref, q_ref, out_ref):
    rows, width = q_ref.shape
    ids = ids_ref[pl.ds(lax.axis_index("cent"), 1), :]
    owner = lax.div(ids, count)
    across = jnp.broadcast_to(owner, (rows, rows))
    down = across.astype(f32).T.astype(jnp.int32)
    earlier = lax.broadcasted_iota(jnp.int32, (rows, rows), 0) < lax.broadcasted_iota(
        jnp.int32, (rows, rows), 1
    )
    rank = jnp.sum(jnp.where((across == down) & earlier, 1.0, 0.0), axis=0, keepdims=True)
    slot = owner * slots + rank.astype(jnp.int32)
    number = lax.broadcasted_iota(jnp.int32, (fetched_ref.shape[0], rows), 0)
    place = (number == slot).astype(f32).astype(bf16)
    for j in range(width // 128):
        lanes = slice(128 * j, 128 * j + 128)
        fetched = lax.dot_general(
            place, fetched_ref[:, lanes], (((0,), (0,)), ((), ())), preferred_element_type=f32
        )
        out_ref[lanes, :] = (q_ref[:, lanes].astype(f32) - fetched).T


def residuals(ids, fetched, q, count, slots):
    rows, width = q.shape
    return pl.pallas_call(
        functools.partial(residual_kernel, count, slots),
        out_shape=pltpu.VMEM((width, rows), f32),
        in_specs=[VM] * 3,
        out_specs=VM,
        cost_estimate=pl.CostEstimate(
            flops=2 * fetched.size * rows, bytes_accessed=fetched.size * 2 + q.size * 6, transcendentals=0
        ),
        compiler_params=LIMIT,
        name="residuals",
    )(ids, on_chip(fetched), on_chip(q))


def nearest_kernel(blocks, first, *refs):
    x_refs, refs = refs[:blocks], refs[blocks:]
    cents_ref, squares_ref, out_ref = refs if not first else (refs[0], refs[2], refs[1])
    step = 256
    groups = [[]]
    for ref in x_refs:
        if sum(r.shape[0] for r in groups[-1]) == 256:
            groups.append([])
        groups[-1].append(ref)
    out_ref[...] = jnp.full(out_ref.shape, jnp.inf, f32)

    @pl.loop(0, cents_ref.shape[0] // step)
    def _(i):
        at = pl.ds(pl.multiple_of(i * step, step), step)
        block = cents_ref[at, :]
        if first:
            total = None
            for b in range(block.shape[1] // 128):
                wide = block[:, 128 * b : 128 * b + 128].astype(f32)
                total = wide * wide if total is None else total + wide * wide
            squares = jnp.broadcast_to(jnp.sum(total, axis=1, keepdims=True), (step, 128))
            squares_ref[at, :] = squares
        else:
            squares = squares_ref[at, :]
        squares = jnp.concatenate([squares, squares], axis=1)
        for j, group in enumerate(groups):
            x = jnp.concatenate([r[...] for r in group], axis=0)
            cross = lax.dot_general(block, x, (((1,), (1,)), ((), ())), preferred_element_type=f32)
            low = jnp.min(squares - 2.0 * cross, axis=0, keepdims=True)
            for k in range(2):
                row = slice(2 * j + k, 2 * j + k + 1)
                out_ref[row, :] = jnp.minimum(out_ref[row, :], low[:, 128 * k : 128 * k + 128])


def nearest(xs, cents, squares=None):
    count, width = cents.shape
    first = squares is None
    rows = sum(x.shape[0] for x in xs)
    out_shape = pltpu.VMEM((rows // 128, 128), f32)
    return pl.pallas_call(
        functools.partial(nearest_kernel, len(xs), first),
        out_shape=(out_shape, pltpu.VMEM((count, 128), f32)) if first else out_shape,
        in_specs=[VM] * (len(xs) + (1 if first else 2)),
        out_specs=(VM, VM) if first else VM,
        cost_estimate=pl.CostEstimate(
            flops=2 * rows * count * width, bytes_accessed=count * width * 2 + rows * width * 2, transcendentals=0
        ),
        compiler_params=LIMIT,
        name="nearest",
    )(*[on_chip(x) for x in xs], on_chip(cents), *([] if first else [on_chip(squares)]))


def halves_of(x):
    high = x.astype(bf16)
    return high, (x - high.astype(f32)).astype(bf16)


def statistics_kernel(where, sub_ref, one_ref, two_ref, *refs):
    gap_refs, (mine_ref, theirs_ref) = refs[:-2], refs[-2:]
    groups, width, rows = sub_ref.shape
    words = 256
    high, low = [], []
    for g in range(groups):
        h, l = halves_of(sub_ref[g])
        high.append(h)
        low.append(l)
    ones = jnp.ones((16, groups * rows), bf16)
    left = jnp.concatenate([jnp.concatenate(high, axis=1), jnp.concatenate(low, axis=1), ones], axis=0)
    word = lax.broadcasted_iota(jnp.int32, (words, groups * rows), 0)
    core = lax.rem(lax.axis_index("cent"), 2)
    odd = core == 1

    def totals(codes_ref):
        hit = (word == codes_ref[...]).astype(f32).astype(bf16)
        out = lax.dot_general(left, hit, (((1,), (1,)), ((), ())), preferred_element_type=f32)
        return out[:width] + out[width : 2 * width], out[2 * width : 2 * width + 8]

    for at, codes_ref in enumerate((one_ref, two_ref)):
        total, count = totals(codes_ref)
        rows_at = slice(width * at, width * at + width)
        a, b = total[:, :128], total[:, 128:]
        mine_ref[rows_at, :] = jnp.where(odd, b, a)
        theirs_ref[rows_at, :] = jnp.where(odd, a, b)
        a, b = count[:4, :128], count[:4, 128:]
        count_at = slice(2 * width + 4 * at, 2 * width + 4 * at + 4)
        mine_ref[count_at, :] = jnp.where(odd, b, a)
        theirs_ref[count_at, :] = jnp.where(odd, a, b)
    for j in range(8):
        for out_ref, d in ((mine_ref, 2 * j), (theirs_ref, 2 * j + 1)):
            k, row = where[d]
            out_ref[STATS + j : STATS + j + 1, :] = gap_refs[k][row : row + 1, :]


def statistics(sub, codes_one, codes_two, lows, where):
    shape = pltpu.VMEM((PAY, 128), f32)
    return pl.pallas_call(
        functools.partial(statistics_kernel, where),
        out_shape=(shape, shape),
        in_specs=[VM] * (3 + len(lows)),
        out_specs=(VM, VM),
        cost_estimate=pl.CostEstimate(
            flops=2 * 2 * sub.size * 512, bytes_accessed=sub.size * 4, transcendentals=0
        ),
        compiler_params=LIMIT,
        name="statistics",
    )(on_chip(sub), codes_one, codes_two, *[on_chip(x) for x in lows])


def join_kernel(shift, a_ref, b_ref, out_ref):
    out_ref[:STATS, :] = a_ref[:STATS, :] + b_ref[:STATS, :]
    keep = PAY - STATS - shift
    out_ref[STATS:PAY, :] = a_ref[STATS:PAY, :]
    out_ref[STATS : STATS + keep, :] = jnp.minimum(
        a_ref[STATS : STATS + keep, :], b_ref[STATS + shift : PAY, :]
    )


def join(a, b, shift):
    return pl.pallas_call(
        functools.partial(join_kernel, shift),
        out_shape=pltpu.VMEM(a.shape, f32),
        in_specs=[VM, VM],
        out_specs=VM,
        cost_estimate=pl.CostEstimate(flops=a.size, bytes_accessed=a.size * 12, transcendentals=0),
        compiler_params=LIMIT,
        name="join",
    )(on_chip(a), on_chip(b))


def update_kernel(width, a_ref, b_ref, c_ref, d_ref, init_ref, squares_ref, books_ref, gap_ref):
    core = lax.rem(lax.axis_index("cent"), 2)
    total = (a_ref[:STATS, :] + b_ref[:STATS, :]) + (c_ref[:STATS, :] + d_ref[:STATS, :])
    init = jnp.where(core == 1, init_ref[:, 128:], init_ref[:, :128])
    count_one = total[2 * width : 2 * width + 1]
    count_two = total[2 * width + 4 : 2 * width + 5]
    one = (total[:width] + prior_weight * init) / (count_one + prior_weight)
    two = (total[width : 2 * width] + prior_weight * one) / (count_two + prior_weight)
    books_ref[:width, :] = one
    books_ref[width:, :] = two
    low = jnp.minimum(
        jnp.minimum(a_ref[STATS : STATS + 1, :], b_ref[STATS + 1 : STATS + 2, :]),
        jnp.minimum(c_ref[STATS + 2 : STATS + 3, :], d_ref[STATS + 3 : STATS + 4, :]),
    )
    gap_ref[...] = (low + squares_ref[...]) * (1.0 / 1024.0)


def update(parts, init, squares):
    width = init.shape[0]
    return pl.pallas_call(
        functools.partial(update_kernel, width),
        out_shape=(
            pltpu.VMEM((2 * width, 128), f32),
            jax.ShapeDtypeStruct((1, 128), f32),
        ),
        in_specs=[VM] * 6,
        out_specs=(VM, VM),
        cost_estimate=pl.CostEstimate(flops=8 * STATS * 128, bytes_accessed=5 * PAY * 512, transcendentals=0),
        compiler_params=LIMIT,
        name="update",
    )(*[on_chip(x) for x in parts], init, on_chip(squares))


def distortion_kernel(sub_ref, two_ref, mine_ref, theirs_ref, one_out_ref, two_out_ref, out_ref):
    groups, width, rows = sub_ref.shape
    odd = lax.rem(lax.axis_index("cent"), 2) == 1
    mine, theirs = mine_ref[...], theirs_ref[...]
    books = jnp.concatenate([jnp.where(odd, theirs, mine), jnp.where(odd, mine, theirs)], axis=1)
    one_out_ref[...] = books[:width]
    book = books[width:]
    two_out_ref[...] = book
    high, low = halves_of(book)
    left = jnp.concatenate([high, low], axis=0)
    words = book.shape[1]
    for g in range(0, groups, 2):
        lanes = slice(rows * g, rows * g + 2 * rows)
        word = lax.broadcasted_iota(jnp.int32, (words, 2 * rows), 0)
        hit = (word == two_ref[:, lanes]).astype(f32).astype(bf16)
        rebuilt = jnp.dot(left, hit, preferred_element_type=f32)
        rebuilt = rebuilt[:width] + rebuilt[width:]
        sub = jnp.concatenate([sub_ref[g], sub_ref[g + 1]], axis=1)
        miss = sub - rebuilt
        out_ref[:, lanes] = jnp.sum(miss * miss, axis=0, keepdims=True) * (1.0 / width)


def distortions(sub, codes_two, mine, theirs):
    groups, width, rows = sub.shape
    return pl.pallas_call(
        distortion_kernel,
        out_shape=(
            jax.ShapeDtypeStruct((width, 256), f32),
            jax.ShapeDtypeStruct((width, 256), f32),
            jax.ShapeDtypeStruct((1, groups * rows), f32),
        ),
        in_specs=[VM] * 4,
        out_specs=(VM, VM, VM),
        cost_estimate=pl.CostEstimate(
            flops=4 * sub.size * 256, bytes_accessed=sub.size * 4, transcendentals=0
        ),
        compiler_params=LIMIT,
        name="distortion",
    )(on_chip(sub), codes_two, on_chip(mine), on_chip(theirs))


def swap(x, offset):
    return lax.ppermute(x, "cent", [(i, i ^ offset) for i in range(16)])


def step(emb_values, emb_scales, coarse_ids, centroids, codes_one, codes_two, codebook_init):
    own_rows, width = emb_values.shape
    count = centroids.shape[0]
    sub_width = codebook_init.shape[2]
    peers = coarse_ids.shape[0]
    slots = 16
    half = own_rows // 2

    centroids = on_chip(centroids)
    q, row_squares = quantize(emb_values, emb_scales)

    core = 1

    a, b, z = swap(q, 2), swap(q, 6), swap(q, 8)
    blocks = {0: [q], core: [swap(q, core)], 2: [a], 6: [b], 8: [z]}

    sent = gather(coarse_ids, centroids, slots).reshape(peers, slots, width)
    fetched = lax.all_to_all(sent, "cent", 0, 0).reshape(peers * slots, width)

    blocks[4] = [swap(b[:half], 2), swap(a[half:], 6)]
    blocks[10], blocks[14] = [swap(z, 2)], [swap(z, 6)]
    blocks[12] = [swap(x, 8) for x in blocks[4]]
    for d in (2, 6, 8, 4, 10, 14, 12):
        blocks[d ^ core] = [swap(x, core) for x in blocks[d]]

    def near(order, squares=None):
        xs = [x for d in order for x in blocks[d]]
        return nearest(xs, centroids, squares)

    orders = ((0, 1, 2, 3), (6, 7, 8, 9), (4, 5, 10, 11, 14, 15, 12, 13))
    first, cent_squares = near(orders[0])
    lows = [first] + [near(orders[k], cent_squares) for k in (1, 2)]
    where = {d: (k, j) for k, order in enumerate(orders) for j, d in enumerate(order)}

    residual = residuals(coarse_ids, fetched, q, count, slots)
    stacked = residual.reshape(width // sub_width, sub_width, own_rows)
    sub = lax.all_to_all(stacked, "rows", 0, 0)

    mine, theirs = statistics(sub, codes_one, codes_two, lows, where)
    mine = join(mine, swap(theirs, 1), 0)
    mine = join(mine, swap(mine, 8), 4)
    parts = [mine] + [swap(mine, d) for d in (2, 4, 6)]
    init = codebook_init[0].T
    books, coarse_gap = update(parts, init, row_squares)
    book_one, book_two, distortion = distortions(sub, codes_two, books, swap(books, 1))
    return coarse_gap[0], book_one.T[None], book_two.T[None], distortion


def solution(mesh):
    placed = (
        P(("cent", "rows"), None),
        P(("cent", "rows"), None),
        P(None, "rows"),
        P("cent", None),
        P("rows", "cent"),
        P("rows", "cent"),
        P("rows", None, None),
    )
    return jax.shard_map(
        step,
        mesh=mesh,
        in_specs=placed,
        out_specs=(
            P(("cent", "rows")),
            P("rows", None, None),
            P("rows", None, None),
            P("rows", "cent"),
        ),
        check_vma=False,
    )
```

profile of v0, /device:TPU:1, one launch (start us, length us, event | category | flops | bytes accessed | tf_op | source)
XLA Modules:
  0.0 93.8 jit_solution(17218528013272976033)
XLA Ops:
  0.6 2.2 %copy-done = bf16[2048,1024]{1,0:T(8,128)(2,1)S(1)} copy-done((bf16[2048,1024]{1,0:T(8,128)(2,1)S(1)}, bf16[2048,1024]{1,0:T(8,128)(2,1)}, u32[]{:S(2)}) %copy-start) | copy-done | bytes 4194328
  3.5 2.2 %gather.1 = bf16[256,1024]{1,0:T(8,128)(2,1)} custom-call(s32[16,128]{1,0:T(8,128)S(1)} %copy-done.4, bf16[2048,1024]{1,0:T(8,128)(2,1)S(1)} %copy-done), custom_call_target="tpu_custom_call" | custom-call | flops 1073741824 | bytes 4194304 | tf_op jit(solution)/shard_map/gather/pallas_call | solution.py:90
  5.8 7.3 %all-to-all-start = ((bf16[16,16,1024]{2,1,0:T(8,128)(2,1)}), bf16[16,16,1024]{2,1,0:T(8,128)(2,1)S(1)}, u32[]{:S(2)}, u32[]{:S(2)}) async-start(bf16[16,16,1024]{2,1,0:T(8,128)(2,1)} %bitcast), calls=%async_computation | async-start | bytes 1048576 | tf_op jit(solution)/shard_map/all_to_all | solution.py:364
  13.5 2.7 %collective-permute-start.3 = (bf16[128,1024]{1,0:T(8,128)(2,1)S(1)}, bf16[128,1024]{1,0:T(8,128)(2,1)S(1)}, u32[]{:S(2)}, u32[]{:S(2)}) collective-permute-start(bf16[128,1024]{1,0:T(8,128)(2,1)S(1)} %get-tuple-element.15.q_ref.refs_0_), channel_id=1, source_target_pairs={{0,6},{1,7},{2,4},{3,5},{4,2},{5,3},{6,0},{7,1},{8,14},{9,15},{10,... | collective-permute-start | bytes 786440 | tf_op jit(solution)/shard_map/ppermute | solution.py:344
  18.2 9.7 %collective-permute-done.3.refs_0_ = bf16[128,1024]{1,0:T(8,128)(2,1)S(1)} collective-permute-done((bf16[128,1024]{1,0:T(8,128)(2,1)S(1)}, bf16[128,1024]{1,0:T(8,128)(2,1)S(1)}, u32[]{:S(2)}, u32[]{:S(2)}) %collective-permute-start.3) | collective-permute-done | bytes 262176 | tf_op jit(solution)/shard_map/ppermute | solution.py:344
  30.7 1.6 %collective-permute-done.7.refs_0_ = bf16[64,1024]{1,0:T(8,128)(2,1)S(1)} collective-permute-done((bf16[64,1024]{1,0:T(8,128)(2,1)S(1)}, bf16[64,1024]{1,0:T(8,128)(2,1)S(1)}, u32[]{:S(2)}, u32[]{:S(2)}) %collective-permute-start.7) | collective-permute-done | bytes 131104 | tf_op jit(solution)/shard_map/ppermute | solution.py:344
  33.2 1.4 %collective-permute-start.13 = (bf16[128,1024]{1,0:T(8,128)(2,1)S(1)}, bf16[128,1024]{1,0:T(8,128)(2,1)S(1)}, u32[]{:S(2)}, u32[]{:S(2)}) collective-permute-start(bf16[128,1024]{1,0:T(8,128)(2,1)S(1)} %collective-permute-done.5.refs_2_), channel_id=1, source_target_pairs={{0,6},{1,7},{2,4},{3,5},{4,2},{5,3},{6,0},{7,1},{8,14},{9,15},{10,... | collective-permute-start | bytes 786440 | tf_op jit(solution)/shard_map/ppermute | solution.py:344
  34.6 1.3 %residuals.1 = f32[1024,128]{1,0:T(8,128)} custom-call(s32[16,128]{1,0:T(8,128)S(1)} %copy-done.5, bf16[256,1024]{1,0:T(8,128)(2,1)S(1)} %bitcast.14, bf16[128,1024]{1,0:T(8,128)(2,1)S(1)} %get-tuple-element.15.q_ref.refs_0_), custom_call_target="tpu_custom_call" | custom-call | flops 67108864 | bytes 1310720 | tf_op jit(solution)/shard_map/residuals/pallas_call | solution.py:127
  35.9 9.9 %all-to-all-start.1 = ((f32[16,64,128]{2,1,0:T(8,128)}), f32[16,64,128]{2,1,0:T(8,128)S(1)}, u32[]{:S(2)}, u32[]{:S(2)}) async-start(f32[16,64,128]{2,1,0:T(8,128)} %bitcast.3), calls=%async_computation.1 | async-start | bytes 1048576 | tf_op jit(solution)/shard_map/all_to_all | solution.py:383
  45.8 2.3 %collective-permute-start.9 = (bf16[64,1024]{1,0:T(8,128)(2,1)S(1)}, bf16[64,1024]{1,0:T(8,128)(2,1)S(1)}, u32[]{:S(2)}, u32[]{:S(2)}) collective-permute-start(bf16[64,1024]{1,0:T(8,128)(2,1)S(1)} %collective-permute-done.7.refs_0_), channel_id=1, source_target_pairs={{0,1},{1,0},{2,3},{3,2},{4,5},{5,4},{6,7},{7,6},{8,9},{9,8},{10,11... | collective-permute-start | bytes 393224 | tf_op jit(solution)/shard_map/ppermute | solution.py:344
  50.3 2.2 %copy-done.1 = bf16[2048,1024]{1,0:T(8,128)(2,1)S(1)} copy-done((bf16[2048,1024]{1,0:T(8,128)(2,1)S(1)}, bf16[2048,1024]{1,0:T(8,128)(2,1)}, u32[]{:S(2)}) %copy-start.1) | copy-done | bytes 4194328
  52.5 4.0 %nearest.3 = (f32[4,128]{1,0:T(4,128)S(1)}, f32[2048,128]{1,0:T(8,128)S(1)}) custom-call(bf16[128,1024]{1,0:T(8,128)(2,1)S(1)} %get-tuple-element.15.q_ref.refs_0_, bf16[128,1024]{1,0:T(8,128)(2,1)S(1)} %collective-permute-done.refs_1_, bf16[128,1024]{1,0:T(8,128)(2,1)S(1)} %collective-permute-done.1.refs_2_, ...), custom_call_target="tpu_custom_call" | custom-call | flops 2147483648 | bytes 5242880 | tf_op jit(solution)/shard_map/nearest/pallas_call | solution.py:179
  57.0 3.5 %collective-permute-done.15.refs_8_ = bf16[64,1024]{1,0:T(8,128)(2,1)S(1)} collective-permute-done((bf16[64,1024]{1,0:T(8,128)(2,1)S(1)}, bf16[64,1024]{1,0:T(8,128)(2,1)S(1)}, u32[]{:S(2)}, u32[]{:S(2)}) %collective-permute-start.15) | collective-permute-done | bytes 131104 | tf_op jit(solution)/shard_map/ppermute | solution.py:344
  60.5 3.5 %collective-permute-start.17 = (bf16[64,1024]{1,0:T(8,128)(2,1)S(1)}, bf16[64,1024]{1,0:T(8,128)(2,1)S(1)}, u32[]{:S(2)}, u32[]{:S(2)}) collective-permute-start(bf16[64,1024]{1,0:T(8,128)(2,1)S(1)} %collective-permute-done.15.refs_8_), channel_id=1, source_target_pairs={{0,1},{1,0},{2,3},{3,2},{4,5},{5,4},{6,7},{7,6},{8,9},{9,8},{10,11... | collective-permute-start | bytes 393224 | tf_op jit(solution)/shard_map/ppermute | solution.py:344
  64.0 1.5 %collective-permute-start.18 = (bf16[64,1024]{1,0:T(8,128)(2,1)S(1)}, bf16[64,1024]{1,0:T(8,128)(2,1)S(1)}, u32[]{:S(2)}, u32[]{:S(2)}) collective-permute-start(bf16[64,1024]{1,0:T(8,128)(2,1)S(1)} %collective-permute-done.16.refs_9_), channel_id=1, source_target_pairs={{0,1},{1,0},{2,3},{3,2},{4,5},{5,4},{6,7},{7,6},{8,9},{9,8},{10,11... | collective-permute-start | bytes 393224 | tf_op jit(solution)/shard_map/ppermute | solution.py:344
  65.6 3.9 %nearest.4.refs_1_ = f32[4,128]{1,0:T(4,128)S(1)} custom-call(bf16[128,1024]{1,0:T(8,128)(2,1)S(1)} %collective-permute-done.3.refs_0_, bf16[128,1024]{1,0:T(8,128)(2,1)S(1)} %collective-permute-done.4.refs_1_, bf16[128,1024]{1,0:T(8,128)(2,1)S(1)} %collective-permute-done.5.refs_2_, bf16[128,1024]{1,0:T(8,128)(2,1)S(1)} %collective-permute-done.6.refs_3_, ...), custom_call_target="tpu_custom_call" | custom-call | flops 2147483648 | bytes 5242880 | tf_op jit(solution)/shard_map/nearest/pallas_call | solution.py:179
  69.6 6.1 %nearest.5.refs_2_ = f32[8,128]{1,0:T(8,128)S(1)} custom-call(bf16[64,1024]{1,0:T(8,128)(2,1)S(1)} %collective-permute-done.7.refs_0_, bf16[64,1024]{1,0:T(8,128)(2,1)S(1)} %collective-permute-done.8.refs_1_, bf16[64,1024]{1,0:T(8,128)(2,1)S(1)} %collective-permute-done.9.refs_2_, bf16[64,1024]{1,0:T(8,128)(2,1)S(1)} %collective-permute-done.10.refs_3_, ...), custom_call_target="tpu_custom_call" | custom-call | flops 4294967296 | bytes 6291456 | tf_op jit(solution)/shard_map/nearest/pallas_call | solution.py:179
  76.7 1.3 %collective-permute-done.19.b_ref = f32[144,128]{1,0:T(8,128)S(1)} collective-permute-done((f32[144,128]{1,0:T(8,128)S(1)}, f32[144,128]{1,0:T(8,128)S(1)}, u32[]{:S(2)}, u32[]{:S(2)}) %collective-permute-start.19) | collective-permute-done | bytes 73760 | tf_op jit(solution)/shard_map/ppermute | solution.py:344
  78.3 3.3 %collective-permute-done.20.b_ref = f32[144,128]{1,0:T(8,128)S(1)} collective-permute-done((f32[144,128]{1,0:T(8,128)S(1)}, f32[144,128]{1,0:T(8,128)S(1)}, u32[]{:S(2)}, u32[]{:S(2)}) %collective-permute-start.20) | collective-permute-done | bytes 73760 | tf_op jit(solution)/shard_map/ppermute | solution.py:344
  81.8 2.5 %collective-permute-start.22 = (f32[144,128]{1,0:T(8,128)S(1)}, f32[144,128]{1,0:T(8,128)S(1)}, u32[]{:S(2)}, u32[]{:S(2)}) collective-permute-start(f32[144,128]{1,0:T(8,128)S(1)} %join.3.a_ref), channel_id=1, source_target_pairs={{0,4},{1,5},{2,6},{3,7},{4,0},{5,1},{6,2},{7,3},{8,12},{9,13},{10,... | collective-permute-start | bytes 221192 | tf_op jit(solution)/shard_map/ppermute | solution.py:344
  84.3 1.3 %collective-permute-start.23 = (f32[144,128]{1,0:T(8,128)S(1)}, f32[144,128]{1,0:T(8,128)S(1)}, u32[]{:S(2)}, u32[]{:S(2)}) collective-permute-start(f32[144,128]{1,0:T(8,128)S(1)} %join.3.a_ref), channel_id=1, source_target_pairs={{0,6},{1,7},{2,4},{3,5},{4,2},{5,3},{6,0},{7,1},{8,14},{9,15},{10,... | collective-permute-start | bytes 221192 | tf_op jit(solution)/shard_map/ppermute | solution.py:344
  85.6 1.3 %collective-permute-done.22.c_ref = f32[144,128]{1,0:T(8,128)S(1)} collective-permute-done((f32[144,128]{1,0:T(8,128)S(1)}, f32[144,128]{1,0:T(8,128)S(1)}, u32[]{:S(2)}, u32[]{:S(2)}) %collective-permute-start.22) | collective-permute-done | bytes 73760 | tf_op jit(solution)/shard_map/ppermute | solution.py:344
  86.9 2.3 %collective-permute-done.23.d_ref = f32[144,128]{1,0:T(8,128)S(1)} collective-permute-done((f32[144,128]{1,0:T(8,128)S(1)}, f32[144,128]{1,0:T(8,128)S(1)}, u32[]{:S(2)}, u32[]{:S(2)}) %collective-permute-start.23) | collective-permute-done | bytes 73760 | tf_op jit(solution)/shard_map/ppermute | solution.py:344
  89.8 2.2 %collective-permute-start.24 = (f32[128,128]{1,0:T(8,128)S(1)}, f32[128,128]{1,0:T(8,128)S(1)}, u32[]{:S(2)}, u32[]{:S(2)}) collective-permute-start(f32[128,128]{1,0:T(8,128)S(1)} %get-tuple-element.22.mine_ref), channel_id=1, source_target_pairs={{0,1},{1,0},{2,3},{3,2},{4,5},{5,4},{6,7},{7,6},{8,9},{9,8},{10,11... | collective-permute-start | bytes 196616 | tf_op jit(solution)/shard_map/ppermute | solution.py:344
  (61 shorter events, 13.4 us)
Async XLA Ops:
  5.8 28.8 %all-to-all-start = ((bf16[16,16,1024]{2,1,0:T(8,128)(2,1)}), bf16[16,16,1024]{2,1,0:T(8,128)(2,1)S(1)}, u32[]{:S(2)}, u32[]{:S(2)}) async-start(bf16[16,16,1024]{2,1,0:T(8,128)(2,1)} %bitcast), calls=%async_computation | async-start | bytes 1048576 | tf_op jit(solution)/shard_map/all_to_all | solution.py:364
  13.5 14.5 %collective-permute-start.3 = (bf16[128,1024]{1,0:T(8,128)(2,1)S(1)}, bf16[128,1024]{1,0:T(8,128)(2,1)S(1)}, u32[]{:S(2)}, u32[]{:S(2)}) collective-permute-start(bf16[128,1024]{1,0:T(8,128)(2,1)S(1)} %get-tuple-element.15.q_ref.refs_0_), channel_id=1, source_target_pairs={{0,6},{1,7},{2,4},{3,5},{4,2},{5,3},{6,0},{7,1},{8,14},{9,15},{10,... | collective-permute-start | bytes 786440 | tf_op jit(solution)/shard_map/ppermute | solution.py:344
  16.1 12.0 %collective-permute-start.1 = (bf16[128,1024]{1,0:T(8,128)(2,1)S(1)}, bf16[128,1024]{1,0:T(8,128)(2,1)S(1)}, u32[]{:S(2)}, u32[]{:S(2)}) collective-permute-start(bf16[128,1024]{1,0:T(8,128)(2,1)S(1)} %get-tuple-element.15.q_ref.refs_0_), channel_id=1, source_target_pairs={{0,2},{1,3},{2,0},{3,1},{4,6},{5,7},{6,4},{7,5},{8,10},{9,11},{10,... | collective-permute-start | bytes 786440 | tf_op jit(solution)/shard_map/ppermute | solution.py:344
  16.1 14.1 %collective-permute-start = (bf16[128,1024]{1,0:T(8,128)(2,1)S(1)}, bf16[128,1024]{1,0:T(8,128)(2,1)S(1)}, u32[]{:S(2)}, u32[]{:S(2)}) collective-permute-start(bf16[128,1024]{1,0:T(8,128)(2,1)S(1)} %get-tuple-element.15.q_ref.refs_0_), channel_id=1, source_target_pairs={{0,1},{1,0},{2,3},{3,2},{4,5},{5,4},{6,7},{7,6},{8,9},{9,8},{10,11... | collective-permute-start | bytes 786440 | tf_op jit(solution)/shard_map/ppermute | solution.py:344
  17.0 13.2 %collective-permute-start.5 = (bf16[128,1024]{1,0:T(8,128)(2,1)S(1)}, bf16[128,1024]{1,0:T(8,128)(2,1)S(1)}, u32[]{:S(2)}, u32[]{:S(2)}) collective-permute-start(bf16[128,1024]{1,0:T(8,128)(2,1)S(1)} %get-tuple-element.15.q_ref.refs_0_), channel_id=1, source_target_pairs={{0,8},{1,9},{2,10},{3,11},{4,12},{5,13},{6,14},{7,15},{8,0},{9,1},... | collective-permute-start | bytes 786440 | tf_op jit(solution)/shard_map/ppermute | solution.py:344
  28.0 4.4 %collective-permute-start.7 = (bf16[64,1024]{1,0:T(8,128)(2,1)S(1)}, bf16[64,1024]{1,0:T(8,128)(2,1)S(1)}, u32[]{:S(2)}, u32[]{:S(2)}) collective-permute-start(bf16[64,1024]{1,0:T(8,128)(2,1)S(1)} %slice.8), channel_id=1, source_target_pairs={{0,2},{1,3},{2,0},{3,1},{4,6},{5,7},{6,4},{7,5},{8,10},{9,11},{10,... | collective-permute-start | bytes 393224 | tf_op jit(solution)/shard_map/ppermute | solution.py:344
  28.1 5.1 %collective-permute-start.8 = (bf16[64,1024]{1,0:T(8,128)(2,1)S(1)}, bf16[64,1024]{1,0:T(8,128)(2,1)S(1)}, u32[]{:S(2)}, u32[]{:S(2)}) collective-permute-start(bf16[64,1024]{1,0:T(8,128)(2,1)S(1)} %slice.9), channel_id=1, source_target_pairs={{0,6},{1,7},{2,4},{3,5},{4,2},{5,3},{6,0},{7,1},{8,14},{9,15},{10,... | collective-permute-start | bytes 393224 | tf_op jit(solution)/shard_map/ppermute | solution.py:344
  29.1 16.7 %collective-permute-start.2 = (bf16[128,1024]{1,0:T(8,128)(2,1)S(1)}, bf16[128,1024]{1,0:T(8,128)(2,1)S(1)}, u32[]{:S(2)}, u32[]{:S(2)}) collective-permute-start(bf16[128,1024]{1,0:T(8,128)(2,1)S(1)} %collective-permute-done.1.refs_2_), channel_id=1, source_target_pairs={{0,1},{1,0},{2,3},{3,2},{4,5},{5,4},{6,7},{7,6},{8,9},{9,8},{10,11... | collective-permute-start | bytes 786440 | tf_op jit(solution)/shard_map/ppermute | solution.py:344
  30.2 17.9 %collective-permute-start.4 = (bf16[128,1024]{1,0:T(8,128)(2,1)S(1)}, bf16[128,1024]{1,0:T(8,128)(2,1)S(1)}, u32[]{:S(2)}, u32[]{:S(2)}) collective-permute-start(bf16[128,1024]{1,0:T(8,128)(2,1)S(1)} %collective-permute-done.3.refs_0_), channel_id=1, source_target_pairs={{0,1},{1,0},{2,3},{3,2},{4,5},{5,4},{6,7},{7,6},{8,9},{9,8},{10,11... | collective-permute-start | bytes 786440 | tf_op jit(solution)/shard_map/ppermute | solution.py:344
  30.2 19.1 %collective-permute-start.6 = (bf16[128,1024]{1,0:T(8,128)(2,1)S(1)}, bf16[128,1024]{1,0:T(8,128)(2,1)S(1)}, u32[]{:S(2)}, u32[]{:S(2)}) collective-permute-start(bf16[128,1024]{1,0:T(8,128)(2,1)S(1)} %collective-permute-done.5.refs_2_), channel_id=1, source_target_pairs={{0,1},{1,0},{2,3},{3,2},{4,5},{5,4},{6,7},{7,6},{8,9},{9,8},{10,11... | collective-permute-start | bytes 786440 | tf_op jit(solution)/shard_map/ppermute | solution.py:344
  32.3 17.2 %collective-permute-start.11 = (bf16[128,1024]{1,0:T(8,128)(2,1)S(1)}, bf16[128,1024]{1,0:T(8,128)(2,1)S(1)}, u32[]{:S(2)}, u32[]{:S(2)}) collective-permute-start(bf16[128,1024]{1,0:T(8,128)(2,1)S(1)} %collective-permute-done.5.refs_2_), channel_id=1, source_target_pairs={{0,2},{1,3},{2,0},{3,1},{4,6},{5,7},{6,4},{7,5},{8,10},{9,11},{10,... | collective-permute-start | bytes 786440 | tf_op jit(solution)/shard_map/ppermute | solution.py:344
  33.2 17.0 %collective-permute-start.13 = (bf16[128,1024]{1,0:T(8,128)(2,1)S(1)}, bf16[128,1024]{1,0:T(8,128)(2,1)S(1)}, u32[]{:S(2)}, u32[]{:S(2)}) collective-permute-start(bf16[128,1024]{1,0:T(8,128)(2,1)S(1)} %collective-permute-done.5.refs_2_), channel_id=1, source_target_pairs={{0,6},{1,7},{2,4},{3,5},{4,2},{5,3},{6,0},{7,1},{8,14},{9,15},{10,... | collective-permute-start | bytes 786440 | tf_op jit(solution)/shard_map/ppermute | solution.py:344
  35.9 39.8 %all-to-all-start.1 = ((f32[16,64,128]{2,1,0:T(8,128)}), f32[16,64,128]{2,1,0:T(8,128)S(1)}, u32[]{:S(2)}, u32[]{:S(2)}) async-start(f32[16,64,128]{2,1,0:T(8,128)} %bitcast.3), calls=%async_computation.1 | async-start | bytes 1048576 | tf_op jit(solution)/shard_map/all_to_all | solution.py:383
  45.8 10.7 %collective-permute-start.9 = (bf16[64,1024]{1,0:T(8,128)(2,1)S(1)}, bf16[64,1024]{1,0:T(8,128)(2,1)S(1)}, u32[]{:S(2)}, u32[]{:S(2)}) collective-permute-start(bf16[64,1024]{1,0:T(8,128)(2,1)S(1)} %collective-permute-done.7.refs_0_), channel_id=1, source_target_pairs={{0,1},{1,0},{2,3},{3,2},{4,5},{5,4},{6,7},{7,6},{8,9},{9,8},{10,11... | collective-permute-start | bytes 393224 | tf_op jit(solution)/shard_map/ppermute | solution.py:344
  48.1 12.4 %collective-permute-start.15 = (bf16[64,1024]{1,0:T(8,128)(2,1)S(1)}, bf16[64,1024]{1,0:T(8,128)(2,1)S(1)}, u32[]{:S(2)}, u32[]{:S(2)}) collective-permute-start(bf16[64,1024]{1,0:T(8,128)(2,1)S(1)} %collective-permute-done.7.refs_0_), channel_id=1, source_target_pairs={{0,8},{1,9},{2,10},{3,11},{4,12},{5,13},{6,14},{7,15},{8,0},{9,1},... | collective-permute-start | bytes 393224 | tf_op jit(solution)/shard_map/ppermute | solution.py:344
  49.3 14.7 %collective-permute-start.16 = (bf16[64,1024]{1,0:T(8,128)(2,1)S(1)}, bf16[64,1024]{1,0:T(8,128)(2,1)S(1)}, u32[]{:S(2)}, u32[]{:S(2)}) collective-permute-start(bf16[64,1024]{1,0:T(8,128)(2,1)S(1)} %collective-permute-done.8.refs_1_), channel_id=1, source_target_pairs={{0,8},{1,9},{2,10},{3,11},{4,12},{5,13},{6,14},{7,15},{8,0},{9,1},... | collective-permute-start | bytes 393224 | tf_op jit(solution)/shard_map/ppermute | solution.py:344
  49.6 20.0 %collective-permute-start.12 = (bf16[128,1024]{1,0:T(8,128)(2,1)S(1)}, bf16[128,1024]{1,0:T(8,128)(2,1)S(1)}, u32[]{:S(2)}, u32[]{:S(2)}) collective-permute-start(bf16[128,1024]{1,0:T(8,128)(2,1)S(1)} %collective-permute-done.11.refs_4_), channel_id=1, source_target_pairs={{0,1},{1,0},{2,3},{3,2},{4,5},{5,4},{6,7},{7,6},{8,9},{9,8},{10,11... | collective-permute-start | bytes 786440 | tf_op jit(solution)/shard_map/ppermute | solution.py:344
  50.2 19.3 %collective-permute-start.14 = (bf16[128,1024]{1,0:T(8,128)(2,1)S(1)}, bf16[128,1024]{1,0:T(8,128)(2,1)S(1)}, u32[]{:S(2)}, u32[]{:S(2)}) collective-permute-start(bf16[128,1024]{1,0:T(8,128)(2,1)S(1)} %collective-permute-done.13.refs_6_), channel_id=1, source_target_pairs={{0,1},{1,0},{2,3},{3,2},{4,5},{5,4},{6,7},{7,6},{8,9},{9,8},{10,11... | collective-permute-start | bytes 786440 | tf_op jit(solution)/shard_map/ppermute | solution.py:344
  56.5 13.0 %collective-permute-start.10 = (bf16[64,1024]{1,0:T(8,128)(2,1)S(1)}, bf16[64,1024]{1,0:T(8,128)(2,1)S(1)}, u32[]{:S(2)}, u32[]{:S(2)}) collective-permute-start(bf16[64,1024]{1,0:T(8,128)(2,1)S(1)} %collective-permute-done.8.refs_1_), channel_id=1, source_target_pairs={{0,1},{1,0},{2,3},{3,2},{4,5},{5,4},{6,7},{7,6},{8,9},{9,8},{10,11... | collective-permute-start | bytes 393224 | tf_op jit(solution)/shard_map/ppermute | solution.py:344
  60.5 9.0 %collective-permute-start.17 = (bf16[64,1024]{1,0:T(8,128)(2,1)S(1)}, bf16[64,1024]{1,0:T(8,128)(2,1)S(1)}, u32[]{:S(2)}, u32[]{:S(2)}) collective-permute-start(bf16[64,1024]{1,0:T(8,128)(2,1)S(1)} %collective-permute-done.15.refs_8_), channel_id=1, source_target_pairs={{0,1},{1,0},{2,3},{3,2},{4,5},{5,4},{6,7},{7,6},{8,9},{9,8},{10,11... | collective-permute-start | bytes 393224 | tf_op jit(solution)/shard_map/ppermute | solution.py:344
  64.0 5.5 %collective-permute-start.18 = (bf16[64,1024]{1,0:T(8,128)(2,1)S(1)}, bf16[64,1024]{1,0:T(8,128)(2,1)S(1)}, u32[]{:S(2)}, u32[]{:S(2)}) collective-permute-start(bf16[64,1024]{1,0:T(8,128)(2,1)S(1)} %collective-permute-done.16.refs_9_), channel_id=1, source_target_pairs={{0,1},{1,0},{2,3},{3,2},{4,5},{5,4},{6,7},{7,6},{8,9},{9,8},{10,11... | collective-permute-start | bytes 393224 | tf_op jit(solution)/shard_map/ppermute | solution.py:344
  81.7 3.9 %collective-permute-start.21 = (f32[144,128]{1,0:T(8,128)S(1)}, f32[144,128]{1,0:T(8,128)S(1)}, u32[]{:S(2)}, u32[]{:S(2)}) collective-permute-start(f32[144,128]{1,0:T(8,128)S(1)} %join.3.a_ref), channel_id=1, source_target_pairs={{0,2},{1,3},{2,0},{3,1},{4,6},{5,7},{6,4},{7,5},{8,10},{9,11},{10,... | collective-permute-start | bytes 221192 | tf_op jit(solution)/shard_map/ppermute | solution.py:344
  81.8 5.2 %collective-permute-start.22 = (f32[144,128]{1,0:T(8,128)S(1)}, f32[144,128]{1,0:T(8,128)S(1)}, u32[]{:S(2)}, u32[]{:S(2)}) collective-permute-start(f32[144,128]{1,0:T(8,128)S(1)} %join.3.a_ref), channel_id=1, source_target_pairs={{0,4},{1,5},{2,6},{3,7},{4,0},{5,1},{6,2},{7,3},{8,12},{9,13},{10,... | collective-permute-start | bytes 221192 | tf_op jit(solution)/shard_map/ppermute | solution.py:344
  84.3 4.9 %collective-permute-start.23 = (f32[144,128]{1,0:T(8,128)S(1)}, f32[144,128]{1,0:T(8,128)S(1)}, u32[]{:S(2)}, u32[]{:S(2)}) collective-permute-start(f32[144,128]{1,0:T(8,128)S(1)} %join.3.a_ref), channel_id=1, source_target_pairs={{0,6},{1,7},{2,4},{3,5},{4,2},{5,3},{6,0},{7,1},{8,14},{9,15},{10,... | collective-permute-start | bytes 221192 | tf_op jit(solution)/shard_map/ppermute | solution.py:344
  (12 other events, 95.7 us)
where the time goes:
time: 94.2 us; the launch traced here: 93.8 us
  starting transfers between devices  42.8 us (45%)
  waiting for transfers between devices  24.8 us (26%)
  Pallas kernels  20.2 us (21%)
  local copies, waits for them, and re-layouts  5.12 us (5%)
    ppermute x25, starting transfers between devices, swap(): return lax.ppermute(x, 'cent', [(i, i ^ offset) for i in range(16)])  25.6 us
    ppermute x25, waiting for transfers between devices, swap(): return lax.ppermute(x, 'cent', [(i, i ^ offset) for i in range(16)])  24.8 us
    pallas_call x3, Pallas kernels, nearest(): pl.pallas_call(functools.partial(nearest_kernel, len(xs), first), out_sha...  14 us
    all_to_all x1, starting transfers between devices, step(): sub = lax.all_to_all(stacked, 'rows', 0, 0)  9.86 us
    all_to_all x1, starting transfers between devices, step(): fetched = lax.all_to_all(sent, 'cent', 0, 0).reshape(peers * slots, width)  7.33 us
    unnamed x18, local copies, waits for them, and re-layouts  5.1 us
    pallas_call x1, Pallas kernels, gather(): pl.pallas_call(functools.partial(gather_kernel, slots), out_shape=pltpu.V...  2.24 us
  transfers between devices with their start and end apart: 27, of which 9 were waited for; matrix products, arithmetic and copies ran while one was open for 0% of the time, Pallas kernels for 17%

commit v1 on v0

--- a/solution.py
+++ b/solution.py
@@ -12,7 +12,12 @@
 f32 = jnp.float32
 prior_weight = 8.0
 VM = pl.BlockSpec(memory_space=pltpu.VMEM)
+HBM = pl.BlockSpec(memory_space=pltpu.HBM)
 LIMIT = pltpu.CompilerParams(vmem_limit_bytes=16 << 20)
+
+
+def off_chip(x):
+    return pltpu.with_memory_space_constraint(x, pltpu.HBM)
 
 
 def on_chip(x):
@@ -23,13 +28,23 @@
 PAY = 144
 
 
-def quantize_kernel(values_ref, scales_t_ref, q_ref, squares_ref):
-    scales = scales_t_ref[...].astype(f32).T
+def quantize_kernel(values_hbm, scales_hbm, top_ref, bottom_ref, squares_ref, values, scales_t, sems):
+    copies = (
+        pltpu.make_async_copy(values_hbm, values, sems.at[0]),
+        pltpu.make_async_copy(scales_hbm, scales_t, sems.at[1]),
+    )
+    for copy in copies:
+        copy.start()
+    for copy in copies:
+        copy.wait()
+    half = top_ref.shape[0]
+    scales = scales_t[...].astype(f32).T
     squares = None
     for b in range(scales.shape[1]):
         lanes = slice(128 * b, 128 * b + 128)
-        q = (values_ref[:, lanes].astype(f32) * scales[:, b : b + 1]).astype(bf16)
-        q_ref[:, lanes] = q
+        q = (values[:, lanes].astype(f32) * scales[:, b : b + 1]).astype(bf16)
+        top_ref[:, lanes] = q[:half]
+        bottom_ref[:, lanes] = q[half:]
         wide = q.astype(f32)
         squares = wide * wide if squares is None else squares + wide * wide
     squares_ref[...] = jnp.sum(squares.T, axis=0, keepdims=True)
@@ -37,24 +52,41 @@
 
 def quantize(values, scales):
     rows, width = values.shape
+    scales = scales.T
     return pl.pallas_call(
         quantize_kernel,
         out_shape=(
-            pltpu.VMEM((rows, width), bf16),
+            pltpu.VMEM((rows // 2, width), bf16),
+            pltpu.VMEM((rows // 2, width), bf16),
             pltpu.VMEM((1, rows), f32),
         ),
-        in_specs=[VM, VM],
-        out_specs=(VM, VM),
+        in_specs=[HBM, HBM],
+        out_specs=(VM, VM, VM),
+        scratch_shapes=[
+            pltpu.VMEM(values.shape, bf16),
+            pltpu.VMEM(scales.shape, bf16),
+            pltpu.SemaphoreType.DMA((2,)),
+        ],
         cost_estimate=pl.CostEstimate(flops=rows * width * 3, bytes_accessed=rows * width * 4, transcendentals=0),
         compiler_params=LIMIT,
         name="quantize",
-    )(values, scales.T)
-
-
-def gather_kernel(slots, ids_ref, cents_ref, out_ref, onehot_ref):
-    count = cents_ref.shape[0]
+    )(off_chip(values), off_chip(scales))
+
+
+def gather_kernel(slots, step, ids_hbm, cents_hbm, out_ref, ids_ref, cents_ref, onehot_ref, sems):
+    count, width = cents_hbm.shape
     groups, rows = ids_ref.shape
-
+    ids_copy = pltpu.make_async_copy(ids_hbm, ids_ref, sems.at[width // step])
+    ids_copy.start()
+    copies = [
+        pltpu.make_async_copy(
+            cents_hbm.at[:, pl.ds(step * j, step)], cents_ref.at[j], sems.at[j]
+        )
+        for j in range(width // step)
+    ]
+    for copy in copies:
+        copy.start()
+    ids_copy.wait()
     local = ids_ref[...] - lax.axis_index("cent") * count
     mine = (local >= 0) & (local < count)
     before = lax.broadcasted_iota(jnp.int32, (rows, rows), 0) <= lax.broadcasted_iota(
@@ -77,32 +109,39 @@
     for j in range(count // 256):
         at = lax.broadcasted_iota(jnp.int32, (groups * slots, 256), 1) + 256 * j
         onehot_ref[:, 256 * j : 256 * j + 256] = (at == chosen).astype(f32).astype(bf16)
-    for j in range(cents_ref.shape[1] // 256):
-        lanes = slice(256 * j, 256 * j + 256)
+    for j, copy in enumerate(copies):
+        copy.wait()
+        lanes = slice(step * j, step * j + step)
         out_ref[:, lanes] = jnp.dot(
-            onehot_ref[...], cents_ref[:, lanes], preferred_element_type=f32
+            onehot_ref[...], cents_ref[j], preferred_element_type=f32
         ).astype(bf16)
 
 
 def gather(ids, cents, slots):
     groups, _ = ids.shape
     count, width = cents.shape
-    return pl.pallas_call(
-        functools.partial(gather_kernel, slots),
+    step = 256
+    return pl.pallas_call(
+        functools.partial(gather_kernel, slots, step),
         out_shape=pltpu.VMEM((groups * slots, width), bf16),
-        in_specs=[VM, VM],
+        in_specs=[HBM, HBM],
         out_specs=VM,
-        scratch_shapes=[pltpu.VMEM((groups * slots, count), bf16)],
+        scratch_shapes=[
+            pltpu.VMEM(ids.shape, jnp.int32),
+            pltpu.VMEM((width // step, count, step), bf16),
+            pltpu.VMEM((groups * slots, count), bf16),
+            pltpu.SemaphoreType.DMA((width // step + 1,)),
+        ],
         cost_estimate=pl.CostEstimate(
             flops=2 * groups * slots * count * width, bytes_accessed=count * width * 2, transcendentals=0
         ),
         compiler_params=LIMIT,
         name="gather",
-    )(ids, on_chip(cents))
-
-
-def residual_kernel(count, slots, ids_ref, fetched_ref, q_ref, out_ref):
-    rows, width = q_ref.shape
+    )(off_chip(ids), off_chip(cents))
+
+
+def residual_kernel(count, slots, ids_ref, fetched_ref, top_ref, bottom_ref, out_ref):
+    width, rows = out_ref.shape
     ids = ids_ref[pl.ds(lax.axis_index("cent"), 1), :]
     owner = lax.div(ids, count)
     across = jnp.broadcast_to(owner, (rows, rows))
@@ -119,28 +158,35 @@
         fetched = lax.dot_general(
             place, fetched_ref[:, lanes], (((0,), (0,)), ((), ())), preferred_element_type=f32
         )
-        out_ref[lanes, :] = (q_ref[:, lanes].astype(f32) - fetched).T
+        q = jnp.concatenate([top_ref[:, lanes], bottom_ref[:, lanes]], axis=0)
+        out_ref[lanes, :] = (q.astype(f32) - fetched).T
 
 
 def residuals(ids, fetched, q, count, slots):
-    rows, width = q.shape
+    rows, width = 2 * q[0].shape[0], q[0].shape[1]
     return pl.pallas_call(
         functools.partial(residual_kernel, count, slots),
         out_shape=pltpu.VMEM((width, rows), f32),
-        in_specs=[VM] * 3,
+        in_specs=[VM] * 4,
         out_specs=VM,
         cost_estimate=pl.CostEstimate(
-            flops=2 * fetched.size * rows, bytes_accessed=fetched.size * 2 + q.size * 6, transcendentals=0
+            flops=2 * fetched.size * rows, bytes_accessed=fetched.size * 2 + rows * width * 6, transcendentals=0
         ),
         compiler_params=LIMIT,
         name="residuals",
-    )(ids, on_chip(fetched), on_chip(q))
-
-
-def nearest_kernel(blocks, first, *refs):
-    x_refs, refs = refs[:blocks], refs[blocks:]
-    cents_ref, squares_ref, out_ref = refs if not first else (refs[0], refs[2], refs[1])
-    step = 256
+    )(ids, on_chip(fetched), *[on_chip(x) for x in q])
+
+
+def nearest_kernel(step, *refs):
+    x_refs, (cents_hbm, out_ref, cents_ref, sems) = refs[:-4], refs[-4:]
+    steps = cents_ref.shape[0]
+
+    def copy(i):
+        at = pl.ds(pl.multiple_of(i * step, step), step)
+        return pltpu.make_async_copy(cents_hbm.at[at, :], cents_ref.at[i], sems.at[i])
+
+    for i in range(steps):
+        copy(i).start()
     groups = [[]]
     for ref in x_refs:
         if sum(r.shape[0] for r in groups[-1]) == 256:
@@ -148,19 +194,15 @@
         groups[-1].append(ref)
     out_ref[...] = jnp.full(out_ref.shape, jnp.inf, f32)
 
-    @pl.loop(0, cents_ref.shape[0] // step)
+    @pl.loop(0, steps)
     def _(i):
-        at = pl.ds(pl.multiple_of(i * step, step), step)
-        block = cents_ref[at, :]
-        if first:
-            total = None
-            for b in range(block.shape[1] // 128):
-                wide = block[:, 128 * b : 128 * b + 128].astype(f32)
-                total = wide * wide if total is None else total + wide * wide
-            squares = jnp.broadcast_to(jnp.sum(total, axis=1, keepdims=True), (step, 128))
-            squares_ref[at, :] = squares
-        else:
-            squares = squares_ref[at, :]
+        copy(i).wait()
+        block = cents_ref[i]
+        total = None
+        for b in range(block.shape[1] // 128):
+            wide = block[:, 128 * b : 128 * b + 128].astype(f32)
+            total = wide * wide if total is None else total + wide * wide
+        squares = jnp.broadcast_to(jnp.sum(total, axis=1, keepdims=True), (step, 128))
         squares = jnp.concatenate([squares, squares], axis=1)
         for j, group in enumerate(groups):
             x = jnp.concatenate([r[...] for r in group], axis=0)
@@ -171,22 +213,25 @@
                 out_ref[row, :] = jnp.minimum(out_ref[row, :], low[:, 128 * k : 128 * k + 128])
 
 
-def nearest(xs, cents, squares=None):
+def nearest(xs, cents):
     count, width = cents.shape
-    first = squares is None
     rows = sum(x.shape[0] for x in xs)
-    out_shape = pltpu.VMEM((rows // 128, 128), f32)
-    return pl.pallas_call(
-        functools.partial(nearest_kernel, len(xs), first),
-        out_shape=(out_shape, pltpu.VMEM((count, 128), f32)) if first else out_shape,
-        in_specs=[VM] * (len(xs) + (1 if first else 2)),
-        out_specs=(VM, VM) if first else VM,
+    step = 256
+    return pl.pallas_call(
+        functools.partial(nearest_kernel, step),
+        out_shape=pltpu.VMEM((rows // 128, 128), f32),
+        in_specs=[VM] * len(xs) + [HBM],
+        out_specs=VM,
+        scratch_shapes=[
+            pltpu.VMEM((count // step, step, width), bf16),
+            pltpu.SemaphoreType.DMA((count // step,)),
+        ],
         cost_estimate=pl.CostEstimate(
             flops=2 * rows * count * width, bytes_accessed=count * width * 2 + rows * width * 2, transcendentals=0
         ),
         compiler_params=LIMIT,
         name="nearest",
-    )(*[on_chip(x) for x in xs], on_chip(cents), *([] if first else [on_chip(squares)]))
+    )(*[on_chip(x) for x in xs], off_chip(cents))
 
 
 def halves_of(x):
@@ -350,32 +395,36 @@
     sub_width = codebook_init.shape[2]
     peers = coarse_ids.shape[0]
     slots = 16
-    half = own_rows // 2
-
-    centroids = on_chip(centroids)
-    q, row_squares = quantize(emb_values, emb_scales)
+
+    *q, row_squares = quantize(emb_values, emb_scales)
 
     core = 1
 
-    a, b, z = swap(q, 2), swap(q, 6), swap(q, 8)
-    blocks = {0: [q], core: [swap(q, core)], 2: [a], 6: [b], 8: [z]}
-
-    sent = gather(coarse_ids, centroids, slots).reshape(peers, slots, width)
-    fetched = lax.all_to_all(sent, "cent", 0, 0).reshape(peers * slots, width)
-
-    blocks[4] = [swap(b[:half], 2), swap(a[half:], 6)]
-    blocks[10], blocks[14] = [swap(z, 2)], [swap(z, 6)]
-    blocks[12] = [swap(x, 8) for x in blocks[4]]
+    def hop(xs, offset):
+        out = []
+        for x in xs:
+            out.append(swap(x, offset))
+        return out
+
+    a = hop(q[::-1], 2)[::-1]
+    b = hop(q, 6)
+    z = hop(q, 8)
+    blocks = {0: q, core: hop(q, core), 2: a, 6: b, 8: z}
+
+    sent = gather(coarse_ids, centroids, slots)
+    fetched = lax.all_to_all(sent.reshape(peers, slots, width), "cent", 0, 0)
+    fetched = fetched.reshape(peers * slots, width)
+
+    blocks[4] = hop(b[:1], 2) + hop(a[1:], 6)
+    blocks[10], blocks[14] = hop(z, 2), hop(z, 6)
+    blocks[12] = hop(blocks[14][:1], 2) + hop(blocks[10][1:], 6)
     for d in (2, 6, 8, 4, 10, 14, 12):
-        blocks[d ^ core] = [swap(x, core) for x in blocks[d]]
-
-    def near(order, squares=None):
-        xs = [x for d in order for x in blocks[d]]
-        return nearest(xs, centroids, squares)
+        blocks[d ^ core] = hop(blocks[d], core)
 
     orders = ((0, 1, 2, 3), (6, 7, 8, 9), (4, 5, 10, 11, 14, 15, 12, 13))
-    first, cent_squares = near(orders[0])
-    lows = [first] + [near(orders[k], cent_squares) for k in (1, 2)]
+    lows = []
+    for order in orders:
+        lows.append(nearest([x for d in order for x in blocks[d]], centroids))
     where = {d: (k, j) for k, order in enumerate(orders) for j, d in enumerate(order)}
 
     residual = residuals(coarse_ids, fetched, q, count, slots)

time: 94.2 us -> 94.6 us (level)
  waiting for transfers between devices: 24.8 us -> 13.3 us
  starting transfers between devices: 42.8 us -> 52.5 us
  Pallas kernels: 20.2 us -> 27.6 us
  local copies, waits for them, and re-layouts: 5.12 us -> 0.02 us
    ppermute x25 -> x36, waiting for transfers between devices: 24.8 us -> 13.3 us  [swap(): return lax.ppermute(x, 'cent', [(i, i ^ offset) for i in range(16)])]
    ppermute x25 -> x36, starting transfers between devices: 25.6 us -> 35.3 us  [swap(): return lax.ppermute(x, 'cent', [(i, i ^ offset) for i in range(16)])]
    pallas_call x5, Pallas kernels: 16.6 us -> 23.9 us  [the longest x3 17.8 us: nearest(): pl.pallas_call(functools.partial(nearest_kernel, step), out_shape=pltpu.V...]
    unnamed x18 -> x8, local copies, waits for them, and re-layouts: 5.1 us -> 0.02 us
  transfers between devices with their start and end apart: 27 -> 38, of which waited for: 9 -> 8; matrix products, arithmetic and copies ran while one was open for 0% -> 0% of each run, Pallas kernels for 17% -> 22%
where the time goes in v1:
time: 94.6 us; the launch traced here: 94.2 us
  starting transfers between devices  52.5 us (55%)
  Pallas kernels  27.6 us (29%)
  waiting for transfers between devices  13.3 us (14%)
    ppermute x36, starting transfers between devices, swap(): return lax.ppermute(x, 'cent', [(i, i ^ offset) for i in range(16)])  35.3 us
    pallas_call x3, Pallas kernels, nearest(): pl.pallas_call(functools.partial(nearest_kernel, step), out_shape=pltpu.V...  17.8 us
    ppermute x36, waiting for transfers between devices, swap(): return lax.ppermute(x, 'cent', [(i, i ^ offset) for i in range(16)])  13.3 us
    all_to_all x1, starting transfers between devices, step(): sub = lax.all_to_all(stacked, 'rows', 0, 0)  9.85 us
    all_to_all x1, starting transfers between devices, step(): fetched = lax.all_to_all(sent.reshape(peers, slots, width), 'cent', 0, 0)  7.34 us
    pallas_call x1, Pallas kernels, gather(): pl.pallas_call(functools.partial(gather_kernel, slots, step), out_shape=p...  4.85 us
  transfers between devices with their start and end apart: 38, of which 8 were waited for; matrix products, arithmetic and copies ran while one was open for 0% of the time, Pallas kernels for 22%

profile of v1, /device:TPU:1, one launch (start us, length us, event | category | flops | bytes accessed | tf_op | source)
XLA Modules:
  0.0 94.2 jit_solution(4437394558647163875)
XLA Ops:
  0.6 4.8 %gather.1 = bf16[256,1024]{1,0:T(8,128)(2,1)} custom-call(s32[16,128]{1,0:T(8,128)} %ids_ref.1, bf16[2048,1024]{1,0:T(8,128)(2,1)} %refs_16_.1), custom_call_target="tpu_custom_call" | custom-call | flops 1073741824 | bytes 4194304 | tf_op jit(solution)/shard_map/gather/pallas_call | solution.py:124
  5.5 7.3 %all-to-all-start = ((bf16[16,16,1024]{2,1,0:T(8,128)(2,1)}), bf16[16,16,1024]{2,1,0:T(8,128)(2,1)S(1)}, u32[]{:S(2)}, u32[]{:S(2)}) async-start(bf16[16,16,1024]{2,1,0:T(8,128)(2,1)} %bitcast), calls=%async_computation | async-start | bytes 1048576 | tf_op jit(solution)/shard_map/all_to_all | solution.py:415
  14.8 1.4 %collective-permute-start.2 = (bf16[64,1024]{1,0:T(8,128)(2,1)S(1)}, bf16[64,1024]{1,0:T(8,128)(2,1)S(1)}, u32[]{:S(2)}, u32[]{:S(2)}) collective-permute-start(bf16[64,1024]{1,0:T(8,128)(2,1)S(1)} %get-tuple-element.14.top_ref.refs_0_), channel_id=1, source_target_pairs={{0,2},{1,3},{2,0},{3,1},{4,6},{5,7},{6,4},{7,5},{8,10},{9,11},{10,... | collective-permute-start | bytes 393224 | tf_op jit(solution)/shard_map/ppermute | solution.py:389
  16.2 2.6 %collective-permute-start.6 = (bf16[64,1024]{1,0:T(8,128)(2,1)S(1)}, bf16[64,1024]{1,0:T(8,128)(2,1)S(1)}, u32[]{:S(2)}, u32[]{:S(2)}) collective-permute-start(bf16[64,1024]{1,0:T(8,128)(2,1)S(1)} %get-tuple-element.14.top_ref.refs_0_), channel_id=1, source_target_pairs={{0,6},{1,7},{2,4},{3,5},{4,2},{5,3},{6,0},{7,1},{8,14},{9,15},{10,... | collective-permute-start | bytes 393224 | tf_op jit(solution)/shard_map/ppermute | solution.py:389
  18.9 1.4 %collective-permute-start.10 = (bf16[64,1024]{1,0:T(8,128)(2,1)S(1)}, bf16[64,1024]{1,0:T(8,128)(2,1)S(1)}, u32[]{:S(2)}, u32[]{:S(2)}) collective-permute-start(bf16[64,1024]{1,0:T(8,128)(2,1)S(1)} %get-tuple-element.14.top_ref.refs_0_), channel_id=1, source_target_pairs={{0,8},{1,9},{2,10},{3,11},{4,12},{5,13},{6,14},{7,15},{8,0},{9,1},... | collective-permute-start | bytes 393224 | tf_op jit(solution)/shard_map/ppermute | solution.py:389
  20.3 3.2 %collective-permute-done.2.refs_4_ = bf16[64,1024]{1,0:T(8,128)(2,1)S(1)} collective-permute-done((bf16[64,1024]{1,0:T(8,128)(2,1)S(1)}, bf16[64,1024]{1,0:T(8,128)(2,1)S(1)}, u32[]{:S(2)}, u32[]{:S(2)}) %collective-permute-start.2) | collective-permute-done | bytes 131104 | tf_op jit(solution)/shard_map/ppermute | solution.py:389
  23.5 1.5 %collective-permute-start.11 = (bf16[64,1024]{1,0:T(8,128)(2,1)S(1)}, bf16[64,1024]{1,0:T(8,128)(2,1)S(1)}, u32[]{:S(2)}, u32[]{:S(2)}) collective-permute-start(bf16[64,1024]{1,0:T(8,128)(2,1)S(1)} %get-tuple-element.15.bottom_ref.refs_1_), channel_id=1, source_target_pairs={{0,8},{1,9},{2,10},{3,11},{4,12},{5,13},{6,14},{7,15},{8,0},{9,1},... | collective-permute-start | bytes 393224 | tf_op jit(solution)/shard_map/ppermute | solution.py:389
  28.5 1.5 %collective-permute-start.12 = (bf16[64,1024]{1,0:T(8,128)(2,1)S(1)}, bf16[64,1024]{1,0:T(8,128)(2,1)S(1)}, u32[]{:S(2)}, u32[]{:S(2)}) collective-permute-start(bf16[64,1024]{1,0:T(8,128)(2,1)S(1)} %collective-permute-done.10.refs_4_), channel_id=1, source_target_pairs={{0,1},{1,0},{2,3},{3,2},{4,5},{5,4},{6,7},{7,6},{8,9},{9,8},{10,11... | collective-permute-start | bytes 393224 | tf_op jit(solution)/shard_map/ppermute | solution.py:389
  31.5 9.8 %all-to-all-start.1 = ((f32[16,64,128]{2,1,0:T(8,128)}), f32[16,64,128]{2,1,0:T(8,128)S(1)}, u32[]{:S(2)}, u32[]{:S(2)}) async-start(f32[16,64,128]{2,1,0:T(8,128)} %bitcast.3), calls=%async_computation.1 | async-start | bytes 1048576 | tf_op jit(solution)/shard_map/all_to_all | solution.py:432
  41.3 2.7 %collective-permute-start.15 = (bf16[64,1024]{1,0:T(8,128)(2,1)S(1)}, bf16[64,1024]{1,0:T(8,128)(2,1)S(1)}, u32[]{:S(2)}, u32[]{:S(2)}) collective-permute-start(bf16[64,1024]{1,0:T(8,128)(2,1)S(1)} %collective-permute-done.3.refs_5_), channel_id=1, source_target_pairs={{0,6},{1,7},{2,4},{3,5},{4,2},{5,3},{6,0},{7,1},{8,14},{9,15},{10,... | collective-permute-start | bytes 393224 | tf_op jit(solution)/shard_map/ppermute | solution.py:389
  44.1 1.5 %collective-permute-start.19 = (bf16[64,1024]{1,0:T(8,128)(2,1)S(1)}, bf16[64,1024]{1,0:T(8,128)(2,1)S(1)}, u32[]{:S(2)}, u32[]{:S(2)}) collective-permute-start(bf16[64,1024]{1,0:T(8,128)(2,1)S(1)} %collective-permute-done.11.refs_5_), channel_id=1, source_target_pairs={{0,2},{1,3},{2,0},{3,1},{4,6},{5,7},{6,4},{7,5},{8,10},{9,11},{10,... | collective-permute-start | bytes 393224 | tf_op jit(solution)/shard_map/ppermute | solution.py:389
  45.8 2.4 %collective-permute-start.23 = (bf16[64,1024]{1,0:T(8,128)(2,1)S(1)}, bf16[64,1024]{1,0:T(8,128)(2,1)S(1)}, u32[]{:S(2)}, u32[]{:S(2)}) collective-permute-start(bf16[64,1024]{1,0:T(8,128)(2,1)S(1)} %collective-permute-done.11.refs_5_), channel_id=1, source_target_pairs={{0,6},{1,7},{2,4},{3,5},{4,2},{5,3},{6,0},{7,1},{8,14},{9,15},{10,... | collective-permute-start | bytes 393224 | tf_op jit(solution)/shard_map/ppermute | solution.py:389
  48.2 2.4 %collective-permute-start.16 = (bf16[64,1024]{1,0:T(8,128)(2,1)S(1)}, bf16[64,1024]{1,0:T(8,128)(2,1)S(1)}, u32[]{:S(2)}, u32[]{:S(2)}) collective-permute-start(bf16[64,1024]{1,0:T(8,128)(2,1)S(1)} %collective-permute-done.14.refs_0_), channel_id=1, source_target_pairs={{0,1},{1,0},{2,3},{3,2},{4,5},{5,4},{6,7},{7,6},{8,9},{9,8},{10,11... | collective-permute-start | bytes 393224 | tf_op jit(solution)/shard_map/ppermute | solution.py:389
  51.4 1.4 %collective-permute-start.20 = (bf16[64,1024]{1,0:T(8,128)(2,1)S(1)}, bf16[64,1024]{1,0:T(8,128)(2,1)S(1)}, u32[]{:S(2)}, u32[]{:S(2)}) collective-permute-start(bf16[64,1024]{1,0:T(8,128)(2,1)S(1)} %collective-permute-done.18.refs_4_), channel_id=1, source_target_pairs={{0,1},{1,0},{2,3},{3,2},{4,5},{5,4},{6,7},{7,6},{8,9},{9,8},{10,11... | collective-permute-start | bytes 393224 | tf_op jit(solution)/shard_map/ppermute | solution.py:389
  52.9 2.5 %collective-permute-start.27 = (bf16[64,1024]{1,0:T(8,128)(2,1)S(1)}, bf16[64,1024]{1,0:T(8,128)(2,1)S(1)}, u32[]{:S(2)}, u32[]{:S(2)}) collective-permute-start(bf16[64,1024]{1,0:T(8,128)(2,1)S(1)} %collective-permute-done.19.refs_5_), channel_id=1, source_target_pairs={{0,6},{1,7},{2,4},{3,5},{4,2},{5,3},{6,0},{7,1},{8,14},{9,15},{10,... | collective-permute-start | bytes 393224 | tf_op jit(solution)/shard_map/ppermute | solution.py:389
  55.4 5.2 %nearest.3.refs_0_ = f32[4,128]{1,0:T(4,128)S(1)} custom-call(bf16[64,1024]{1,0:T(8,128)(2,1)S(1)} %get-tuple-element.14.top_ref.refs_0_, bf16[64,1024]{1,0:T(8,128)(2,1)S(1)} %get-tuple-element.15.bottom_ref.refs_1_, bf16[64,1024]{1,0:T(8,128)(2,1)S(1)} %collective-permute-done.refs_2_, bf16[64,1024]{1,0:T(8,128)(2,1)S(1)} %collective-permute-done.1.refs_3_, ...), custom_call_target="tpu_custom_call" | custom-call | flops 2147483648 | bytes 5242880 | tf_op jit(solution)/shard_map/nearest/pallas_call | solution.py:220
  60.6 1.9 %collective-permute-start.21 = (bf16[64,1024]{1,0:T(8,128)(2,1)S(1)}, bf16[64,1024]{1,0:T(8,128)(2,1)S(1)}, u32[]{:S(2)}, u32[]{:S(2)}) collective-permute-start(bf16[64,1024]{1,0:T(8,128)(2,1)S(1)} %collective-permute-done.19.refs_5_), channel_id=1, source_target_pairs={{0,1},{1,0},{2,3},{3,2},{4,5},{5,4},{6,7},{7,6},{8,9},{9,8},{10,11... | collective-permute-start | bytes 393224 | tf_op jit(solution)/shard_map/ppermute | solution.py:389
  63.5 5.2 %nearest.4.refs_1_ = f32[4,128]{1,0:T(4,128)S(1)} custom-call(bf16[64,1024]{1,0:T(8,128)(2,1)S(1)} %collective-permute-done.6.refs_0_, bf16[64,1024]{1,0:T(8,128)(2,1)S(1)} %collective-permute-done.7.refs_1_, bf16[64,1024]{1,0:T(8,128)(2,1)S(1)} %collective-permute-done.8.refs_2_, bf16[64,1024]{1,0:T(8,128)(2,1)S(1)} %collective-permute-done.9.refs_3_, ...), custom_call_target="tpu_custom_call" | custom-call | flops 2147483648 | bytes 5242880 | tf_op jit(solution)/shard_map/nearest/pallas_call | solution.py:220
  68.8 7.4 %nearest.5.refs_2_ = f32[8,128]{1,0:T(8,128)S(1)} custom-call(bf16[64,1024]{1,0:T(8,128)(2,1)S(1)} %collective-permute-done.14.refs_0_, bf16[64,1024]{1,0:T(8,128)(2,1)S(1)} %collective-permute-done.15.refs_1_, bf16[64,1024]{1,0:T(8,128)(2,1)S(1)} %collective-permute-done.16.refs_2_, bf16[64,1024]{1,0:T(8,128)(2,1)S(1)} %collective-permute-done.17.refs_3_, ...), custom_call_target="tpu_custom_call" | custom-call | flops 4294967296 | bytes 6291456 | tf_op jit(solution)/shard_map/nearest/pallas_call | solution.py:220
  79.6 2.6 %collective-permute-done.31.b_ref = f32[144,128]{1,0:T(8,128)S(1)} collective-permute-done((f32[144,128]{1,0:T(8,128)S(1)}, f32[144,128]{1,0:T(8,128)S(1)}, u32[]{:S(2)}, u32[]{:S(2)}) %collective-permute-start.31) | collective-permute-done | bytes 73760 | tf_op jit(solution)/shard_map/ppermute | solution.py:389
  82.3 2.5 %collective-permute-start.33 = (f32[144,128]{1,0:T(8,128)S(1)}, f32[144,128]{1,0:T(8,128)S(1)}, u32[]{:S(2)}, u32[]{:S(2)}) collective-permute-start(f32[144,128]{1,0:T(8,128)S(1)} %join.3.a_ref), channel_id=1, source_target_pairs={{0,4},{1,5},{2,6},{3,7},{4,0},{5,1},{6,2},{7,3},{8,12},{9,13},{10,... | collective-permute-start | bytes 221192 | tf_op jit(solution)/shard_map/ppermute | solution.py:389
  84.7 1.4 %collective-permute-start.34 = (f32[144,128]{1,0:T(8,128)S(1)}, f32[144,128]{1,0:T(8,128)S(1)}, u32[]{:S(2)}, u32[]{:S(2)}) collective-permute-start(f32[144,128]{1,0:T(8,128)S(1)} %join.3.a_ref), channel_id=1, source_target_pairs={{0,6},{1,7},{2,4},{3,5},{4,2},{5,3},{6,0},{7,1},{8,14},{9,15},{10,... | collective-permute-start | bytes 221192 | tf_op jit(solution)/shard_map/ppermute | solution.py:389
  87.4 2.3 %collective-permute-done.34.d_ref = f32[144,128]{1,0:T(8,128)S(1)} collective-permute-done((f32[144,128]{1,0:T(8,128)S(1)}, f32[144,128]{1,0:T(8,128)S(1)}, u32[]{:S(2)}, u32[]{:S(2)}) %collective-permute-start.34) | collective-permute-done | bytes 73760 | tf_op jit(solution)/shard_map/ppermute | solution.py:389
  90.2 2.2 %collective-permute-start.35 = (f32[128,128]{1,0:T(8,128)S(1)}, f32[128,128]{1,0:T(8,128)S(1)}, u32[]{:S(2)}, u32[]{:S(2)}) collective-permute-start(f32[128,128]{1,0:T(8,128)S(1)} %get-tuple-element.20.mine_ref), channel_id=1, source_target_pairs={{0,1},{1,0},{2,3},{3,2},{4,5},{5,4},{6,7},{7,6},{8,9},{9,8},{10,11... | collective-permute-start | bytes 196616 | tf_op jit(solution)/shard_map/ppermute | solution.py:389
  (71 shorter events, 16.4 us)
Async XLA Ops:
  5.5 24.6 %all-to-all-start = ((bf16[16,16,1024]{2,1,0:T(8,128)(2,1)}), bf16[16,16,1024]{2,1,0:T(8,128)(2,1)S(1)}, u32[]{:S(2)}, u32[]{:S(2)}) async-start(bf16[16,16,1024]{2,1,0:T(8,128)(2,1)} %bitcast), calls=%async_computation | async-start | bytes 1048576 | tf_op jit(solution)/shard_map/all_to_all | solution.py:415
  14.8 8.7 %collective-permute-start.2 = (bf16[64,1024]{1,0:T(8,128)(2,1)S(1)}, bf16[64,1024]{1,0:T(8,128)(2,1)S(1)}, u32[]{:S(2)}, u32[]{:S(2)}) collective-permute-start(bf16[64,1024]{1,0:T(8,128)(2,1)S(1)} %get-tuple-element.14.top_ref.refs_0_), channel_id=1, source_target_pairs={{0,2},{1,3},{2,0},{3,1},{4,6},{5,7},{6,4},{7,5},{8,10},{9,11},{10,... | collective-permute-start | bytes 393224 | tf_op jit(solution)/shard_map/ppermute | solution.py:389
  16.1 10.2 %collective-permute-start.3 = (bf16[64,1024]{1,0:T(8,128)(2,1)S(1)}, bf16[64,1024]{1,0:T(8,128)(2,1)S(1)}, u32[]{:S(2)}, u32[]{:S(2)}) collective-permute-start(bf16[64,1024]{1,0:T(8,128)(2,1)S(1)} %get-tuple-element.15.bottom_ref.refs_1_), channel_id=1, source_target_pairs={{0,2},{1,3},{2,0},{3,1},{4,6},{5,7},{6,4},{7,5},{8,10},{9,11},{10,... | collective-permute-start | bytes 393224 | tf_op jit(solution)/shard_map/ppermute | solution.py:389
  16.2 11.0 %collective-permute-start.6 = (bf16[64,1024]{1,0:T(8,128)(2,1)S(1)}, bf16[64,1024]{1,0:T(8,128)(2,1)S(1)}, u32[]{:S(2)}, u32[]{:S(2)}) collective-permute-start(bf16[64,1024]{1,0:T(8,128)(2,1)S(1)} %get-tuple-element.14.top_ref.refs_0_), channel_id=1, source_target_pairs={{0,6},{1,7},{2,4},{3,5},{4,2},{5,3},{6,0},{7,1},{8,14},{9,15},{10,... | collective-permute-start | bytes 393224 | tf_op jit(solution)/shard_map/ppermute | solution.py:389
  18.8 9.1 %collective-permute-start.7 = (bf16[64,1024]{1,0:T(8,128)(2,1)S(1)}, bf16[64,1024]{1,0:T(8,128)(2,1)S(1)}, u32[]{:S(2)}, u32[]{:S(2)}) collective-permute-start(bf16[64,1024]{1,0:T(8,128)(2,1)S(1)} %get-tuple-element.15.bottom_ref.refs_1_), channel_id=1, source_target_pairs={{0,6},{1,7},{2,4},{3,5},{4,2},{5,3},{6,0},{7,1},{8,14},{9,15},{10,... | collective-permute-start | bytes 393224 | tf_op jit(solution)/shard_map/ppermute | solution.py:389
  18.9 9.6 %collective-permute-start.10 = (bf16[64,1024]{1,0:T(8,128)(2,1)S(1)}, bf16[64,1024]{1,0:T(8,128)(2,1)S(1)}, u32[]{:S(2)}, u32[]{:S(2)}) collective-permute-start(bf16[64,1024]{1,0:T(8,128)(2,1)S(1)} %get-tuple-element.14.top_ref.refs_0_), channel_id=1, source_target_pairs={{0,8},{1,9},{2,10},{3,11},{4,12},{5,13},{6,14},{7,15},{8,0},{9,1},... | collective-permute-start | bytes 393224 | tf_op jit(solution)/shard_map/ppermute | solution.py:389
  27.9 13.5 %collective-permute-start.8 = (bf16[64,1024]{1,0:T(8,128)(2,1)S(1)}, bf16[64,1024]{1,0:T(8,128)(2,1)S(1)}, u32[]{:S(2)}, u32[]{:S(2)}) collective-permute-start(bf16[64,1024]{1,0:T(8,128)(2,1)S(1)} %collective-permute-done.6.refs_0_), channel_id=1, source_target_pairs={{0,1},{1,0},{2,3},{3,2},{4,5},{5,4},{6,7},{7,6},{8,9},{9,8},{10,11... | collective-permute-start | bytes 393224 | tf_op jit(solution)/shard_map/ppermute | solution.py:389
  28.5 15.6 %collective-permute-start.9 = (bf16[64,1024]{1,0:T(8,128)(2,1)S(1)}, bf16[64,1024]{1,0:T(8,128)(2,1)S(1)}, u32[]{:S(2)}, u32[]{:S(2)}) collective-permute-start(bf16[64,1024]{1,0:T(8,128)(2,1)S(1)} %collective-permute-done.7.refs_1_), channel_id=1, source_target_pairs={{0,1},{1,0},{2,3},{3,2},{4,5},{5,4},{6,7},{7,6},{8,9},{9,8},{10,11... | collective-permute-start | bytes 393224 | tf_op jit(solution)/shard_map/ppermute | solution.py:389
  28.5 15.6 %collective-permute-start.12 = (bf16[64,1024]{1,0:T(8,128)(2,1)S(1)}, bf16[64,1024]{1,0:T(8,128)(2,1)S(1)}, u32[]{:S(2)}, u32[]{:S(2)}) collective-permute-start(bf16[64,1024]{1,0:T(8,128)(2,1)S(1)} %collective-permute-done.10.refs_4_), channel_id=1, source_target_pairs={{0,1},{1,0},{2,3},{3,2},{4,5},{5,4},{6,7},{7,6},{8,9},{9,8},{10,11... | collective-permute-start | bytes 393224 | tf_op jit(solution)/shard_map/ppermute | solution.py:389
  30.0 15.6 %collective-permute-start.13 = (bf16[64,1024]{1,0:T(8,128)(2,1)S(1)}, bf16[64,1024]{1,0:T(8,128)(2,1)S(1)}, u32[]{:S(2)}, u32[]{:S(2)}) collective-permute-start(bf16[64,1024]{1,0:T(8,128)(2,1)S(1)} %collective-permute-done.11.refs_5_), channel_id=1, source_target_pairs={{0,1},{1,0},{2,3},{3,2},{4,5},{5,4},{6,7},{7,6},{8,9},{9,8},{10,11... | collective-permute-start | bytes 393224 | tf_op jit(solution)/shard_map/ppermute | solution.py:389
  30.0 15.8 %collective-permute-start.14 = (bf16[64,1024]{1,0:T(8,128)(2,1)S(1)}, bf16[64,1024]{1,0:T(8,128)(2,1)S(1)}, u32[]{:S(2)}, u32[]{:S(2)}) collective-permute-start(bf16[64,1024]{1,0:T(8,128)(2,1)S(1)} %collective-permute-done.6.refs_0_), channel_id=1, source_target_pairs={{0,2},{1,3},{2,0},{3,1},{4,6},{5,7},{6,4},{7,5},{8,10},{9,11},{10,... | collective-permute-start | bytes 393224 | tf_op jit(solution)/shard_map/ppermute | solution.py:389
  31.5 44.7 %all-to-all-start.1 = ((f32[16,64,128]{2,1,0:T(8,128)}), f32[16,64,128]{2,1,0:T(8,128)S(1)}, u32[]{:S(2)}, u32[]{:S(2)}) async-start(f32[16,64,128]{2,1,0:T(8,128)} %bitcast.3), calls=%async_computation.1 | async-start | bytes 1048576 | tf_op jit(solution)/shard_map/all_to_all | solution.py:432
  41.3 6.9 %collective-permute-start.15 = (bf16[64,1024]{1,0:T(8,128)(2,1)S(1)}, bf16[64,1024]{1,0:T(8,128)(2,1)S(1)}, u32[]{:S(2)}, u32[]{:S(2)}) collective-permute-start(bf16[64,1024]{1,0:T(8,128)(2,1)S(1)} %collective-permute-done.3.refs_5_), channel_id=1, source_target_pairs={{0,6},{1,7},{2,4},{3,5},{4,2},{5,3},{6,0},{7,1},{8,14},{9,15},{10,... | collective-permute-start | bytes 393224 | tf_op jit(solution)/shard_map/ppermute | solution.py:389
  44.1 6.6 %collective-permute-start.18 = (bf16[64,1024]{1,0:T(8,128)(2,1)S(1)}, bf16[64,1024]{1,0:T(8,128)(2,1)S(1)}, u32[]{:S(2)}, u32[]{:S(2)}) collective-permute-start(bf16[64,1024]{1,0:T(8,128)(2,1)S(1)} %collective-permute-done.10.refs_4_), channel_id=1, source_target_pairs={{0,2},{1,3},{2,0},{3,1},{4,6},{5,7},{6,4},{7,5},{8,10},{9,11},{10,... | collective-permute-start | bytes 393224 | tf_op jit(solution)/shard_map/ppermute | solution.py:389
  44.1 7.3 %collective-permute-start.19 = (bf16[64,1024]{1,0:T(8,128)(2,1)S(1)}, bf16[64,1024]{1,0:T(8,128)(2,1)S(1)}, u32[]{:S(2)}, u32[]{:S(2)}) collective-permute-start(bf16[64,1024]{1,0:T(8,128)(2,1)S(1)} %collective-permute-done.11.refs_5_), channel_id=1, source_target_pairs={{0,2},{1,3},{2,0},{3,1},{4,6},{5,7},{6,4},{7,5},{8,10},{9,11},{10,... | collective-permute-start | bytes 393224 | tf_op jit(solution)/shard_map/ppermute | solution.py:389
  45.6 7.3 %collective-permute-start.22 = (bf16[64,1024]{1,0:T(8,128)(2,1)S(1)}, bf16[64,1024]{1,0:T(8,128)(2,1)S(1)}, u32[]{:S(2)}, u32[]{:S(2)}) collective-permute-start(bf16[64,1024]{1,0:T(8,128)(2,1)S(1)} %collective-permute-done.10.refs_4_), channel_id=1, source_target_pairs={{0,6},{1,7},{2,4},{3,5},{4,2},{5,3},{6,0},{7,1},{8,14},{9,15},{10,... | collective-permute-start | bytes 393224 | tf_op jit(solution)/shard_map/ppermute | solution.py:389
  45.8 7.0 %collective-permute-start.23 = (bf16[64,1024]{1,0:T(8,128)(2,1)S(1)}, bf16[64,1024]{1,0:T(8,128)(2,1)S(1)}, u32[]{:S(2)}, u32[]{:S(2)}) collective-permute-start(bf16[64,1024]{1,0:T(8,128)(2,1)S(1)} %collective-permute-done.11.refs_5_), channel_id=1, source_target_pairs={{0,6},{1,7},{2,4},{3,5},{4,2},{5,3},{6,0},{7,1},{8,14},{9,15},{10,... | collective-permute-start | bytes 393224 | tf_op jit(solution)/shard_map/ppermute | solution.py:389
  48.2 12.3 %collective-permute-start.16 = (bf16[64,1024]{1,0:T(8,128)(2,1)S(1)}, bf16[64,1024]{1,0:T(8,128)(2,1)S(1)}, u32[]{:S(2)}, u32[]{:S(2)}) collective-permute-start(bf16[64,1024]{1,0:T(8,128)(2,1)S(1)} %collective-permute-done.14.refs_0_), channel_id=1, source_target_pairs={{0,1},{1,0},{2,3},{3,2},{4,5},{5,4},{6,7},{7,6},{8,9},{9,8},{10,11... | collective-permute-start | bytes 393224 | tf_op jit(solution)/shard_map/ppermute | solution.py:389
  50.6 11.8 %collective-permute-start.17 = (bf16[64,1024]{1,0:T(8,128)(2,1)S(1)}, bf16[64,1024]{1,0:T(8,128)(2,1)S(1)}, u32[]{:S(2)}, u32[]{:S(2)}) collective-permute-start(bf16[64,1024]{1,0:T(8,128)(2,1)S(1)} %collective-permute-done.15.refs_1_), channel_id=1, source_target_pairs={{0,1},{1,0},{2,3},{3,2},{4,5},{5,4},{6,7},{7,6},{8,9},{9,8},{10,11... | collective-permute-start | bytes 393224 | tf_op jit(solution)/shard_map/ppermute | solution.py:389
  51.4 11.1 %collective-permute-start.20 = (bf16[64,1024]{1,0:T(8,128)(2,1)S(1)}, bf16[64,1024]{1,0:T(8,128)(2,1)S(1)}, u32[]{:S(2)}, u32[]{:S(2)}) collective-permute-start(bf16[64,1024]{1,0:T(8,128)(2,1)S(1)} %collective-permute-done.18.refs_4_), channel_id=1, source_target_pairs={{0,1},{1,0},{2,3},{3,2},{4,5},{5,4},{6,7},{7,6},{8,9},{9,8},{10,11... | collective-permute-start | bytes 393224 | tf_op jit(solution)/shard_map/ppermute | solution.py:389
  52.8 10.1 %collective-permute-start.26 = (bf16[64,1024]{1,0:T(8,128)(2,1)S(1)}, bf16[64,1024]{1,0:T(8,128)(2,1)S(1)}, u32[]{:S(2)}, u32[]{:S(2)}) collective-permute-start(bf16[64,1024]{1,0:T(8,128)(2,1)S(1)} %collective-permute-done.22.refs_8_), channel_id=1, source_target_pairs={{0,2},{1,3},{2,0},{3,1},{4,6},{5,7},{6,4},{7,5},{8,10},{9,11},{10,... | collective-permute-start | bytes 393224 | tf_op jit(solution)/shard_map/ppermute | solution.py:389
  52.9 10.2 %collective-permute-start.27 = (bf16[64,1024]{1,0:T(8,128)(2,1)S(1)}, bf16[64,1024]{1,0:T(8,128)(2,1)S(1)}, u32[]{:S(2)}, u32[]{:S(2)}) collective-permute-start(bf16[64,1024]{1,0:T(8,128)(2,1)S(1)} %collective-permute-done.19.refs_5_), channel_id=1, source_target_pairs={{0,6},{1,7},{2,4},{3,5},{4,2},{5,3},{6,0},{7,1},{8,14},{9,15},{10,... | collective-permute-start | bytes 393224 | tf_op jit(solution)/shard_map/ppermute | solution.py:389
  60.6 8.1 %collective-permute-start.21 = (bf16[64,1024]{1,0:T(8,128)(2,1)S(1)}, bf16[64,1024]{1,0:T(8,128)(2,1)S(1)}, u32[]{:S(2)}, u32[]{:S(2)}) collective-permute-start(bf16[64,1024]{1,0:T(8,128)(2,1)S(1)} %collective-permute-done.19.refs_5_), channel_id=1, source_target_pairs={{0,1},{1,0},{2,3},{3,2},{4,5},{5,4},{6,7},{7,6},{8,9},{9,8},{10,11... | collective-permute-start | bytes 393224 | tf_op jit(solution)/shard_map/ppermute | solution.py:389
  62.4 6.3 %collective-permute-start.24 = (bf16[64,1024]{1,0:T(8,128)(2,1)S(1)}, bf16[64,1024]{1,0:T(8,128)(2,1)S(1)}, u32[]{:S(2)}, u32[]{:S(2)}) collective-permute-start(bf16[64,1024]{1,0:T(8,128)(2,1)S(1)} %collective-permute-done.22.refs_8_), channel_id=1, source_target_pairs={{0,1},{1,0},{2,3},{3,2},{4,5},{5,4},{6,7},{7,6},{8,9},{9,8},{10,11... | collective-permute-start | bytes 393224 | tf_op jit(solution)/shard_map/ppermute | solution.py:389
  (18 other events, 126.0 us)

commit v2 on v1

--- a/solution.py
+++ b/solution.py
@@ -28,7 +28,7 @@
 PAY = 144
 
 
-def quantize_kernel(values_hbm, scales_hbm, top_ref, bottom_ref, squares_ref, values, scales_t, sems):
+def quantize_kernel(values_hbm, scales_hbm, q_ref, squares_ref, values, scales_t, sems):
     copies = (
         pltpu.make_async_copy(values_hbm, values, sems.at[0]),
         pltpu.make_async_copy(scales_hbm, scales_t, sems.at[1]),
@@ -37,14 +37,12 @@
         copy.start()
     for copy in copies:
         copy.wait()
-    half = top_ref.shape[0]
     scales = scales_t[...].astype(f32).T
     squares = None
     for b in range(scales.shape[1]):
         lanes = slice(128 * b, 128 * b + 128)
         q = (values[:, lanes].astype(f32) * scales[:, b : b + 1]).astype(bf16)
-        top_ref[:, lanes] = q[:half]
-        bottom_ref[:, lanes] = q[half:]
+        q_ref[:, lanes] = q
         wide = q.astype(f32)
         squares = wide * wide if squares is None else squares + wide * wide
     squares_ref[...] = jnp.sum(squares.T, axis=0, keepdims=True)
@@ -56,12 +54,11 @@
     return pl.pallas_call(
         quantize_kernel,
         out_shape=(
-            pltpu.VMEM((rows // 2, width), bf16),
-            pltpu.VMEM((rows // 2, width), bf16),
+            pltpu.VMEM((rows, width), bf16),
             pltpu.VMEM((1, rows), f32),
         ),
         in_specs=[HBM, HBM],
-        out_specs=(VM, VM, VM),
+        out_specs=(VM, VM),
         scratch_shapes=[
             pltpu.VMEM(values.shape, bf16),
             pltpu.VMEM(scales.shape, bf16),
@@ -84,7 +81,7 @@
         )
         for j in range(width // step)
     ]
-    for copy in copies:
+    for copy in copies[:2]:
         copy.start()
     ids_copy.wait()
     local = ids_ref[...] - lax.axis_index("cent") * count
@@ -111,6 +108,8 @@
         onehot_ref[:, 256 * j : 256 * j + 256] = (at == chosen).astype(f32).astype(bf16)
     for j, copy in enumerate(copies):
         copy.wait()
+        if j + 2 < len(copies):
+            copies[j + 2].start()
         lanes = slice(step * j, step * j + step)
         out_ref[:, lanes] = jnp.dot(
             onehot_ref[...], cents_ref[j], preferred_element_type=f32
@@ -140,7 +139,7 @@
     )(off_chip(ids), off_chip(cents))
 
 
-def residual_kernel(count, slots, ids_ref, fetched_ref, top_ref, bottom_ref, out_ref):
+def residual_kernel(count, slots, ids_ref, fetched_ref, q_ref, out_ref):
     width, rows = out_ref.shape
     ids = ids_ref[pl.ds(lax.axis_index("cent"), 1), :]
     owner = lax.div(ids, count)
@@ -158,73 +157,68 @@
         fetched = lax.dot_general(
             place, fetched_ref[:, lanes], (((0,), (0,)), ((), ())), preferred_element_type=f32
         )
-        q = jnp.concatenate([top_ref[:, lanes], bottom_ref[:, lanes]], axis=0)
-        out_ref[lanes, :] = (q.astype(f32) - fetched).T
+        out_ref[lanes, :] = (q_ref[:, lanes].astype(f32) - fetched).T
 
 
 def residuals(ids, fetched, q, count, slots):
-    rows, width = 2 * q[0].shape[0], q[0].shape[1]
+    rows, width = q.shape
     return pl.pallas_call(
         functools.partial(residual_kernel, count, slots),
         out_shape=pltpu.VMEM((width, rows), f32),
-        in_specs=[VM] * 4,
+        in_specs=[VM] * 3,
         out_specs=VM,
         cost_estimate=pl.CostEstimate(
             flops=2 * fetched.size * rows, bytes_accessed=fetched.size * 2 + rows * width * 6, transcendentals=0
         ),
         compiler_params=LIMIT,
         name="residuals",
-    )(ids, on_chip(fetched), *[on_chip(x) for x in q])
-
-
-def nearest_kernel(step, *refs):
+    )(ids, on_chip(fetched), on_chip(q))
+
+
+def nearest_kernel(step, ahead, *refs):
     x_refs, (cents_hbm, out_ref, cents_ref, sems) = refs[:-4], refs[-4:]
-    steps = cents_ref.shape[0]
-
-    def copy(i):
-        at = pl.ds(pl.multiple_of(i * step, step), step)
-        return pltpu.make_async_copy(cents_hbm.at[at, :], cents_ref.at[i], sems.at[i])
-
-    for i in range(steps):
-        copy(i).start()
-    groups = [[]]
-    for ref in x_refs:
-        if sum(r.shape[0] for r in groups[-1]) == 256:
-            groups.append([])
-        groups[-1].append(ref)
-    out_ref[...] = jnp.full(out_ref.shape, jnp.inf, f32)
-
-    @pl.loop(0, steps)
-    def _(i):
-        copy(i).wait()
-        block = cents_ref[i]
+    half = step // 2
+    copies = [
+        pltpu.make_async_copy(cents_hbm.at[pl.ds(half * i, half), :], cents_ref.at[i], sems.at[i])
+        for i in range(cents_ref.shape[0])
+    ]
+    for copy in copies[:ahead]:
+        copy.start()
+    best = [None] * (len(x_refs) // 2)
+    for i in range(0, len(copies), 2):
+        for k in (i, i + 1):
+            copies[k].wait()
+            if k + ahead < len(copies):
+                copies[k + ahead].start()
+        block = jnp.concatenate([cents_ref[i], cents_ref[i + 1]], axis=0)
         total = None
         for b in range(block.shape[1] // 128):
             wide = block[:, 128 * b : 128 * b + 128].astype(f32)
             total = wide * wide if total is None else total + wide * wide
         squares = jnp.broadcast_to(jnp.sum(total, axis=1, keepdims=True), (step, 128))
         squares = jnp.concatenate([squares, squares], axis=1)
-        for j, group in enumerate(groups):
-            x = jnp.concatenate([r[...] for r in group], axis=0)
+        for j in range(len(best)):
+            x = jnp.concatenate([x_refs[2 * j][...], x_refs[2 * j + 1][...]], axis=0)
             cross = lax.dot_general(block, x, (((1,), (1,)), ((), ())), preferred_element_type=f32)
             low = jnp.min(squares - 2.0 * cross, axis=0, keepdims=True)
-            for k in range(2):
-                row = slice(2 * j + k, 2 * j + k + 1)
-                out_ref[row, :] = jnp.minimum(out_ref[row, :], low[:, 128 * k : 128 * k + 128])
+            best[j] = low if best[j] is None else jnp.minimum(best[j], low)
+    for j, low in enumerate(best):
+        for k in range(2):
+            out_ref[2 * j + k : 2 * j + k + 1, :] = low[:, 128 * k : 128 * k + 128]
 
 
 def nearest(xs, cents):
     count, width = cents.shape
     rows = sum(x.shape[0] for x in xs)
-    step = 256
-    return pl.pallas_call(
-        functools.partial(nearest_kernel, step),
+    step = 512
+    return pl.pallas_call(
+        functools.partial(nearest_kernel, step, 3),
         out_shape=pltpu.VMEM((rows // 128, 128), f32),
         in_specs=[VM] * len(xs) + [HBM],
         out_specs=VM,
         scratch_shapes=[
-            pltpu.VMEM((count // step, step, width), bf16),
-            pltpu.SemaphoreType.DMA((count // step,)),
+            pltpu.VMEM((2 * count // step, step // 2, width), bf16),
+            pltpu.SemaphoreType.DMA((2 * count // step,)),
         ],
         cost_estimate=pl.CostEstimate(
             flops=2 * rows * count * width, bytes_accessed=count * width * 2 + rows * width * 2, transcendentals=0
@@ -396,35 +390,28 @@
     peers = coarse_ids.shape[0]
     slots = 16
 
-    *q, row_squares = quantize(emb_values, emb_scales)
+    q, row_squares = quantize(emb_values, emb_scales)
 
     core = 1
 
-    def hop(xs, offset):
-        out = []
-        for x in xs:
-            out.append(swap(x, offset))
-        return out
-
-    a = hop(q[::-1], 2)[::-1]
-    b = hop(q, 6)
-    z = hop(q, 8)
-    blocks = {0: q, core: hop(q, core), 2: a, 6: b, 8: z}
+    blocks = {0: q, 2: swap(q, 2), 6: swap(q, 6), 8: swap(q, 8)}
+    blocks[core] = swap(q, core)
 
     sent = gather(coarse_ids, centroids, slots)
     fetched = lax.all_to_all(sent.reshape(peers, slots, width), "cent", 0, 0)
     fetched = fetched.reshape(peers * slots, width)
 
-    blocks[4] = hop(b[:1], 2) + hop(a[1:], 6)
-    blocks[10], blocks[14] = hop(z, 2), hop(z, 6)
-    blocks[12] = hop(blocks[14][:1], 2) + hop(blocks[10][1:], 6)
+    blocks[14] = swap(blocks[8], 6)
+    blocks[10] = swap(blocks[8], 2)
+    blocks[4] = swap(blocks[6], 2)
+    blocks[12] = swap(blocks[14], 2)
     for d in (2, 6, 8, 4, 10, 14, 12):
-        blocks[d ^ core] = hop(blocks[d], core)
-
-    orders = ((0, 1, 2, 3), (6, 7, 8, 9), (4, 5, 10, 11, 14, 15, 12, 13))
+        blocks[d ^ core] = swap(blocks[d], core)
+
+    orders = ((0, 1, 2, 3, 6, 7, 8, 9), (4, 5, 10, 11, 14, 15, 12, 13))
     lows = []
     for order in orders:
-        lows.append(nearest([x for d in order for x in blocks[d]], centroids))
+        lows.append(nearest([blocks[d] for d in order], centroids))
     where = {d: (k, j) for k, order in enumerate(orders) for j, d in enumerate(order)}
 
     residual = residuals(coarse_ids, fetched, q, count, slots)

time: 94.6 us -> 85.5 us (0.904)
  starting transfers between devices: 52.5 us -> 40.2 us
  waiting for transfers between devices: 13.3 us -> 20.1 us
  Pallas kernels: 27.6 us -> 24 us
    ppermute x36 -> x21, starting transfers between devices: 35.3 us -> 23 us  [swap(): return lax.ppermute(x, 'cent', [(i, i ^ offset) for i in range(16)])]
    ppermute x36 -> x21, waiting for transfers between devices: 13.3 us -> 19.5 us  [swap(): return lax.ppermute(x, 'cent', [(i, i ^ offset) for i in range(16)])]
    pallas_call x4 -> x3, Pallas kernels: 19.1 us -> 15.4 us  [the longest x2 14.1 us: nearest(): pl.pallas_call(functools.partial(nearest_kernel, step, 3), out_shape=pltp...]
  transfers between devices with their start and end apart: 38 -> 23, of which waited for: 8 -> 9; matrix products, arithmetic and copies ran while one was open for 0% -> 0% of each run, Pallas kernels for 22% -> 20%
where the time goes in v2:
time: 85.5 us; the launch traced here: 85.1 us
  starting transfers between devices  40.2 us (47%)
  Pallas kernels  24 us (28%)
  waiting for transfers between devices  20.1 us (24%)
    ppermute x21, starting transfers between devices, swap(): return lax.ppermute(x, 'cent', [(i, i ^ offset) for i in range(16)])  23 us
    ppermute x21, waiting for transfers between devices, swap(): return lax.ppermute(x, 'cent', [(i, i ^ offset) for i in range(16)])  19.5 us
    pallas_call x2, Pallas kernels, nearest(): pl.pallas_call(functools.partial(nearest_kernel, step, 3), out_shape=pltp...  14.1 us
    all_to_all x1, starting transfers between devices, step(): sub = lax.all_to_all(stacked, 'rows', 0, 0)  9.84 us
    all_to_all x1, starting transfers between devices, step(): fetched = lax.all_to_all(sent.reshape(peers, slots, width), 'cent', 0, 0)  7.34 us
    pallas_call x1, Pallas kernels, gather(): pl.pallas_call(functools.partial(gather_kernel, slots, step), out_shape=p...  4.86 us
  transfers between devices with their start and end apart: 23, of which 9 were waited for; matrix products, arithmetic and copies ran while one was open for 0% of the time, Pallas kernels for 20%

profile of v2, /device:TPU:1, one launch (start us, length us, event | category | flops | bytes accessed | tf_op | source)
XLA Modules:
  0.0 85.1 jit_solution(7974528646471307247)
XLA Ops:
  0.6 4.9 %gather.1 = bf16[256,1024]{1,0:T(8,128)(2,1)} custom-call(s32[16,128]{1,0:T(8,128)} %ids_ref.1, bf16[2048,1024]{1,0:T(8,128)(2,1)} %refs_8_.3), custom_call_target="tpu_custom_call" | custom-call | flops 1073741824 | bytes 4194304 | tf_op jit(solution)/shard_map/gather/pallas_call | solution.py:123
  5.5 7.3 %all-to-all-start = ((bf16[16,16,1024]{2,1,0:T(8,128)(2,1)}), bf16[16,16,1024]{2,1,0:T(8,128)(2,1)S(1)}, u32[]{:S(2)}, u32[]{:S(2)}) async-start(bf16[16,16,1024]{2,1,0:T(8,128)(2,1)} %bitcast), calls=%async_computation | async-start | bytes 1048576 | tf_op jit(solution)/shard_map/all_to_all | solution.py:401
  12.8 1.3 %quantize.1 = (bf16[128,1024]{1,0:T(8,128)(2,1)S(1)}, f32[1,128]{1,0:T(1,128)S(1)}) custom-call(bf16[128,1024]{1,0:T(8,128)(2,1)} %values_hbm.1, bf16[8,128]{1,0:T(8,128)(2,1)} %bitcast.16), custom_call_target="tpu_custom_call" | custom-call | flops 393216 | bytes 524288 | tf_op jit(solution)/shard_map/quantize/pallas_call | solution.py:54
  14.2 1.4 %collective-permute-start.5 = (bf16[128,1024]{1,0:T(8,128)(2,1)S(1)}, bf16[128,1024]{1,0:T(8,128)(2,1)S(1)}, u32[]{:S(2)}, u32[]{:S(2)}) collective-permute-start(bf16[128,1024]{1,0:T(8,128)(2,1)S(1)} %get-tuple-element.13.q_ref.refs_0_), channel_id=1, source_target_pairs={{0,8},{1,9},{2,10},{3,11},{4,12},{5,13},{6,14},{7,15},{8,0},{9,1},... | collective-permute-start | bytes 786440 | tf_op jit(solution)/shard_map/ppermute | solution.py:383
  16.8 1.8 %collective-permute-start.3 = (bf16[128,1024]{1,0:T(8,128)(2,1)S(1)}, bf16[128,1024]{1,0:T(8,128)(2,1)S(1)}, u32[]{:S(2)}, u32[]{:S(2)}) collective-permute-start(bf16[128,1024]{1,0:T(8,128)(2,1)S(1)} %get-tuple-element.13.q_ref.refs_0_), channel_id=1, source_target_pairs={{0,6},{1,7},{2,4},{3,5},{4,2},{5,3},{6,0},{7,1},{8,14},{9,15},{10,... | collective-permute-start | bytes 786440 | tf_op jit(solution)/shard_map/ppermute | solution.py:383
  18.6 1.2 %collective-permute-start = (bf16[128,1024]{1,0:T(8,128)(2,1)S(1)}, bf16[128,1024]{1,0:T(8,128)(2,1)S(1)}, u32[]{:S(2)}, u32[]{:S(2)}) collective-permute-start(bf16[128,1024]{1,0:T(8,128)(2,1)S(1)} %get-tuple-element.13.q_ref.refs_0_), channel_id=1, source_target_pairs={{0,1},{1,0},{2,3},{3,2},{4,5},{5,4},{6,7},{7,6},{8,9},{9,8},{10,11... | collective-permute-start | bytes 786440 | tf_op jit(solution)/shard_map/ppermute | solution.py:383
  19.8 6.5 %collective-permute-done.5.refs_6_ = bf16[128,1024]{1,0:T(8,128)(2,1)S(1)} collective-permute-done((bf16[128,1024]{1,0:T(8,128)(2,1)S(1)}, bf16[128,1024]{1,0:T(8,128)(2,1)S(1)}, u32[]{:S(2)}, u32[]{:S(2)}) %collective-permute-start.5) | collective-permute-done | bytes 262176 | tf_op jit(solution)/shard_map/ppermute | solution.py:383
  26.3 2.4 %collective-permute-start.11 = (bf16[128,1024]{1,0:T(8,128)(2,1)S(1)}, bf16[128,1024]{1,0:T(8,128)(2,1)S(1)}, u32[]{:S(2)}, u32[]{:S(2)}) collective-permute-start(bf16[128,1024]{1,0:T(8,128)(2,1)S(1)} %collective-permute-done.5.refs_6_), channel_id=1, source_target_pairs={{0,6},{1,7},{2,4},{3,5},{4,2},{5,3},{6,0},{7,1},{8,14},{9,15},{10,... | collective-permute-start | bytes 786440 | tf_op jit(solution)/shard_map/ppermute | solution.py:383
  28.7 1.3 %collective-permute-start.2 = (bf16[128,1024]{1,0:T(8,128)(2,1)S(1)}, bf16[128,1024]{1,0:T(8,128)(2,1)S(1)}, u32[]{:S(2)}, u32[]{:S(2)}) collective-permute-start(bf16[128,1024]{1,0:T(8,128)(2,1)S(1)} %collective-permute-done.1.refs_2_), channel_id=1, source_target_pairs={{0,1},{1,0},{2,3},{3,2},{4,5},{5,4},{6,7},{7,6},{8,9},{9,8},{10,11... | collective-permute-start | bytes 786440 | tf_op jit(solution)/shard_map/ppermute | solution.py:383
  30.1 1.5 %collective-permute-start.9 = (bf16[128,1024]{1,0:T(8,128)(2,1)S(1)}, bf16[128,1024]{1,0:T(8,128)(2,1)S(1)}, u32[]{:S(2)}, u32[]{:S(2)}) collective-permute-start(bf16[128,1024]{1,0:T(8,128)(2,1)S(1)} %collective-permute-done.5.refs_6_), channel_id=1, source_target_pairs={{0,2},{1,3},{2,0},{3,1},{4,6},{5,7},{6,4},{7,5},{8,10},{9,11},{10,... | collective-permute-start | bytes 786440 | tf_op jit(solution)/shard_map/ppermute | solution.py:383
  31.5 2.9 %collective-permute-done.11.refs_4_ = bf16[128,1024]{1,0:T(8,128)(2,1)S(1)} collective-permute-done((bf16[128,1024]{1,0:T(8,128)(2,1)S(1)}, bf16[128,1024]{1,0:T(8,128)(2,1)S(1)}, u32[]{:S(2)}, u32[]{:S(2)}) %collective-permute-start.11) | collective-permute-done | bytes 262176 | tf_op jit(solution)/shard_map/ppermute | solution.py:383
  34.4 2.1 %collective-permute-start.6 = (bf16[128,1024]{1,0:T(8,128)(2,1)S(1)}, bf16[128,1024]{1,0:T(8,128)(2,1)}, u32[]{:S(2)}, u32[]{:S(2)}) collective-permute-start(bf16[128,1024]{1,0:T(8,128)(2,1)S(1)} %collective-permute-done.5.refs_6_), channel_id=1, source_target_pairs={{0,1},{1,0},{2,3},{3,2},{4,5},{5,4},{6,7},{7,6},{8,9},{9,8},{10,11... | collective-permute-start | bytes 786440 | tf_op jit(solution)/shard_map/ppermute | solution.py:383
  36.5 1.4 %residuals.1 = f32[1024,128]{1,0:T(8,128)} custom-call(s32[16,128]{1,0:T(8,128)S(1)} %copy-done.1, bf16[256,1024]{1,0:T(8,128)(2,1)S(1)} %bitcast.14, bf16[128,1024]{1,0:T(8,128)(2,1)S(1)} %get-tuple-element.13.q_ref.refs_0_), custom_call_target="tpu_custom_call" | custom-call | flops 67108864 | bytes 1310720 | tf_op jit(solution)/shard_map/residuals/pallas_call | solution.py:165
  37.9 9.8 %all-to-all-start.1 = ((f32[16,64,128]{2,1,0:T(8,128)}), f32[16,64,128]{2,1,0:T(8,128)S(1)}, u32[]{:S(2)}, u32[]{:S(2)}) async-start(f32[16,64,128]{2,1,0:T(8,128)} %bitcast.3), calls=%async_computation.1 | async-start | bytes 1048576 | tf_op jit(solution)/shard_map/all_to_all | solution.py:419
  48.7 1.3 %collective-permute-start.14 = (bf16[128,1024]{1,0:T(8,128)(2,1)S(1)}, bf16[128,1024]{1,0:T(8,128)(2,1)S(1)}, u32[]{:S(2)}, u32[]{:S(2)}) collective-permute-start(bf16[128,1024]{1,0:T(8,128)(2,1)S(1)} %collective-permute-done.13.refs_6_), channel_id=1, source_target_pairs={{0,1},{1,0},{2,3},{3,2},{4,5},{5,4},{6,7},{7,6},{8,9},{9,8},{10,11... | collective-permute-start | bytes 786440 | tf_op jit(solution)/shard_map/ppermute | solution.py:383
  50.0 7.5 %nearest.2.refs_0_ = f32[8,128]{1,0:T(8,128)S(1)} custom-call(bf16[128,1024]{1,0:T(8,128)(2,1)S(1)} %get-tuple-element.13.q_ref.refs_0_, bf16[128,1024]{1,0:T(8,128)(2,1)S(1)} %collective-permute-done.refs_1_, bf16[128,1024]{1,0:T(8,128)(2,1)S(1)} %collective-permute-done.1.refs_2_, bf16[128,1024]{1,0:T(8,128)(2,1)S(1)} %collective-permute-done.2.refs_3_, ...), custom_call_target="tpu_custom_call" | custom-call | flops 4294967296 | bytes 6291456 | tf_op jit(solution)/shard_map/nearest/pallas_call | solution.py:214
  57.6 6.6 %nearest.3.refs_1_ = f32[8,128]{1,0:T(8,128)S(1)} custom-call(bf16[128,1024]{1,0:T(8,128)(2,1)S(1)} %collective-permute-done.7.refs_0_, bf16[128,1024]{1,0:T(8,128)(2,1)S(1)} %collective-permute-done.8.refs_1_, bf16[128,1024]{1,0:T(8,128)(2,1)S(1)} %collective-permute-done.9.refs_2_, bf16[128,1024]{1,0:T(8,128)(2,1)S(1)} %collective-permute-done.10.refs_3_, ...), custom_call_target="tpu_custom_call" | custom-call | flops 4294967296 | bytes 6291456 | tf_op jit(solution)/shard_map/nearest/pallas_call | solution.py:214
  65.7 1.7 %collective-permute-start.15 = (f32[144,128]{1,0:T(8,128)S(1)}, f32[144,128]{1,0:T(8,128)S(1)}, u32[]{:S(2)}, u32[]{:S(2)}) collective-permute-start(f32[144,128]{1,0:T(8,128)S(1)} %get-tuple-element.15), channel_id=1, source_target_pairs={{0,1},{1,0},{2,3},{3,2},{4,5},{5,4},{6,7},{7,6},{8,9},{9,8},{10,11... | collective-permute-start | bytes 221192 | tf_op jit(solution)/shard_map/ppermute | solution.py:383
  68.4 3.2 %collective-permute-done.16.b_ref = f32[144,128]{1,0:T(8,128)S(1)} collective-permute-done((f32[144,128]{1,0:T(8,128)S(1)}, f32[144,128]{1,0:T(8,128)S(1)}, u32[]{:S(2)}, u32[]{:S(2)}) %collective-permute-start.16) | collective-permute-done | bytes 73760 | tf_op jit(solution)/shard_map/ppermute | solution.py:383
  71.6 1.4 %collective-permute-start.17 = (f32[144,128]{1,0:T(8,128)S(1)}, f32[144,128]{1,0:T(8,128)S(1)}, u32[]{:S(2)}, u32[]{:S(2)}) collective-permute-start(f32[144,128]{1,0:T(8,128)S(1)} %join.3.a_ref), channel_id=1, source_target_pairs={{0,2},{1,3},{2,0},{3,1},{4,6},{5,7},{6,4},{7,5},{8,10},{9,11},{10,... | collective-permute-start | bytes 221192 | tf_op jit(solution)/shard_map/ppermute | solution.py:383
  73.1 2.3 %collective-permute-start.18 = (f32[144,128]{1,0:T(8,128)S(1)}, f32[144,128]{1,0:T(8,128)S(1)}, u32[]{:S(2)}, u32[]{:S(2)}) collective-permute-start(f32[144,128]{1,0:T(8,128)S(1)} %join.3.a_ref), channel_id=1, source_target_pairs={{0,4},{1,5},{2,6},{3,7},{4,0},{5,1},{6,2},{7,3},{8,12},{9,13},{10,... | collective-permute-start | bytes 221192 | tf_op jit(solution)/shard_map/ppermute | solution.py:383
  75.6 2.2 %collective-permute-done.18.c_ref = f32[144,128]{1,0:T(8,128)S(1)} collective-permute-done((f32[144,128]{1,0:T(8,128)S(1)}, f32[144,128]{1,0:T(8,128)S(1)}, u32[]{:S(2)}, u32[]{:S(2)}) %collective-permute-start.18) | collective-permute-done | bytes 73760 | tf_op jit(solution)/shard_map/ppermute | solution.py:383
  77.8 2.8 %collective-permute-done.19.d_ref = f32[144,128]{1,0:T(8,128)S(1)} collective-permute-done((f32[144,128]{1,0:T(8,128)S(1)}, f32[144,128]{1,0:T(8,128)S(1)}, u32[]{:S(2)}, u32[]{:S(2)}) %collective-permute-start.19) | collective-permute-done | bytes 73760 | tf_op jit(solution)/shard_map/ppermute | solution.py:383
  81.1 2.1 %collective-permute-start.20 = (f32[128,128]{1,0:T(8,128)S(1)}, f32[128,128]{1,0:T(8,128)S(1)}, u32[]{:S(2)}, u32[]{:S(2)}) collective-permute-start(f32[128,128]{1,0:T(8,128)S(1)} %get-tuple-element.18.mine_ref), channel_id=1, source_target_pairs={{0,1},{1,0},{2,3},{3,2},{4,5},{5,4},{6,7},{7,6},{8,9},{9,8},{10,11... | collective-permute-start | bytes 196616 | tf_op jit(solution)/shard_map/ppermute | solution.py:383
  (40 shorter events, 7.4 us)
Async XLA Ops:
  0.6 35.9 %copy-start.1 = (s32[16,128]{1,0:T(8,128)S(1)}, s32[16,128]{1,0:T(8,128)}, u32[]{:S(2)}) copy-start(s32[16,128]{1,0:T(8,128)} %ids_ref.1) | copy-start | bytes 24580
  5.5 31.0 %all-to-all-start = ((bf16[16,16,1024]{2,1,0:T(8,128)(2,1)}), bf16[16,16,1024]{2,1,0:T(8,128)(2,1)S(1)}, u32[]{:S(2)}, u32[]{:S(2)}) async-start(bf16[16,16,1024]{2,1,0:T(8,128)(2,1)} %bitcast), calls=%async_computation | async-start | bytes 1048576 | tf_op jit(solution)/shard_map/all_to_all | solution.py:401
  14.2 12.1 %collective-permute-start.5 = (bf16[128,1024]{1,0:T(8,128)(2,1)S(1)}, bf16[128,1024]{1,0:T(8,128)(2,1)S(1)}, u32[]{:S(2)}, u32[]{:S(2)}) collective-permute-start(bf16[128,1024]{1,0:T(8,128)(2,1)S(1)} %get-tuple-element.13.q_ref.refs_0_), channel_id=1, source_target_pairs={{0,8},{1,9},{2,10},{3,11},{4,12},{5,13},{6,14},{7,15},{8,0},{9,1},... | collective-permute-start | bytes 786440 | tf_op jit(solution)/shard_map/ppermute | solution.py:383
  15.6 13.1 %collective-permute-start.1 = (bf16[128,1024]{1,0:T(8,128)(2,1)S(1)}, bf16[128,1024]{1,0:T(8,128)(2,1)S(1)}, u32[]{:S(2)}, u32[]{:S(2)}) collective-permute-start(bf16[128,1024]{1,0:T(8,128)(2,1)S(1)} %get-tuple-element.13.q_ref.refs_0_), channel_id=1, source_target_pairs={{0,2},{1,3},{2,0},{3,1},{4,6},{5,7},{6,4},{7,5},{8,10},{9,11},{10,... | collective-permute-start | bytes 786440 | tf_op jit(solution)/shard_map/ppermute | solution.py:383
  16.8 13.2 %collective-permute-start.3 = (bf16[128,1024]{1,0:T(8,128)(2,1)S(1)}, bf16[128,1024]{1,0:T(8,128)(2,1)S(1)}, u32[]{:S(2)}, u32[]{:S(2)}) collective-permute-start(bf16[128,1024]{1,0:T(8,128)(2,1)S(1)} %get-tuple-element.13.q_ref.refs_0_), channel_id=1, source_target_pairs={{0,6},{1,7},{2,4},{3,5},{4,2},{5,3},{6,0},{7,1},{8,14},{9,15},{10,... | collective-permute-start | bytes 786440 | tf_op jit(solution)/shard_map/ppermute | solution.py:383
  18.6 11.5 %collective-permute-start = (bf16[128,1024]{1,0:T(8,128)(2,1)S(1)}, bf16[128,1024]{1,0:T(8,128)(2,1)S(1)}, u32[]{:S(2)}, u32[]{:S(2)}) collective-permute-start(bf16[128,1024]{1,0:T(8,128)(2,1)S(1)} %get-tuple-element.13.q_ref.refs_0_), channel_id=1, source_target_pairs={{0,1},{1,0},{2,3},{3,2},{4,5},{5,4},{6,7},{7,6},{8,9},{9,8},{10,11... | collective-permute-start | bytes 786440 | tf_op jit(solution)/shard_map/ppermute | solution.py:383
  26.3 8.1 %collective-permute-start.11 = (bf16[128,1024]{1,0:T(8,128)(2,1)S(1)}, bf16[128,1024]{1,0:T(8,128)(2,1)S(1)}, u32[]{:S(2)}, u32[]{:S(2)}) collective-permute-start(bf16[128,1024]{1,0:T(8,128)(2,1)S(1)} %collective-permute-done.5.refs_6_), channel_id=1, source_target_pairs={{0,6},{1,7},{2,4},{3,5},{4,2},{5,3},{6,0},{7,1},{8,14},{9,15},{10,... | collective-permute-start | bytes 786440 | tf_op jit(solution)/shard_map/ppermute | solution.py:383
  28.7 5.7 %collective-permute-start.2 = (bf16[128,1024]{1,0:T(8,128)(2,1)S(1)}, bf16[128,1024]{1,0:T(8,128)(2,1)S(1)}, u32[]{:S(2)}, u32[]{:S(2)}) collective-permute-start(bf16[128,1024]{1,0:T(8,128)(2,1)S(1)} %collective-permute-done.1.refs_2_), channel_id=1, source_target_pairs={{0,1},{1,0},{2,3},{3,2},{4,5},{5,4},{6,7},{7,6},{8,9},{9,8},{10,11... | collective-permute-start | bytes 786440 | tf_op jit(solution)/shard_map/ppermute | solution.py:383
  30.0 17.8 %collective-permute-start.4 = (bf16[128,1024]{1,0:T(8,128)(2,1)S(1)}, bf16[128,1024]{1,0:T(8,128)(2,1)S(1)}, u32[]{:S(2)}, u32[]{:S(2)}) collective-permute-start(bf16[128,1024]{1,0:T(8,128)(2,1)S(1)} %collective-permute-done.3.refs_4_), channel_id=1, source_target_pairs={{0,1},{1,0},{2,3},{3,2},{4,5},{5,4},{6,7},{7,6},{8,9},{9,8},{10,11... | collective-permute-start | bytes 786440 | tf_op jit(solution)/shard_map/ppermute | solution.py:383
  30.1 18.0 %collective-permute-start.7 = (bf16[128,1024]{1,0:T(8,128)(2,1)S(1)}, bf16[128,1024]{1,0:T(8,128)(2,1)S(1)}, u32[]{:S(2)}, u32[]{:S(2)}) collective-permute-start(bf16[128,1024]{1,0:T(8,128)(2,1)S(1)} %collective-permute-done.3.refs_4_), channel_id=1, source_target_pairs={{0,2},{1,3},{2,0},{3,1},{4,6},{5,7},{6,4},{7,5},{8,10},{9,11},{10,... | collective-permute-start | bytes 786440 | tf_op jit(solution)/shard_map/ppermute | solution.py:383
  30.1 18.3 %collective-permute-start.9 = (bf16[128,1024]{1,0:T(8,128)(2,1)S(1)}, bf16[128,1024]{1,0:T(8,128)(2,1)S(1)}, u32[]{:S(2)}, u32[]{:S(2)}) collective-permute-start(bf16[128,1024]{1,0:T(8,128)(2,1)S(1)} %collective-permute-done.5.refs_6_), channel_id=1, source_target_pairs={{0,2},{1,3},{2,0},{3,1},{4,6},{5,7},{6,4},{7,5},{8,10},{9,11},{10,... | collective-permute-start | bytes 786440 | tf_op jit(solution)/shard_map/ppermute | solution.py:383
  34.4 14.3 %collective-permute-start.13 = (bf16[128,1024]{1,0:T(8,128)(2,1)S(1)}, bf16[128,1024]{1,0:T(8,128)(2,1)S(1)}, u32[]{:S(2)}, u32[]{:S(2)}) collective-permute-start(bf16[128,1024]{1,0:T(8,128)(2,1)S(1)} %collective-permute-done.11.refs_4_), channel_id=1, source_target_pairs={{0,2},{1,3},{2,0},{3,1},{4,6},{5,7},{6,4},{7,5},{8,10},{9,11},{10,... | collective-permute-start | bytes 786440 | tf_op jit(solution)/shard_map/ppermute | solution.py:383
  34.4 15.6 %collective-permute-start.6 = (bf16[128,1024]{1,0:T(8,128)(2,1)S(1)}, bf16[128,1024]{1,0:T(8,128)(2,1)}, u32[]{:S(2)}, u32[]{:S(2)}) collective-permute-start(bf16[128,1024]{1,0:T(8,128)(2,1)S(1)} %collective-permute-done.5.refs_6_), channel_id=1, source_target_pairs={{0,1},{1,0},{2,3},{3,2},{4,5},{5,4},{6,7},{7,6},{8,9},{9,8},{10,11... | collective-permute-start | bytes 786440 | tf_op jit(solution)/shard_map/ppermute | solution.py:383
  37.9 27.0 %all-to-all-start.1 = ((f32[16,64,128]{2,1,0:T(8,128)}), f32[16,64,128]{2,1,0:T(8,128)S(1)}, u32[]{:S(2)}, u32[]{:S(2)}) async-start(f32[16,64,128]{2,1,0:T(8,128)} %bitcast.3), calls=%async_computation.1 | async-start | bytes 1048576 | tf_op jit(solution)/shard_map/all_to_all | solution.py:419
  47.7 9.9 %collective-permute-start.12 = (bf16[128,1024]{1,0:T(8,128)(2,1)S(1)}, bf16[128,1024]{1,0:T(8,128)(2,1)S(1)}, u32[]{:S(2)}, u32[]{:S(2)}) collective-permute-start(bf16[128,1024]{1,0:T(8,128)(2,1)S(1)} %collective-permute-done.11.refs_4_), channel_id=1, source_target_pairs={{0,1},{1,0},{2,3},{3,2},{4,5},{5,4},{6,7},{7,6},{8,9},{9,8},{10,11... | collective-permute-start | bytes 786440 | tf_op jit(solution)/shard_map/ppermute | solution.py:383
  48.1 9.5 %collective-permute-start.8 = (bf16[128,1024]{1,0:T(8,128)(2,1)S(1)}, bf16[128,1024]{1,0:T(8,128)(2,1)S(1)}, u32[]{:S(2)}, u32[]{:S(2)}) collective-permute-start(bf16[128,1024]{1,0:T(8,128)(2,1)S(1)} %collective-permute-done.7.refs_0_), channel_id=1, source_target_pairs={{0,1},{1,0},{2,3},{3,2},{4,5},{5,4},{6,7},{7,6},{8,9},{9,8},{10,11... | collective-permute-start | bytes 786440 | tf_op jit(solution)/shard_map/ppermute | solution.py:383
  48.3 9.3 %collective-permute-start.10 = (bf16[128,1024]{1,0:T(8,128)(2,1)S(1)}, bf16[128,1024]{1,0:T(8,128)(2,1)S(1)}, u32[]{:S(2)}, u32[]{:S(2)}) collective-permute-start(bf16[128,1024]{1,0:T(8,128)(2,1)S(1)} %collective-permute-done.9.refs_2_), channel_id=1, source_target_pairs={{0,1},{1,0},{2,3},{3,2},{4,5},{5,4},{6,7},{7,6},{8,9},{9,8},{10,11... | collective-permute-start | bytes 786440 | tf_op jit(solution)/shard_map/ppermute | solution.py:383
  48.7 8.9 %collective-permute-start.14 = (bf16[128,1024]{1,0:T(8,128)(2,1)S(1)}, bf16[128,1024]{1,0:T(8,128)(2,1)S(1)}, u32[]{:S(2)}, u32[]{:S(2)}) collective-permute-start(bf16[128,1024]{1,0:T(8,128)(2,1)S(1)} %collective-permute-done.13.refs_6_), channel_id=1, source_target_pairs={{0,1},{1,0},{2,3},{3,2},{4,5},{5,4},{6,7},{7,6},{8,9},{9,8},{10,11... | collective-permute-start | bytes 786440 | tf_op jit(solution)/shard_map/ppermute | solution.py:383
  65.7 2.7 %collective-permute-start.15 = (f32[144,128]{1,0:T(8,128)S(1)}, f32[144,128]{1,0:T(8,128)S(1)}, u32[]{:S(2)}, u32[]{:S(2)}) collective-permute-start(f32[144,128]{1,0:T(8,128)S(1)} %get-tuple-element.15), channel_id=1, source_target_pairs={{0,1},{1,0},{2,3},{3,2},{4,5},{5,4},{6,7},{7,6},{8,9},{9,8},{10,11... | collective-permute-start | bytes 221192 | tf_op jit(solution)/shard_map/ppermute | solution.py:383
  68.3 3.3 %collective-permute-start.16 = (f32[144,128]{1,0:T(8,128)S(1)}, f32[144,128]{1,0:T(8,128)S(1)}, u32[]{:S(2)}, u32[]{:S(2)}) collective-permute-start(f32[144,128]{1,0:T(8,128)S(1)} %join.2.a_ref), channel_id=1, source_target_pairs={{0,8},{1,9},{2,10},{3,11},{4,12},{5,13},{6,14},{7,15},{8,0},{9,1},... | collective-permute-start | bytes 221192 | tf_op jit(solution)/shard_map/ppermute | solution.py:383
  71.6 3.9 %collective-permute-start.17 = (f32[144,128]{1,0:T(8,128)S(1)}, f32[144,128]{1,0:T(8,128)S(1)}, u32[]{:S(2)}, u32[]{:S(2)}) collective-permute-start(f32[144,128]{1,0:T(8,128)S(1)} %join.3.a_ref), channel_id=1, source_target_pairs={{0,2},{1,3},{2,0},{3,1},{4,6},{5,7},{6,4},{7,5},{8,10},{9,11},{10,... | collective-permute-start | bytes 221192 | tf_op jit(solution)/shard_map/ppermute | solution.py:383
  73.1 4.7 %collective-permute-start.18 = (f32[144,128]{1,0:T(8,128)S(1)}, f32[144,128]{1,0:T(8,128)S(1)}, u32[]{:S(2)}, u32[]{:S(2)}) collective-permute-start(f32[144,128]{1,0:T(8,128)S(1)} %join.3.a_ref), channel_id=1, source_target_pairs={{0,4},{1,5},{2,6},{3,7},{4,0},{5,1},{6,2},{7,3},{8,12},{9,13},{10,... | collective-permute-start | bytes 221192 | tf_op jit(solution)/shard_map/ppermute | solution.py:383
  75.3 5.2 %collective-permute-start.19 = (f32[144,128]{1,0:T(8,128)S(1)}, f32[144,128]{1,0:T(8,128)S(1)}, u32[]{:S(2)}, u32[]{:S(2)}) collective-permute-start(f32[144,128]{1,0:T(8,128)S(1)} %join.3.a_ref), channel_id=1, source_target_pairs={{0,6},{1,7},{2,4},{3,5},{4,2},{5,3},{6,0},{7,1},{8,14},{9,15},{10,... | collective-permute-start | bytes 221192 | tf_op jit(solution)/shard_map/ppermute | solution.py:383
  81.1 3.0 %collective-permute-start.20 = (f32[128,128]{1,0:T(8,128)S(1)}, f32[128,128]{1,0:T(8,128)S(1)}, u32[]{:S(2)}, u32[]{:S(2)}) collective-permute-start(f32[128,128]{1,0:T(8,128)S(1)} %get-tuple-element.18.mine_ref), channel_id=1, source_target_pairs={{0,1},{1,0},{2,3},{3,2},{4,5},{5,4},{6,7},{7,6},{8,9},{9,8},{10,11... | collective-permute-start | bytes 196616 | tf_op jit(solution)/shard_map/ppermute | solution.py:383
  (3 other events, 37.5 us)

commit v3 on v2

--- a/solution.py
+++ b/solution.py
@@ -28,15 +28,49 @@
 PAY = 144
 
 
-def quantize_kernel(values_hbm, scales_hbm, q_ref, squares_ref, values, scales_t, sems):
-    copies = (
-        pltpu.make_async_copy(values_hbm, values, sems.at[0]),
+def prepare_kernel(
+    slots, step, values_hbm, scales_hbm, ids_hbm, cents_hbm, q_ref, squares_ref, out_ref,
+    values, scales_t, ids_ref, cents_ref, onehot_ref, sems,
+):
+    count, width = cents_hbm.shape
+    groups, rows = ids_ref.shape
+    small = (
+        pltpu.make_async_copy(ids_hbm, ids_ref, sems.at[0]),
         pltpu.make_async_copy(scales_hbm, scales_t, sems.at[1]),
-    )
-    for copy in copies:
+        pltpu.make_async_copy(values_hbm, values, sems.at[2]),
+    )
+    large = [
+        pltpu.make_async_copy(cents_hbm.at[:, pl.ds(step * j, step)], cents_ref.at[j], sems.at[3 + j])
+        for j in range(width // step)
+    ]
+    for copy in small:
         copy.start()
-    for copy in copies:
-        copy.wait()
+    for copy in large[:2]:
+        copy.start()
+
+    small[0].wait()
+    local = ids_ref[...] - lax.axis_index("cent") * count
+    mine = (local >= 0) & (local < count)
+    before = lax.broadcasted_iota(jnp.int32, (rows, rows), 0) <= lax.broadcasted_iota(
+        jnp.int32, (rows, rows), 1
+    )
+    rank = jnp.dot(
+        mine.astype(f32).astype(bf16), before.astype(f32).astype(bf16), preferred_element_type=f32
+    )
+    slot = jnp.where(mine, rank - 1.0, -1.0)
+    local = local.astype(f32)
+    spread_slot = jnp.concatenate(
+        [jnp.broadcast_to(slot[g : g + 1], (slots, rows)) for g in range(groups)], axis=0
+    )
+    spread_local = jnp.concatenate(
+        [jnp.broadcast_to(local[g : g + 1], (slots, rows)) for g in range(groups)], axis=0
+    )
+    number = lax.rem(lax.broadcasted_iota(jnp.int32, (groups * slots, rows), 0), slots).astype(f32)
+    chosen = jnp.sum(jnp.where(spread_slot == number, spread_local + 1.0, 0.0), axis=1, keepdims=True)
+    chosen = chosen.astype(jnp.int32) - 1
+
+    small[1].wait()
+    small[2].wait()
     scales = scales_t[...].astype(f32).T
     squares = None
     for b in range(scales.shape[1]):
@@ -47,96 +81,48 @@
         squares = wide * wide if squares is None else squares + wide * wide
     squares_ref[...] = jnp.sum(squares.T, axis=0, keepdims=True)
 
-
-def quantize(values, scales):
-    rows, width = values.shape
-    scales = scales.T
-    return pl.pallas_call(
-        quantize_kernel,
-        out_shape=(
-            pltpu.VMEM((rows, width), bf16),
-            pltpu.VMEM((1, rows), f32),
-        ),
-        in_specs=[HBM, HBM],
-        out_specs=(VM, VM),
-        scratch_shapes=[
-            pltpu.VMEM(values.shape, bf16),
-            pltpu.VMEM(scales.shape, bf16),
-            pltpu.SemaphoreType.DMA((2,)),
-        ],
-        cost_estimate=pl.CostEstimate(flops=rows * width * 3, bytes_accessed=rows * width * 4, transcendentals=0),
-        compiler_params=LIMIT,
-        name="quantize",
-    )(off_chip(values), off_chip(scales))
-
-
-def gather_kernel(slots, step, ids_hbm, cents_hbm, out_ref, ids_ref, cents_ref, onehot_ref, sems):
-    count, width = cents_hbm.shape
-    groups, rows = ids_ref.shape
-    ids_copy = pltpu.make_async_copy(ids_hbm, ids_ref, sems.at[width // step])
-    ids_copy.start()
-    copies = [
-        pltpu.make_async_copy(
-            cents_hbm.at[:, pl.ds(step * j, step)], cents_ref.at[j], sems.at[j]
-        )
-        for j in range(width // step)
-    ]
-    for copy in copies[:2]:
-        copy.start()
-    ids_copy.wait()
-    local = ids_ref[...] - lax.axis_index("cent") * count
-    mine = (local >= 0) & (local < count)
-    before = lax.broadcasted_iota(jnp.int32, (rows, rows), 0) <= lax.broadcasted_iota(
-        jnp.int32, (rows, rows), 1
-    )
-    rank = jnp.dot(
-        mine.astype(f32).astype(bf16), before.astype(f32).astype(bf16), preferred_element_type=f32
-    )
-    slot = jnp.where(mine, rank - 1.0, -1.0)
-    local = local.astype(f32)
-    spread_slot = jnp.concatenate(
-        [jnp.broadcast_to(slot[g : g + 1], (slots, rows)) for g in range(groups)], axis=0
-    )
-    spread_local = jnp.concatenate(
-        [jnp.broadcast_to(local[g : g + 1], (slots, rows)) for g in range(groups)], axis=0
-    )
-    number = lax.rem(lax.broadcasted_iota(jnp.int32, (groups * slots, rows), 0), slots).astype(f32)
-    chosen = jnp.sum(jnp.where(spread_slot == number, spread_local + 1.0, 0.0), axis=1, keepdims=True)
-    chosen = chosen.astype(jnp.int32) - 1
     for j in range(count // 256):
         at = lax.broadcasted_iota(jnp.int32, (groups * slots, 256), 1) + 256 * j
         onehot_ref[:, 256 * j : 256 * j + 256] = (at == chosen).astype(f32).astype(bf16)
-    for j, copy in enumerate(copies):
+    for j, copy in enumerate(large):
         copy.wait()
-        if j + 2 < len(copies):
-            copies[j + 2].start()
+        if j + 2 < len(large):
+            large[j + 2].start()
         lanes = slice(step * j, step * j + step)
         out_ref[:, lanes] = jnp.dot(
             onehot_ref[...], cents_ref[j], preferred_element_type=f32
         ).astype(bf16)
 
 
-def gather(ids, cents, slots):
-    groups, _ = ids.shape
-    count, width = cents.shape
+def prepare(values, scales, ids, cents, slots):
+    rows, width = values.shape
+    groups = ids.shape[0]
+    count = cents.shape[0]
+    scales = scales.T
     step = 256
     return pl.pallas_call(
-        functools.partial(gather_kernel, slots, step),
-        out_shape=pltpu.VMEM((groups * slots, width), bf16),
-        in_specs=[HBM, HBM],
-        out_specs=VM,
+        functools.partial(prepare_kernel, slots, step),
+        out_shape=(
+            pltpu.VMEM((rows, width), bf16),
+            pltpu.VMEM((1, rows), f32),
+            pltpu.VMEM((groups * slots, width), bf16),
+        ),
+        in_specs=[HBM] * 4,
+        out_specs=(VM, VM, VM),
         scratch_shapes=[
+            pltpu.VMEM(values.shape, bf16),
+            pltpu.VMEM(scales.shape, bf16),
             pltpu.VMEM(ids.shape, jnp.int32),
             pltpu.VMEM((width // step, count, step), bf16),
             pltpu.VMEM((groups * slots, count), bf16),
-            pltpu.SemaphoreType.DMA((width // step + 1,)),
+            pltpu.SemaphoreType.DMA((width // step + 3,)),
         ],
         cost_estimate=pl.CostEstimate(
             flops=2 * groups * slots * count * width, bytes_accessed=count * width * 2, transcendentals=0
         ),
         compiler_params=LIMIT,
-        name="gather",
-    )(off_chip(ids), off_chip(cents))
+        name="prepare",
+    )(off_chip(values), off_chip(scales), off_chip(ids), off_chip(cents))
 
 
 def residual_kernel(count, slots, ids_ref, fetched_ref, q_ref, out_ref):
@@ -175,27 +161,37 @@
     )(ids, on_chip(fetched), on_chip(q))
 
 
-def nearest_kernel(step, ahead, *refs):
-    x_refs, (cents_hbm, out_ref, cents_ref, sems) = refs[:-4], refs[-4:]
-    half = step // 2
-    copies = [
-        pltpu.make_async_copy(cents_hbm.at[pl.ds(half * i, half), :], cents_ref.at[i], sems.at[i])
-        for i in range(cents_ref.shape[0])
-    ]
+def nearest_kernel(step, ahead, blocks, mode, *refs):
+    x_refs, refs = refs[:blocks], refs[blocks:]
+    if mode == "again":
+        cents_ref, squares_ref, out_ref = refs
+        copies = []
+    else:
+        cents_hbm, out_ref, cents_ref, squares_ref, sems = refs
+        half = step // 2
+        copies = [
+            pltpu.make_async_copy(cents_hbm.at[pl.ds(half * i, half), :], cents_ref.at[i], sems.at[i])
+            for i in range(cents_ref.shape[0])
+        ]
     for copy in copies[:ahead]:
         copy.start()
-    best = [None] * (len(x_refs) // 2)
-    for i in range(0, len(copies), 2):
-        for k in (i, i + 1):
+    best = [None] * (blocks // 2)
+    for i in range(0, cents_ref.shape[0], 2):
+        for k in (i, i + 1) if copies else ():
             copies[k].wait()
             if k + ahead < len(copies):
                 copies[k + ahead].start()
         block = jnp.concatenate([cents_ref[i], cents_ref[i + 1]], axis=0)
-        total = None
-        for b in range(block.shape[1] // 128):
-            wide = block[:, 128 * b : 128 * b + 128].astype(f32)
-            total = wide * wide if total is None else total + wide * wide
-        squares = jnp.broadcast_to(jnp.sum(total, axis=1, keepdims=True), (step, 128))
+        at = slice(step // 2 * i, step // 2 * i + step)
+        if mode == "again":
+            squares = squares_ref[at, :]
+        else:
+            total = None
+            for b in range(block.shape[1] // 128):
+                wide = block[:, 128 * b : 128 * b + 128].astype(f32)
+                total = wide * wide if total is None else total + wide * wide
+            squares = jnp.broadcast_to(jnp.sum(total, axis=1, keepdims=True), (step, 128))
+            squares_ref[at, :] = squares
         squares = jnp.concatenate([squares, squares], axis=1)
         for j in range(len(best)):
             x = jnp.concatenate([x_refs[2 * j][...], x_refs[2 * j + 1][...]], axis=0)
@@ -207,25 +203,32 @@
             out_ref[2 * j + k : 2 * j + k + 1, :] = low[:, 128 * k : 128 * k + 128]
 
 
-def nearest(xs, cents):
+def nearest(xs, cents, mode, kept=()):
     count, width = cents.shape
     rows = sum(x.shape[0] for x in xs)
     step = 512
-    return pl.pallas_call(
-        functools.partial(nearest_kernel, step, 3),
-        out_shape=pltpu.VMEM((rows // 128, 128), f32),
-        in_specs=[VM] * len(xs) + [HBM],
-        out_specs=VM,
-        scratch_shapes=[
-            pltpu.VMEM((2 * count // step, step // 2, width), bf16),
-            pltpu.SemaphoreType.DMA((2 * count // step,)),
-        ],
+    out = [pltpu.VMEM((rows // 128, 128), f32)]
+    held = [pltpu.VMEM((2 * count // step, step // 2, width), bf16), pltpu.VMEM((count, 128), f32)]
+    sems = [pltpu.SemaphoreType.DMA((2 * count // step,))]
+    more = {
+        "once": ([HBM], out, held + sems),
+        "keep": ([HBM], out + held, sems),
+        "again": ([VM, VM], out, []),
+    }
+    ins, outs, scratch = more[mode]
+    result = pl.pallas_call(
+        functools.partial(nearest_kernel, step, 3, len(xs), mode),
+        out_shape=tuple(outs),
+        in_specs=[VM] * len(xs) + ins,
+        out_specs=tuple([VM] * len(outs)),
+        scratch_shapes=scratch,
         cost_estimate=pl.CostEstimate(
             flops=2 * rows * count * width, bytes_accessed=count * width * 2 + rows * width * 2, transcendentals=0
         ),
         compiler_params=LIMIT,
         name="nearest",
-    )(*[on_chip(x) for x in xs], off_chip(cents))
+    )(*[on_chip(x) for x in xs], *([on_chip(x) for x in kept] or [off_chip(cents)]))
+    return result[0], result[1:]
 
 
 def halves_of(x):
@@ -390,14 +393,13 @@
     peers = coarse_ids.shape[0]
     slots = 16
 
-    q, row_squares = quantize(emb_values, emb_scales)
+    q, row_squares, sent = prepare(emb_values, emb_scales, coarse_ids, centroids, slots)
 
     core = 1
 
     blocks = {0: q, 2: swap(q, 2), 6: swap(q, 6), 8: swap(q, 8)}
     blocks[core] = swap(q, core)
 
-    sent = gather(coarse_ids, centroids, slots)
     fetched = lax.all_to_all(sent.reshape(peers, slots, width), "cent", 0, 0)
     fetched = fetched.reshape(peers * slots, width)
 
@@ -408,10 +410,11 @@
     for d in (2, 6, 8, 4, 10, 14, 12):
         blocks[d ^ core] = swap(blocks[d], core)
 
-    orders = ((0, 1, 2, 3, 6, 7, 8, 9), (4, 5, 10, 11, 14, 15, 12, 13))
-    lows = []
-    for order in orders:
-        lows.append(nearest([blocks[d] for d in order], centroids))
+    orders = ((0, 1, 2, 3), (6, 7, 8, 9, 4, 5, 10, 11, 14, 15), (12, 13))
+    lows, kept = [], ()
+    for order, mode in zip(orders, ("once", "keep", "again")):
+        low, kept = nearest([blocks[d] for d in order], centroids, mode, kept)
+        lows.append(low)
     where = {d: (k, j) for k, order in enumerate(orders) for j, d in enumerate(order)}
 
     residual = residuals(coarse_ids, fetched, q, count, slots)

time: 85.5 us -> 80.3 us (0.939)
  starting transfers between devices: 40.2 us -> 37.3 us
  waiting for transfers between devices: 20.1 us -> 17.9 us
    ppermute x21, starting transfers between devices: 23 us -> 20.1 us  [swap(): return lax.ppermute(x, 'cent', [(i, i ^ offset) for i in range(16)])]
    ppermute x21, waiting for transfers between devices: 19.5 us -> 17.9 us  [swap(): return lax.ppermute(x, 'cent', [(i, i ^ offset) for i in range(16)])]
  transfers between devices with their start and end apart: 23 -> 23, of which waited for: 9 -> 7; matrix products, arithmetic and copies ran while one was open for 0% -> 0% of each run, Pallas kernels for 20% -> 20%
where the time goes in v3:
time: 80.3 us; the launch traced here: 79.9 us
  starting transfers between devices  37.3 us (46%)
  Pallas kernels  23.9 us (30%)
  waiting for transfers between devices  17.9 us (22%)
    ppermute x21, starting transfers between devices, swap(): return lax.ppermute(x, 'cent', [(i, i ^ offset) for i in range(16)])  20.1 us
    ppermute x21, waiting for transfers between devices, swap(): return lax.ppermute(x, 'cent', [(i, i ^ offset) for i in range(16)])  17.9 us
    pallas_call x3, Pallas kernels, nearest(): pl.pallas_call(functools.partial(nearest_kernel, step, 3, len(xs), mode),...  15 us
    all_to_all x1, starting transfers between devices, step(): sub = lax.all_to_all(stacked, 'rows', 0, 0)  9.85 us
    all_to_all x1, starting transfers between devices, step(): fetched = lax.all_to_all(sent.reshape(peers, slots, width), 'cent', 0, 0)  7.34 us
    pallas_call x1, Pallas kernels, prepare(): pl.pallas_call(functools.partial(prepare_kernel, slots, step), out_shape=...  5.2 us
  transfers between devices with their start and end apart: 23, of which 7 were waited for; matrix products, arithmetic and copies ran while one was open for 0% of the time, Pallas kernels for 20%

profile of v3, /device:TPU:1, one launch (start us, length us, event | category | flops | bytes accessed | tf_op | source)
XLA Modules:
  0.0 79.9 jit_solution(7215869507527211466)
XLA Ops:
  0.6 5.2 %prepare.1 = (bf16[128,1024]{1,0:T(8,128)(2,1)S(1)}, f32[1,128]{1,0:T(1,128)S(1)}, bf16[256,1024]{1,0:T(8,128)(2,1)}) custom-call(bf16[128,1024]{1,0:T(8,128)(2,1)} %values_hbm.1, bf16[8,128]{1,0:T(8,128)(2,1)} %bitcast.16, s32[16,128]{1,0:T(8,128)} %ids_ref.1, bf16[2048,1024]{1,0:T(8,128)(2,1)} %refs_10_.1), custom_call_target="tpu_custom_call" | custom-call | flops 1073741824 | bytes 4194304 | tf_op jit(solution)/shard_map/prepare/pallas_call | solution.py:103
  5.8 7.3 %all-to-all-start = ((bf16[16,16,1024]{2,1,0:T(8,128)(2,1)}), bf16[16,16,1024]{2,1,0:T(8,128)(2,1)S(1)}, u32[]{:S(2)}, u32[]{:S(2)}) async-start(bf16[16,16,1024]{2,1,0:T(8,128)(2,1)} %bitcast.1), calls=%async_computation | async-start | bytes 1048576 | tf_op jit(solution)/shard_map/all_to_all | solution.py:403
  13.2 1.4 %collective-permute-start.1 = (bf16[128,1024]{1,0:T(8,128)(2,1)S(1)}, bf16[128,1024]{1,0:T(8,128)(2,1)S(1)}, u32[]{:S(2)}, u32[]{:S(2)}) collective-permute-start(bf16[128,1024]{1,0:T(8,128)(2,1)S(1)} %get-tuple-element.18.q_ref.refs_0_), channel_id=1, source_target_pairs={{0,2},{1,3},{2,0},{3,1},{4,6},{5,7},{6,4},{7,5},{8,10},{9,11},{10,... | collective-permute-start | bytes 786440 | tf_op jit(solution)/shard_map/ppermute | solution.py:386
  14.5 1.2 %collective-permute-start.5 = (bf16[128,1024]{1,0:T(8,128)(2,1)S(1)}, bf16[128,1024]{1,0:T(8,128)(2,1)S(1)}, u32[]{:S(2)}, u32[]{:S(2)}) collective-permute-start(bf16[128,1024]{1,0:T(8,128)(2,1)S(1)} %get-tuple-element.18.q_ref.refs_0_), channel_id=1, source_target_pairs={{0,8},{1,9},{2,10},{3,11},{4,12},{5,13},{6,14},{7,15},{8,0},{9,1},... | collective-permute-start | bytes 786440 | tf_op jit(solution)/shard_map/ppermute | solution.py:386
  15.7 1.8 %collective-permute-start.3 = (bf16[128,1024]{1,0:T(8,128)(2,1)S(1)}, bf16[128,1024]{1,0:T(8,128)(2,1)S(1)}, u32[]{:S(2)}, u32[]{:S(2)}) collective-permute-start(bf16[128,1024]{1,0:T(8,128)(2,1)S(1)} %get-tuple-element.18.q_ref.refs_0_), channel_id=1, source_target_pairs={{0,6},{1,7},{2,4},{3,5},{4,2},{5,3},{6,0},{7,1},{8,14},{9,15},{10,... | collective-permute-start | bytes 786440 | tf_op jit(solution)/shard_map/ppermute | solution.py:386
  17.5 1.2 %collective-permute-start = (bf16[128,1024]{1,0:T(8,128)(2,1)S(1)}, bf16[128,1024]{1,0:T(8,128)(2,1)S(1)}, u32[]{:S(2)}, u32[]{:S(2)}) collective-permute-start(bf16[128,1024]{1,0:T(8,128)(2,1)S(1)} %get-tuple-element.18.q_ref.refs_0_), channel_id=1, source_target_pairs={{0,1},{1,0},{2,3},{3,2},{4,5},{5,4},{6,7},{7,6},{8,9},{9,8},{10,11... | collective-permute-start | bytes 786440 | tf_op jit(solution)/shard_map/ppermute | solution.py:386
  18.8 7.9 %collective-permute-done.1.refs_2_ = bf16[128,1024]{1,0:T(8,128)(2,1)S(1)} collective-permute-done((bf16[128,1024]{1,0:T(8,128)(2,1)S(1)}, bf16[128,1024]{1,0:T(8,128)(2,1)S(1)}, u32[]{:S(2)}, u32[]{:S(2)}) %collective-permute-start.1) | collective-permute-done | bytes 262176 | tf_op jit(solution)/shard_map/ppermute | solution.py:386
  27.6 1.8 %collective-permute-start.11 = (bf16[128,1024]{1,0:T(8,128)(2,1)S(1)}, bf16[128,1024]{1,0:T(8,128)(2,1)S(1)}, u32[]{:S(2)}, u32[]{:S(2)}) collective-permute-start(bf16[128,1024]{1,0:T(8,128)(2,1)S(1)} %collective-permute-done.5.refs_2_), channel_id=1, source_target_pairs={{0,6},{1,7},{2,4},{3,5},{4,2},{5,3},{6,0},{7,1},{8,14},{9,15},{10,... | collective-permute-start | bytes 786440 | tf_op jit(solution)/shard_map/ppermute | solution.py:386
  29.7 1.2 %collective-permute-start.9 = (bf16[128,1024]{1,0:T(8,128)(2,1)S(1)}, bf16[128,1024]{1,0:T(8,128)(2,1)S(1)}, u32[]{:S(2)}, u32[]{:S(2)}) collective-permute-start(bf16[128,1024]{1,0:T(8,128)(2,1)S(1)} %collective-permute-done.5.refs_2_), channel_id=1, source_target_pairs={{0,2},{1,3},{2,0},{3,1},{4,6},{5,7},{6,4},{7,5},{8,10},{9,11},{10,... | collective-permute-start | bytes 786440 | tf_op jit(solution)/shard_map/ppermute | solution.py:386
  30.9 1.4 %collective-permute-start.4 = (bf16[128,1024]{1,0:T(8,128)(2,1)S(1)}, bf16[128,1024]{1,0:T(8,128)(2,1)S(1)}, u32[]{:S(2)}, u32[]{:S(2)}) collective-permute-start(bf16[128,1024]{1,0:T(8,128)(2,1)S(1)} %collective-permute-done.3.refs_0_), channel_id=1, source_target_pairs={{0,1},{1,0},{2,3},{3,2},{4,5},{5,4},{6,7},{7,6},{8,9},{9,8},{10,11... | collective-permute-start | bytes 786440 | tf_op jit(solution)/shard_map/ppermute | solution.py:386
  32.3 1.3 %residuals.1 = f32[1024,128]{1,0:T(8,128)} custom-call(s32[16,128]{1,0:T(8,128)S(1)} %copy-done.1, bf16[256,1024]{1,0:T(8,128)(2,1)S(1)} %bitcast.14, bf16[128,1024]{1,0:T(8,128)(2,1)S(1)} %get-tuple-element.18.q_ref.refs_0_), custom_call_target="tpu_custom_call" | custom-call | flops 67108864 | bytes 1310720 | tf_op jit(solution)/shard_map/residuals/pallas_call | solution.py:151
  33.7 9.9 %all-to-all-start.1 = ((f32[16,64,128]{2,1,0:T(8,128)}), f32[16,64,128]{2,1,0:T(8,128)S(1)}, u32[]{:S(2)}, u32[]{:S(2)}) async-start(f32[16,64,128]{2,1,0:T(8,128)} %bitcast.3), calls=%async_computation.1 | async-start | bytes 1048576 | tf_op jit(solution)/shard_map/all_to_all | solution.py:422
  44.9 4.9 %nearest.3.refs_0_ = f32[4,128]{1,0:T(4,128)S(1)} custom-call(bf16[128,1024]{1,0:T(8,128)(2,1)S(1)} %get-tuple-element.18.q_ref.refs_0_, bf16[128,1024]{1,0:T(8,128)(2,1)S(1)} %collective-permute-done.refs_1_, bf16[128,1024]{1,0:T(8,128)(2,1)S(1)} %collective-permute-done.1.refs_2_, bf16[128,1024]{1,0:T(8,128)(2,1)S(1)} %collective-permute-done.2.refs_3_, ...), custom_call_target="tpu_custom_call" | custom-call | flops 2147483648 | bytes 5242880 | tf_op jit(solution)/shard_map/nearest/pallas_call | solution.py:219
  49.8 1.7 %collective-permute-done.13.refs_0_ = bf16[128,1024]{1,0:T(8,128)(2,1)S(1)} collective-permute-done((bf16[128,1024]{1,0:T(8,128)(2,1)S(1)}, bf16[128,1024]{1,0:T(8,128)(2,1)S(1)}, u32[]{:S(2)}, u32[]{:S(2)}) %collective-permute-start.13) | collective-permute-done | bytes 262176 | tf_op jit(solution)/shard_map/ppermute | solution.py:386
  51.6 1.1 %collective-permute-start.14 = (bf16[128,1024]{1,0:T(8,128)(2,1)S(1)}, bf16[128,1024]{1,0:T(8,128)(2,1)S(1)}, u32[]{:S(2)}, u32[]{:S(2)}) collective-permute-start(bf16[128,1024]{1,0:T(8,128)(2,1)S(1)} %collective-permute-done.13.refs_0_), channel_id=1, source_target_pairs={{0,1},{1,0},{2,3},{3,2},{4,5},{5,4},{6,7},{7,6},{8,9},{9,8},{10,11... | collective-permute-start | bytes 786440 | tf_op jit(solution)/shard_map/ppermute | solution.py:386
  52.7 8.8 %nearest.4 = (f32[10,128]{1,0:T(8,128)S(1)}, bf16[8,256,1024]{2,1,0:T(8,128)(2,1)S(1)}, f32[2048,128]{1,0:T(8,128)S(1)}) custom-call(bf16[128,1024]{1,0:T(8,128)(2,1)S(1)} %collective-permute-done.3.refs_0_, bf16[128,1024]{1,0:T(8,128)(2,1)S(1)} %collective-permute-done.4.refs_1_, bf16[128,1024]{1,0:T(8,128)(2,1)S(1)} %collective-permute-done.5.refs_2_, ...), custom_call_target="tpu_custom_call" | custom-call | flops 5368709120 | bytes 6815744 | tf_op jit(solution)/shard_map/nearest/pallas_call | solution.py:219
  61.5 1.3 %nearest.5.refs_2_ = f32[2,128]{1,0:T(2,128)S(1)} custom-call(bf16[128,1024]{1,0:T(8,128)(2,1)S(1)} %collective-permute-done.13.refs_0_, bf16[128,1024]{1,0:T(8,128)(2,1)S(1)} %collective-permute-done.14.refs_1_, bf16[8,256,1024]{2,1,0:T(8,128)(2,1)S(1)} %get-tuple-element.20.refs_2_, f32[2048,128]{1,0:T(8,128)S(1)} %get-tuple-element.21.refs_3_), custom_call_target="tpu_custom_call" | custom-call | flops 1073741824 | bytes 4718592 | tf_op jit(solution)/shard_map/nearest/pallas_call | solution.py:219
  63.8 1.3 %collective-permute-done.15.b_ref = f32[144,128]{1,0:T(8,128)S(1)} collective-permute-done((f32[144,128]{1,0:T(8,128)S(1)}, f32[144,128]{1,0:T(8,128)S(1)}, u32[]{:S(2)}, u32[]{:S(2)}) %collective-permute-start.15) | collective-permute-done | bytes 73760 | tf_op jit(solution)/shard_map/ppermute | solution.py:386
  65.8 3.0 %collective-permute-done.16.b_ref = f32[144,128]{1,0:T(8,128)S(1)} collective-permute-done((f32[144,128]{1,0:T(8,128)S(1)}, f32[144,128]{1,0:T(8,128)S(1)}, u32[]{:S(2)}, u32[]{:S(2)}) %collective-permute-start.16) | collective-permute-done | bytes 73760 | tf_op jit(solution)/shard_map/ppermute | solution.py:386
  68.9 1.4 %collective-permute-start.18 = (f32[144,128]{1,0:T(8,128)S(1)}, f32[144,128]{1,0:T(8,128)S(1)}, u32[]{:S(2)}, u32[]{:S(2)}) collective-permute-start(f32[144,128]{1,0:T(8,128)S(1)} %join.3.a_ref), channel_id=1, source_target_pairs={{0,4},{1,5},{2,6},{3,7},{4,0},{5,1},{6,2},{7,3},{8,12},{9,13},{10,... | collective-permute-start | bytes 221192 | tf_op jit(solution)/shard_map/ppermute | solution.py:386
  70.4 2.4 %collective-permute-start.19 = (f32[144,128]{1,0:T(8,128)S(1)}, f32[144,128]{1,0:T(8,128)S(1)}, u32[]{:S(2)}, u32[]{:S(2)}) collective-permute-start(f32[144,128]{1,0:T(8,128)S(1)} %join.3.a_ref), channel_id=1, source_target_pairs={{0,6},{1,7},{2,4},{3,5},{4,2},{5,3},{6,0},{7,1},{8,14},{9,15},{10,... | collective-permute-start | bytes 221192 | tf_op jit(solution)/shard_map/ppermute | solution.py:386
  72.8 1.7 %collective-permute-done.18.c_ref = f32[144,128]{1,0:T(8,128)S(1)} collective-permute-done((f32[144,128]{1,0:T(8,128)S(1)}, f32[144,128]{1,0:T(8,128)S(1)}, u32[]{:S(2)}, u32[]{:S(2)}) %collective-permute-start.18) | collective-permute-done | bytes 73760 | tf_op jit(solution)/shard_map/ppermute | solution.py:386
  74.5 1.4 %collective-permute-done.19.d_ref = f32[144,128]{1,0:T(8,128)S(1)} collective-permute-done((f32[144,128]{1,0:T(8,128)S(1)}, f32[144,128]{1,0:T(8,128)S(1)}, u32[]{:S(2)}, u32[]{:S(2)}) %collective-permute-start.19) | collective-permute-done | bytes 73760 | tf_op jit(solution)/shard_map/ppermute | solution.py:386
  76.4 1.7 %collective-permute-start.20 = (f32[128,128]{1,0:T(8,128)S(1)}, f32[128,128]{1,0:T(8,128)S(1)}, u32[]{:S(2)}, u32[]{:S(2)}) collective-permute-start(f32[128,128]{1,0:T(8,128)S(1)} %get-tuple-element.26.mine_ref), channel_id=1, source_target_pairs={{0,1},{1,0},{2,3},{3,2},{4,5},{5,4},{6,7},{7,6},{8,9},{9,8},{10,11... | collective-permute-start | bytes 196616 | tf_op jit(solution)/shard_map/ppermute | solution.py:386
  (40 shorter events, 6.8 us)
Async XLA Ops:
  0.6 31.7 %copy-start.1 = (s32[16,128]{1,0:T(8,128)S(1)}, s32[16,128]{1,0:T(8,128)}, u32[]{:S(2)}) copy-start(s32[16,128]{1,0:T(8,128)} %ids_ref.1) | copy-start | bytes 24580
  5.8 26.5 %all-to-all-start = ((bf16[16,16,1024]{2,1,0:T(8,128)(2,1)}), bf16[16,16,1024]{2,1,0:T(8,128)(2,1)S(1)}, u32[]{:S(2)}, u32[]{:S(2)}) async-start(bf16[16,16,1024]{2,1,0:T(8,128)(2,1)} %bitcast.1), calls=%async_computation | async-start | bytes 1048576 | tf_op jit(solution)/shard_map/all_to_all | solution.py:403
  13.2 13.5 %collective-permute-start.1 = (bf16[128,1024]{1,0:T(8,128)(2,1)S(1)}, bf16[128,1024]{1,0:T(8,128)(2,1)S(1)}, u32[]{:S(2)}, u32[]{:S(2)}) collective-permute-start(bf16[128,1024]{1,0:T(8,128)(2,1)S(1)} %get-tuple-element.18.q_ref.refs_0_), channel_id=1, source_target_pairs={{0,2},{1,3},{2,0},{3,1},{4,6},{5,7},{6,4},{7,5},{8,10},{9,11},{10,... | collective-permute-start | bytes 786440 | tf_op jit(solution)/shard_map/ppermute | solution.py:386
  14.5 13.1 %collective-permute-start.5 = (bf16[128,1024]{1,0:T(8,128)(2,1)S(1)}, bf16[128,1024]{1,0:T(8,128)(2,1)S(1)}, u32[]{:S(2)}, u32[]{:S(2)}) collective-permute-start(bf16[128,1024]{1,0:T(8,128)(2,1)S(1)} %get-tuple-element.18.q_ref.refs_0_), channel_id=1, source_target_pairs={{0,8},{1,9},{2,10},{3,11},{4,12},{5,13},{6,14},{7,15},{8,0},{9,1},... | collective-permute-start | bytes 786440 | tf_op jit(solution)/shard_map/ppermute | solution.py:386
  15.7 13.7 %collective-permute-start.3 = (bf16[128,1024]{1,0:T(8,128)(2,1)S(1)}, bf16[128,1024]{1,0:T(8,128)(2,1)S(1)}, u32[]{:S(2)}, u32[]{:S(2)}) collective-permute-start(bf16[128,1024]{1,0:T(8,128)(2,1)S(1)} %get-tuple-element.18.q_ref.refs_0_), channel_id=1, source_target_pairs={{0,6},{1,7},{2,4},{3,5},{4,2},{5,3},{6,0},{7,1},{8,14},{9,15},{10,... | collective-permute-start | bytes 786440 | tf_op jit(solution)/shard_map/ppermute | solution.py:386
  17.5 13.4 %collective-permute-start = (bf16[128,1024]{1,0:T(8,128)(2,1)S(1)}, bf16[128,1024]{1,0:T(8,128)(2,1)S(1)}, u32[]{:S(2)}, u32[]{:S(2)}) collective-permute-start(bf16[128,1024]{1,0:T(8,128)(2,1)S(1)} %get-tuple-element.18.q_ref.refs_0_), channel_id=1, source_target_pairs={{0,1},{1,0},{2,3},{3,2},{4,5},{5,4},{6,7},{7,6},{8,9},{9,8},{10,11... | collective-permute-start | bytes 786440 | tf_op jit(solution)/shard_map/ppermute | solution.py:386
  26.6 16.9 %collective-permute-start.2 = (bf16[128,1024]{1,0:T(8,128)(2,1)S(1)}, bf16[128,1024]{1,0:T(8,128)(2,1)S(1)}, u32[]{:S(2)}, u32[]{:S(2)}) collective-permute-start(bf16[128,1024]{1,0:T(8,128)(2,1)S(1)} %collective-permute-done.1.refs_2_), channel_id=1, source_target_pairs={{0,1},{1,0},{2,3},{3,2},{4,5},{5,4},{6,7},{7,6},{8,9},{9,8},{10,11... | collective-permute-start | bytes 786440 | tf_op jit(solution)/shard_map/ppermute | solution.py:386
  27.6 16.3 %collective-permute-start.11 = (bf16[128,1024]{1,0:T(8,128)(2,1)S(1)}, bf16[128,1024]{1,0:T(8,128)(2,1)S(1)}, u32[]{:S(2)}, u32[]{:S(2)}) collective-permute-start(bf16[128,1024]{1,0:T(8,128)(2,1)S(1)} %collective-permute-done.5.refs_2_), channel_id=1, source_target_pairs={{0,6},{1,7},{2,4},{3,5},{4,2},{5,3},{6,0},{7,1},{8,14},{9,15},{10,... | collective-permute-start | bytes 786440 | tf_op jit(solution)/shard_map/ppermute | solution.py:386
  29.4 14.5 %collective-permute-start.7 = (bf16[128,1024]{1,0:T(8,128)(2,1)S(1)}, bf16[128,1024]{1,0:T(8,128)(2,1)S(1)}, u32[]{:S(2)}, u32[]{:S(2)}) collective-permute-start(bf16[128,1024]{1,0:T(8,128)(2,1)S(1)} %collective-permute-done.3.refs_0_), channel_id=1, source_target_pairs={{0,2},{1,3},{2,0},{3,1},{4,6},{5,7},{6,4},{7,5},{8,10},{9,11},{10,... | collective-permute-start | bytes 786440 | tf_op jit(solution)/shard_map/ppermute | solution.py:386
  29.7 14.7 %collective-permute-start.9 = (bf16[128,1024]{1,0:T(8,128)(2,1)S(1)}, bf16[128,1024]{1,0:T(8,128)(2,1)S(1)}, u32[]{:S(2)}, u32[]{:S(2)}) collective-permute-start(bf16[128,1024]{1,0:T(8,128)(2,1)S(1)} %collective-permute-done.5.refs_2_), channel_id=1, source_target_pairs={{0,2},{1,3},{2,0},{3,1},{4,6},{5,7},{6,4},{7,5},{8,10},{9,11},{10,... | collective-permute-start | bytes 786440 | tf_op jit(solution)/shard_map/ppermute | solution.py:386
  30.9 13.6 %collective-permute-start.4 = (bf16[128,1024]{1,0:T(8,128)(2,1)S(1)}, bf16[128,1024]{1,0:T(8,128)(2,1)S(1)}, u32[]{:S(2)}, u32[]{:S(2)}) collective-permute-start(bf16[128,1024]{1,0:T(8,128)(2,1)S(1)} %collective-permute-done.3.refs_0_), channel_id=1, source_target_pairs={{0,1},{1,0},{2,3},{3,2},{4,5},{5,4},{6,7},{7,6},{8,9},{9,8},{10,11... | collective-permute-start | bytes 786440 | tf_op jit(solution)/shard_map/ppermute | solution.py:386
  33.7 29.2 %all-to-all-start.1 = ((f32[16,64,128]{2,1,0:T(8,128)}), f32[16,64,128]{2,1,0:T(8,128)S(1)}, u32[]{:S(2)}, u32[]{:S(2)}) async-start(f32[16,64,128]{2,1,0:T(8,128)} %bitcast.3), calls=%async_computation.1 | async-start | bytes 1048576 | tf_op jit(solution)/shard_map/all_to_all | solution.py:422
  43.5 9.1 %collective-permute-start.6 = (bf16[128,1024]{1,0:T(8,128)(2,1)S(1)}, bf16[128,1024]{1,0:T(8,128)(2,1)S(1)}, u32[]{:S(2)}, u32[]{:S(2)}) collective-permute-start(bf16[128,1024]{1,0:T(8,128)(2,1)S(1)} %collective-permute-done.5.refs_2_), channel_id=1, source_target_pairs={{0,1},{1,0},{2,3},{3,2},{4,5},{5,4},{6,7},{7,6},{8,9},{9,8},{10,11... | collective-permute-start | bytes 786440 | tf_op jit(solution)/shard_map/ppermute | solution.py:386
  43.9 7.6 %collective-permute-start.13 = (bf16[128,1024]{1,0:T(8,128)(2,1)S(1)}, bf16[128,1024]{1,0:T(8,128)(2,1)S(1)}, u32[]{:S(2)}, u32[]{:S(2)}) collective-permute-start(bf16[128,1024]{1,0:T(8,128)(2,1)S(1)} %collective-permute-done.11.refs_8_), channel_id=1, source_target_pairs={{0,2},{1,3},{2,0},{3,1},{4,6},{5,7},{6,4},{7,5},{8,10},{9,11},{10,... | collective-permute-start | bytes 786440 | tf_op jit(solution)/shard_map/ppermute | solution.py:386
  43.9 8.7 %collective-permute-start.8 = (bf16[128,1024]{1,0:T(8,128)(2,1)S(1)}, bf16[128,1024]{1,0:T(8,128)(2,1)S(1)}, u32[]{:S(2)}, u32[]{:S(2)}) collective-permute-start(bf16[128,1024]{1,0:T(8,128)(2,1)S(1)} %collective-permute-done.7.refs_4_), channel_id=1, source_target_pairs={{0,1},{1,0},{2,3},{3,2},{4,5},{5,4},{6,7},{7,6},{8,9},{9,8},{10,11... | collective-permute-start | bytes 786440 | tf_op jit(solution)/shard_map/ppermute | solution.py:386
  44.4 8.3 %collective-permute-start.10 = (bf16[128,1024]{1,0:T(8,128)(2,1)S(1)}, bf16[128,1024]{1,0:T(8,128)(2,1)S(1)}, u32[]{:S(2)}, u32[]{:S(2)}) collective-permute-start(bf16[128,1024]{1,0:T(8,128)(2,1)S(1)} %collective-permute-done.9.refs_6_), channel_id=1, source_target_pairs={{0,1},{1,0},{2,3},{3,2},{4,5},{5,4},{6,7},{7,6},{8,9},{9,8},{10,11... | collective-permute-start | bytes 786440 | tf_op jit(solution)/shard_map/ppermute | solution.py:386
  44.5 8.1 %collective-permute-start.12 = (bf16[128,1024]{1,0:T(8,128)(2,1)S(1)}, bf16[128,1024]{1,0:T(8,128)(2,1)S(1)}, u32[]{:S(2)}, u32[]{:S(2)}) collective-permute-start(bf16[128,1024]{1,0:T(8,128)(2,1)S(1)} %collective-permute-done.11.refs_8_), channel_id=1, source_target_pairs={{0,1},{1,0},{2,3},{3,2},{4,5},{5,4},{6,7},{7,6},{8,9},{9,8},{10,11... | collective-permute-start | bytes 786440 | tf_op jit(solution)/shard_map/ppermute | solution.py:386
  51.6 9.9 %collective-permute-start.14 = (bf16[128,1024]{1,0:T(8,128)(2,1)S(1)}, bf16[128,1024]{1,0:T(8,128)(2,1)S(1)}, u32[]{:S(2)}, u32[]{:S(2)}) collective-permute-start(bf16[128,1024]{1,0:T(8,128)(2,1)S(1)} %collective-permute-done.13.refs_0_), channel_id=1, source_target_pairs={{0,1},{1,0},{2,3},{3,2},{4,5},{5,4},{6,7},{7,6},{8,9},{9,8},{10,11... | collective-permute-start | bytes 786440 | tf_op jit(solution)/shard_map/ppermute | solution.py:386
  63.7 1.4 %collective-permute-start.15 = (f32[144,128]{1,0:T(8,128)S(1)}, f32[144,128]{1,0:T(8,128)S(1)}, u32[]{:S(2)}, u32[]{:S(2)}) collective-permute-start(f32[144,128]{1,0:T(8,128)S(1)} %get-tuple-element.23), channel_id=1, source_target_pairs={{0,1},{1,0},{2,3},{3,2},{4,5},{5,4},{6,7},{7,6},{8,9},{9,8},{10,11... | collective-permute-start | bytes 221192 | tf_op jit(solution)/shard_map/ppermute | solution.py:386
  65.1 3.8 %collective-permute-start.16 = (f32[144,128]{1,0:T(8,128)S(1)}, f32[144,128]{1,0:T(8,128)S(1)}, u32[]{:S(2)}, u32[]{:S(2)}) collective-permute-start(f32[144,128]{1,0:T(8,128)S(1)} %join.2.a_ref), channel_id=1, source_target_pairs={{0,8},{1,9},{2,10},{3,11},{4,12},{5,13},{6,14},{7,15},{8,0},{9,1},... | collective-permute-start | bytes 221192 | tf_op jit(solution)/shard_map/ppermute | solution.py:386
  68.8 3.9 %collective-permute-start.17 = (f32[144,128]{1,0:T(8,128)S(1)}, f32[144,128]{1,0:T(8,128)S(1)}, u32[]{:S(2)}, u32[]{:S(2)}) collective-permute-start(f32[144,128]{1,0:T(8,128)S(1)} %join.3.a_ref), channel_id=1, source_target_pairs={{0,2},{1,3},{2,0},{3,1},{4,6},{5,7},{6,4},{7,5},{8,10},{9,11},{10,... | collective-permute-start | bytes 221192 | tf_op jit(solution)/shard_map/ppermute | solution.py:386
  68.9 5.5 %collective-permute-start.18 = (f32[144,128]{1,0:T(8,128)S(1)}, f32[144,128]{1,0:T(8,128)S(1)}, u32[]{:S(2)}, u32[]{:S(2)}) collective-permute-start(f32[144,128]{1,0:T(8,128)S(1)} %join.3.a_ref), channel_id=1, source_target_pairs={{0,4},{1,5},{2,6},{3,7},{4,0},{5,1},{6,2},{7,3},{8,12},{9,13},{10,... | collective-permute-start | bytes 221192 | tf_op jit(solution)/shard_map/ppermute | solution.py:386
  70.4 5.5 %collective-permute-start.19 = (f32[144,128]{1,0:T(8,128)S(1)}, f32[144,128]{1,0:T(8,128)S(1)}, u32[]{:S(2)}, u32[]{:S(2)}) collective-permute-start(f32[144,128]{1,0:T(8,128)S(1)} %join.3.a_ref), channel_id=1, source_target_pairs={{0,6},{1,7},{2,4},{3,5},{4,2},{5,3},{6,0},{7,1},{8,14},{9,15},{10,... | collective-permute-start | bytes 221192 | tf_op jit(solution)/shard_map/ppermute | solution.py:386
  76.4 2.6 %collective-permute-start.20 = (f32[128,128]{1,0:T(8,128)S(1)}, f32[128,128]{1,0:T(8,128)S(1)}, u32[]{:S(2)}, u32[]{:S(2)}) collective-permute-start(f32[128,128]{1,0:T(8,128)S(1)} %get-tuple-element.26.mine_ref), channel_id=1, source_target_pairs={{0,1},{1,0},{2,3},{3,2},{4,5},{5,4},{6,7},{7,6},{8,9},{9,8},{10,11... | collective-permute-start | bytes 196616 | tf_op jit(solution)/shard_map/ppermute | solution.py:386
  (3 other events, 17.1 us)

commit v4 on v3

--- a/solution.py
+++ b/solution.py
@@ -45,7 +45,7 @@
     ]
     for copy in small:
         copy.start()
-    for copy in large[:2]:
+    for copy in large:
         copy.start()
 
     small[0].wait()
@@ -86,8 +86,6 @@
         onehot_ref[:, 256 * j : 256 * j + 256] = (at == chosen).astype(f32).astype(bf16)
     for j, copy in enumerate(large):
         copy.wait()
-        if j + 2 < len(large):
-            large[j + 2].start()
         lanes = slice(step * j, step * j + step)
         out_ref[:, lanes] = jnp.dot(
             onehot_ref[...], cents_ref[j], preferred_element_type=f32
@@ -211,7 +209,6 @@
     held = [pltpu.VMEM((2 * count // step, step // 2, width), bf16), pltpu.VMEM((count, 128), f32)]
     sems = [pltpu.SemaphoreType.DMA((2 * count // step,))]
     more = {
-        "once": ([HBM], out, held + sems),
         "keep": ([HBM], out + held, sems),
         "again": ([VM, VM], out, []),
     }
@@ -410,9 +407,9 @@
     for d in (2, 6, 8, 4, 10, 14, 12):
         blocks[d ^ core] = swap(blocks[d], core)
 
-    orders = ((0, 1, 2, 3), (6, 7, 8, 9, 4, 5, 10, 11, 14, 15), (12, 13))
+    orders = ((0, 1, 2, 3, 6, 7, 8, 9), (4, 5, 10, 11, 14, 15, 12, 13))
     lows, kept = [], ()
-    for order, mode in zip(orders, ("once", "keep", "again")):
+    for order, mode in zip(orders, ("keep", "again")):
         low, kept = nearest([blocks[d] for d in order], centroids, mode, kept)
         lows.append(low)
     where = {d: (k, j) for k, order in enumerate(orders) for j, d in enumerate(order)}

time: 80.3 us -> 85.7 us (1.067)
  waiting for transfers between devices: 17.9 us -> 23.7 us
  Pallas kernels: 23.9 us -> 20.9 us
  starting transfers between devices: 37.3 us -> 40 us
    ppermute x21, waiting for transfers between devices: 17.9 us -> 20.9 us  [swap(): return lax.ppermute(x, 'cent', [(i, i ^ offset) for i in range(16)])]
    pallas_call x3 -> x2, Pallas kernels: 15 us -> 12.1 us  [nearest(): pl.pallas_call(functools.partial(nearest_kernel, step, 3, len(xs), mode),...]
    all_to_all x1, waiting for transfers between devices: 0.01 us -> 2.72 us  [step(): sub = lax.all_to_all(stacked, 'rows', 0, 0)]
    ppermute x21, starting transfers between devices: 20.1 us -> 22.8 us  [swap(): return lax.ppermute(x, 'cent', [(i, i ^ offset) for i in range(16)])]
  transfers between devices with their start and end apart: 23 -> 23, of which waited for: 7 -> 9; matrix products, arithmetic and copies ran while one was open for 0% -> 0% of each run, Pallas kernels for 20% -> 16%
where the time goes in v4:
time: 85.7 us; the launch traced here: 85.4 us
  starting transfers between devices  40 us (47%)
  waiting for transfers between devices  23.7 us (28%)
  Pallas kernels  20.9 us (24%)
    ppermute x21, starting transfers between devices, swap(): return lax.ppermute(x, 'cent', [(i, i ^ offset) for i in range(16)])  22.8 us
    ppermute x21, waiting for transfers between devices, swap(): return lax.ppermute(x, 'cent', [(i, i ^ offset) for i in range(16)])  20.9 us
    pallas_call x2, Pallas kernels, nearest(): pl.pallas_call(functools.partial(nearest_kernel, step, 3, len(xs), mode),...  12.1 us
    all_to_all x1, starting transfers between devices, step(): sub = lax.all_to_all(stacked, 'rows', 0, 0)  9.86 us
    all_to_all x1, starting transfers between devices, step(): fetched = lax.all_to_all(sent.reshape(peers, slots, width), 'cent', 0, 0)  7.34 us
    pallas_call x1, Pallas kernels, prepare(): pl.pallas_call(functools.partial(prepare_kernel, slots, step), out_shape=...  5.2 us
    all_to_all x1, waiting for transfers between devices, step(): sub = lax.all_to_all(stacked, 'rows', 0, 0)  2.72 us
  transfers between devices with their start and end apart: 23, of which 9 were waited for; matrix products, arithmetic and copies ran while one was open for 0% of the time, Pallas kernels for 16%

profile of v4, /device:TPU:1, one launch (start us, length us, event | category | flops | bytes accessed | tf_op | source)
XLA Modules:
  0.0 85.4 jit_solution(17181174819845598239)
XLA Ops:
  0.6 5.2 %prepare.1 = (bf16[128,1024]{1,0:T(8,128)(2,1)S(1)}, f32[1,128]{1,0:T(1,128)S(1)}, bf16[256,1024]{1,0:T(8,128)(2,1)}) custom-call(bf16[128,1024]{1,0:T(8,128)(2,1)} %values_hbm.1, bf16[8,128]{1,0:T(8,128)(2,1)} %bitcast.16, s32[16,128]{1,0:T(8,128)} %ids_ref.1, bf16[2048,1024]{1,0:T(8,128)(2,1)} %refs_8_.1), custom_call_target="tpu_custom_call" | custom-call | flops 1073741824 | bytes 4194304 | tf_op jit(solution)/shard_map/prepare/pallas_call | solution.py:101
  5.8 7.3 %all-to-all-start = ((bf16[16,16,1024]{2,1,0:T(8,128)(2,1)}), bf16[16,16,1024]{2,1,0:T(8,128)(2,1)S(1)}, u32[]{:S(2)}, u32[]{:S(2)}) async-start(bf16[16,16,1024]{2,1,0:T(8,128)(2,1)} %bitcast.1), calls=%async_computation | async-start | bytes 1048576 | tf_op jit(solution)/shard_map/all_to_all | solution.py:400
  13.2 1.4 %collective-permute-start.5 = (bf16[128,1024]{1,0:T(8,128)(2,1)S(1)}, bf16[128,1024]{1,0:T(8,128)(2,1)S(1)}, u32[]{:S(2)}, u32[]{:S(2)}) collective-permute-start(bf16[128,1024]{1,0:T(8,128)(2,1)S(1)} %get-tuple-element.18.q_ref.refs_0_), channel_id=1, source_target_pairs={{0,8},{1,9},{2,10},{3,11},{4,12},{5,13},{6,14},{7,15},{8,0},{9,1},... | collective-permute-start | bytes 786440 | tf_op jit(solution)/shard_map/ppermute | solution.py:383
  15.7 1.8 %collective-permute-start.3 = (bf16[128,1024]{1,0:T(8,128)(2,1)S(1)}, bf16[128,1024]{1,0:T(8,128)(2,1)S(1)}, u32[]{:S(2)}, u32[]{:S(2)}) collective-permute-start(bf16[128,1024]{1,0:T(8,128)(2,1)S(1)} %get-tuple-element.18.q_ref.refs_0_), channel_id=1, source_target_pairs={{0,6},{1,7},{2,4},{3,5},{4,2},{5,3},{6,0},{7,1},{8,14},{9,15},{10,... | collective-permute-start | bytes 786440 | tf_op jit(solution)/shard_map/ppermute | solution.py:383
  17.5 1.2 %collective-permute-start = (bf16[128,1024]{1,0:T(8,128)(2,1)S(1)}, bf16[128,1024]{1,0:T(8,128)(2,1)S(1)}, u32[]{:S(2)}, u32[]{:S(2)}) collective-permute-start(bf16[128,1024]{1,0:T(8,128)(2,1)S(1)} %get-tuple-element.18.q_ref.refs_0_), channel_id=1, source_target_pairs={{0,1},{1,0},{2,3},{3,2},{4,5},{5,4},{6,7},{7,6},{8,9},{9,8},{10,11... | collective-permute-start | bytes 786440 | tf_op jit(solution)/shard_map/ppermute | solution.py:383
  18.7 7.9 %collective-permute-done.5.refs_6_ = bf16[128,1024]{1,0:T(8,128)(2,1)S(1)} collective-permute-done((bf16[128,1024]{1,0:T(8,128)(2,1)S(1)}, bf16[128,1024]{1,0:T(8,128)(2,1)S(1)}, u32[]{:S(2)}, u32[]{:S(2)}) %collective-permute-start.5) | collective-permute-done | bytes 262176 | tf_op jit(solution)/shard_map/ppermute | solution.py:383
  26.6 2.4 %collective-permute-start.11 = (bf16[128,1024]{1,0:T(8,128)(2,1)S(1)}, bf16[128,1024]{1,0:T(8,128)(2,1)S(1)}, u32[]{:S(2)}, u32[]{:S(2)}) collective-permute-start(bf16[128,1024]{1,0:T(8,128)(2,1)S(1)} %collective-permute-done.5.refs_6_), channel_id=1, source_target_pairs={{0,6},{1,7},{2,4},{3,5},{4,2},{5,3},{6,0},{7,1},{8,14},{9,15},{10,... | collective-permute-start | bytes 786440 | tf_op jit(solution)/shard_map/ppermute | solution.py:383
  29.0 1.3 %collective-permute-start.2 = (bf16[128,1024]{1,0:T(8,128)(2,1)S(1)}, bf16[128,1024]{1,0:T(8,128)(2,1)S(1)}, u32[]{:S(2)}, u32[]{:S(2)}) collective-permute-start(bf16[128,1024]{1,0:T(8,128)(2,1)S(1)} %collective-permute-done.1.refs_2_), channel_id=1, source_target_pairs={{0,1},{1,0},{2,3},{3,2},{4,5},{5,4},{6,7},{7,6},{8,9},{9,8},{10,11... | collective-permute-start | bytes 786440 | tf_op jit(solution)/shard_map/ppermute | solution.py:383
  30.4 1.5 %collective-permute-start.9 = (bf16[128,1024]{1,0:T(8,128)(2,1)S(1)}, bf16[128,1024]{1,0:T(8,128)(2,1)S(1)}, u32[]{:S(2)}, u32[]{:S(2)}) collective-permute-start(bf16[128,1024]{1,0:T(8,128)(2,1)S(1)} %collective-permute-done.5.refs_6_), channel_id=1, source_target_pairs={{0,2},{1,3},{2,0},{3,1},{4,6},{5,7},{6,4},{7,5},{8,10},{9,11},{10,... | collective-permute-start | bytes 786440 | tf_op jit(solution)/shard_map/ppermute | solution.py:383
  31.9 2.9 %collective-permute-done.11.refs_4_ = bf16[128,1024]{1,0:T(8,128)(2,1)S(1)} collective-permute-done((bf16[128,1024]{1,0:T(8,128)(2,1)S(1)}, bf16[128,1024]{1,0:T(8,128)(2,1)S(1)}, u32[]{:S(2)}, u32[]{:S(2)}) %collective-permute-start.11) | collective-permute-done | bytes 262176 | tf_op jit(solution)/shard_map/ppermute | solution.py:383
  34.8 2.1 %collective-permute-start.6 = (bf16[128,1024]{1,0:T(8,128)(2,1)S(1)}, bf16[128,1024]{1,0:T(8,128)(2,1)}, u32[]{:S(2)}, u32[]{:S(2)}) collective-permute-start(bf16[128,1024]{1,0:T(8,128)(2,1)S(1)} %collective-permute-done.5.refs_6_), channel_id=1, source_target_pairs={{0,1},{1,0},{2,3},{3,2},{4,5},{5,4},{6,7},{7,6},{8,9},{9,8},{10,11... | collective-permute-start | bytes 786440 | tf_op jit(solution)/shard_map/ppermute | solution.py:383
  36.8 1.3 %residuals.1 = f32[1024,128]{1,0:T(8,128)} custom-call(s32[16,128]{1,0:T(8,128)S(1)} %copy-done.1, bf16[256,1024]{1,0:T(8,128)(2,1)S(1)} %bitcast.14, bf16[128,1024]{1,0:T(8,128)(2,1)S(1)} %get-tuple-element.18.q_ref.refs_0_), custom_call_target="tpu_custom_call" | custom-call | flops 67108864 | bytes 1310720 | tf_op jit(solution)/shard_map/residuals/pallas_call | solution.py:149
  38.2 9.9 %all-to-all-start.1 = ((f32[16,64,128]{2,1,0:T(8,128)}), f32[16,64,128]{2,1,0:T(8,128)S(1)}, u32[]{:S(2)}, u32[]{:S(2)}) async-start(f32[16,64,128]{2,1,0:T(8,128)} %bitcast.3), calls=%async_computation.1 | async-start | bytes 1048576 | tf_op jit(solution)/shard_map/all_to_all | solution.py:419
  49.1 1.3 %collective-permute-start.14 = (bf16[128,1024]{1,0:T(8,128)(2,1)S(1)}, bf16[128,1024]{1,0:T(8,128)(2,1)S(1)}, u32[]{:S(2)}, u32[]{:S(2)}) collective-permute-start(bf16[128,1024]{1,0:T(8,128)(2,1)S(1)} %collective-permute-done.13.refs_6_), channel_id=1, source_target_pairs={{0,1},{1,0},{2,3},{3,2},{4,5},{5,4},{6,7},{7,6},{8,9},{9,8},{10,11... | collective-permute-start | bytes 786440 | tf_op jit(solution)/shard_map/ppermute | solution.py:383
  50.4 7.5 %nearest.2 = (f32[8,128]{1,0:T(8,128)S(1)}, bf16[8,256,1024]{2,1,0:T(8,128)(2,1)S(1)}, f32[2048,128]{1,0:T(8,128)S(1)}) custom-call(bf16[128,1024]{1,0:T(8,128)(2,1)S(1)} %get-tuple-element.18.q_ref.refs_0_, bf16[128,1024]{1,0:T(8,128)(2,1)S(1)} %collective-permute-done.refs_1_, bf16[128,1024]{1,0:T(8,128)(2,1)S(1)} %collective-permute-done.1.refs_2_, ...), custom_call_target="tpu_custom_call" | custom-call | flops 4294967296 | bytes 6291456 | tf_op jit(solution)/shard_map/nearest/pallas_call | solution.py:216
  57.9 4.6 %nearest.3.refs_1_ = f32[8,128]{1,0:T(8,128)S(1)} custom-call(bf16[128,1024]{1,0:T(8,128)(2,1)S(1)} %collective-permute-done.7.refs_0_, bf16[128,1024]{1,0:T(8,128)(2,1)S(1)} %collective-permute-done.8.refs_1_, bf16[128,1024]{1,0:T(8,128)(2,1)S(1)} %collective-permute-done.9.refs_2_, bf16[128,1024]{1,0:T(8,128)(2,1)S(1)} %collective-permute-done.10.refs_3_, ...), custom_call_target="tpu_custom_call" | custom-call | flops 4294967296 | bytes 6291456 | tf_op jit(solution)/shard_map/nearest/pallas_call | solution.py:216
  62.5 2.7 %all-to-all-done.1.sub_ref = f32[16,64,128]{2,1,0:T(8,128)S(1)} async-done(((f32[16,64,128]{2,1,0:T(8,128)}), f32[16,64,128]{2,1,0:T(8,128)S(1)}, u32[]{:S(2)}, u32[]{:S(2)}) %all-to-all-start.1) | async-done | bytes 524320 | tf_op jit(solution)/shard_map/all_to_all | solution.py:419
  66.1 1.6 %collective-permute-start.15 = (f32[144,128]{1,0:T(8,128)S(1)}, f32[144,128]{1,0:T(8,128)S(1)}, u32[]{:S(2)}, u32[]{:S(2)}) collective-permute-start(f32[144,128]{1,0:T(8,128)S(1)} %get-tuple-element.23), channel_id=1, source_target_pairs={{0,1},{1,0},{2,3},{3,2},{4,5},{5,4},{6,7},{7,6},{8,9},{9,8},{10,11... | collective-permute-start | bytes 221192 | tf_op jit(solution)/shard_map/ppermute | solution.py:383
  68.7 3.2 %collective-permute-done.16.b_ref = f32[144,128]{1,0:T(8,128)S(1)} collective-permute-done((f32[144,128]{1,0:T(8,128)S(1)}, f32[144,128]{1,0:T(8,128)S(1)}, u32[]{:S(2)}, u32[]{:S(2)}) %collective-permute-start.16) | collective-permute-done | bytes 73760 | tf_op jit(solution)/shard_map/ppermute | solution.py:383
  71.9 1.4 %collective-permute-start.17 = (f32[144,128]{1,0:T(8,128)S(1)}, f32[144,128]{1,0:T(8,128)S(1)}, u32[]{:S(2)}, u32[]{:S(2)}) collective-permute-start(f32[144,128]{1,0:T(8,128)S(1)} %join.3.a_ref), channel_id=1, source_target_pairs={{0,2},{1,3},{2,0},{3,1},{4,6},{5,7},{6,4},{7,5},{8,10},{9,11},{10,... | collective-permute-start | bytes 221192 | tf_op jit(solution)/shard_map/ppermute | solution.py:383
  73.4 2.3 %collective-permute-start.18 = (f32[144,128]{1,0:T(8,128)S(1)}, f32[144,128]{1,0:T(8,128)S(1)}, u32[]{:S(2)}, u32[]{:S(2)}) collective-permute-start(f32[144,128]{1,0:T(8,128)S(1)} %join.3.a_ref), channel_id=1, source_target_pairs={{0,4},{1,5},{2,6},{3,7},{4,0},{5,1},{6,2},{7,3},{8,12},{9,13},{10,... | collective-permute-start | bytes 221192 | tf_op jit(solution)/shard_map/ppermute | solution.py:383
  75.9 2.2 %collective-permute-done.18.c_ref = f32[144,128]{1,0:T(8,128)S(1)} collective-permute-done((f32[144,128]{1,0:T(8,128)S(1)}, f32[144,128]{1,0:T(8,128)S(1)}, u32[]{:S(2)}, u32[]{:S(2)}) %collective-permute-start.18) | collective-permute-done | bytes 73760 | tf_op jit(solution)/shard_map/ppermute | solution.py:383
  78.1 2.8 %collective-permute-done.19.d_ref = f32[144,128]{1,0:T(8,128)S(1)} collective-permute-done((f32[144,128]{1,0:T(8,128)S(1)}, f32[144,128]{1,0:T(8,128)S(1)}, u32[]{:S(2)}, u32[]{:S(2)}) %collective-permute-start.19) | collective-permute-done | bytes 73760 | tf_op jit(solution)/shard_map/ppermute | solution.py:383
  81.4 2.1 %collective-permute-start.20 = (f32[128,128]{1,0:T(8,128)S(1)}, f32[128,128]{1,0:T(8,128)S(1)}, u32[]{:S(2)}, u32[]{:S(2)}) collective-permute-start(f32[128,128]{1,0:T(8,128)S(1)} %get-tuple-element.26.mine_ref), channel_id=1, source_target_pairs={{0,1},{1,0},{2,3},{3,2},{4,5},{5,4},{6,7},{7,6},{8,9},{9,8},{10,11... | collective-permute-start | bytes 196616 | tf_op jit(solution)/shard_map/ppermute | solution.py:383
  (39 shorter events, 6.8 us)
Async XLA Ops:
  0.6 36.2 %copy-start.1 = (s32[16,128]{1,0:T(8,128)S(1)}, s32[16,128]{1,0:T(8,128)}, u32[]{:S(2)}) copy-start(s32[16,128]{1,0:T(8,128)} %ids_ref.1) | copy-start | bytes 24580
  5.8 31.0 %all-to-all-start = ((bf16[16,16,1024]{2,1,0:T(8,128)(2,1)}), bf16[16,16,1024]{2,1,0:T(8,128)(2,1)S(1)}, u32[]{:S(2)}, u32[]{:S(2)}) async-start(bf16[16,16,1024]{2,1,0:T(8,128)(2,1)} %bitcast.1), calls=%async_computation | async-start | bytes 1048576 | tf_op jit(solution)/shard_map/all_to_all | solution.py:400
  13.2 13.5 %collective-permute-start.5 = (bf16[128,1024]{1,0:T(8,128)(2,1)S(1)}, bf16[128,1024]{1,0:T(8,128)(2,1)S(1)}, u32[]{:S(2)}, u32[]{:S(2)}) collective-permute-start(bf16[128,1024]{1,0:T(8,128)(2,1)S(1)} %get-tuple-element.18.q_ref.refs_0_), channel_id=1, source_target_pairs={{0,8},{1,9},{2,10},{3,11},{4,12},{5,13},{6,14},{7,15},{8,0},{9,1},... | collective-permute-start | bytes 786440 | tf_op jit(solution)/shard_map/ppermute | solution.py:383
  14.5 14.5 %collective-permute-start.1 = (bf16[128,1024]{1,0:T(8,128)(2,1)S(1)}, bf16[128,1024]{1,0:T(8,128)(2,1)S(1)}, u32[]{:S(2)}, u32[]{:S(2)}) collective-permute-start(bf16[128,1024]{1,0:T(8,128)(2,1)S(1)} %get-tuple-element.18.q_ref.refs_0_), channel_id=1, source_target_pairs={{0,2},{1,3},{2,0},{3,1},{4,6},{5,7},{6,4},{7,5},{8,10},{9,11},{10,... | collective-permute-start | bytes 786440 | tf_op jit(solution)/shard_map/ppermute | solution.py:383
  15.7 14.6 %collective-permute-start.3 = (bf16[128,1024]{1,0:T(8,128)(2,1)S(1)}, bf16[128,1024]{1,0:T(8,128)(2,1)S(1)}, u32[]{:S(2)}, u32[]{:S(2)}) collective-permute-start(bf16[128,1024]{1,0:T(8,128)(2,1)S(1)} %get-tuple-element.18.q_ref.refs_0_), channel_id=1, source_target_pairs={{0,6},{1,7},{2,4},{3,5},{4,2},{5,3},{6,0},{7,1},{8,14},{9,15},{10,... | collective-permute-start | bytes 786440 | tf_op jit(solution)/shard_map/ppermute | solution.py:383
  17.5 12.9 %collective-permute-start = (bf16[128,1024]{1,0:T(8,128)(2,1)S(1)}, bf16[128,1024]{1,0:T(8,128)(2,1)S(1)}, u32[]{:S(2)}, u32[]{:S(2)}) collective-permute-start(bf16[128,1024]{1,0:T(8,128)(2,1)S(1)} %get-tuple-element.18.q_ref.refs_0_), channel_id=1, source_target_pairs={{0,1},{1,0},{2,3},{3,2},{4,5},{5,4},{6,7},{7,6},{8,9},{9,8},{10,11... | collective-permute-start | bytes 786440 | tf_op jit(solution)/shard_map/ppermute | solution.py:383
  26.6 8.1 %collective-permute-start.11 = (bf16[128,1024]{1,0:T(8,128)(2,1)S(1)}, bf16[128,1024]{1,0:T(8,128)(2,1)S(1)}, u32[]{:S(2)}, u32[]{:S(2)}) collective-permute-start(bf16[128,1024]{1,0:T(8,128)(2,1)S(1)} %collective-permute-done.5.refs_6_), channel_id=1, source_target_pairs={{0,6},{1,7},{2,4},{3,5},{4,2},{5,3},{6,0},{7,1},{8,14},{9,15},{10,... | collective-permute-start | bytes 786440 | tf_op jit(solution)/shard_map/ppermute | solution.py:383
  29.0 5.7 %collective-permute-start.2 = (bf16[128,1024]{1,0:T(8,128)(2,1)S(1)}, bf16[128,1024]{1,0:T(8,128)(2,1)S(1)}, u32[]{:S(2)}, u32[]{:S(2)}) collective-permute-start(bf16[128,1024]{1,0:T(8,128)(2,1)S(1)} %collective-permute-done.1.refs_2_), channel_id=1, source_target_pairs={{0,1},{1,0},{2,3},{3,2},{4,5},{5,4},{6,7},{7,6},{8,9},{9,8},{10,11... | collective-permute-start | bytes 786440 | tf_op jit(solution)/shard_map/ppermute | solution.py:383
  30.3 17.7 %collective-permute-start.4 = (bf16[128,1024]{1,0:T(8,128)(2,1)S(1)}, bf16[128,1024]{1,0:T(8,128)(2,1)S(1)}, u32[]{:S(2)}, u32[]{:S(2)}) collective-permute-start(bf16[128,1024]{1,0:T(8,128)(2,1)S(1)} %collective-permute-done.3.refs_4_), channel_id=1, source_target_pairs={{0,1},{1,0},{2,3},{3,2},{4,5},{5,4},{6,7},{7,6},{8,9},{9,8},{10,11... | collective-permute-start | bytes 786440 | tf_op jit(solution)/shard_map/ppermute | solution.py:383
  30.4 18.0 %collective-permute-start.7 = (bf16[128,1024]{1,0:T(8,128)(2,1)S(1)}, bf16[128,1024]{1,0:T(8,128)(2,1)S(1)}, u32[]{:S(2)}, u32[]{:S(2)}) collective-permute-start(bf16[128,1024]{1,0:T(8,128)(2,1)S(1)} %collective-permute-done.3.refs_4_), channel_id=1, source_target_pairs={{0,2},{1,3},{2,0},{3,1},{4,6},{5,7},{6,4},{7,5},{8,10},{9,11},{10,... | collective-permute-start | bytes 786440 | tf_op jit(solution)/shard_map/ppermute | solution.py:383
  30.4 18.3 %collective-permute-start.9 = (bf16[128,1024]{1,0:T(8,128)(2,1)S(1)}, bf16[128,1024]{1,0:T(8,128)(2,1)S(1)}, u32[]{:S(2)}, u32[]{:S(2)}) collective-permute-start(bf16[128,1024]{1,0:T(8,128)(2,1)S(1)} %collective-permute-done.5.refs_6_), channel_id=1, source_target_pairs={{0,2},{1,3},{2,0},{3,1},{4,6},{5,7},{6,4},{7,5},{8,10},{9,11},{10,... | collective-permute-start | bytes 786440 | tf_op jit(solution)/shard_map/ppermute | solution.py:383
  34.8 14.3 %collective-permute-start.13 = (bf16[128,1024]{1,0:T(8,128)(2,1)S(1)}, bf16[128,1024]{1,0:T(8,128)(2,1)S(1)}, u32[]{:S(2)}, u32[]{:S(2)}) collective-permute-start(bf16[128,1024]{1,0:T(8,128)(2,1)S(1)} %collective-permute-done.11.refs_4_), channel_id=1, source_target_pairs={{0,2},{1,3},{2,0},{3,1},{4,6},{5,7},{6,4},{7,5},{8,10},{9,11},{10,... | collective-permute-start | bytes 786440 | tf_op jit(solution)/shard_map/ppermute | solution.py:383
  34.8 15.6 %collective-permute-start.6 = (bf16[128,1024]{1,0:T(8,128)(2,1)S(1)}, bf16[128,1024]{1,0:T(8,128)(2,1)}, u32[]{:S(2)}, u32[]{:S(2)}) collective-permute-start(bf16[128,1024]{1,0:T(8,128)(2,1)S(1)} %collective-permute-done.5.refs_6_), channel_id=1, source_target_pairs={{0,1},{1,0},{2,3},{3,2},{4,5},{5,4},{6,7},{7,6},{8,9},{9,8},{10,11... | collective-permute-start | bytes 786440 | tf_op jit(solution)/shard_map/ppermute | solution.py:383
  38.2 27.1 %all-to-all-start.1 = ((f32[16,64,128]{2,1,0:T(8,128)}), f32[16,64,128]{2,1,0:T(8,128)S(1)}, u32[]{:S(2)}, u32[]{:S(2)}) async-start(f32[16,64,128]{2,1,0:T(8,128)} %bitcast.3), calls=%async_computation.1 | async-start | bytes 1048576 | tf_op jit(solution)/shard_map/all_to_all | solution.py:419
  48.0 9.8 %collective-permute-start.12 = (bf16[128,1024]{1,0:T(8,128)(2,1)S(1)}, bf16[128,1024]{1,0:T(8,128)(2,1)S(1)}, u32[]{:S(2)}, u32[]{:S(2)}) collective-permute-start(bf16[128,1024]{1,0:T(8,128)(2,1)S(1)} %collective-permute-done.11.refs_4_), channel_id=1, source_target_pairs={{0,1},{1,0},{2,3},{3,2},{4,5},{5,4},{6,7},{7,6},{8,9},{9,8},{10,11... | collective-permute-start | bytes 786440 | tf_op jit(solution)/shard_map/ppermute | solution.py:383
  48.4 9.4 %collective-permute-start.8 = (bf16[128,1024]{1,0:T(8,128)(2,1)S(1)}, bf16[128,1024]{1,0:T(8,128)(2,1)S(1)}, u32[]{:S(2)}, u32[]{:S(2)}) collective-permute-start(bf16[128,1024]{1,0:T(8,128)(2,1)S(1)} %collective-permute-done.7.refs_0_), channel_id=1, source_target_pairs={{0,1},{1,0},{2,3},{3,2},{4,5},{5,4},{6,7},{7,6},{8,9},{9,8},{10,11... | collective-permute-start | bytes 786440 | tf_op jit(solution)/shard_map/ppermute | solution.py:383
  48.7 9.2 %collective-permute-start.10 = (bf16[128,1024]{1,0:T(8,128)(2,1)S(1)}, bf16[128,1024]{1,0:T(8,128)(2,1)S(1)}, u32[]{:S(2)}, u32[]{:S(2)}) collective-permute-start(bf16[128,1024]{1,0:T(8,128)(2,1)S(1)} %collective-permute-done.9.refs_2_), channel_id=1, source_target_pairs={{0,1},{1,0},{2,3},{3,2},{4,5},{5,4},{6,7},{7,6},{8,9},{9,8},{10,11... | collective-permute-start | bytes 786440 | tf_op jit(solution)/shard_map/ppermute | solution.py:383
  49.1 8.8 %collective-permute-start.14 = (bf16[128,1024]{1,0:T(8,128)(2,1)S(1)}, bf16[128,1024]{1,0:T(8,128)(2,1)S(1)}, u32[]{:S(2)}, u32[]{:S(2)}) collective-permute-start(bf16[128,1024]{1,0:T(8,128)(2,1)S(1)} %collective-permute-done.13.refs_6_), channel_id=1, source_target_pairs={{0,1},{1,0},{2,3},{3,2},{4,5},{5,4},{6,7},{7,6},{8,9},{9,8},{10,11... | collective-permute-start | bytes 786440 | tf_op jit(solution)/shard_map/ppermute | solution.py:383
  66.1 2.5 %collective-permute-start.15 = (f32[144,128]{1,0:T(8,128)S(1)}, f32[144,128]{1,0:T(8,128)S(1)}, u32[]{:S(2)}, u32[]{:S(2)}) collective-permute-start(f32[144,128]{1,0:T(8,128)S(1)} %get-tuple-element.23), channel_id=1, source_target_pairs={{0,1},{1,0},{2,3},{3,2},{4,5},{5,4},{6,7},{7,6},{8,9},{9,8},{10,11... | collective-permute-start | bytes 221192 | tf_op jit(solution)/shard_map/ppermute | solution.py:383
  68.6 3.3 %collective-permute-start.16 = (f32[144,128]{1,0:T(8,128)S(1)}, f32[144,128]{1,0:T(8,128)S(1)}, u32[]{:S(2)}, u32[]{:S(2)}) collective-permute-start(f32[144,128]{1,0:T(8,128)S(1)} %join.2.a_ref), channel_id=1, source_target_pairs={{0,8},{1,9},{2,10},{3,11},{4,12},{5,13},{6,14},{7,15},{8,0},{9,1},... | collective-permute-start | bytes 221192 | tf_op jit(solution)/shard_map/ppermute | solution.py:383
  71.9 3.9 %collective-permute-start.17 = (f32[144,128]{1,0:T(8,128)S(1)}, f32[144,128]{1,0:T(8,128)S(1)}, u32[]{:S(2)}, u32[]{:S(2)}) collective-permute-start(f32[144,128]{1,0:T(8,128)S(1)} %join.3.a_ref), channel_id=1, source_target_pairs={{0,2},{1,3},{2,0},{3,1},{4,6},{5,7},{6,4},{7,5},{8,10},{9,11},{10,... | collective-permute-start | bytes 221192 | tf_op jit(solution)/shard_map/ppermute | solution.py:383
  73.4 4.7 %collective-permute-start.18 = (f32[144,128]{1,0:T(8,128)S(1)}, f32[144,128]{1,0:T(8,128)S(1)}, u32[]{:S(2)}, u32[]{:S(2)}) collective-permute-start(f32[144,128]{1,0:T(8,128)S(1)} %join.3.a_ref), channel_id=1, source_target_pairs={{0,4},{1,5},{2,6},{3,7},{4,0},{5,1},{6,2},{7,3},{8,12},{9,13},{10,... | collective-permute-start | bytes 221192 | tf_op jit(solution)/shard_map/ppermute | solution.py:383
  75.7 5.2 %collective-permute-start.19 = (f32[144,128]{1,0:T(8,128)S(1)}, f32[144,128]{1,0:T(8,128)S(1)}, u32[]{:S(2)}, u32[]{:S(2)}) collective-permute-start(f32[144,128]{1,0:T(8,128)S(1)} %join.3.a_ref), channel_id=1, source_target_pairs={{0,6},{1,7},{2,4},{3,5},{4,2},{5,3},{6,0},{7,1},{8,14},{9,15},{10,... | collective-permute-start | bytes 221192 | tf_op jit(solution)/shard_map/ppermute | solution.py:383
  81.4 3.0 %collective-permute-start.20 = (f32[128,128]{1,0:T(8,128)S(1)}, f32[128,128]{1,0:T(8,128)S(1)}, u32[]{:S(2)}, u32[]{:S(2)}) collective-permute-start(f32[128,128]{1,0:T(8,128)S(1)} %get-tuple-element.26.mine_ref), channel_id=1, source_target_pairs={{0,1},{1,0},{2,3},{3,2},{4,5},{5,4},{6,7},{7,6},{8,9},{9,8},{10,11... | collective-permute-start | bytes 196616 | tf_op jit(solution)/shard_map/ppermute | solution.py:383
  (3 other events, 37.6 us)

commit v5 on v4

--- a/solution.py
+++ b/solution.py
@@ -123,8 +123,29 @@
     )(off_chip(values), off_chip(scales), off_chip(ids), off_chip(cents))
 
 
-def residual_kernel(count, slots, ids_ref, fetched_ref, q_ref, out_ref):
-    width, rows = out_ref.shape
+def pack(out_ref, first, residual, sub_width):
+    half = sub_width // 2
+    for k in range(residual.shape[0] // sub_width):
+        part = residual[sub_width * k : sub_width * (k + 1)]
+        most = jnp.maximum(jnp.max(jnp.abs(part), axis=0, keepdims=True), 1e-30)
+        power = jnp.floor(jnp.log2(most)) + 1.0
+        coded = jnp.clip(jnp.round(part * jnp.exp2(15.0 - power)), -32767.0, 32767.0).astype(jnp.int32)
+        word = lax.shift_left(coded[:half], 16) | (coded[half:] & 0xFFFF)
+        out_ref[first + k, :half, :] = word
+        out_ref[first + k, half:, :] = jnp.broadcast_to(power.astype(jnp.int32), (8, part.shape[1]))
+
+
+def unpack(words):
+    half = words.shape[0] - 8
+    unit = jnp.exp2(words[half : half + 1].astype(f32) - 15.0)
+    words = words[:half]
+    high = lax.shift_right_arithmetic(words, 16)
+    low = lax.shift_right_arithmetic(lax.shift_left(words, 16), 16)
+    return jnp.concatenate([high, low], axis=0).astype(f32) * unit
+
+
+def residual_kernel(count, slots, sub_width, ids_ref, fetched_ref, q_ref, out_ref):
+    rows, width = q_ref.shape
     ids = ids_ref[pl.ds(lax.axis_index("cent"), 1), :]
     owner = lax.div(ids, count)
     across = jnp.broadcast_to(owner, (rows, rows))
@@ -141,14 +162,14 @@
         fetched = lax.dot_general(
             place, fetched_ref[:, lanes], (((0,), (0,)), ((), ())), preferred_element_type=f32
         )
-        out_ref[lanes, :] = (q_ref[:, lanes].astype(f32) - fetched).T
-
-
-def residuals(ids, fetched, q, count, slots):
+        pack(out_ref, 2 * j, (q_ref[:, lanes].astype(f32) - fetched).T, sub_width)
+
+
+def residuals(ids, fetched, q, count, slots, sub_width):
     rows, width = q.shape
     return pl.pallas_call(
-        functools.partial(residual_kernel, count, slots),
-        out_shape=pltpu.VMEM((width, rows), f32),
+        functools.partial(residual_kernel, count, slots, sub_width),
+        out_shape=pltpu.VMEM((width // sub_width, sub_width // 2 + 8, rows), jnp.int32),
         in_specs=[VM] * 3,
         out_specs=VM,
         cost_estimate=pl.CostEstimate(
@@ -209,6 +230,7 @@
     held = [pltpu.VMEM((2 * count // step, step // 2, width), bf16), pltpu.VMEM((count, 128), f32)]
     sems = [pltpu.SemaphoreType.DMA((2 * count // step,))]
     more = {
+        "once": ([HBM], out, held + sems),
         "keep": ([HBM], out + held, sems),
         "again": ([VM, VM], out, []),
     }
@@ -233,13 +255,15 @@
     return high, (x - high.astype(f32)).astype(bf16)
 
 
-def statistics_kernel(where, sub_ref, one_ref, two_ref, *refs):
-    gap_refs, (mine_ref, theirs_ref) = refs[:-2], refs[-2:]
-    groups, width, rows = sub_ref.shape
+def statistics_kernel(where, coded_ref, one_ref, two_ref, *refs):
+    gap_refs, (mine_ref, theirs_ref, sub_out_ref) = refs[:-3], refs[-3:]
+    groups, width, rows = sub_out_ref.shape
     words = 256
     high, low = [], []
     for g in range(groups):
-        h, l = halves_of(sub_ref[g])
+        sub = unpack(coded_ref[g])
+        sub_out_ref[g] = sub
+        h, l = halves_of(sub)
         high.append(h)
         low.append(l)
     ones = jnp.ones((16, groups * rows), bf16)
@@ -269,19 +293,21 @@
             out_ref[STATS + j : STATS + j + 1, :] = gap_refs[k][row : row + 1, :]
 
 
-def statistics(sub, codes_one, codes_two, lows, where):
+def statistics(coded, codes_one, codes_two, lows, where):
+    groups, words, rows = coded.shape
+    sub = jax.ShapeDtypeStruct((groups, 2 * (words - 8), rows), f32)
     shape = pltpu.VMEM((PAY, 128), f32)
     return pl.pallas_call(
         functools.partial(statistics_kernel, where),
-        out_shape=(shape, shape),
+        out_shape=(shape, shape, pltpu.VMEM(sub.shape, f32)),
         in_specs=[VM] * (3 + len(lows)),
-        out_specs=(VM, VM),
+        out_specs=(VM, VM, VM),
         cost_estimate=pl.CostEstimate(
             flops=2 * 2 * sub.size * 512, bytes_accessed=sub.size * 4, transcendentals=0
         ),
         compiler_params=LIMIT,
         name="statistics",
-    )(on_chip(sub), codes_one, codes_two, *[on_chip(x) for x in lows])
+    )(on_chip(coded), codes_one, codes_two, *[on_chip(x) for x in lows])
 
 
 def join_kernel(shift, a_ref, b_ref, out_ref):
@@ -384,7 +410,7 @@
 
 
 def step(emb_values, emb_scales, coarse_ids, centroids, codes_one, codes_two, codebook_init):
-    own_rows, width = emb_values.shape
+    _, width = emb_values.shape
     count = centroids.shape[0]
     sub_width = codebook_init.shape[2]
     peers = coarse_ids.shape[0]
@@ -403,22 +429,21 @@
     blocks[14] = swap(blocks[8], 6)
     blocks[10] = swap(blocks[8], 2)
     blocks[4] = swap(blocks[6], 2)
-    blocks[12] = swap(blocks[14], 2)
+    blocks[12] = swap(blocks[10], 6)
     for d in (2, 6, 8, 4, 10, 14, 12):
         blocks[d ^ core] = swap(blocks[d], core)
 
-    orders = ((0, 1, 2, 3, 6, 7, 8, 9), (4, 5, 10, 11, 14, 15, 12, 13))
+    orders = ((0, 1, 8, 9), (2, 3, 6, 7, 10, 11, 14, 15), (4, 5, 12, 13))
     lows, kept = [], ()
-    for order, mode in zip(orders, ("keep", "again")):
+    for order, mode in zip(orders, ("once", "keep", "again")):
         low, kept = nearest([blocks[d] for d in order], centroids, mode, kept)
         lows.append(low)
     where = {d: (k, j) for k, order in enumerate(orders) for j, d in enumerate(order)}
 
-    residual = residuals(coarse_ids, fetched, q, count, slots)
-    stacked = residual.reshape(width // sub_width, sub_width, own_rows)
-    sub = lax.all_to_all(stacked, "rows", 0, 0)
-
-    mine, theirs = statistics(sub, codes_one, codes_two, lows, where)
+    coded = residuals(coarse_ids, fetched, q, count, slots, sub_width)
+    coded = lax.all_to_all(coded, "rows", 0, 0)
+
+    mine, theirs, sub = statistics(coded, codes_one, codes_two, lows, where)
     mine = join(mine, swap(theirs, 1), 0)
     mine = join(mine, swap(mine, 8), 4)
     parts = [mine] + [swap(mine, d) for d in (2, 4, 6)]

time: 85.7 us -> 85.8 us (level)
  waiting for transfers between devices: 23.7 us -> 19.8 us
  Pallas kernels: 20.9 us -> 23.7 us
  local copies, waits for them, and re-layouts: 0.02 us -> 1.67 us
    pallas_call x2 -> x3, Pallas kernels: 12.1 us -> 14.9 us  [nearest(): pl.pallas_call(functools.partial(nearest_kernel, step, 3, len(xs), mode),...]
    all_to_all x1, waiting for transfers between devices: 2.72 us -> 0.01 us  [step(): coded = lax.all_to_all(coded, 'rows', 0, 0)]
    unnamed x8 -> x12, local copies, waits for them, and re-layouts: 0.02 us -> 1.67 us
    ppermute x21, waiting for transfers between devices: 20.9 us -> 19.8 us  [swap(): return lax.ppermute(x, 'cent', [(i, i ^ offset) for i in range(16)])]
  transfers between devices with their start and end apart: 23 -> 23, of which waited for: 9 -> 7; matrix products, arithmetic and copies ran while one was open for 0% -> 0% of each run, Pallas kernels for 16% -> 19%
where the time goes in v5:
time: 85.8 us; the launch traced here: 85.3 us
  starting transfers between devices  39.3 us (46%)
  Pallas kernels  23.7 us (28%)
  waiting for transfers between devices  19.8 us (23%)
  local copies, waits for them, and re-layouts  1.67 us (2%)
    ppermute x21, starting transfers between devices, swap(): return lax.ppermute(x, 'cent', [(i, i ^ offset) for i in range(16)])  22.1 us
    ppermute x21, waiting for transfers between devices, swap(): return lax.ppermute(x, 'cent', [(i, i ^ offset) for i in range(16)])  19.8 us
    pallas_call x3, Pallas kernels, nearest(): pl.pallas_call(functools.partial(nearest_kernel, step, 3, len(xs), mode),...  14.9 us
    all_to_all x1, starting transfers between devices, step(): coded = lax.all_to_all(coded, 'rows', 0, 0)  9.86 us
    all_to_all x1, starting transfers between devices, step(): fetched = lax.all_to_all(sent.reshape(peers, slots, width), 'cent', 0, 0)  7.34 us
    pallas_call x1, Pallas kernels, prepare(): pl.pallas_call(functools.partial(prepare_kernel, slots, step), out_shape=...  5.19 us
  transfers between devices with their start and end apart: 23, of which 7 were waited for; matrix products, arithmetic and copies ran while one was open for 0% of the time, Pallas kernels for 19%

profile of v5, /device:TPU:1, one launch (start us, length us, event | category | flops | bytes accessed | tf_op | source)
XLA Modules:
  0.0 85.3 jit_solution(7616952344631811673)
XLA Ops:
  0.6 5.2 %prepare.1 = (bf16[128,1024]{1,0:T(8,128)(2,1)S(1)}, f32[1,128]{1,0:T(1,128)S(1)}, bf16[256,1024]{1,0:T(8,128)(2,1)}) custom-call(bf16[128,1024]{1,0:T(8,128)(2,1)} %values_hbm.1, bf16[8,128]{1,0:T(8,128)(2,1)} %bitcast.15, s32[16,128]{1,0:T(8,128)} %ids_ref.1, bf16[2048,1024]{1,0:T(8,128)(2,1)} %refs_8_.1), custom_call_target="tpu_custom_call" | custom-call | flops 1073741824 | bytes 4194304 | tf_op jit(solution)/shard_map/prepare/pallas_call | solution.py:101
  5.8 7.3 %all-to-all-start = ((bf16[16,16,1024]{2,1,0:T(8,128)(2,1)}), bf16[16,16,1024]{2,1,0:T(8,128)(2,1)S(1)}, u32[]{:S(2)}, u32[]{:S(2)}) async-start(bf16[16,16,1024]{2,1,0:T(8,128)(2,1)} %bitcast.1), calls=%async_computation | async-start | bytes 1048576 | tf_op jit(solution)/shard_map/all_to_all | solution.py:426
  13.2 1.4 %collective-permute-start.1 = (bf16[128,1024]{1,0:T(8,128)(2,1)S(1)}, bf16[128,1024]{1,0:T(8,128)(2,1)S(1)}, u32[]{:S(2)}, u32[]{:S(2)}) collective-permute-start(bf16[128,1024]{1,0:T(8,128)(2,1)S(1)} %get-tuple-element.19.q_ref.refs_0_), channel_id=1, source_target_pairs={{0,8},{1,9},{2,10},{3,11},{4,12},{5,13},{6,14},{7,15},{8,0},{9,1},... | collective-permute-start | bytes 786440 | tf_op jit(solution)/shard_map/ppermute | solution.py:409
  14.5 1.2 %collective-permute-start.3 = (bf16[128,1024]{1,0:T(8,128)(2,1)S(1)}, bf16[128,1024]{1,0:T(8,128)(2,1)S(1)}, u32[]{:S(2)}, u32[]{:S(2)}) collective-permute-start(bf16[128,1024]{1,0:T(8,128)(2,1)S(1)} %get-tuple-element.19.q_ref.refs_0_), channel_id=1, source_target_pairs={{0,2},{1,3},{2,0},{3,1},{4,6},{5,7},{6,4},{7,5},{8,10},{9,11},{10,... | collective-permute-start | bytes 786440 | tf_op jit(solution)/shard_map/ppermute | solution.py:409
  15.7 1.0 %collective-permute-start = (bf16[128,1024]{1,0:T(8,128)(2,1)S(1)}, bf16[128,1024]{1,0:T(8,128)(2,1)S(1)}, u32[]{:S(2)}, u32[]{:S(2)}) collective-permute-start(bf16[128,1024]{1,0:T(8,128)(2,1)S(1)} %get-tuple-element.19.q_ref.refs_0_), channel_id=1, source_target_pairs={{0,1},{1,0},{2,3},{3,2},{4,5},{5,4},{6,7},{7,6},{8,9},{9,8},{10,11... | collective-permute-start | bytes 786440 | tf_op jit(solution)/shard_map/ppermute | solution.py:409
  16.7 1.8 %collective-permute-start.5 = (bf16[128,1024]{1,0:T(8,128)(2,1)S(1)}, bf16[128,1024]{1,0:T(8,128)(2,1)S(1)}, u32[]{:S(2)}, u32[]{:S(2)}) collective-permute-start(bf16[128,1024]{1,0:T(8,128)(2,1)S(1)} %get-tuple-element.19.q_ref.refs_0_), channel_id=1, source_target_pairs={{0,6},{1,7},{2,4},{3,5},{4,2},{5,3},{6,0},{7,1},{8,14},{9,15},{10,... | collective-permute-start | bytes 786440 | tf_op jit(solution)/shard_map/ppermute | solution.py:409
  18.5 8.2 %collective-permute-done.1.refs_2_ = bf16[128,1024]{1,0:T(8,128)(2,1)S(1)} collective-permute-done((bf16[128,1024]{1,0:T(8,128)(2,1)S(1)}, bf16[128,1024]{1,0:T(8,128)(2,1)S(1)}, u32[]{:S(2)}, u32[]{:S(2)}) %collective-permute-start.1) | collective-permute-done | bytes 262176 | tf_op jit(solution)/shard_map/ppermute | solution.py:409
  26.6 1.0 %collective-permute-start.2 = (bf16[128,1024]{1,0:T(8,128)(2,1)S(1)}, bf16[128,1024]{1,0:T(8,128)(2,1)S(1)}, u32[]{:S(2)}, u32[]{:S(2)}) collective-permute-start(bf16[128,1024]{1,0:T(8,128)(2,1)S(1)} %collective-permute-done.1.refs_2_), channel_id=1, source_target_pairs={{0,1},{1,0},{2,3},{3,2},{4,5},{5,4},{6,7},{7,6},{8,9},{9,8},{10,11... | collective-permute-start | bytes 786440 | tf_op jit(solution)/shard_map/ppermute | solution.py:409
  27.6 1.2 %collective-permute-start.7 = (bf16[128,1024]{1,0:T(8,128)(2,1)S(1)}, bf16[128,1024]{1,0:T(8,128)(2,1)S(1)}, u32[]{:S(2)}, u32[]{:S(2)}) collective-permute-start(bf16[128,1024]{1,0:T(8,128)(2,1)S(1)} %collective-permute-done.1.refs_2_), channel_id=1, source_target_pairs={{0,2},{1,3},{2,0},{3,1},{4,6},{5,7},{6,4},{7,5},{8,10},{9,11},{10,... | collective-permute-start | bytes 786440 | tf_op jit(solution)/shard_map/ppermute | solution.py:409
  29.1 1.8 %collective-permute-start.9 = (bf16[128,1024]{1,0:T(8,128)(2,1)S(1)}, bf16[128,1024]{1,0:T(8,128)(2,1)S(1)}, u32[]{:S(2)}, u32[]{:S(2)}) collective-permute-start(bf16[128,1024]{1,0:T(8,128)(2,1)S(1)} %collective-permute-done.1.refs_2_), channel_id=1, source_target_pairs={{0,6},{1,7},{2,4},{3,5},{4,2},{5,3},{6,0},{7,1},{8,14},{9,15},{10,... | collective-permute-start | bytes 786440 | tf_op jit(solution)/shard_map/ppermute | solution.py:409
  32.4 3.1 %collective-permute-done.7.refs_4_ = bf16[128,1024]{1,0:T(8,128)(2,1)S(1)} collective-permute-done((bf16[128,1024]{1,0:T(8,128)(2,1)S(1)}, bf16[128,1024]{1,0:T(8,128)(2,1)S(1)}, u32[]{:S(2)}, u32[]{:S(2)}) %collective-permute-start.7) | collective-permute-done | bytes 262176 | tf_op jit(solution)/shard_map/ppermute | solution.py:409
  35.5 2.4 %collective-permute-start.13 = (bf16[128,1024]{1,0:T(8,128)(2,1)S(1)}, bf16[128,1024]{1,0:T(8,128)(2,1)S(1)}, u32[]{:S(2)}, u32[]{:S(2)}) collective-permute-start(bf16[128,1024]{1,0:T(8,128)(2,1)S(1)} %collective-permute-done.7.refs_4_), channel_id=1, source_target_pairs={{0,6},{1,7},{2,4},{3,5},{4,2},{5,3},{6,0},{7,1},{8,14},{9,15},{10,... | collective-permute-start | bytes 786440 | tf_op jit(solution)/shard_map/ppermute | solution.py:409
  37.9 1.6 %collective-permute-start.8 = (bf16[128,1024]{1,0:T(8,128)(2,1)S(1)}, bf16[128,1024]{1,0:T(8,128)(2,1)}, u32[]{:S(2)}, u32[]{:S(2)}) collective-permute-start(bf16[128,1024]{1,0:T(8,128)(2,1)S(1)} %collective-permute-done.7.refs_4_), channel_id=1, source_target_pairs={{0,1},{1,0},{2,3},{3,2},{4,5},{5,4},{6,7},{7,6},{8,9},{9,8},{10,11... | collective-permute-start | bytes 786440 | tf_op jit(solution)/shard_map/ppermute | solution.py:409
  39.6 1.3 %residuals.1 = s32[16,40,128]{2,1,0:T(8,128)} custom-call(s32[16,128]{1,0:T(8,128)S(1)} %copy-done.1, bf16[256,1024]{1,0:T(8,128)(2,1)S(1)} %bitcast.13, bf16[128,1024]{1,0:T(8,128)(2,1)S(1)} %get-tuple-element.19.q_ref.refs_0_), custom_call_target="tpu_custom_call" | custom-call | flops 67108864 | bytes 1310720 | tf_op jit(solution)/shard_map/residuals/pallas_call | solution.py:170
  40.9 9.9 %all-to-all-start.1 = ((s32[16,40,128]{2,1,0:T(8,128)}), s32[16,40,128]{2,1,0:T(8,128)S(1)}, u32[]{:S(2)}, u32[]{:S(2)}) async-start(s32[16,40,128]{2,1,0:T(8,128)} %residuals.1), calls=%async_computation.1 | async-start | bytes 655360 | tf_op jit(solution)/shard_map/all_to_all | solution.py:444
  51.7 4.9 %nearest.3.refs_0_ = f32[4,128]{1,0:T(4,128)S(1)} custom-call(bf16[128,1024]{1,0:T(8,128)(2,1)S(1)} %get-tuple-element.19.q_ref.refs_0_, bf16[128,1024]{1,0:T(8,128)(2,1)S(1)} %collective-permute-done.refs_1_, bf16[128,1024]{1,0:T(8,128)(2,1)S(1)} %collective-permute-done.1.refs_2_, bf16[128,1024]{1,0:T(8,128)(2,1)S(1)} %copy-done.4, bf16[2048,1024]{1,0:T(8,128)(2,1)} %refs_8_.1), custom_call_target="tpu_custom_call" | custom-call | flops 2147483648 | bytes 5242880 | tf_op jit(solution)/shard_map/nearest/pallas_call | solution.py:238
  57.6 7.6 %nearest.4 = (f32[8,128]{1,0:T(8,128)S(1)}, bf16[8,256,1024]{2,1,0:T(8,128)(2,1)S(1)}, f32[2048,128]{1,0:T(8,128)S(1)}) custom-call(bf16[128,1024]{1,0:T(8,128)(2,1)S(1)} %collective-permute-done.3.refs_0_, bf16[128,1024]{1,0:T(8,128)(2,1)S(1)} %collective-permute-done.4.refs_1_, bf16[128,1024]{1,0:T(8,128)(2,1)S(1)} %collective-permute-done.5.refs_2_, ...), custom_call_target="tpu_custom_call" | custom-call | flops 4294967296 | bytes 6291456 | tf_op jit(solution)/shard_map/nearest/pallas_call | solution.py:238
  65.2 2.4 %nearest.5.refs_2_ = f32[4,128]{1,0:T(4,128)S(1)} custom-call(bf16[128,1024]{1,0:T(8,128)(2,1)S(1)} %collective-permute-done.11.refs_0_, bf16[128,1024]{1,0:T(8,128)(2,1)S(1)} %collective-permute-done.12.refs_1_, bf16[128,1024]{1,0:T(8,128)(2,1)S(1)} %collective-permute-done.13.refs_2_, bf16[128,1024]{1,0:T(8,128)(2,1)S(1)} %collective-permute-done.14.refs_3_, ...), custom_call_target="tpu_custom_call" | custom-call | flops 2147483648 | bytes 5242880 | tf_op jit(solution)/shard_map/nearest/pallas_call | solution.py:238
  70.3 2.9 %collective-permute-done.16.b_ref = f32[144,128]{1,0:T(8,128)S(1)} collective-permute-done((f32[144,128]{1,0:T(8,128)S(1)}, f32[144,128]{1,0:T(8,128)S(1)}, u32[]{:S(2)}, u32[]{:S(2)}) %collective-permute-start.16) | collective-permute-done | bytes 73760 | tf_op jit(solution)/shard_map/ppermute | solution.py:409
  73.3 2.4 %collective-permute-start.18 = (f32[144,128]{1,0:T(8,128)S(1)}, f32[144,128]{1,0:T(8,128)S(1)}, u32[]{:S(2)}, u32[]{:S(2)}) collective-permute-start(f32[144,128]{1,0:T(8,128)S(1)} %join.3.a_ref), channel_id=1, source_target_pairs={{0,4},{1,5},{2,6},{3,7},{4,0},{5,1},{6,2},{7,3},{8,12},{9,13},{10,... | collective-permute-start | bytes 221192 | tf_op jit(solution)/shard_map/ppermute | solution.py:409
  75.7 1.4 %collective-permute-start.19 = (f32[144,128]{1,0:T(8,128)S(1)}, f32[144,128]{1,0:T(8,128)S(1)}, u32[]{:S(2)}, u32[]{:S(2)}) collective-permute-start(f32[144,128]{1,0:T(8,128)S(1)} %join.3.a_ref), channel_id=1, source_target_pairs={{0,6},{1,7},{2,4},{3,5},{4,2},{5,3},{6,0},{7,1},{8,14},{9,15},{10,... | collective-permute-start | bytes 221192 | tf_op jit(solution)/shard_map/ppermute | solution.py:409
  77.2 1.1 %collective-permute-done.18.c_ref = f32[144,128]{1,0:T(8,128)S(1)} collective-permute-done((f32[144,128]{1,0:T(8,128)S(1)}, f32[144,128]{1,0:T(8,128)S(1)}, u32[]{:S(2)}, u32[]{:S(2)}) %collective-permute-start.18) | collective-permute-done | bytes 73760 | tf_op jit(solution)/shard_map/ppermute | solution.py:409
  78.2 2.7 %collective-permute-done.19.d_ref = f32[144,128]{1,0:T(8,128)S(1)} collective-permute-done((f32[144,128]{1,0:T(8,128)S(1)}, f32[144,128]{1,0:T(8,128)S(1)}, u32[]{:S(2)}, u32[]{:S(2)}) %collective-permute-start.19) | collective-permute-done | bytes 73760 | tf_op jit(solution)/shard_map/ppermute | solution.py:409
  81.5 2.1 %collective-permute-start.20 = (f32[128,128]{1,0:T(8,128)S(1)}, f32[128,128]{1,0:T(8,128)S(1)}, u32[]{:S(2)}, u32[]{:S(2)}) collective-permute-start(f32[128,128]{1,0:T(8,128)S(1)} %get-tuple-element.28.mine_ref), channel_id=1, source_target_pairs={{0,1},{1,0},{2,3},{3,2},{4,5},{5,4},{6,7},{7,6},{8,9},{9,8},{10,11... | collective-permute-start | bytes 196616 | tf_op jit(solution)/shard_map/ppermute | solution.py:409
  (44 shorter events, 8.8 us)
Async XLA Ops:
  0.6 38.9 %copy-start.1 = (s32[16,128]{1,0:T(8,128)S(1)}, s32[16,128]{1,0:T(8,128)}, u32[]{:S(2)}) copy-start(s32[16,128]{1,0:T(8,128)} %ids_ref.1) | copy-start | bytes 24580
  5.8 33.7 %all-to-all-start = ((bf16[16,16,1024]{2,1,0:T(8,128)(2,1)}), bf16[16,16,1024]{2,1,0:T(8,128)(2,1)S(1)}, u32[]{:S(2)}, u32[]{:S(2)}) async-start(bf16[16,16,1024]{2,1,0:T(8,128)(2,1)} %bitcast.1), calls=%async_computation | async-start | bytes 1048576 | tf_op jit(solution)/shard_map/all_to_all | solution.py:426
  13.2 13.5 %collective-permute-start.1 = (bf16[128,1024]{1,0:T(8,128)(2,1)S(1)}, bf16[128,1024]{1,0:T(8,128)(2,1)S(1)}, u32[]{:S(2)}, u32[]{:S(2)}) collective-permute-start(bf16[128,1024]{1,0:T(8,128)(2,1)S(1)} %get-tuple-element.19.q_ref.refs_0_), channel_id=1, source_target_pairs={{0,8},{1,9},{2,10},{3,11},{4,12},{5,13},{6,14},{7,15},{8,0},{9,1},... | collective-permute-start | bytes 786440 | tf_op jit(solution)/shard_map/ppermute | solution.py:409
  14.5 14.3 %collective-permute-start.3 = (bf16[128,1024]{1,0:T(8,128)(2,1)S(1)}, bf16[128,1024]{1,0:T(8,128)(2,1)S(1)}, u32[]{:S(2)}, u32[]{:S(2)}) collective-permute-start(bf16[128,1024]{1,0:T(8,128)(2,1)S(1)} %get-tuple-element.19.q_ref.refs_0_), channel_id=1, source_target_pairs={{0,2},{1,3},{2,0},{3,1},{4,6},{5,7},{6,4},{7,5},{8,10},{9,11},{10,... | collective-permute-start | bytes 786440 | tf_op jit(solution)/shard_map/ppermute | solution.py:409
  15.7 13.4 %collective-permute-start = (bf16[128,1024]{1,0:T(8,128)(2,1)S(1)}, bf16[128,1024]{1,0:T(8,128)(2,1)S(1)}, u32[]{:S(2)}, u32[]{:S(2)}) collective-permute-start(bf16[128,1024]{1,0:T(8,128)(2,1)S(1)} %get-tuple-element.19.q_ref.refs_0_), channel_id=1, source_target_pairs={{0,1},{1,0},{2,3},{3,2},{4,5},{5,4},{6,7},{7,6},{8,9},{9,8},{10,11... | collective-permute-start | bytes 786440 | tf_op jit(solution)/shard_map/ppermute | solution.py:409
  16.7 14.2 %collective-permute-start.5 = (bf16[128,1024]{1,0:T(8,128)(2,1)S(1)}, bf16[128,1024]{1,0:T(8,128)(2,1)S(1)}, u32[]{:S(2)}, u32[]{:S(2)}) collective-permute-start(bf16[128,1024]{1,0:T(8,128)(2,1)S(1)} %get-tuple-element.19.q_ref.refs_0_), channel_id=1, source_target_pairs={{0,6},{1,7},{2,4},{3,5},{4,2},{5,3},{6,0},{7,1},{8,14},{9,15},{10,... | collective-permute-start | bytes 786440 | tf_op jit(solution)/shard_map/ppermute | solution.py:409
  26.6 4.7 %collective-permute-start.2 = (bf16[128,1024]{1,0:T(8,128)(2,1)S(1)}, bf16[128,1024]{1,0:T(8,128)(2,1)S(1)}, u32[]{:S(2)}, u32[]{:S(2)}) collective-permute-start(bf16[128,1024]{1,0:T(8,128)(2,1)S(1)} %collective-permute-done.1.refs_2_), channel_id=1, source_target_pairs={{0,1},{1,0},{2,3},{3,2},{4,5},{5,4},{6,7},{7,6},{8,9},{9,8},{10,11... | collective-permute-start | bytes 786440 | tf_op jit(solution)/shard_map/ppermute | solution.py:409
  27.6 7.9 %collective-permute-start.7 = (bf16[128,1024]{1,0:T(8,128)(2,1)S(1)}, bf16[128,1024]{1,0:T(8,128)(2,1)S(1)}, u32[]{:S(2)}, u32[]{:S(2)}) collective-permute-start(bf16[128,1024]{1,0:T(8,128)(2,1)S(1)} %collective-permute-done.1.refs_2_), channel_id=1, source_target_pairs={{0,2},{1,3},{2,0},{3,1},{4,6},{5,7},{6,4},{7,5},{8,10},{9,11},{10,... | collective-permute-start | bytes 786440 | tf_op jit(solution)/shard_map/ppermute | solution.py:409
  28.8 9.1 %collective-permute-start.4 = (bf16[128,1024]{1,0:T(8,128)(2,1)S(1)}, bf16[128,1024]{1,0:T(8,128)(2,1)S(1)}, u32[]{:S(2)}, u32[]{:S(2)}) collective-permute-start(bf16[128,1024]{1,0:T(8,128)(2,1)S(1)} %collective-permute-done.3.refs_0_), channel_id=1, source_target_pairs={{0,1},{1,0},{2,3},{3,2},{4,5},{5,4},{6,7},{7,6},{8,9},{9,8},{10,11... | collective-permute-start | bytes 786440 | tf_op jit(solution)/shard_map/ppermute | solution.py:409
  29.1 10.4 %collective-permute-start.9 = (bf16[128,1024]{1,0:T(8,128)(2,1)S(1)}, bf16[128,1024]{1,0:T(8,128)(2,1)S(1)}, u32[]{:S(2)}, u32[]{:S(2)}) collective-permute-start(bf16[128,1024]{1,0:T(8,128)(2,1)S(1)} %collective-permute-done.1.refs_2_), channel_id=1, source_target_pairs={{0,6},{1,7},{2,4},{3,5},{4,2},{5,3},{6,0},{7,1},{8,14},{9,15},{10,... | collective-permute-start | bytes 786440 | tf_op jit(solution)/shard_map/ppermute | solution.py:409
  30.9 26.7 %collective-permute-start.6 = (bf16[128,1024]{1,0:T(8,128)(2,1)S(1)}, bf16[128,1024]{1,0:T(8,128)(2,1)S(1)}, u32[]{:S(2)}, u32[]{:S(2)}) collective-permute-start(bf16[128,1024]{1,0:T(8,128)(2,1)S(1)} %collective-permute-done.5.refs_2_), channel_id=1, source_target_pairs={{0,1},{1,0},{2,3},{3,2},{4,5},{5,4},{6,7},{7,6},{8,9},{9,8},{10,11... | collective-permute-start | bytes 786440 | tf_op jit(solution)/shard_map/ppermute | solution.py:409
  32.1 24.6 %collective-permute-start.11 = (bf16[128,1024]{1,0:T(8,128)(2,1)S(1)}, bf16[128,1024]{1,0:T(8,128)(2,1)S(1)}, u32[]{:S(2)}, u32[]{:S(2)}) collective-permute-start(bf16[128,1024]{1,0:T(8,128)(2,1)S(1)} %collective-permute-done.5.refs_2_), channel_id=1, source_target_pairs={{0,2},{1,3},{2,0},{3,1},{4,6},{5,7},{6,4},{7,5},{8,10},{9,11},{10,... | collective-permute-start | bytes 786440 | tf_op jit(solution)/shard_map/ppermute | solution.py:409
  35.5 22.0 %collective-permute-start.13 = (bf16[128,1024]{1,0:T(8,128)(2,1)S(1)}, bf16[128,1024]{1,0:T(8,128)(2,1)S(1)}, u32[]{:S(2)}, u32[]{:S(2)}) collective-permute-start(bf16[128,1024]{1,0:T(8,128)(2,1)S(1)} %collective-permute-done.7.refs_4_), channel_id=1, source_target_pairs={{0,6},{1,7},{2,4},{3,5},{4,2},{5,3},{6,0},{7,1},{8,14},{9,15},{10,... | collective-permute-start | bytes 786440 | tf_op jit(solution)/shard_map/ppermute | solution.py:409
  37.9 19.7 %collective-permute-start.8 = (bf16[128,1024]{1,0:T(8,128)(2,1)S(1)}, bf16[128,1024]{1,0:T(8,128)(2,1)}, u32[]{:S(2)}, u32[]{:S(2)}) collective-permute-start(bf16[128,1024]{1,0:T(8,128)(2,1)S(1)} %collective-permute-done.7.refs_4_), channel_id=1, source_target_pairs={{0,1},{1,0},{2,3},{3,2},{4,5},{5,4},{6,7},{7,6},{8,9},{9,8},{10,11... | collective-permute-start | bytes 786440 | tf_op jit(solution)/shard_map/ppermute | solution.py:409
  39.5 18.1 %collective-permute-start.10 = (bf16[128,1024]{1,0:T(8,128)(2,1)S(1)}, bf16[128,1024]{1,0:T(8,128)(2,1)}, u32[]{:S(2)}, u32[]{:S(2)}) collective-permute-start(bf16[128,1024]{1,0:T(8,128)(2,1)S(1)} %collective-permute-done.9.refs_6_), channel_id=1, source_target_pairs={{0,1},{1,0},{2,3},{3,2},{4,5},{5,4},{6,7},{7,6},{8,9},{9,8},{10,11... | collective-permute-start | bytes 786440 | tf_op jit(solution)/shard_map/ppermute | solution.py:409
  40.9 26.7 %all-to-all-start.1 = ((s32[16,40,128]{2,1,0:T(8,128)}), s32[16,40,128]{2,1,0:T(8,128)S(1)}, u32[]{:S(2)}, u32[]{:S(2)}) async-start(s32[16,40,128]{2,1,0:T(8,128)} %residuals.1), calls=%async_computation.1 | async-start | bytes 655360 | tf_op jit(solution)/shard_map/all_to_all | solution.py:444
  56.7 8.5 %collective-permute-start.12 = (bf16[128,1024]{1,0:T(8,128)(2,1)S(1)}, bf16[128,1024]{1,0:T(8,128)(2,1)S(1)}, u32[]{:S(2)}, u32[]{:S(2)}) collective-permute-start(bf16[128,1024]{1,0:T(8,128)(2,1)S(1)} %collective-permute-done.11.refs_0_), channel_id=1, source_target_pairs={{0,1},{1,0},{2,3},{3,2},{4,5},{5,4},{6,7},{7,6},{8,9},{9,8},{10,11... | collective-permute-start | bytes 786440 | tf_op jit(solution)/shard_map/ppermute | solution.py:409
  57.4 7.7 %collective-permute-start.14 = (bf16[128,1024]{1,0:T(8,128)(2,1)S(1)}, bf16[128,1024]{1,0:T(8,128)(2,1)S(1)}, u32[]{:S(2)}, u32[]{:S(2)}) collective-permute-start(bf16[128,1024]{1,0:T(8,128)(2,1)S(1)} %collective-permute-done.13.refs_2_), channel_id=1, source_target_pairs={{0,1},{1,0},{2,3},{3,2},{4,5},{5,4},{6,7},{7,6},{8,9},{9,8},{10,11... | collective-permute-start | bytes 786440 | tf_op jit(solution)/shard_map/ppermute | solution.py:409
  68.5 1.4 %collective-permute-start.15 = (f32[144,128]{1,0:T(8,128)S(1)}, f32[144,128]{1,0:T(8,128)S(1)}, u32[]{:S(2)}, u32[]{:S(2)}) collective-permute-start(f32[144,128]{1,0:T(8,128)S(1)} %get-tuple-element.24), channel_id=1, source_target_pairs={{0,1},{1,0},{2,3},{3,2},{4,5},{5,4},{6,7},{7,6},{8,9},{9,8},{10,11... | collective-permute-start | bytes 221192 | tf_op jit(solution)/shard_map/ppermute | solution.py:409
  69.9 3.3 %collective-permute-start.16 = (f32[144,128]{1,0:T(8,128)S(1)}, f32[144,128]{1,0:T(8,128)S(1)}, u32[]{:S(2)}, u32[]{:S(2)}) collective-permute-start(f32[144,128]{1,0:T(8,128)S(1)} %join.2.a_ref), channel_id=1, source_target_pairs={{0,8},{1,9},{2,10},{3,11},{4,12},{5,13},{6,14},{7,15},{8,0},{9,1},... | collective-permute-start | bytes 221192 | tf_op jit(solution)/shard_map/ppermute | solution.py:409
  73.2 3.9 %collective-permute-start.17 = (f32[144,128]{1,0:T(8,128)S(1)}, f32[144,128]{1,0:T(8,128)S(1)}, u32[]{:S(2)}, u32[]{:S(2)}) collective-permute-start(f32[144,128]{1,0:T(8,128)S(1)} %join.3.a_ref), channel_id=1, source_target_pairs={{0,2},{1,3},{2,0},{3,1},{4,6},{5,7},{6,4},{7,5},{8,10},{9,11},{10,... | collective-permute-start | bytes 221192 | tf_op jit(solution)/shard_map/ppermute | solution.py:409
  73.3 4.9 %collective-permute-start.18 = (f32[144,128]{1,0:T(8,128)S(1)}, f32[144,128]{1,0:T(8,128)S(1)}, u32[]{:S(2)}, u32[]{:S(2)}) collective-permute-start(f32[144,128]{1,0:T(8,128)S(1)} %join.3.a_ref), channel_id=1, source_target_pairs={{0,4},{1,5},{2,6},{3,7},{4,0},{5,1},{6,2},{7,3},{8,12},{9,13},{10,... | collective-permute-start | bytes 221192 | tf_op jit(solution)/shard_map/ppermute | solution.py:409
  75.7 5.2 %collective-permute-start.19 = (f32[144,128]{1,0:T(8,128)S(1)}, f32[144,128]{1,0:T(8,128)S(1)}, u32[]{:S(2)}, u32[]{:S(2)}) collective-permute-start(f32[144,128]{1,0:T(8,128)S(1)} %join.3.a_ref), channel_id=1, source_target_pairs={{0,6},{1,7},{2,4},{3,5},{4,2},{5,3},{6,0},{7,1},{8,14},{9,15},{10,... | collective-permute-start | bytes 221192 | tf_op jit(solution)/shard_map/ppermute | solution.py:409
  81.5 3.0 %collective-permute-start.20 = (f32[128,128]{1,0:T(8,128)S(1)}, f32[128,128]{1,0:T(8,128)S(1)}, u32[]{:S(2)}, u32[]{:S(2)}) collective-permute-start(f32[128,128]{1,0:T(8,128)S(1)} %get-tuple-element.28.mine_ref), channel_id=1, source_target_pairs={{0,1},{1,0},{2,3},{3,2},{4,5},{5,4},{6,7},{7,6},{8,9},{9,8},{10,11... | collective-permute-start | bytes 196616 | tf_op jit(solution)/shard_map/ppermute | solution.py:409
  (5 other events, 22.4 us)

commit v6 on v5

--- a/solution.py
+++ b/solution.py
@@ -310,18 +310,17 @@
     )(on_chip(coded), codes_one, codes_two, *[on_chip(x) for x in lows])
 
 
-def join_kernel(shift, a_ref, b_ref, out_ref):
+def join_kernel(lows, a_ref, b_ref, out_ref):
     out_ref[:STATS, :] = a_ref[:STATS, :] + b_ref[:STATS, :]
-    keep = PAY - STATS - shift
     out_ref[STATS:PAY, :] = a_ref[STATS:PAY, :]
-    out_ref[STATS : STATS + keep, :] = jnp.minimum(
-        a_ref[STATS : STATS + keep, :], b_ref[STATS + shift : PAY, :]
-    )
-
-
-def join(a, b, shift):
-    return pl.pallas_call(
-        functools.partial(join_kernel, shift),
+    for mine, theirs in lows:
+        at, of = STATS + mine, STATS + theirs
+        out_ref[at : at + 1, :] = jnp.minimum(a_ref[at : at + 1, :], b_ref[of : of + 1, :])
+
+
+def join(a, b, lows):
+    return pl.pallas_call(
+        functools.partial(join_kernel, lows),
         out_shape=pltpu.VMEM(a.shape, f32),
         in_specs=[VM, VM],
         out_specs=VM,
@@ -331,9 +330,9 @@
     )(on_chip(a), on_chip(b))
 
 
-def update_kernel(width, a_ref, b_ref, c_ref, d_ref, init_ref, squares_ref, books_ref, gap_ref):
+def update_kernel(width, a_ref, b_ref, init_ref, squares_ref, books_ref, gap_ref):
     core = lax.rem(lax.axis_index("cent"), 2)
-    total = (a_ref[:STATS, :] + b_ref[:STATS, :]) + (c_ref[:STATS, :] + d_ref[:STATS, :])
+    total = a_ref[:STATS, :] + b_ref[:STATS, :]
     init = jnp.where(core == 1, init_ref[:, 128:], init_ref[:, :128])
     count_one = total[2 * width : 2 * width + 1]
     count_two = total[2 * width + 4 : 2 * width + 5]
@@ -341,10 +340,7 @@
     two = (total[width : 2 * width] + prior_weight * one) / (count_two + prior_weight)
     books_ref[:width, :] = one
     books_ref[width:, :] = two
-    low = jnp.minimum(
-        jnp.minimum(a_ref[STATS : STATS + 1, :], b_ref[STATS + 1 : STATS + 2, :]),
-        jnp.minimum(c_ref[STATS + 2 : STATS + 3, :], d_ref[STATS + 3 : STATS + 4, :]),
-    )
+    low = jnp.minimum(a_ref[STATS : STATS + 1, :], b_ref[STATS + 3 : STATS + 4, :])
     gap_ref[...] = (low + squares_ref[...]) * (1.0 / 1024.0)
 
 
@@ -356,7 +352,7 @@
             pltpu.VMEM((2 * width, 128), f32),
             jax.ShapeDtypeStruct((1, 128), f32),
         ),
-        in_specs=[VM] * 6,
+        in_specs=[VM] * 4,
         out_specs=(VM, VM),
         cost_estimate=pl.CostEstimate(flops=8 * STATS * 128, bytes_accessed=5 * PAY * 512, transcendentals=0),
         compiler_params=LIMIT,
@@ -444,9 +440,10 @@
     coded = lax.all_to_all(coded, "rows", 0, 0)
 
     mine, theirs, sub = statistics(coded, codes_one, codes_two, lows, where)
-    mine = join(mine, swap(theirs, 1), 0)
-    mine = join(mine, swap(mine, 8), 4)
-    parts = [mine] + [swap(mine, d) for d in (2, 4, 6)]
+    mine = join(mine, swap(theirs, 1), [(i, i) for i in range(8)])
+    mine = join(mine, swap(mine, 8), [(i, i + 4) for i in range(4)])
+    mine = join(mine, swap(mine, 2), [(0, 1), (3, 2)])
+    parts = [mine, swap(mine, 6)]
     init = codebook_init[0].T
     books, coarse_gap = update(parts, init, row_squares)
     book_one, book_two, distortion = distortions(sub, codes_two, books, swap(books, 1))

time: 85.8 us -> 87.6 us (1.021)
  waiting for transfers between devices: 19.8 us -> 22.4 us
    ppermute x21 -> x20, waiting for transfers between devices: 19.8 us -> 22.4 us  [swap(): return lax.ppermute(x, 'cent', [(i, i ^ offset) for i in range(16)])]
    ppermute x21 -> x20, starting transfers between devices: 22.1 us -> 21.3 us  [swap(): return lax.ppermute(x, 'cent', [(i, i ^ offset) for i in range(16)])]
  transfers between devices with their start and end apart: 23 -> 22, of which waited for: 7 -> 7; matrix products, arithmetic and copies ran while one was open for 0% -> 0% of each run, Pallas kernels for 19% -> 19%
where the time goes in v6:
time: 87.6 us; the launch traced here: 87.2 us
  starting transfers between devices  38.5 us (44%)
  Pallas kernels  23.8 us (27%)
  waiting for transfers between devices  22.4 us (26%)
  local copies, waits for them, and re-layouts  1.67 us (2%)
    ppermute x20, waiting for transfers between devices, swap(): return lax.ppermute(x, 'cent', [(i, i ^ offset) for i in range(16)])  22.4 us
    ppermute x20, starting transfers between devices, swap(): return lax.ppermute(x, 'cent', [(i, i ^ offset) for i in range(16)])  21.3 us
    pallas_call x3, Pallas kernels, nearest(): pl.pallas_call(functools.partial(nearest_kernel, step, 3, len(xs), mode),...  14.9 us
    all_to_all x1, starting transfers between devices, step(): coded = lax.all_to_all(coded, 'rows', 0, 0)  9.86 us
    all_to_all x1, starting transfers between devices, step(): fetched = lax.all_to_all(sent.reshape(peers, slots, width), 'cent', 0, 0)  7.34 us
    pallas_call x1, Pallas kernels, prepare(): pl.pallas_call(functools.partial(prepare_kernel, slots, step), out_shape=...  5.2 us
  transfers between devices with their start and end apart: 22, of which 7 were waited for; matrix products, arithmetic and copies ran while one was open for 0% of the time, Pallas kernels for 19%

profile of v6, /device:TPU:1, one launch (start us, length us, event | category | flops | bytes accessed | tf_op | source)
XLA Modules:
  0.0 87.2 jit_solution(10235614035331586722)
XLA Ops:
  0.6 5.2 %prepare.1 = (bf16[128,1024]{1,0:T(8,128)(2,1)S(1)}, f32[1,128]{1,0:T(1,128)S(1)}, bf16[256,1024]{1,0:T(8,128)(2,1)}) custom-call(bf16[128,1024]{1,0:T(8,128)(2,1)} %values_hbm.1, bf16[8,128]{1,0:T(8,128)(2,1)} %bitcast.15, s32[16,128]{1,0:T(8,128)} %ids_ref.1, bf16[2048,1024]{1,0:T(8,128)(2,1)} %refs_8_.1), custom_call_target="tpu_custom_call" | custom-call | flops 1073741824 | bytes 4194304 | tf_op jit(solution)/shard_map/prepare/pallas_call | solution.py:101
  5.9 7.3 %all-to-all-start = ((bf16[16,16,1024]{2,1,0:T(8,128)(2,1)}), bf16[16,16,1024]{2,1,0:T(8,128)(2,1)S(1)}, u32[]{:S(2)}, u32[]{:S(2)}) async-start(bf16[16,16,1024]{2,1,0:T(8,128)(2,1)} %bitcast.1), calls=%async_computation | async-start | bytes 1048576 | tf_op jit(solution)/shard_map/all_to_all | solution.py:422
  13.2 1.4 %collective-permute-start.1 = (bf16[128,1024]{1,0:T(8,128)(2,1)S(1)}, bf16[128,1024]{1,0:T(8,128)(2,1)S(1)}, u32[]{:S(2)}, u32[]{:S(2)}) collective-permute-start(bf16[128,1024]{1,0:T(8,128)(2,1)S(1)} %get-tuple-element.19.q_ref.refs_0_), channel_id=1, source_target_pairs={{0,8},{1,9},{2,10},{3,11},{4,12},{5,13},{6,14},{7,15},{8,0},{9,1},... | collective-permute-start | bytes 786440 | tf_op jit(solution)/shard_map/ppermute | solution.py:405
  14.5 1.2 %collective-permute-start.3 = (bf16[128,1024]{1,0:T(8,128)(2,1)S(1)}, bf16[128,1024]{1,0:T(8,128)(2,1)S(1)}, u32[]{:S(2)}, u32[]{:S(2)}) collective-permute-start(bf16[128,1024]{1,0:T(8,128)(2,1)S(1)} %get-tuple-element.19.q_ref.refs_0_), channel_id=1, source_target_pairs={{0,2},{1,3},{2,0},{3,1},{4,6},{5,7},{6,4},{7,5},{8,10},{9,11},{10,... | collective-permute-start | bytes 786440 | tf_op jit(solution)/shard_map/ppermute | solution.py:405
  15.7 1.0 %collective-permute-start = (bf16[128,1024]{1,0:T(8,128)(2,1)S(1)}, bf16[128,1024]{1,0:T(8,128)(2,1)S(1)}, u32[]{:S(2)}, u32[]{:S(2)}) collective-permute-start(bf16[128,1024]{1,0:T(8,128)(2,1)S(1)} %get-tuple-element.19.q_ref.refs_0_), channel_id=1, source_target_pairs={{0,1},{1,0},{2,3},{3,2},{4,5},{5,4},{6,7},{7,6},{8,9},{9,8},{10,11... | collective-permute-start | bytes 786440 | tf_op jit(solution)/shard_map/ppermute | solution.py:405
  16.7 1.8 %collective-permute-start.5 = (bf16[128,1024]{1,0:T(8,128)(2,1)S(1)}, bf16[128,1024]{1,0:T(8,128)(2,1)S(1)}, u32[]{:S(2)}, u32[]{:S(2)}) collective-permute-start(bf16[128,1024]{1,0:T(8,128)(2,1)S(1)} %get-tuple-element.19.q_ref.refs_0_), channel_id=1, source_target_pairs={{0,6},{1,7},{2,4},{3,5},{4,2},{5,3},{6,0},{7,1},{8,14},{9,15},{10,... | collective-permute-start | bytes 786440 | tf_op jit(solution)/shard_map/ppermute | solution.py:405
  18.5 8.2 %collective-permute-done.1.refs_2_ = bf16[128,1024]{1,0:T(8,128)(2,1)S(1)} collective-permute-done((bf16[128,1024]{1,0:T(8,128)(2,1)S(1)}, bf16[128,1024]{1,0:T(8,128)(2,1)S(1)}, u32[]{:S(2)}, u32[]{:S(2)}) %collective-permute-start.1) | collective-permute-done | bytes 262176 | tf_op jit(solution)/shard_map/ppermute | solution.py:405
  26.7 1.0 %collective-permute-start.2 = (bf16[128,1024]{1,0:T(8,128)(2,1)S(1)}, bf16[128,1024]{1,0:T(8,128)(2,1)S(1)}, u32[]{:S(2)}, u32[]{:S(2)}) collective-permute-start(bf16[128,1024]{1,0:T(8,128)(2,1)S(1)} %collective-permute-done.1.refs_2_), channel_id=1, source_target_pairs={{0,1},{1,0},{2,3},{3,2},{4,5},{5,4},{6,7},{7,6},{8,9},{9,8},{10,11... | collective-permute-start | bytes 786440 | tf_op jit(solution)/shard_map/ppermute | solution.py:405
  27.6 1.2 %collective-permute-start.7 = (bf16[128,1024]{1,0:T(8,128)(2,1)S(1)}, bf16[128,1024]{1,0:T(8,128)(2,1)S(1)}, u32[]{:S(2)}, u32[]{:S(2)}) collective-permute-start(bf16[128,1024]{1,0:T(8,128)(2,1)S(1)} %collective-permute-done.1.refs_2_), channel_id=1, source_target_pairs={{0,2},{1,3},{2,0},{3,1},{4,6},{5,7},{6,4},{7,5},{8,10},{9,11},{10,... | collective-permute-start | bytes 786440 | tf_op jit(solution)/shard_map/ppermute | solution.py:405
  29.1 1.8 %collective-permute-start.9 = (bf16[128,1024]{1,0:T(8,128)(2,1)S(1)}, bf16[128,1024]{1,0:T(8,128)(2,1)S(1)}, u32[]{:S(2)}, u32[]{:S(2)}) collective-permute-start(bf16[128,1024]{1,0:T(8,128)(2,1)S(1)} %collective-permute-done.1.refs_2_), channel_id=1, source_target_pairs={{0,6},{1,7},{2,4},{3,5},{4,2},{5,3},{6,0},{7,1},{8,14},{9,15},{10,... | collective-permute-start | bytes 786440 | tf_op jit(solution)/shard_map/ppermute | solution.py:405
  32.4 3.1 %collective-permute-done.7.refs_4_ = bf16[128,1024]{1,0:T(8,128)(2,1)S(1)} collective-permute-done((bf16[128,1024]{1,0:T(8,128)(2,1)S(1)}, bf16[128,1024]{1,0:T(8,128)(2,1)S(1)}, u32[]{:S(2)}, u32[]{:S(2)}) %collective-permute-start.7) | collective-permute-done | bytes 262176 | tf_op jit(solution)/shard_map/ppermute | solution.py:405
  35.5 2.4 %collective-permute-start.13 = (bf16[128,1024]{1,0:T(8,128)(2,1)S(1)}, bf16[128,1024]{1,0:T(8,128)(2,1)S(1)}, u32[]{:S(2)}, u32[]{:S(2)}) collective-permute-start(bf16[128,1024]{1,0:T(8,128)(2,1)S(1)} %collective-permute-done.7.refs_4_), channel_id=1, source_target_pairs={{0,6},{1,7},{2,4},{3,5},{4,2},{5,3},{6,0},{7,1},{8,14},{9,15},{10,... | collective-permute-start | bytes 786440 | tf_op jit(solution)/shard_map/ppermute | solution.py:405
  37.9 1.6 %collective-permute-start.8 = (bf16[128,1024]{1,0:T(8,128)(2,1)S(1)}, bf16[128,1024]{1,0:T(8,128)(2,1)}, u32[]{:S(2)}, u32[]{:S(2)}) collective-permute-start(bf16[128,1024]{1,0:T(8,128)(2,1)S(1)} %collective-permute-done.7.refs_4_), channel_id=1, source_target_pairs={{0,1},{1,0},{2,3},{3,2},{4,5},{5,4},{6,7},{7,6},{8,9},{9,8},{10,11... | collective-permute-start | bytes 786440 | tf_op jit(solution)/shard_map/ppermute | solution.py:405
  39.6 1.3 %residuals.1 = s32[16,40,128]{2,1,0:T(8,128)} custom-call(s32[16,128]{1,0:T(8,128)S(1)} %copy-done.1, bf16[256,1024]{1,0:T(8,128)(2,1)S(1)} %bitcast.13, bf16[128,1024]{1,0:T(8,128)(2,1)S(1)} %get-tuple-element.19.q_ref.refs_0_), custom_call_target="tpu_custom_call" | custom-call | flops 67108864 | bytes 1310720 | tf_op jit(solution)/shard_map/residuals/pallas_call | solution.py:170
  40.9 9.9 %all-to-all-start.1 = ((s32[16,40,128]{2,1,0:T(8,128)}), s32[16,40,128]{2,1,0:T(8,128)S(1)}, u32[]{:S(2)}, u32[]{:S(2)}) async-start(s32[16,40,128]{2,1,0:T(8,128)} %residuals.1), calls=%async_computation.1 | async-start | bytes 655360 | tf_op jit(solution)/shard_map/all_to_all | solution.py:440
  50.8 0.9 %copy-done.4 = bf16[128,1024]{1,0:T(8,128)(2,1)S(1)} copy-done((bf16[128,1024]{1,0:T(8,128)(2,1)S(1)}, bf16[128,1024]{1,0:T(8,128)(2,1)}, u32[]{:S(2)}) %copy-start.4) | copy-done | bytes 262168
  51.7 4.9 %nearest.3.refs_0_ = f32[4,128]{1,0:T(4,128)S(1)} custom-call(bf16[128,1024]{1,0:T(8,128)(2,1)S(1)} %get-tuple-element.19.q_ref.refs_0_, bf16[128,1024]{1,0:T(8,128)(2,1)S(1)} %collective-permute-done.refs_1_, bf16[128,1024]{1,0:T(8,128)(2,1)S(1)} %collective-permute-done.1.refs_2_, bf16[128,1024]{1,0:T(8,128)(2,1)S(1)} %copy-done.4, bf16[2048,1024]{1,0:T(8,128)(2,1)} %refs_8_.1), custom_call_target="tpu_custom_call" | custom-call | flops 2147483648 | bytes 5242880 | tf_op jit(solution)/shard_map/nearest/pallas_call | solution.py:238
  57.6 7.6 %nearest.4 = (f32[8,128]{1,0:T(8,128)S(1)}, bf16[8,256,1024]{2,1,0:T(8,128)(2,1)S(1)}, f32[2048,128]{1,0:T(8,128)S(1)}) custom-call(bf16[128,1024]{1,0:T(8,128)(2,1)S(1)} %collective-permute-done.3.refs_0_, bf16[128,1024]{1,0:T(8,128)(2,1)S(1)} %collective-permute-done.4.refs_1_, bf16[128,1024]{1,0:T(8,128)(2,1)S(1)} %collective-permute-done.5.refs_2_, ...), custom_call_target="tpu_custom_call" | custom-call | flops 4294967296 | bytes 6291456 | tf_op jit(solution)/shard_map/nearest/pallas_call | solution.py:238
  65.2 2.4 %nearest.5.refs_2_ = f32[4,128]{1,0:T(4,128)S(1)} custom-call(bf16[128,1024]{1,0:T(8,128)(2,1)S(1)} %collective-permute-done.11.refs_0_, bf16[128,1024]{1,0:T(8,128)(2,1)S(1)} %collective-permute-done.12.refs_1_, bf16[128,1024]{1,0:T(8,128)(2,1)S(1)} %collective-permute-done.13.refs_2_, bf16[128,1024]{1,0:T(8,128)(2,1)S(1)} %collective-permute-done.14.refs_3_, ...), custom_call_target="tpu_custom_call" | custom-call | flops 2147483648 | bytes 5242880 | tf_op jit(solution)/shard_map/nearest/pallas_call | solution.py:238
  70.3 2.9 %collective-permute-done.16.b_ref = f32[144,128]{1,0:T(8,128)S(1)} collective-permute-done((f32[144,128]{1,0:T(8,128)S(1)}, f32[144,128]{1,0:T(8,128)S(1)}, u32[]{:S(2)}, u32[]{:S(2)}) %collective-permute-start.16) | collective-permute-done | bytes 73760 | tf_op jit(solution)/shard_map/ppermute | solution.py:405
  73.3 3.2 %collective-permute-done.17.b_ref = f32[144,128]{1,0:T(8,128)S(1)} collective-permute-done((f32[144,128]{1,0:T(8,128)S(1)}, f32[144,128]{1,0:T(8,128)S(1)}, u32[]{:S(2)}, u32[]{:S(2)}) %collective-permute-start.17) | collective-permute-done | bytes 73760 | tf_op jit(solution)/shard_map/ppermute | solution.py:405
  76.5 1.3 %collective-permute-start.18 = (f32[144,128]{1,0:T(8,128)S(1)}, f32[144,128]{1,0:T(8,128)S(1)}, u32[]{:S(2)}, u32[]{:S(2)}) collective-permute-start(f32[144,128]{1,0:T(8,128)S(1)} %join.5.a_ref), channel_id=1, source_target_pairs={{0,6},{1,7},{2,4},{3,5},{4,2},{5,3},{6,0},{7,1},{8,14},{9,15},{10,... | collective-permute-start | bytes 221192 | tf_op jit(solution)/shard_map/ppermute | solution.py:405
  77.9 3.2 %collective-permute-done.18.b_ref = f32[144,128]{1,0:T(8,128)S(1)} collective-permute-done((f32[144,128]{1,0:T(8,128)S(1)}, f32[144,128]{1,0:T(8,128)S(1)}, u32[]{:S(2)}, u32[]{:S(2)}) %collective-permute-start.18) | collective-permute-done | bytes 73760 | tf_op jit(solution)/shard_map/ppermute | solution.py:405
  81.6 3.8 %collective-permute-start.19 = (f32[128,128]{1,0:T(8,128)S(1)}, f32[128,128]{1,0:T(8,128)S(1)}, u32[]{:S(2)}, u32[]{:S(2)}) collective-permute-start(f32[128,128]{1,0:T(8,128)S(1)} %get-tuple-element.28.mine_ref), channel_id=1, source_target_pairs={{0,1},{1,0},{2,3},{3,2},{4,5},{5,4},{6,7},{7,6},{8,9},{9,8},{10,11... | collective-permute-start | bytes 196616 | tf_op jit(solution)/shard_map/ppermute | solution.py:405
  (43 shorter events, 7.9 us)
Async XLA Ops:
  0.6 39.0 %copy-start.1 = (s32[16,128]{1,0:T(8,128)S(1)}, s32[16,128]{1,0:T(8,128)}, u32[]{:S(2)}) copy-start(s32[16,128]{1,0:T(8,128)} %ids_ref.1) | copy-start | bytes 24580
  5.9 33.7 %all-to-all-start = ((bf16[16,16,1024]{2,1,0:T(8,128)(2,1)}), bf16[16,16,1024]{2,1,0:T(8,128)(2,1)S(1)}, u32[]{:S(2)}, u32[]{:S(2)}) async-start(bf16[16,16,1024]{2,1,0:T(8,128)(2,1)} %bitcast.1), calls=%async_computation | async-start | bytes 1048576 | tf_op jit(solution)/shard_map/all_to_all | solution.py:422
  13.2 13.5 %collective-permute-start.1 = (bf16[128,1024]{1,0:T(8,128)(2,1)S(1)}, bf16[128,1024]{1,0:T(8,128)(2,1)S(1)}, u32[]{:S(2)}, u32[]{:S(2)}) collective-permute-start(bf16[128,1024]{1,0:T(8,128)(2,1)S(1)} %get-tuple-element.19.q_ref.refs_0_), channel_id=1, source_target_pairs={{0,8},{1,9},{2,10},{3,11},{4,12},{5,13},{6,14},{7,15},{8,0},{9,1},... | collective-permute-start | bytes 786440 | tf_op jit(solution)/shard_map/ppermute | solution.py:405
  14.5 14.3 %collective-permute-start.3 = (bf16[128,1024]{1,0:T(8,128)(2,1)S(1)}, bf16[128,1024]{1,0:T(8,128)(2,1)S(1)}, u32[]{:S(2)}, u32[]{:S(2)}) collective-permute-start(bf16[128,1024]{1,0:T(8,128)(2,1)S(1)} %get-tuple-element.19.q_ref.refs_0_), channel_id=1, source_target_pairs={{0,2},{1,3},{2,0},{3,1},{4,6},{5,7},{6,4},{7,5},{8,10},{9,11},{10,... | collective-permute-start | bytes 786440 | tf_op jit(solution)/shard_map/ppermute | solution.py:405
  15.7 13.4 %collective-permute-start = (bf16[128,1024]{1,0:T(8,128)(2,1)S(1)}, bf16[128,1024]{1,0:T(8,128)(2,1)S(1)}, u32[]{:S(2)}, u32[]{:S(2)}) collective-permute-start(bf16[128,1024]{1,0:T(8,128)(2,1)S(1)} %get-tuple-element.19.q_ref.refs_0_), channel_id=1, source_target_pairs={{0,1},{1,0},{2,3},{3,2},{4,5},{5,4},{6,7},{7,6},{8,9},{9,8},{10,11... | collective-permute-start | bytes 786440 | tf_op jit(solution)/shard_map/ppermute | solution.py:405
  16.7 14.2 %collective-permute-start.5 = (bf16[128,1024]{1,0:T(8,128)(2,1)S(1)}, bf16[128,1024]{1,0:T(8,128)(2,1)S(1)}, u32[]{:S(2)}, u32[]{:S(2)}) collective-permute-start(bf16[128,1024]{1,0:T(8,128)(2,1)S(1)} %get-tuple-element.19.q_ref.refs_0_), channel_id=1, source_target_pairs={{0,6},{1,7},{2,4},{3,5},{4,2},{5,3},{6,0},{7,1},{8,14},{9,15},{10,... | collective-permute-start | bytes 786440 | tf_op jit(solution)/shard_map/ppermute | solution.py:405
  26.7 4.7 %collective-permute-start.2 = (bf16[128,1024]{1,0:T(8,128)(2,1)S(1)}, bf16[128,1024]{1,0:T(8,128)(2,1)S(1)}, u32[]{:S(2)}, u32[]{:S(2)}) collective-permute-start(bf16[128,1024]{1,0:T(8,128)(2,1)S(1)} %collective-permute-done.1.refs_2_), channel_id=1, source_target_pairs={{0,1},{1,0},{2,3},{3,2},{4,5},{5,4},{6,7},{7,6},{8,9},{9,8},{10,11... | collective-permute-start | bytes 786440 | tf_op jit(solution)/shard_map/ppermute | solution.py:405
  27.6 7.9 %collective-permute-start.7 = (bf16[128,1024]{1,0:T(8,128)(2,1)S(1)}, bf16[128,1024]{1,0:T(8,128)(2,1)S(1)}, u32[]{:S(2)}, u32[]{:S(2)}) collective-permute-start(bf16[128,1024]{1,0:T(8,128)(2,1)S(1)} %collective-permute-done.1.refs_2_), channel_id=1, source_target_pairs={{0,2},{1,3},{2,0},{3,1},{4,6},{5,7},{6,4},{7,5},{8,10},{9,11},{10,... | collective-permute-start | bytes 786440 | tf_op jit(solution)/shard_map/ppermute | solution.py:405
  28.8 9.1 %collective-permute-start.4 = (bf16[128,1024]{1,0:T(8,128)(2,1)S(1)}, bf16[128,1024]{1,0:T(8,128)(2,1)S(1)}, u32[]{:S(2)}, u32[]{:S(2)}) collective-permute-start(bf16[128,1024]{1,0:T(8,128)(2,1)S(1)} %collective-permute-done.3.refs_0_), channel_id=1, source_target_pairs={{0,1},{1,0},{2,3},{3,2},{4,5},{5,4},{6,7},{7,6},{8,9},{9,8},{10,11... | collective-permute-start | bytes 786440 | tf_op jit(solution)/shard_map/ppermute | solution.py:405
  29.1 10.4 %collective-permute-start.9 = (bf16[128,1024]{1,0:T(8,128)(2,1)S(1)}, bf16[128,1024]{1,0:T(8,128)(2,1)S(1)}, u32[]{:S(2)}, u32[]{:S(2)}) collective-permute-start(bf16[128,1024]{1,0:T(8,128)(2,1)S(1)} %collective-permute-done.1.refs_2_), channel_id=1, source_target_pairs={{0,6},{1,7},{2,4},{3,5},{4,2},{5,3},{6,0},{7,1},{8,14},{9,15},{10,... | collective-permute-start | bytes 786440 | tf_op jit(solution)/shard_map/ppermute | solution.py:405
  30.9 26.7 %collective-permute-start.6 = (bf16[128,1024]{1,0:T(8,128)(2,1)S(1)}, bf16[128,1024]{1,0:T(8,128)(2,1)S(1)}, u32[]{:S(2)}, u32[]{:S(2)}) collective-permute-start(bf16[128,1024]{1,0:T(8,128)(2,1)S(1)} %collective-permute-done.5.refs_2_), channel_id=1, source_target_pairs={{0,1},{1,0},{2,3},{3,2},{4,5},{5,4},{6,7},{7,6},{8,9},{9,8},{10,11... | collective-permute-start | bytes 786440 | tf_op jit(solution)/shard_map/ppermute | solution.py:405
  32.1 24.6 %collective-permute-start.11 = (bf16[128,1024]{1,0:T(8,128)(2,1)S(1)}, bf16[128,1024]{1,0:T(8,128)(2,1)S(1)}, u32[]{:S(2)}, u32[]{:S(2)}) collective-permute-start(bf16[128,1024]{1,0:T(8,128)(2,1)S(1)} %collective-permute-done.5.refs_2_), channel_id=1, source_target_pairs={{0,2},{1,3},{2,0},{3,1},{4,6},{5,7},{6,4},{7,5},{8,10},{9,11},{10,... | collective-permute-start | bytes 786440 | tf_op jit(solution)/shard_map/ppermute | solution.py:405
  35.5 22.0 %collective-permute-start.13 = (bf16[128,1024]{1,0:T(8,128)(2,1)S(1)}, bf16[128,1024]{1,0:T(8,128)(2,1)S(1)}, u32[]{:S(2)}, u32[]{:S(2)}) collective-permute-start(bf16[128,1024]{1,0:T(8,128)(2,1)S(1)} %collective-permute-done.7.refs_4_), channel_id=1, source_target_pairs={{0,6},{1,7},{2,4},{3,5},{4,2},{5,3},{6,0},{7,1},{8,14},{9,15},{10,... | collective-permute-start | bytes 786440 | tf_op jit(solution)/shard_map/ppermute | solution.py:405
  37.9 19.7 %collective-permute-start.8 = (bf16[128,1024]{1,0:T(8,128)(2,1)S(1)}, bf16[128,1024]{1,0:T(8,128)(2,1)}, u32[]{:S(2)}, u32[]{:S(2)}) collective-permute-start(bf16[128,1024]{1,0:T(8,128)(2,1)S(1)} %collective-permute-done.7.refs_4_), channel_id=1, source_target_pairs={{0,1},{1,0},{2,3},{3,2},{4,5},{5,4},{6,7},{7,6},{8,9},{9,8},{10,11... | collective-permute-start | bytes 786440 | tf_op jit(solution)/shard_map/ppermute | solution.py:405
  39.5 18.1 %collective-permute-start.10 = (bf16[128,1024]{1,0:T(8,128)(2,1)S(1)}, bf16[128,1024]{1,0:T(8,128)(2,1)}, u32[]{:S(2)}, u32[]{:S(2)}) collective-permute-start(bf16[128,1024]{1,0:T(8,128)(2,1)S(1)} %collective-permute-done.9.refs_6_), channel_id=1, source_target_pairs={{0,1},{1,0},{2,3},{3,2},{4,5},{5,4},{6,7},{7,6},{8,9},{9,8},{10,11... | collective-permute-start | bytes 786440 | tf_op jit(solution)/shard_map/ppermute | solution.py:405
  40.9 26.7 %all-to-all-start.1 = ((s32[16,40,128]{2,1,0:T(8,128)}), s32[16,40,128]{2,1,0:T(8,128)S(1)}, u32[]{:S(2)}, u32[]{:S(2)}) async-start(s32[16,40,128]{2,1,0:T(8,128)} %residuals.1), calls=%async_computation.1 | async-start | bytes 655360 | tf_op jit(solution)/shard_map/all_to_all | solution.py:440
  56.7 8.5 %collective-permute-start.12 = (bf16[128,1024]{1,0:T(8,128)(2,1)S(1)}, bf16[128,1024]{1,0:T(8,128)(2,1)S(1)}, u32[]{:S(2)}, u32[]{:S(2)}) collective-permute-start(bf16[128,1024]{1,0:T(8,128)(2,1)S(1)} %collective-permute-done.11.refs_0_), channel_id=1, source_target_pairs={{0,1},{1,0},{2,3},{3,2},{4,5},{5,4},{6,7},{7,6},{8,9},{9,8},{10,11... | collective-permute-start | bytes 786440 | tf_op jit(solution)/shard_map/ppermute | solution.py:405
  57.5 7.7 %collective-permute-start.14 = (bf16[128,1024]{1,0:T(8,128)(2,1)S(1)}, bf16[128,1024]{1,0:T(8,128)(2,1)S(1)}, u32[]{:S(2)}, u32[]{:S(2)}) collective-permute-start(bf16[128,1024]{1,0:T(8,128)(2,1)S(1)} %collective-permute-done.13.refs_2_), channel_id=1, source_target_pairs={{0,1},{1,0},{2,3},{3,2},{4,5},{5,4},{6,7},{7,6},{8,9},{9,8},{10,11... | collective-permute-start | bytes 786440 | tf_op jit(solution)/shard_map/ppermute | solution.py:405
  65.2 15.8 %copy-start = (f32[1,256,64]{1,2,0:T(8,128)S(1)}, f32[1,256,64]{1,2,0:T(8,128)}, u32[]{:S(2)}) copy-start(f32[1,256,64]{1,2,0:T(8,128)} %param.13) | copy-start | bytes 196612
  68.5 1.4 %collective-permute-start.15 = (f32[144,128]{1,0:T(8,128)S(1)}, f32[144,128]{1,0:T(8,128)S(1)}, u32[]{:S(2)}, u32[]{:S(2)}) collective-permute-start(f32[144,128]{1,0:T(8,128)S(1)} %get-tuple-element.24), channel_id=1, source_target_pairs={{0,1},{1,0},{2,3},{3,2},{4,5},{5,4},{6,7},{7,6},{8,9},{9,8},{10,11... | collective-permute-start | bytes 221192 | tf_op jit(solution)/shard_map/ppermute | solution.py:405
  69.9 3.3 %collective-permute-start.16 = (f32[144,128]{1,0:T(8,128)S(1)}, f32[144,128]{1,0:T(8,128)S(1)}, u32[]{:S(2)}, u32[]{:S(2)}) collective-permute-start(f32[144,128]{1,0:T(8,128)S(1)} %join.3.a_ref), channel_id=1, source_target_pairs={{0,8},{1,9},{2,10},{3,11},{4,12},{5,13},{6,14},{7,15},{8,0},{9,1},... | collective-permute-start | bytes 221192 | tf_op jit(solution)/shard_map/ppermute | solution.py:405
  73.2 3.3 %collective-permute-start.17 = (f32[144,128]{1,0:T(8,128)S(1)}, f32[144,128]{1,0:T(8,128)S(1)}, u32[]{:S(2)}, u32[]{:S(2)}) collective-permute-start(f32[144,128]{1,0:T(8,128)S(1)} %join.4.a_ref), channel_id=1, source_target_pairs={{0,2},{1,3},{2,0},{3,1},{4,6},{5,7},{6,4},{7,5},{8,10},{9,11},{10,... | collective-permute-start | bytes 221192 | tf_op jit(solution)/shard_map/ppermute | solution.py:405
  76.5 4.5 %collective-permute-start.18 = (f32[144,128]{1,0:T(8,128)S(1)}, f32[144,128]{1,0:T(8,128)S(1)}, u32[]{:S(2)}, u32[]{:S(2)}) collective-permute-start(f32[144,128]{1,0:T(8,128)S(1)} %join.5.a_ref), channel_id=1, source_target_pairs={{0,6},{1,7},{2,4},{3,5},{4,2},{5,3},{6,0},{7,1},{8,14},{9,15},{10,... | collective-permute-start | bytes 221192 | tf_op jit(solution)/shard_map/ppermute | solution.py:405
  81.6 4.7 %collective-permute-start.19 = (f32[128,128]{1,0:T(8,128)S(1)}, f32[128,128]{1,0:T(8,128)S(1)}, u32[]{:S(2)}, u32[]{:S(2)}) collective-permute-start(f32[128,128]{1,0:T(8,128)S(1)} %get-tuple-element.28.mine_ref), channel_id=1, source_target_pairs={{0,1},{1,0},{2,3},{3,2},{4,5},{5,4},{6,7},{7,6},{8,9},{9,8},{10,11... | collective-permute-start | bytes 196616 | tf_op jit(solution)/shard_map/ppermute | solution.py:405
  (4 other events, 6.6 us)

commit v7 on v5

--- a/solution.py
+++ b/solution.py
@@ -182,11 +182,14 @@
 
 def nearest_kernel(step, ahead, blocks, mode, *refs):
     x_refs, refs = refs[:blocks], refs[blocks:]
+    copies = []
     if mode == "again":
         cents_ref, squares_ref, out_ref = refs
-        copies = []
     else:
-        cents_hbm, out_ref, cents_ref, squares_ref, sems = refs
+        if mode == "first":
+            cents_hbm, out_ref, squares_ref, cents_ref, sems = refs
+        else:
+            cents_hbm, squares_ref, out_ref, cents_ref, sems = refs
         half = step // 2
         copies = [
             pltpu.make_async_copy(cents_hbm.at[pl.ds(half * i, half), :], cents_ref.at[i], sems.at[i])
@@ -202,7 +205,7 @@
                 copies[k + ahead].start()
         block = jnp.concatenate([cents_ref[i], cents_ref[i + 1]], axis=0)
         at = slice(step // 2 * i, step // 2 * i + step)
-        if mode == "again":
+        if mode != "first":
             squares = squares_ref[at, :]
         else:
             total = None
@@ -222,20 +225,23 @@
             out_ref[2 * j + k : 2 * j + k + 1, :] = low[:, 128 * k : 128 * k + 128]
 
 
-def nearest(xs, cents, mode, kept=()):
+def nearest(xs, cents, squares=None, kept=None):
     count, width = cents.shape
     rows = sum(x.shape[0] for x in xs)
     step = 512
+    mode = "first" if squares is None else "keep" if kept is None else "again"
     out = [pltpu.VMEM((rows // 128, 128), f32)]
-    held = [pltpu.VMEM((2 * count // step, step // 2, width), bf16), pltpu.VMEM((count, 128), f32)]
+    held = [pltpu.VMEM((2 * count // step, step // 2, width), bf16)]
     sems = [pltpu.SemaphoreType.DMA((2 * count // step,))]
-    more = {
-        "once": ([HBM], out, held + sems),
-        "keep": ([HBM], out + held, sems),
-        "again": ([VM, VM], out, []),
-    }
-    ins, outs, scratch = more[mode]
-    result = pl.pallas_call(
+    ins, operands, outs, scratch = {
+        "first": ([HBM], [off_chip(cents)], out + [pltpu.VMEM((count, 128), f32)], held + sems),
+        "keep": ([HBM, VM], [off_chip(cents), squares], out + held, sems),
+        "again": ([VM, VM], [kept, squares], out, []),
+    }[mode]
+    operands = operands[:1] + [on_chip(x) for x in operands[1:]]
+    if mode == "again":
+        operands[0] = on_chip(operands[0])
+    return pl.pallas_call(
         functools.partial(nearest_kernel, step, 3, len(xs), mode),
         out_shape=tuple(outs),
         in_specs=[VM] * len(xs) + ins,
@@ -246,8 +252,7 @@
         ),
         compiler_params=LIMIT,
         name="nearest",
-    )(*[on_chip(x) for x in xs], *([on_chip(x) for x in kept] or [off_chip(cents)]))
-    return result[0], result[1:]
+    )(*[on_chip(x) for x in xs], *operands)
 
 
 def halves_of(x):
@@ -433,11 +438,15 @@
     for d in (2, 6, 8, 4, 10, 14, 12):
         blocks[d ^ core] = swap(blocks[d], core)
 
-    orders = ((0, 1, 8, 9), (2, 3, 6, 7, 10, 11, 14, 15), (4, 5, 12, 13))
-    lows, kept = [], ()
-    for order, mode in zip(orders, ("once", "keep", "again")):
-        low, kept = nearest([blocks[d] for d in order], centroids, mode, kept)
+    orders = ((0, 1, 8, 9), (2, 3, 6, 7, 10, 11, 14, 15), (4, 12), (5, 13))
+    lows, squares, kept = [], None, None
+    for k, order in enumerate(orders):
+        low, *more = nearest([blocks[d] for d in order], centroids, squares, kept)
         lows.append(low)
+        if k == 0:
+            (squares,) = more
+        elif k == 1:
+            (kept,) = more
     where = {d: (k, j) for k, order in enumerate(orders) for j, d in enumerate(order)}
 
     coded = residuals(coarse_ids, fetched, q, count, slots, sub_width)

time: 85.8 us -> 86 us (level)
    pallas_call x3 -> x4, Pallas kernels: 14.9 us -> 15.1 us  [nearest(): pl.pallas_call(functools.partial(nearest_kernel, step, 3, len(xs), mode),...]
where the time goes in v7:
time: 86 us; the launch traced here: 85.5 us
  starting transfers between devices  39.3 us (46%)
  Pallas kernels  23.9 us (28%)
  waiting for transfers between devices  19.8 us (23%)
  local copies, waits for them, and re-layouts  1.66 us (2%)
    ppermute x21, starting transfers between devices, swap(): return lax.ppermute(x, 'cent', [(i, i ^ offset) for i in range(16)])  22.2 us
    ppermute x21, waiting for transfers between devices, swap(): return lax.ppermute(x, 'cent', [(i, i ^ offset) for i in range(16)])  19.8 us
    pallas_call x4, Pallas kernels, nearest(): pl.pallas_call(functools.partial(nearest_kernel, step, 3, len(xs), mode),...  15.1 us
    all_to_all x1, starting transfers between devices, step(): coded = lax.all_to_all(coded, 'rows', 0, 0)  9.86 us
    all_to_all x1, starting transfers between devices, step(): fetched = lax.all_to_all(sent.reshape(peers, slots, width), 'cent', 0, 0)  7.34 us
    pallas_call x1, Pallas kernels, prepare(): pl.pallas_call(functools.partial(prepare_kernel, slots, step), out_shape=...  5.2 us
  transfers between devices with their start and end apart: 23, of which 7 were waited for; matrix products, arithmetic and copies ran while one was open for 0% of the time, Pallas kernels for 19%

profile of v7, /device:TPU:1, one launch (start us, length us, event | category | flops | bytes accessed | tf_op | source)
XLA Modules:
  0.0 85.5 jit_solution(13602154446727817252)
XLA Ops:
  0.6 5.2 %prepare.1 = (bf16[128,1024]{1,0:T(8,128)(2,1)S(1)}, f32[1,128]{1,0:T(1,128)S(1)}, bf16[256,1024]{1,0:T(8,128)(2,1)}) custom-call(bf16[128,1024]{1,0:T(8,128)(2,1)} %values_hbm.1, bf16[8,128]{1,0:T(8,128)(2,1)} %bitcast.15, s32[16,128]{1,0:T(8,128)} %ids_ref.1, bf16[2048,1024]{1,0:T(8,128)(2,1)} %refs_8_.1), custom_call_target="tpu_custom_call" | custom-call | flops 1073741824 | bytes 4194304 | tf_op jit(solution)/shard_map/prepare/pallas_call | solution.py:101
  5.9 7.3 %all-to-all-start = ((bf16[16,16,1024]{2,1,0:T(8,128)(2,1)}), bf16[16,16,1024]{2,1,0:T(8,128)(2,1)S(1)}, u32[]{:S(2)}, u32[]{:S(2)}) async-start(bf16[16,16,1024]{2,1,0:T(8,128)(2,1)} %bitcast.1), calls=%async_computation | async-start | bytes 1048576 | tf_op jit(solution)/shard_map/all_to_all | solution.py:431
  13.2 1.4 %collective-permute-start.1 = (bf16[128,1024]{1,0:T(8,128)(2,1)S(1)}, bf16[128,1024]{1,0:T(8,128)(2,1)S(1)}, u32[]{:S(2)}, u32[]{:S(2)}) collective-permute-start(bf16[128,1024]{1,0:T(8,128)(2,1)S(1)} %get-tuple-element.20.q_ref.refs_0_), channel_id=1, source_target_pairs={{0,8},{1,9},{2,10},{3,11},{4,12},{5,13},{6,14},{7,15},{8,0},{9,1},... | collective-permute-start | bytes 786440 | tf_op jit(solution)/shard_map/ppermute | solution.py:414
  14.5 1.2 %collective-permute-start.3 = (bf16[128,1024]{1,0:T(8,128)(2,1)S(1)}, bf16[128,1024]{1,0:T(8,128)(2,1)S(1)}, u32[]{:S(2)}, u32[]{:S(2)}) collective-permute-start(bf16[128,1024]{1,0:T(8,128)(2,1)S(1)} %get-tuple-element.20.q_ref.refs_0_), channel_id=1, source_target_pairs={{0,2},{1,3},{2,0},{3,1},{4,6},{5,7},{6,4},{7,5},{8,10},{9,11},{10,... | collective-permute-start | bytes 786440 | tf_op jit(solution)/shard_map/ppermute | solution.py:414
  16.7 1.8 %collective-permute-start.5 = (bf16[128,1024]{1,0:T(8,128)(2,1)S(1)}, bf16[128,1024]{1,0:T(8,128)(2,1)S(1)}, u32[]{:S(2)}, u32[]{:S(2)}) collective-permute-start(bf16[128,1024]{1,0:T(8,128)(2,1)S(1)} %get-tuple-element.20.q_ref.refs_0_), channel_id=1, source_target_pairs={{0,6},{1,7},{2,4},{3,5},{4,2},{5,3},{6,0},{7,1},{8,14},{9,15},{10,... | collective-permute-start | bytes 786440 | tf_op jit(solution)/shard_map/ppermute | solution.py:414
  18.5 8.2 %collective-permute-done.1.refs_2_ = bf16[128,1024]{1,0:T(8,128)(2,1)S(1)} collective-permute-done((bf16[128,1024]{1,0:T(8,128)(2,1)S(1)}, bf16[128,1024]{1,0:T(8,128)(2,1)S(1)}, u32[]{:S(2)}, u32[]{:S(2)}) %collective-permute-start.1) | collective-permute-done | bytes 262176 | tf_op jit(solution)/shard_map/ppermute | solution.py:414
  26.7 1.0 %collective-permute-start.2 = (bf16[128,1024]{1,0:T(8,128)(2,1)S(1)}, bf16[128,1024]{1,0:T(8,128)(2,1)S(1)}, u32[]{:S(2)}, u32[]{:S(2)}) collective-permute-start(bf16[128,1024]{1,0:T(8,128)(2,1)S(1)} %collective-permute-done.1.refs_2_), channel_id=1, source_target_pairs={{0,1},{1,0},{2,3},{3,2},{4,5},{5,4},{6,7},{7,6},{8,9},{9,8},{10,11... | collective-permute-start | bytes 786440 | tf_op jit(solution)/shard_map/ppermute | solution.py:414
  27.6 1.2 %collective-permute-start.7 = (bf16[128,1024]{1,0:T(8,128)(2,1)S(1)}, bf16[128,1024]{1,0:T(8,128)(2,1)S(1)}, u32[]{:S(2)}, u32[]{:S(2)}) collective-permute-start(bf16[128,1024]{1,0:T(8,128)(2,1)S(1)} %collective-permute-done.1.refs_2_), channel_id=1, source_target_pairs={{0,2},{1,3},{2,0},{3,1},{4,6},{5,7},{6,4},{7,5},{8,10},{9,11},{10,... | collective-permute-start | bytes 786440 | tf_op jit(solution)/shard_map/ppermute | solution.py:414
  29.1 1.8 %collective-permute-start.9 = (bf16[128,1024]{1,0:T(8,128)(2,1)S(1)}, bf16[128,1024]{1,0:T(8,128)(2,1)S(1)}, u32[]{:S(2)}, u32[]{:S(2)}) collective-permute-start(bf16[128,1024]{1,0:T(8,128)(2,1)S(1)} %collective-permute-done.1.refs_2_), channel_id=1, source_target_pairs={{0,6},{1,7},{2,4},{3,5},{4,2},{5,3},{6,0},{7,1},{8,14},{9,15},{10,... | collective-permute-start | bytes 786440 | tf_op jit(solution)/shard_map/ppermute | solution.py:414
  32.4 3.1 %collective-permute-done.7.refs_4_ = bf16[128,1024]{1,0:T(8,128)(2,1)S(1)} collective-permute-done((bf16[128,1024]{1,0:T(8,128)(2,1)S(1)}, bf16[128,1024]{1,0:T(8,128)(2,1)S(1)}, u32[]{:S(2)}, u32[]{:S(2)}) %collective-permute-start.7) | collective-permute-done | bytes 262176 | tf_op jit(solution)/shard_map/ppermute | solution.py:414
  35.5 2.4 %collective-permute-start.12 = (bf16[128,1024]{1,0:T(8,128)(2,1)S(1)}, bf16[128,1024]{1,0:T(8,128)(2,1)S(1)}, u32[]{:S(2)}, u32[]{:S(2)}) collective-permute-start(bf16[128,1024]{1,0:T(8,128)(2,1)S(1)} %collective-permute-done.7.refs_4_), channel_id=1, source_target_pairs={{0,6},{1,7},{2,4},{3,5},{4,2},{5,3},{6,0},{7,1},{8,14},{9,15},{10,... | collective-permute-start | bytes 786440 | tf_op jit(solution)/shard_map/ppermute | solution.py:414
  37.9 1.6 %collective-permute-start.8 = (bf16[128,1024]{1,0:T(8,128)(2,1)S(1)}, bf16[128,1024]{1,0:T(8,128)(2,1)}, u32[]{:S(2)}, u32[]{:S(2)}) collective-permute-start(bf16[128,1024]{1,0:T(8,128)(2,1)S(1)} %collective-permute-done.7.refs_4_), channel_id=1, source_target_pairs={{0,1},{1,0},{2,3},{3,2},{4,5},{5,4},{6,7},{7,6},{8,9},{9,8},{10,11... | collective-permute-start | bytes 786440 | tf_op jit(solution)/shard_map/ppermute | solution.py:414
  39.6 1.3 %residuals.1 = s32[16,40,128]{2,1,0:T(8,128)} custom-call(s32[16,128]{1,0:T(8,128)S(1)} %copy-done.1, bf16[256,1024]{1,0:T(8,128)(2,1)S(1)} %bitcast.13, bf16[128,1024]{1,0:T(8,128)(2,1)S(1)} %get-tuple-element.20.q_ref.refs_0_), custom_call_target="tpu_custom_call" | custom-call | flops 67108864 | bytes 1310720 | tf_op jit(solution)/shard_map/residuals/pallas_call | solution.py:170
  40.9 9.9 %all-to-all-start.1 = ((s32[16,40,128]{2,1,0:T(8,128)}), s32[16,40,128]{2,1,0:T(8,128)S(1)}, u32[]{:S(2)}, u32[]{:S(2)}) async-start(s32[16,40,128]{2,1,0:T(8,128)} %residuals.1), calls=%async_computation.1 | async-start | bytes 655360 | tf_op jit(solution)/shard_map/all_to_all | solution.py:453
  51.7 4.9 %nearest.4 = (f32[4,128]{1,0:T(4,128)S(1)}, f32[2048,128]{1,0:T(8,128)S(1)}) custom-call(bf16[128,1024]{1,0:T(8,128)(2,1)S(1)} %get-tuple-element.20.q_ref.refs_0_, bf16[128,1024]{1,0:T(8,128)(2,1)S(1)} %collective-permute-done.refs_1_, bf16[128,1024]{1,0:T(8,128)(2,1)S(1)} %collective-permute-done.1.refs_2_, bf16[128,1024]{1,0:T(8,128)(2,1)S(1)} %copy-done.4, ...), custom_call_target="tpu_custom_call" | custom-call | flops 2147483648 | bytes 5242880 | tf_op jit(solution)/shard_map/nearest/pallas_call | solution.py:244
  57.6 7.5 %nearest.5 = (f32[8,128]{1,0:T(8,128)S(1)}, bf16[8,256,1024]{2,1,0:T(8,128)(2,1)S(1)}) custom-call(bf16[128,1024]{1,0:T(8,128)(2,1)S(1)} %collective-permute-done.3.refs_0_, bf16[128,1024]{1,0:T(8,128)(2,1)S(1)} %collective-permute-done.4.refs_1_, bf16[128,1024]{1,0:T(8,128)(2,1)S(1)} %collective-permute-done.5.refs_2_, ...), custom_call_target="tpu_custom_call" | custom-call | flops 4294967296 | bytes 6291456 | tf_op jit(solution)/shard_map/nearest/pallas_call | solution.py:244
  65.1 1.3 %nearest.6.refs_2_ = f32[2,128]{1,0:T(2,128)S(1)} custom-call(bf16[128,1024]{1,0:T(8,128)(2,1)S(1)} %collective-permute-done.11.refs_0_, bf16[128,1024]{1,0:T(8,128)(2,1)S(1)} %collective-permute-done.12.refs_1_, bf16[8,256,1024]{2,1,0:T(8,128)(2,1)S(1)} %get-tuple-element.24.refs_2_, f32[2048,128]{1,0:T(8,128)S(1)} %get-tuple-element.22.refs_9_.refs_3_), custom_call_target="tpu_custom_call" | custom-call | flops 1073741824 | bytes 4718592 | tf_op jit(solution)/shard_map/nearest/pallas_call | solution.py:244
  66.5 1.3 %nearest.7.refs_3_ = f32[2,128]{1,0:T(2,128)S(1)} custom-call(bf16[128,1024]{1,0:T(8,128)(2,1)S(1)} %collective-permute-done.13.refs_0_, bf16[128,1024]{1,0:T(8,128)(2,1)S(1)} %collective-permute-done.14.refs_1_, bf16[8,256,1024]{2,1,0:T(8,128)(2,1)S(1)} %get-tuple-element.24.refs_2_, f32[2048,128]{1,0:T(8,128)S(1)} %get-tuple-element.22.refs_9_.refs_3_), custom_call_target="tpu_custom_call" | custom-call | flops 1073741824 | bytes 4718592 | tf_op jit(solution)/shard_map/nearest/pallas_call | solution.py:244
  70.5 2.9 %collective-permute-done.16.b_ref = f32[144,128]{1,0:T(8,128)S(1)} collective-permute-done((f32[144,128]{1,0:T(8,128)S(1)}, f32[144,128]{1,0:T(8,128)S(1)}, u32[]{:S(2)}, u32[]{:S(2)}) %collective-permute-start.16) | collective-permute-done | bytes 73760 | tf_op jit(solution)/shard_map/ppermute | solution.py:414
  73.5 2.4 %collective-permute-start.18 = (f32[144,128]{1,0:T(8,128)S(1)}, f32[144,128]{1,0:T(8,128)S(1)}, u32[]{:S(2)}, u32[]{:S(2)}) collective-permute-start(f32[144,128]{1,0:T(8,128)S(1)} %join.3.a_ref), channel_id=1, source_target_pairs={{0,4},{1,5},{2,6},{3,7},{4,0},{5,1},{6,2},{7,3},{8,12},{9,13},{10,... | collective-permute-start | bytes 221192 | tf_op jit(solution)/shard_map/ppermute | solution.py:414
  75.9 1.5 %collective-permute-start.19 = (f32[144,128]{1,0:T(8,128)S(1)}, f32[144,128]{1,0:T(8,128)S(1)}, u32[]{:S(2)}, u32[]{:S(2)}) collective-permute-start(f32[144,128]{1,0:T(8,128)S(1)} %join.3.a_ref), channel_id=1, source_target_pairs={{0,6},{1,7},{2,4},{3,5},{4,2},{5,3},{6,0},{7,1},{8,14},{9,15},{10,... | collective-permute-start | bytes 221192 | tf_op jit(solution)/shard_map/ppermute | solution.py:414
  77.3 1.1 %collective-permute-done.18.c_ref = f32[144,128]{1,0:T(8,128)S(1)} collective-permute-done((f32[144,128]{1,0:T(8,128)S(1)}, f32[144,128]{1,0:T(8,128)S(1)}, u32[]{:S(2)}, u32[]{:S(2)}) %collective-permute-start.18) | collective-permute-done | bytes 73760 | tf_op jit(solution)/shard_map/ppermute | solution.py:414
  78.4 2.7 %collective-permute-done.19.d_ref = f32[144,128]{1,0:T(8,128)S(1)} collective-permute-done((f32[144,128]{1,0:T(8,128)S(1)}, f32[144,128]{1,0:T(8,128)S(1)}, u32[]{:S(2)}, u32[]{:S(2)}) %collective-permute-start.19) | collective-permute-done | bytes 73760 | tf_op jit(solution)/shard_map/ppermute | solution.py:414
  81.6 2.1 %collective-permute-start.20 = (f32[128,128]{1,0:T(8,128)S(1)}, f32[128,128]{1,0:T(8,128)S(1)}, u32[]{:S(2)}, u32[]{:S(2)}) collective-permute-start(f32[128,128]{1,0:T(8,128)S(1)} %get-tuple-element.30.mine_ref), channel_id=1, source_target_pairs={{0,1},{1,0},{2,3},{3,2},{4,5},{5,4},{6,7},{7,6},{8,9},{9,8},{10,11... | collective-permute-start | bytes 196616 | tf_op jit(solution)/shard_map/ppermute | solution.py:414
  (45 shorter events, 9.8 us)
Async XLA Ops:
  0.6 39.0 %copy-start.1 = (s32[16,128]{1,0:T(8,128)S(1)}, s32[16,128]{1,0:T(8,128)}, u32[]{:S(2)}) copy-start(s32[16,128]{1,0:T(8,128)} %ids_ref.1) | copy-start | bytes 24580
  5.9 33.7 %all-to-all-start = ((bf16[16,16,1024]{2,1,0:T(8,128)(2,1)}), bf16[16,16,1024]{2,1,0:T(8,128)(2,1)S(1)}, u32[]{:S(2)}, u32[]{:S(2)}) async-start(bf16[16,16,1024]{2,1,0:T(8,128)(2,1)} %bitcast.1), calls=%async_computation | async-start | bytes 1048576 | tf_op jit(solution)/shard_map/all_to_all | solution.py:431
  13.2 13.5 %collective-permute-start.1 = (bf16[128,1024]{1,0:T(8,128)(2,1)S(1)}, bf16[128,1024]{1,0:T(8,128)(2,1)S(1)}, u32[]{:S(2)}, u32[]{:S(2)}) collective-permute-start(bf16[128,1024]{1,0:T(8,128)(2,1)S(1)} %get-tuple-element.20.q_ref.refs_0_), channel_id=1, source_target_pairs={{0,8},{1,9},{2,10},{3,11},{4,12},{5,13},{6,14},{7,15},{8,0},{9,1},... | collective-permute-start | bytes 786440 | tf_op jit(solution)/shard_map/ppermute | solution.py:414
  14.5 14.3 %collective-permute-start.3 = (bf16[128,1024]{1,0:T(8,128)(2,1)S(1)}, bf16[128,1024]{1,0:T(8,128)(2,1)S(1)}, u32[]{:S(2)}, u32[]{:S(2)}) collective-permute-start(bf16[128,1024]{1,0:T(8,128)(2,1)S(1)} %get-tuple-element.20.q_ref.refs_0_), channel_id=1, source_target_pairs={{0,2},{1,3},{2,0},{3,1},{4,6},{5,7},{6,4},{7,5},{8,10},{9,11},{10,... | collective-permute-start | bytes 786440 | tf_op jit(solution)/shard_map/ppermute | solution.py:414
  15.7 13.4 %collective-permute-start = (bf16[128,1024]{1,0:T(8,128)(2,1)S(1)}, bf16[128,1024]{1,0:T(8,128)(2,1)S(1)}, u32[]{:S(2)}, u32[]{:S(2)}) collective-permute-start(bf16[128,1024]{1,0:T(8,128)(2,1)S(1)} %get-tuple-element.20.q_ref.refs_0_), channel_id=1, source_target_pairs={{0,1},{1,0},{2,3},{3,2},{4,5},{5,4},{6,7},{7,6},{8,9},{9,8},{10,11... | collective-permute-start | bytes 786440 | tf_op jit(solution)/shard_map/ppermute | solution.py:414
  16.7 14.2 %collective-permute-start.5 = (bf16[128,1024]{1,0:T(8,128)(2,1)S(1)}, bf16[128,1024]{1,0:T(8,128)(2,1)S(1)}, u32[]{:S(2)}, u32[]{:S(2)}) collective-permute-start(bf16[128,1024]{1,0:T(8,128)(2,1)S(1)} %get-tuple-element.20.q_ref.refs_0_), channel_id=1, source_target_pairs={{0,6},{1,7},{2,4},{3,5},{4,2},{5,3},{6,0},{7,1},{8,14},{9,15},{10,... | collective-permute-start | bytes 786440 | tf_op jit(solution)/shard_map/ppermute | solution.py:414
  26.7 4.7 %collective-permute-start.2 = (bf16[128,1024]{1,0:T(8,128)(2,1)S(1)}, bf16[128,1024]{1,0:T(8,128)(2,1)S(1)}, u32[]{:S(2)}, u32[]{:S(2)}) collective-permute-start(bf16[128,1024]{1,0:T(8,128)(2,1)S(1)} %collective-permute-done.1.refs_2_), channel_id=1, source_target_pairs={{0,1},{1,0},{2,3},{3,2},{4,5},{5,4},{6,7},{7,6},{8,9},{9,8},{10,11... | collective-permute-start | bytes 786440 | tf_op jit(solution)/shard_map/ppermute | solution.py:414
  27.6 7.9 %collective-permute-start.7 = (bf16[128,1024]{1,0:T(8,128)(2,1)S(1)}, bf16[128,1024]{1,0:T(8,128)(2,1)S(1)}, u32[]{:S(2)}, u32[]{:S(2)}) collective-permute-start(bf16[128,1024]{1,0:T(8,128)(2,1)S(1)} %collective-permute-done.1.refs_2_), channel_id=1, source_target_pairs={{0,2},{1,3},{2,0},{3,1},{4,6},{5,7},{6,4},{7,5},{8,10},{9,11},{10,... | collective-permute-start | bytes 786440 | tf_op jit(solution)/shard_map/ppermute | solution.py:414
  28.8 9.1 %collective-permute-start.4 = (bf16[128,1024]{1,0:T(8,128)(2,1)S(1)}, bf16[128,1024]{1,0:T(8,128)(2,1)S(1)}, u32[]{:S(2)}, u32[]{:S(2)}) collective-permute-start(bf16[128,1024]{1,0:T(8,128)(2,1)S(1)} %collective-permute-done.3.refs_0_), channel_id=1, source_target_pairs={{0,1},{1,0},{2,3},{3,2},{4,5},{5,4},{6,7},{7,6},{8,9},{9,8},{10,11... | collective-permute-start | bytes 786440 | tf_op jit(solution)/shard_map/ppermute | solution.py:414
  29.1 10.4 %collective-permute-start.9 = (bf16[128,1024]{1,0:T(8,128)(2,1)S(1)}, bf16[128,1024]{1,0:T(8,128)(2,1)S(1)}, u32[]{:S(2)}, u32[]{:S(2)}) collective-permute-start(bf16[128,1024]{1,0:T(8,128)(2,1)S(1)} %collective-permute-done.1.refs_2_), channel_id=1, source_target_pairs={{0,6},{1,7},{2,4},{3,5},{4,2},{5,3},{6,0},{7,1},{8,14},{9,15},{10,... | collective-permute-start | bytes 786440 | tf_op jit(solution)/shard_map/ppermute | solution.py:414
  30.9 26.7 %collective-permute-start.6 = (bf16[128,1024]{1,0:T(8,128)(2,1)S(1)}, bf16[128,1024]{1,0:T(8,128)(2,1)S(1)}, u32[]{:S(2)}, u32[]{:S(2)}) collective-permute-start(bf16[128,1024]{1,0:T(8,128)(2,1)S(1)} %collective-permute-done.5.refs_2_), channel_id=1, source_target_pairs={{0,1},{1,0},{2,3},{3,2},{4,5},{5,4},{6,7},{7,6},{8,9},{9,8},{10,11... | collective-permute-start | bytes 786440 | tf_op jit(solution)/shard_map/ppermute | solution.py:414
  32.1 24.6 %collective-permute-start.11 = (bf16[128,1024]{1,0:T(8,128)(2,1)S(1)}, bf16[128,1024]{1,0:T(8,128)(2,1)S(1)}, u32[]{:S(2)}, u32[]{:S(2)}) collective-permute-start(bf16[128,1024]{1,0:T(8,128)(2,1)S(1)} %collective-permute-done.5.refs_2_), channel_id=1, source_target_pairs={{0,2},{1,3},{2,0},{3,1},{4,6},{5,7},{6,4},{7,5},{8,10},{9,11},{10,... | collective-permute-start | bytes 786440 | tf_op jit(solution)/shard_map/ppermute | solution.py:414
  35.5 22.0 %collective-permute-start.12 = (bf16[128,1024]{1,0:T(8,128)(2,1)S(1)}, bf16[128,1024]{1,0:T(8,128)(2,1)S(1)}, u32[]{:S(2)}, u32[]{:S(2)}) collective-permute-start(bf16[128,1024]{1,0:T(8,128)(2,1)S(1)} %collective-permute-done.7.refs_4_), channel_id=1, source_target_pairs={{0,6},{1,7},{2,4},{3,5},{4,2},{5,3},{6,0},{7,1},{8,14},{9,15},{10,... | collective-permute-start | bytes 786440 | tf_op jit(solution)/shard_map/ppermute | solution.py:414
  37.9 19.7 %collective-permute-start.8 = (bf16[128,1024]{1,0:T(8,128)(2,1)S(1)}, bf16[128,1024]{1,0:T(8,128)(2,1)}, u32[]{:S(2)}, u32[]{:S(2)}) collective-permute-start(bf16[128,1024]{1,0:T(8,128)(2,1)S(1)} %collective-permute-done.7.refs_4_), channel_id=1, source_target_pairs={{0,1},{1,0},{2,3},{3,2},{4,5},{5,4},{6,7},{7,6},{8,9},{9,8},{10,11... | collective-permute-start | bytes 786440 | tf_op jit(solution)/shard_map/ppermute | solution.py:414
  39.5 18.1 %collective-permute-start.10 = (bf16[128,1024]{1,0:T(8,128)(2,1)S(1)}, bf16[128,1024]{1,0:T(8,128)(2,1)}, u32[]{:S(2)}, u32[]{:S(2)}) collective-permute-start(bf16[128,1024]{1,0:T(8,128)(2,1)S(1)} %collective-permute-done.9.refs_6_), channel_id=1, source_target_pairs={{0,1},{1,0},{2,3},{3,2},{4,5},{5,4},{6,7},{7,6},{8,9},{9,8},{10,11... | collective-permute-start | bytes 786440 | tf_op jit(solution)/shard_map/ppermute | solution.py:414
  40.9 26.9 %all-to-all-start.1 = ((s32[16,40,128]{2,1,0:T(8,128)}), s32[16,40,128]{2,1,0:T(8,128)S(1)}, u32[]{:S(2)}, u32[]{:S(2)}) async-start(s32[16,40,128]{2,1,0:T(8,128)} %residuals.1), calls=%async_computation.1 | async-start | bytes 655360 | tf_op jit(solution)/shard_map/all_to_all | solution.py:453
  56.7 9.8 %collective-permute-start.13 = (bf16[128,1024]{1,0:T(8,128)(2,1)S(1)}, bf16[128,1024]{1,0:T(8,128)(2,1)S(1)}, u32[]{:S(2)}, u32[]{:S(2)}) collective-permute-start(bf16[128,1024]{1,0:T(8,128)(2,1)S(1)} %collective-permute-done.11.refs_0_), channel_id=1, source_target_pairs={{0,1},{1,0},{2,3},{3,2},{4,5},{5,4},{6,7},{7,6},{8,9},{9,8},{10,11... | collective-permute-start | bytes 786440 | tf_op jit(solution)/shard_map/ppermute | solution.py:414
  57.5 9.0 %collective-permute-start.14 = (bf16[128,1024]{1,0:T(8,128)(2,1)S(1)}, bf16[128,1024]{1,0:T(8,128)(2,1)S(1)}, u32[]{:S(2)}, u32[]{:S(2)}) collective-permute-start(bf16[128,1024]{1,0:T(8,128)(2,1)S(1)} %collective-permute-done.12.refs_1_), channel_id=1, source_target_pairs={{0,1},{1,0},{2,3},{3,2},{4,5},{5,4},{6,7},{7,6},{8,9},{9,8},{10,11... | collective-permute-start | bytes 786440 | tf_op jit(solution)/shard_map/ppermute | solution.py:414
  68.7 1.4 %collective-permute-start.15 = (f32[144,128]{1,0:T(8,128)S(1)}, f32[144,128]{1,0:T(8,128)S(1)}, u32[]{:S(2)}, u32[]{:S(2)}) collective-permute-start(f32[144,128]{1,0:T(8,128)S(1)} %get-tuple-element.26), channel_id=1, source_target_pairs={{0,1},{1,0},{2,3},{3,2},{4,5},{5,4},{6,7},{7,6},{8,9},{9,8},{10,11... | collective-permute-start | bytes 221192 | tf_op jit(solution)/shard_map/ppermute | solution.py:414
  70.1 3.3 %collective-permute-start.16 = (f32[144,128]{1,0:T(8,128)S(1)}, f32[144,128]{1,0:T(8,128)S(1)}, u32[]{:S(2)}, u32[]{:S(2)}) collective-permute-start(f32[144,128]{1,0:T(8,128)S(1)} %join.2.a_ref), channel_id=1, source_target_pairs={{0,8},{1,9},{2,10},{3,11},{4,12},{5,13},{6,14},{7,15},{8,0},{9,1},... | collective-permute-start | bytes 221192 | tf_op jit(solution)/shard_map/ppermute | solution.py:414
  73.4 3.9 %collective-permute-start.17 = (f32[144,128]{1,0:T(8,128)S(1)}, f32[144,128]{1,0:T(8,128)S(1)}, u32[]{:S(2)}, u32[]{:S(2)}) collective-permute-start(f32[144,128]{1,0:T(8,128)S(1)} %join.3.a_ref), channel_id=1, source_target_pairs={{0,2},{1,3},{2,0},{3,1},{4,6},{5,7},{6,4},{7,5},{8,10},{9,11},{10,... | collective-permute-start | bytes 221192 | tf_op jit(solution)/shard_map/ppermute | solution.py:414
  73.5 4.9 %collective-permute-start.18 = (f32[144,128]{1,0:T(8,128)S(1)}, f32[144,128]{1,0:T(8,128)S(1)}, u32[]{:S(2)}, u32[]{:S(2)}) collective-permute-start(f32[144,128]{1,0:T(8,128)S(1)} %join.3.a_ref), channel_id=1, source_target_pairs={{0,4},{1,5},{2,6},{3,7},{4,0},{5,1},{6,2},{7,3},{8,12},{9,13},{10,... | collective-permute-start | bytes 221192 | tf_op jit(solution)/shard_map/ppermute | solution.py:414
  75.9 5.2 %collective-permute-start.19 = (f32[144,128]{1,0:T(8,128)S(1)}, f32[144,128]{1,0:T(8,128)S(1)}, u32[]{:S(2)}, u32[]{:S(2)}) collective-permute-start(f32[144,128]{1,0:T(8,128)S(1)} %join.3.a_ref), channel_id=1, source_target_pairs={{0,6},{1,7},{2,4},{3,5},{4,2},{5,3},{6,0},{7,1},{8,14},{9,15},{10,... | collective-permute-start | bytes 221192 | tf_op jit(solution)/shard_map/ppermute | solution.py:414
  81.6 3.0 %collective-permute-start.20 = (f32[128,128]{1,0:T(8,128)S(1)}, f32[128,128]{1,0:T(8,128)S(1)}, u32[]{:S(2)}, u32[]{:S(2)}) collective-permute-start(f32[128,128]{1,0:T(8,128)S(1)} %get-tuple-element.30.mine_ref), channel_id=1, source_target_pairs={{0,1},{1,0},{2,3},{3,2},{4,5},{5,4},{6,7},{7,6},{8,9},{9,8},{10,11... | collective-permute-start | bytes 196616 | tf_op jit(solution)/shard_map/ppermute | solution.py:414
  (5 other events, 19.0 us)

commit v8 on v5

--- a/solution.py
+++ b/solution.py
@@ -30,9 +30,9 @@
 
 def prepare_kernel(
     slots, step, values_hbm, scales_hbm, ids_hbm, cents_hbm, q_ref, squares_ref, out_ref,
-    values, scales_t, ids_ref, cents_ref, onehot_ref, sems,
+    values, scales_t, ids_ref, cents_ref, onehot_ref, total_ref, sems,
 ):
-    count, width = cents_hbm.shape
+    count, _ = cents_hbm.shape
     groups, rows = ids_ref.shape
     small = (
         pltpu.make_async_copy(ids_hbm, ids_ref, sems.at[0]),
@@ -40,8 +40,8 @@
         pltpu.make_async_copy(values_hbm, values, sems.at[2]),
     )
     large = [
-        pltpu.make_async_copy(cents_hbm.at[:, pl.ds(step * j, step)], cents_ref.at[j], sems.at[3 + j])
-        for j in range(width // step)
+        pltpu.make_async_copy(cents_hbm.at[pl.ds(step * j, step), :], cents_ref.at[j], sems.at[3 + j])
+        for j in range(count // step)
     ]
     for copy in small:
         copy.start()
@@ -86,10 +86,15 @@
         onehot_ref[:, 256 * j : 256 * j + 256] = (at == chosen).astype(f32).astype(bf16)
     for j, copy in enumerate(large):
         copy.wait()
-        lanes = slice(step * j, step * j + step)
-        out_ref[:, lanes] = jnp.dot(
-            onehot_ref[...], cents_ref[j], preferred_element_type=f32
-        ).astype(bf16)
+        part = jnp.dot(
+            onehot_ref[:, step * j : step * j + step], cents_ref[j], preferred_element_type=f32
+        )
+        if j > 0:
+            part = total_ref[...] + part
+        if j + 1 < len(large):
+            total_ref[...] = part
+        else:
+            out_ref[...] = part.astype(bf16)
 
 
 def prepare(values, scales, ids, cents, slots):
@@ -97,7 +102,7 @@
     groups = ids.shape[0]
     count = cents.shape[0]
     scales = scales.T
-    step = 256
+    step = 512
     return pl.pallas_call(
         functools.partial(prepare_kernel, slots, step),
         out_shape=(
@@ -111,9 +116,10 @@
             pltpu.VMEM(values.shape, bf16),
             pltpu.VMEM(scales.shape, bf16),
             pltpu.VMEM(ids.shape, jnp.int32),
-            pltpu.VMEM((width // step, count, step), bf16),
+            pltpu.VMEM((count // step, step, width), bf16),
             pltpu.VMEM((groups * slots, count), bf16),
-            pltpu.SemaphoreType.DMA((width // step + 3,)),
+            pltpu.VMEM((groups * slots, width), f32),
+            pltpu.SemaphoreType.DMA((count // step + 3,)),
         ],
         cost_estimate=pl.CostEstimate(
             flops=2 * groups * slots * count * width, bytes_accessed=count * width * 2, transcendentals=0
@@ -182,27 +188,39 @@
 
 def nearest_kernel(step, ahead, blocks, mode, *refs):
     x_refs, refs = refs[:blocks], refs[blocks:]
-    if mode == "again":
-        cents_ref, squares_ref, out_ref = refs
-        copies = []
+    if mode == "first":
+        cents_hbm, out_ref, squares_ref, head_ref, tail_ref, sems = refs
+    elif mode == "keep":
+        cents_hbm, squares_ref, head_ref, out_ref, tail_ref, sems = refs
     else:
-        cents_hbm, out_ref, cents_ref, squares_ref, sems = refs
-        half = step // 2
-        copies = [
-            pltpu.make_async_copy(cents_hbm.at[pl.ds(half * i, half), :], cents_ref.at[i], sems.at[i])
-            for i in range(cents_ref.shape[0])
-        ]
-    for copy in copies[:ahead]:
-        copy.start()
+        squares_ref, head_ref, tail_ref, out_ref = refs
+    half = step // 2
+    kept = head_ref.shape[0]
+    parts = kept + tail_ref.shape[0]
+
+    def place(i):
+        return head_ref.at[i] if i < kept else tail_ref.at[i - kept]
+
+    copies = {}
+    if mode != "again":
+        for i in range(0 if mode == "first" else kept, parts):
+            copies[i] = pltpu.make_async_copy(
+                cents_hbm.at[pl.ds(half * i, half), :], place(i), sems.at[i]
+            )
+    waiting = list(copies)
+    for i in waiting[:ahead]:
+        copies[i].start()
+    waiting = waiting[ahead:]
     best = [None] * (blocks // 2)
-    for i in range(0, cents_ref.shape[0], 2):
-        for k in (i, i + 1) if copies else ():
-            copies[k].wait()
-            if k + ahead < len(copies):
-                copies[k + ahead].start()
-        block = jnp.concatenate([cents_ref[i], cents_ref[i + 1]], axis=0)
+    for i in range(0, parts, 2):
+        for k in (i, i + 1):
+            if k in copies:
+                copies[k].wait()
+                if waiting:
+                    copies[waiting.pop(0)].start()
+        block = jnp.concatenate([place(i)[...], place(i + 1)[...]], axis=0)
         at = slice(step // 2 * i, step // 2 * i + step)
-        if mode == "again":
+        if mode != "first":
             squares = squares_ref[at, :]
         else:
             total = None
@@ -222,23 +240,24 @@
             out_ref[2 * j + k : 2 * j + k + 1, :] = low[:, 128 * k : 128 * k + 128]
 
 
-def nearest(xs, cents, mode, kept=()):
+def nearest(xs, cents, squares=None, head=None, tail=None):
     count, width = cents.shape
     rows = sum(x.shape[0] for x in xs)
     step = 512
-    out = [pltpu.VMEM((rows // 128, 128), f32)]
-    held = [pltpu.VMEM((2 * count // step, step // 2, width), bf16), pltpu.VMEM((count, 128), f32)]
-    sems = [pltpu.SemaphoreType.DMA((2 * count // step,))]
-    more = {
-        "once": ([HBM], out, held + sems),
-        "keep": ([HBM], out + held, sems),
-        "again": ([VM, VM], out, []),
-    }
-    ins, outs, scratch = more[mode]
-    result = pl.pallas_call(
+    parts = 2 * count // step
+    mode = "first" if squares is None else "keep" if tail is None else "again"
+    out = pltpu.VMEM((rows // 128, 128), f32)
+    first, rest = (pltpu.VMEM((n, step // 2, width), bf16) for n in (2, parts - 2))
+    sems = pltpu.SemaphoreType.DMA((parts,))
+    far, near, outs, scratch = {
+        "first": ([cents], [], [out, pltpu.VMEM((count, 128), f32), first], [rest, sems]),
+        "keep": ([cents], [squares, head], [out, rest], [sems]),
+        "again": ([], [squares, head, tail], [out], []),
+    }[mode]
+    return pl.pallas_call(
         functools.partial(nearest_kernel, step, 3, len(xs), mode),
         out_shape=tuple(outs),
-        in_specs=[VM] * len(xs) + ins,
+        in_specs=[VM] * len(xs) + [HBM] * len(far) + [VM] * len(near),
         out_specs=tuple([VM] * len(outs)),
         scratch_shapes=scratch,
         cost_estimate=pl.CostEstimate(
@@ -246,8 +265,7 @@
         ),
         compiler_params=LIMIT,
         name="nearest",
-    )(*[on_chip(x) for x in xs], *([on_chip(x) for x in kept] or [off_chip(cents)]))
-    return result[0], result[1:]
+    )(*[on_chip(x) for x in xs], *[off_chip(x) for x in far], *[on_chip(x) for x in near])
 
 
 def halves_of(x):
@@ -433,11 +451,12 @@
     for d in (2, 6, 8, 4, 10, 14, 12):
         blocks[d ^ core] = swap(blocks[d], core)
 
-    orders = ((0, 1, 8, 9), (2, 3, 6, 7, 10, 11, 14, 15), (4, 5, 12, 13))
-    lows, kept = [], ()
-    for order, mode in zip(orders, ("once", "keep", "again")):
-        low, kept = nearest([blocks[d] for d in order], centroids, mode, kept)
+    orders = ((0, 1, 8, 9), (2, 3, 6, 7, 10, 11, 14, 15), (4, 12), (5, 13))
+    lows, kept = [], []
+    for order in orders:
+        low, *more = nearest([blocks[d] for d in order], centroids, *kept)
         lows.append(low)
+        kept += more
     where = {d: (k, j) for k, order in enumerate(orders) for j, d in enumerate(order)}
 
     coded = residuals(coarse_ids, fetched, q, count, slots, sub_width)

time: 85.8 us -> 83.9 us (0.978)
  Pallas kernels: 23.7 us -> 21.9 us
    pallas_call x1, Pallas kernels: 5.19 us -> 3.99 us  [prepare(): pl.pallas_call(functools.partial(prepare_kernel, slots, step), out_shape=...]
    pallas_call x3 -> x4, Pallas kernels: 14.9 us -> 14.3 us  [nearest(): pl.pallas_call(functools.partial(nearest_kernel, step, 3, len(xs), mode),...]
where the time goes in v8:
time: 83.9 us; the launch traced here: 83.5 us
  starting transfers between devices  39.3 us (47%)
  Pallas kernels  21.9 us (26%)
  waiting for transfers between devices  19.8 us (24%)
  local copies, waits for them, and re-layouts  1.66 us (2%)
    ppermute x21, starting transfers between devices, swap(): return lax.ppermute(x, 'cent', [(i, i ^ offset) for i in range(16)])  22.1 us
    ppermute x21, waiting for transfers between devices, swap(): return lax.ppermute(x, 'cent', [(i, i ^ offset) for i in range(16)])  19.8 us
    pallas_call x4, Pallas kernels, nearest(): pl.pallas_call(functools.partial(nearest_kernel, step, 3, len(xs), mode),...  14.3 us
    all_to_all x1, starting transfers between devices, step(): coded = lax.all_to_all(coded, 'rows', 0, 0)  9.86 us
    all_to_all x1, starting transfers between devices, step(): fetched = lax.all_to_all(sent.reshape(peers, slots, width), 'cent', 0, 0)  7.34 us
    pallas_call x1, Pallas kernels, prepare(): pl.pallas_call(functools.partial(prepare_kernel, slots, step), out_shape=...  3.99 us
  transfers between devices with their start and end apart: 23, of which 7 were waited for; matrix products, arithmetic and copies ran while one was open for 0% of the time, Pallas kernels for 19%

profile of v8, /device:TPU:1, one launch (start us, length us, event | category | flops | bytes accessed | tf_op | source)
XLA Modules:
  0.0 83.5 jit_solution(17732570929840616351)
XLA Ops:
  0.6 4.0 %prepare.1 = (bf16[128,1024]{1,0:T(8,128)(2,1)S(1)}, f32[1,128]{1,0:T(1,128)S(1)}, bf16[256,1024]{1,0:T(8,128)(2,1)}) custom-call(bf16[128,1024]{1,0:T(8,128)(2,1)} %values_hbm.1, bf16[8,128]{1,0:T(8,128)(2,1)} %bitcast.15, s32[16,128]{1,0:T(8,128)} %ids_ref.1, bf16[2048,1024]{1,0:T(8,128)(2,1)} %refs_8_.1), custom_call_target="tpu_custom_call" | custom-call | flops 1073741824 | bytes 4194304 | tf_op jit(solution)/shard_map/prepare/pallas_call | solution.py:106
  4.6 7.3 %all-to-all-start = ((bf16[16,16,1024]{2,1,0:T(8,128)(2,1)}), bf16[16,16,1024]{2,1,0:T(8,128)(2,1)S(1)}, u32[]{:S(2)}, u32[]{:S(2)}) async-start(bf16[16,16,1024]{2,1,0:T(8,128)(2,1)} %bitcast.1), calls=%async_computation | async-start | bytes 1048576 | tf_op jit(solution)/shard_map/all_to_all | solution.py:444
  12.0 1.4 %collective-permute-start.1 = (bf16[128,1024]{1,0:T(8,128)(2,1)S(1)}, bf16[128,1024]{1,0:T(8,128)(2,1)S(1)}, u32[]{:S(2)}, u32[]{:S(2)}) collective-permute-start(bf16[128,1024]{1,0:T(8,128)(2,1)S(1)} %get-tuple-element.21.q_ref.refs_0_), channel_id=1, source_target_pairs={{0,8},{1,9},{2,10},{3,11},{4,12},{5,13},{6,14},{7,15},{8,0},{9,1},... | collective-permute-start | bytes 786440 | tf_op jit(solution)/shard_map/ppermute | solution.py:427
  13.3 1.2 %collective-permute-start.3 = (bf16[128,1024]{1,0:T(8,128)(2,1)S(1)}, bf16[128,1024]{1,0:T(8,128)(2,1)S(1)}, u32[]{:S(2)}, u32[]{:S(2)}) collective-permute-start(bf16[128,1024]{1,0:T(8,128)(2,1)S(1)} %get-tuple-element.21.q_ref.refs_0_), channel_id=1, source_target_pairs={{0,2},{1,3},{2,0},{3,1},{4,6},{5,7},{6,4},{7,5},{8,10},{9,11},{10,... | collective-permute-start | bytes 786440 | tf_op jit(solution)/shard_map/ppermute | solution.py:427
  15.5 1.8 %collective-permute-start.5 = (bf16[128,1024]{1,0:T(8,128)(2,1)S(1)}, bf16[128,1024]{1,0:T(8,128)(2,1)S(1)}, u32[]{:S(2)}, u32[]{:S(2)}) collective-permute-start(bf16[128,1024]{1,0:T(8,128)(2,1)S(1)} %get-tuple-element.21.q_ref.refs_0_), channel_id=1, source_target_pairs={{0,6},{1,7},{2,4},{3,5},{4,2},{5,3},{6,0},{7,1},{8,14},{9,15},{10,... | collective-permute-start | bytes 786440 | tf_op jit(solution)/shard_map/ppermute | solution.py:427
  17.3 8.2 %collective-permute-done.1.refs_2_ = bf16[128,1024]{1,0:T(8,128)(2,1)S(1)} collective-permute-done((bf16[128,1024]{1,0:T(8,128)(2,1)S(1)}, bf16[128,1024]{1,0:T(8,128)(2,1)S(1)}, u32[]{:S(2)}, u32[]{:S(2)}) %collective-permute-start.1) | collective-permute-done | bytes 262176 | tf_op jit(solution)/shard_map/ppermute | solution.py:427
  25.4 1.0 %collective-permute-start.2 = (bf16[128,1024]{1,0:T(8,128)(2,1)S(1)}, bf16[128,1024]{1,0:T(8,128)(2,1)S(1)}, u32[]{:S(2)}, u32[]{:S(2)}) collective-permute-start(bf16[128,1024]{1,0:T(8,128)(2,1)S(1)} %collective-permute-done.1.refs_2_), channel_id=1, source_target_pairs={{0,1},{1,0},{2,3},{3,2},{4,5},{5,4},{6,7},{7,6},{8,9},{9,8},{10,11... | collective-permute-start | bytes 786440 | tf_op jit(solution)/shard_map/ppermute | solution.py:427
  26.4 1.2 %collective-permute-start.7 = (bf16[128,1024]{1,0:T(8,128)(2,1)S(1)}, bf16[128,1024]{1,0:T(8,128)(2,1)S(1)}, u32[]{:S(2)}, u32[]{:S(2)}) collective-permute-start(bf16[128,1024]{1,0:T(8,128)(2,1)S(1)} %collective-permute-done.1.refs_2_), channel_id=1, source_target_pairs={{0,2},{1,3},{2,0},{3,1},{4,6},{5,7},{6,4},{7,5},{8,10},{9,11},{10,... | collective-permute-start | bytes 786440 | tf_op jit(solution)/shard_map/ppermute | solution.py:427
  27.9 1.8 %collective-permute-start.9 = (bf16[128,1024]{1,0:T(8,128)(2,1)S(1)}, bf16[128,1024]{1,0:T(8,128)(2,1)S(1)}, u32[]{:S(2)}, u32[]{:S(2)}) collective-permute-start(bf16[128,1024]{1,0:T(8,128)(2,1)S(1)} %collective-permute-done.1.refs_2_), channel_id=1, source_target_pairs={{0,6},{1,7},{2,4},{3,5},{4,2},{5,3},{6,0},{7,1},{8,14},{9,15},{10,... | collective-permute-start | bytes 786440 | tf_op jit(solution)/shard_map/ppermute | solution.py:427
  31.2 3.1 %collective-permute-done.7.refs_4_ = bf16[128,1024]{1,0:T(8,128)(2,1)S(1)} collective-permute-done((bf16[128,1024]{1,0:T(8,128)(2,1)S(1)}, bf16[128,1024]{1,0:T(8,128)(2,1)S(1)}, u32[]{:S(2)}, u32[]{:S(2)}) %collective-permute-start.7) | collective-permute-done | bytes 262176 | tf_op jit(solution)/shard_map/ppermute | solution.py:427
  34.3 2.4 %collective-permute-start.12 = (bf16[128,1024]{1,0:T(8,128)(2,1)S(1)}, bf16[128,1024]{1,0:T(8,128)(2,1)S(1)}, u32[]{:S(2)}, u32[]{:S(2)}) collective-permute-start(bf16[128,1024]{1,0:T(8,128)(2,1)S(1)} %collective-permute-done.7.refs_4_), channel_id=1, source_target_pairs={{0,6},{1,7},{2,4},{3,5},{4,2},{5,3},{6,0},{7,1},{8,14},{9,15},{10,... | collective-permute-start | bytes 786440 | tf_op jit(solution)/shard_map/ppermute | solution.py:427
  36.7 1.6 %collective-permute-start.8 = (bf16[128,1024]{1,0:T(8,128)(2,1)S(1)}, bf16[128,1024]{1,0:T(8,128)(2,1)}, u32[]{:S(2)}, u32[]{:S(2)}) collective-permute-start(bf16[128,1024]{1,0:T(8,128)(2,1)S(1)} %collective-permute-done.7.refs_4_), channel_id=1, source_target_pairs={{0,1},{1,0},{2,3},{3,2},{4,5},{5,4},{6,7},{7,6},{8,9},{9,8},{10,11... | collective-permute-start | bytes 786440 | tf_op jit(solution)/shard_map/ppermute | solution.py:427
  38.4 1.3 %residuals.1 = s32[16,40,128]{2,1,0:T(8,128)} custom-call(s32[16,128]{1,0:T(8,128)S(1)} %copy-done.1, bf16[256,1024]{1,0:T(8,128)(2,1)S(1)} %bitcast.13, bf16[128,1024]{1,0:T(8,128)(2,1)S(1)} %get-tuple-element.21.q_ref.refs_0_), custom_call_target="tpu_custom_call" | custom-call | flops 67108864 | bytes 1310720 | tf_op jit(solution)/shard_map/residuals/pallas_call | solution.py:176
  39.7 9.9 %all-to-all-start.1 = ((s32[16,40,128]{2,1,0:T(8,128)}), s32[16,40,128]{2,1,0:T(8,128)S(1)}, u32[]{:S(2)}, u32[]{:S(2)}) async-start(s32[16,40,128]{2,1,0:T(8,128)} %residuals.1), calls=%async_computation.1 | async-start | bytes 655360 | tf_op jit(solution)/shard_map/all_to_all | solution.py:463
  50.5 4.9 %nearest.4 = (f32[4,128]{1,0:T(4,128)S(1)}, f32[2048,128]{1,0:T(8,128)S(1)}, bf16[2,256,1024]{2,1,0:T(8,128)(2,1)S(1)}) custom-call(bf16[128,1024]{1,0:T(8,128)(2,1)S(1)} %get-tuple-element.21.q_ref.refs_0_, bf16[128,1024]{1,0:T(8,128)(2,1)S(1)} %collective-permute-done.refs_1_, bf16[128,1024]{1,0:T(8,128)(2,1)S(1)} %collective-permute-done.1.refs_2_, ...), custom_call_target="tpu_custom_call" | custom-call | flops 2147483648 | bytes 5242880 | tf_op jit(solution)/shard_map/nearest/pallas_call | solution.py:257
  56.4 6.7 %nearest.5 = (f32[8,128]{1,0:T(8,128)S(1)}, bf16[6,256,1024]{2,1,0:T(8,128)(2,1)S(1)}) custom-call(bf16[128,1024]{1,0:T(8,128)(2,1)S(1)} %collective-permute-done.3.refs_0_, bf16[128,1024]{1,0:T(8,128)(2,1)S(1)} %collective-permute-done.4.refs_1_, bf16[128,1024]{1,0:T(8,128)(2,1)S(1)} %collective-permute-done.5.refs_2_, ...), custom_call_target="tpu_custom_call" | custom-call | flops 4294967296 | bytes 6291456 | tf_op jit(solution)/shard_map/nearest/pallas_call | solution.py:257
  63.1 1.3 %nearest.6.refs_2_ = f32[2,128]{1,0:T(2,128)S(1)} custom-call(bf16[128,1024]{1,0:T(8,128)(2,1)S(1)} %collective-permute-done.11.refs_0_, bf16[128,1024]{1,0:T(8,128)(2,1)S(1)} %collective-permute-done.12.refs_1_, f32[2048,128]{1,0:T(8,128)S(1)} %get-tuple-element.23.refs_9_.refs_2_, bf16[2,256,1024]{2,1,0:T(8,128)(2,1)S(1)} %get-tuple-element.24.refs_10_.refs_3_, ...), custom_call_target="tpu_custom_call" | custom-call | flops 1073741824 | bytes 4718592 | tf_op jit(solution)/shard_map/nearest/pallas_call | solution.py:257
  64.5 1.3 %nearest.7.refs_3_ = f32[2,128]{1,0:T(2,128)S(1)} custom-call(bf16[128,1024]{1,0:T(8,128)(2,1)S(1)} %collective-permute-done.13.refs_0_, bf16[128,1024]{1,0:T(8,128)(2,1)S(1)} %collective-permute-done.14.refs_1_, f32[2048,128]{1,0:T(8,128)S(1)} %get-tuple-element.23.refs_9_.refs_2_, bf16[2,256,1024]{2,1,0:T(8,128)(2,1)S(1)} %get-tuple-element.24.refs_10_.refs_3_, ...), custom_call_target="tpu_custom_call" | custom-call | flops 1073741824 | bytes 4718592 | tf_op jit(solution)/shard_map/nearest/pallas_call | solution.py:257
  68.4 2.9 %collective-permute-done.16.b_ref = f32[144,128]{1,0:T(8,128)S(1)} collective-permute-done((f32[144,128]{1,0:T(8,128)S(1)}, f32[144,128]{1,0:T(8,128)S(1)}, u32[]{:S(2)}, u32[]{:S(2)}) %collective-permute-start.16) | collective-permute-done | bytes 73760 | tf_op jit(solution)/shard_map/ppermute | solution.py:427
  71.5 2.4 %collective-permute-start.18 = (f32[144,128]{1,0:T(8,128)S(1)}, f32[144,128]{1,0:T(8,128)S(1)}, u32[]{:S(2)}, u32[]{:S(2)}) collective-permute-start(f32[144,128]{1,0:T(8,128)S(1)} %join.3.a_ref), channel_id=1, source_target_pairs={{0,4},{1,5},{2,6},{3,7},{4,0},{5,1},{6,2},{7,3},{8,12},{9,13},{10,... | collective-permute-start | bytes 221192 | tf_op jit(solution)/shard_map/ppermute | solution.py:427
  73.9 1.5 %collective-permute-start.19 = (f32[144,128]{1,0:T(8,128)S(1)}, f32[144,128]{1,0:T(8,128)S(1)}, u32[]{:S(2)}, u32[]{:S(2)}) collective-permute-start(f32[144,128]{1,0:T(8,128)S(1)} %join.3.a_ref), channel_id=1, source_target_pairs={{0,6},{1,7},{2,4},{3,5},{4,2},{5,3},{6,0},{7,1},{8,14},{9,15},{10,... | collective-permute-start | bytes 221192 | tf_op jit(solution)/shard_map/ppermute | solution.py:427
  75.3 1.1 %collective-permute-done.18.c_ref = f32[144,128]{1,0:T(8,128)S(1)} collective-permute-done((f32[144,128]{1,0:T(8,128)S(1)}, f32[144,128]{1,0:T(8,128)S(1)}, u32[]{:S(2)}, u32[]{:S(2)}) %collective-permute-start.18) | collective-permute-done | bytes 73760 | tf_op jit(solution)/shard_map/ppermute | solution.py:427
  76.4 2.7 %collective-permute-done.19.d_ref = f32[144,128]{1,0:T(8,128)S(1)} collective-permute-done((f32[144,128]{1,0:T(8,128)S(1)}, f32[144,128]{1,0:T(8,128)S(1)}, u32[]{:S(2)}, u32[]{:S(2)}) %collective-permute-start.19) | collective-permute-done | bytes 73760 | tf_op jit(solution)/shard_map/ppermute | solution.py:427
  79.6 2.1 %collective-permute-start.20 = (f32[128,128]{1,0:T(8,128)S(1)}, f32[128,128]{1,0:T(8,128)S(1)}, u32[]{:S(2)}, u32[]{:S(2)}) collective-permute-start(f32[128,128]{1,0:T(8,128)S(1)} %get-tuple-element.32.mine_ref), channel_id=1, source_target_pairs={{0,1},{1,0},{2,3},{3,2},{4,5},{5,4},{6,7},{7,6},{8,9},{9,8},{10,11... | collective-permute-start | bytes 196616 | tf_op jit(solution)/shard_map/ppermute | solution.py:427
  (45 shorter events, 9.8 us)
Async XLA Ops:
  0.6 37.7 %copy-start.1 = (s32[16,128]{1,0:T(8,128)S(1)}, s32[16,128]{1,0:T(8,128)}, u32[]{:S(2)}) copy-start(s32[16,128]{1,0:T(8,128)} %ids_ref.1) | copy-start | bytes 24580
  4.6 33.7 %all-to-all-start = ((bf16[16,16,1024]{2,1,0:T(8,128)(2,1)}), bf16[16,16,1024]{2,1,0:T(8,128)(2,1)S(1)}, u32[]{:S(2)}, u32[]{:S(2)}) async-start(bf16[16,16,1024]{2,1,0:T(8,128)(2,1)} %bitcast.1), calls=%async_computation | async-start | bytes 1048576 | tf_op jit(solution)/shard_map/all_to_all | solution.py:444
  12.0 13.5 %collective-permute-start.1 = (bf16[128,1024]{1,0:T(8,128)(2,1)S(1)}, bf16[128,1024]{1,0:T(8,128)(2,1)S(1)}, u32[]{:S(2)}, u32[]{:S(2)}) collective-permute-start(bf16[128,1024]{1,0:T(8,128)(2,1)S(1)} %get-tuple-element.21.q_ref.refs_0_), channel_id=1, source_target_pairs={{0,8},{1,9},{2,10},{3,11},{4,12},{5,13},{6,14},{7,15},{8,0},{9,1},... | collective-permute-start | bytes 786440 | tf_op jit(solution)/shard_map/ppermute | solution.py:427
  13.3 14.3 %collective-permute-start.3 = (bf16[128,1024]{1,0:T(8,128)(2,1)S(1)}, bf16[128,1024]{1,0:T(8,128)(2,1)S(1)}, u32[]{:S(2)}, u32[]{:S(2)}) collective-permute-start(bf16[128,1024]{1,0:T(8,128)(2,1)S(1)} %get-tuple-element.21.q_ref.refs_0_), channel_id=1, source_target_pairs={{0,2},{1,3},{2,0},{3,1},{4,6},{5,7},{6,4},{7,5},{8,10},{9,11},{10,... | collective-permute-start | bytes 786440 | tf_op jit(solution)/shard_map/ppermute | solution.py:427
  14.5 13.4 %collective-permute-start = (bf16[128,1024]{1,0:T(8,128)(2,1)S(1)}, bf16[128,1024]{1,0:T(8,128)(2,1)S(1)}, u32[]{:S(2)}, u32[]{:S(2)}) collective-permute-start(bf16[128,1024]{1,0:T(8,128)(2,1)S(1)} %get-tuple-element.21.q_ref.refs_0_), channel_id=1, source_target_pairs={{0,1},{1,0},{2,3},{3,2},{4,5},{5,4},{6,7},{7,6},{8,9},{9,8},{10,11... | collective-permute-start | bytes 786440 | tf_op jit(solution)/shard_map/ppermute | solution.py:427
  15.5 14.2 %collective-permute-start.5 = (bf16[128,1024]{1,0:T(8,128)(2,1)S(1)}, bf16[128,1024]{1,0:T(8,128)(2,1)S(1)}, u32[]{:S(2)}, u32[]{:S(2)}) collective-permute-start(bf16[128,1024]{1,0:T(8,128)(2,1)S(1)} %get-tuple-element.21.q_ref.refs_0_), channel_id=1, source_target_pairs={{0,6},{1,7},{2,4},{3,5},{4,2},{5,3},{6,0},{7,1},{8,14},{9,15},{10,... | collective-permute-start | bytes 786440 | tf_op jit(solution)/shard_map/ppermute | solution.py:427
  25.4 4.7 %collective-permute-start.2 = (bf16[128,1024]{1,0:T(8,128)(2,1)S(1)}, bf16[128,1024]{1,0:T(8,128)(2,1)S(1)}, u32[]{:S(2)}, u32[]{:S(2)}) collective-permute-start(bf16[128,1024]{1,0:T(8,128)(2,1)S(1)} %collective-permute-done.1.refs_2_), channel_id=1, source_target_pairs={{0,1},{1,0},{2,3},{3,2},{4,5},{5,4},{6,7},{7,6},{8,9},{9,8},{10,11... | collective-permute-start | bytes 786440 | tf_op jit(solution)/shard_map/ppermute | solution.py:427
  26.4 7.9 %collective-permute-start.7 = (bf16[128,1024]{1,0:T(8,128)(2,1)S(1)}, bf16[128,1024]{1,0:T(8,128)(2,1)S(1)}, u32[]{:S(2)}, u32[]{:S(2)}) collective-permute-start(bf16[128,1024]{1,0:T(8,128)(2,1)S(1)} %collective-permute-done.1.refs_2_), channel_id=1, source_target_pairs={{0,2},{1,3},{2,0},{3,1},{4,6},{5,7},{6,4},{7,5},{8,10},{9,11},{10,... | collective-permute-start | bytes 786440 | tf_op jit(solution)/shard_map/ppermute | solution.py:427
  27.6 9.1 %collective-permute-start.4 = (bf16[128,1024]{1,0:T(8,128)(2,1)S(1)}, bf16[128,1024]{1,0:T(8,128)(2,1)S(1)}, u32[]{:S(2)}, u32[]{:S(2)}) collective-permute-start(bf16[128,1024]{1,0:T(8,128)(2,1)S(1)} %collective-permute-done.3.refs_0_), channel_id=1, source_target_pairs={{0,1},{1,0},{2,3},{3,2},{4,5},{5,4},{6,7},{7,6},{8,9},{9,8},{10,11... | collective-permute-start | bytes 786440 | tf_op jit(solution)/shard_map/ppermute | solution.py:427
  27.9 10.4 %collective-permute-start.9 = (bf16[128,1024]{1,0:T(8,128)(2,1)S(1)}, bf16[128,1024]{1,0:T(8,128)(2,1)S(1)}, u32[]{:S(2)}, u32[]{:S(2)}) collective-permute-start(bf16[128,1024]{1,0:T(8,128)(2,1)S(1)} %collective-permute-done.1.refs_2_), channel_id=1, source_target_pairs={{0,6},{1,7},{2,4},{3,5},{4,2},{5,3},{6,0},{7,1},{8,14},{9,15},{10,... | collective-permute-start | bytes 786440 | tf_op jit(solution)/shard_map/ppermute | solution.py:427
  29.7 26.7 %collective-permute-start.6 = (bf16[128,1024]{1,0:T(8,128)(2,1)S(1)}, bf16[128,1024]{1,0:T(8,128)(2,1)S(1)}, u32[]{:S(2)}, u32[]{:S(2)}) collective-permute-start(bf16[128,1024]{1,0:T(8,128)(2,1)S(1)} %collective-permute-done.5.refs_2_), channel_id=1, source_target_pairs={{0,1},{1,0},{2,3},{3,2},{4,5},{5,4},{6,7},{7,6},{8,9},{9,8},{10,11... | collective-permute-start | bytes 786440 | tf_op jit(solution)/shard_map/ppermute | solution.py:427
  30.9 24.6 %collective-permute-start.11 = (bf16[128,1024]{1,0:T(8,128)(2,1)S(1)}, bf16[128,1024]{1,0:T(8,128)(2,1)S(1)}, u32[]{:S(2)}, u32[]{:S(2)}) collective-permute-start(bf16[128,1024]{1,0:T(8,128)(2,1)S(1)} %collective-permute-done.5.refs_2_), channel_id=1, source_target_pairs={{0,2},{1,3},{2,0},{3,1},{4,6},{5,7},{6,4},{7,5},{8,10},{9,11},{10,... | collective-permute-start | bytes 786440 | tf_op jit(solution)/shard_map/ppermute | solution.py:427
  34.3 22.0 %collective-permute-start.12 = (bf16[128,1024]{1,0:T(8,128)(2,1)S(1)}, bf16[128,1024]{1,0:T(8,128)(2,1)S(1)}, u32[]{:S(2)}, u32[]{:S(2)}) collective-permute-start(bf16[128,1024]{1,0:T(8,128)(2,1)S(1)} %collective-permute-done.7.refs_4_), channel_id=1, source_target_pairs={{0,6},{1,7},{2,4},{3,5},{4,2},{5,3},{6,0},{7,1},{8,14},{9,15},{10,... | collective-permute-start | bytes 786440 | tf_op jit(solution)/shard_map/ppermute | solution.py:427
  36.7 19.7 %collective-permute-start.8 = (bf16[128,1024]{1,0:T(8,128)(2,1)S(1)}, bf16[128,1024]{1,0:T(8,128)(2,1)}, u32[]{:S(2)}, u32[]{:S(2)}) collective-permute-start(bf16[128,1024]{1,0:T(8,128)(2,1)S(1)} %collective-permute-done.7.refs_4_), channel_id=1, source_target_pairs={{0,1},{1,0},{2,3},{3,2},{4,5},{5,4},{6,7},{7,6},{8,9},{9,8},{10,11... | collective-permute-start | bytes 786440 | tf_op jit(solution)/shard_map/ppermute | solution.py:427
  38.3 18.1 %collective-permute-start.10 = (bf16[128,1024]{1,0:T(8,128)(2,1)S(1)}, bf16[128,1024]{1,0:T(8,128)(2,1)}, u32[]{:S(2)}, u32[]{:S(2)}) collective-permute-start(bf16[128,1024]{1,0:T(8,128)(2,1)S(1)} %collective-permute-done.9.refs_6_), channel_id=1, source_target_pairs={{0,1},{1,0},{2,3},{3,2},{4,5},{5,4},{6,7},{7,6},{8,9},{9,8},{10,11... | collective-permute-start | bytes 786440 | tf_op jit(solution)/shard_map/ppermute | solution.py:427
  39.7 26.1 %all-to-all-start.1 = ((s32[16,40,128]{2,1,0:T(8,128)}), s32[16,40,128]{2,1,0:T(8,128)S(1)}, u32[]{:S(2)}, u32[]{:S(2)}) async-start(s32[16,40,128]{2,1,0:T(8,128)} %residuals.1), calls=%async_computation.1 | async-start | bytes 655360 | tf_op jit(solution)/shard_map/all_to_all | solution.py:463
  55.4 9.0 %collective-permute-start.13 = (bf16[128,1024]{1,0:T(8,128)(2,1)S(1)}, bf16[128,1024]{1,0:T(8,128)(2,1)S(1)}, u32[]{:S(2)}, u32[]{:S(2)}) collective-permute-start(bf16[128,1024]{1,0:T(8,128)(2,1)S(1)} %collective-permute-done.11.refs_0_), channel_id=1, source_target_pairs={{0,1},{1,0},{2,3},{3,2},{4,5},{5,4},{6,7},{7,6},{8,9},{9,8},{10,11... | collective-permute-start | bytes 786440 | tf_op jit(solution)/shard_map/ppermute | solution.py:427
  56.2 8.2 %collective-permute-start.14 = (bf16[128,1024]{1,0:T(8,128)(2,1)S(1)}, bf16[128,1024]{1,0:T(8,128)(2,1)S(1)}, u32[]{:S(2)}, u32[]{:S(2)}) collective-permute-start(bf16[128,1024]{1,0:T(8,128)(2,1)S(1)} %collective-permute-done.12.refs_1_), channel_id=1, source_target_pairs={{0,1},{1,0},{2,3},{3,2},{4,5},{5,4},{6,7},{7,6},{8,9},{9,8},{10,11... | collective-permute-start | bytes 786440 | tf_op jit(solution)/shard_map/ppermute | solution.py:427
  66.7 1.4 %collective-permute-start.15 = (f32[144,128]{1,0:T(8,128)S(1)}, f32[144,128]{1,0:T(8,128)S(1)}, u32[]{:S(2)}, u32[]{:S(2)}) collective-permute-start(f32[144,128]{1,0:T(8,128)S(1)} %get-tuple-element.28), channel_id=1, source_target_pairs={{0,1},{1,0},{2,3},{3,2},{4,5},{5,4},{6,7},{7,6},{8,9},{9,8},{10,11... | collective-permute-start | bytes 221192 | tf_op jit(solution)/shard_map/ppermute | solution.py:427
  68.1 3.3 %collective-permute-start.16 = (f32[144,128]{1,0:T(8,128)S(1)}, f32[144,128]{1,0:T(8,128)S(1)}, u32[]{:S(2)}, u32[]{:S(2)}) collective-permute-start(f32[144,128]{1,0:T(8,128)S(1)} %join.2.a_ref), channel_id=1, source_target_pairs={{0,8},{1,9},{2,10},{3,11},{4,12},{5,13},{6,14},{7,15},{8,0},{9,1},... | collective-permute-start | bytes 221192 | tf_op jit(solution)/shard_map/ppermute | solution.py:427
  71.4 3.9 %collective-permute-start.17 = (f32[144,128]{1,0:T(8,128)S(1)}, f32[144,128]{1,0:T(8,128)S(1)}, u32[]{:S(2)}, u32[]{:S(2)}) collective-permute-start(f32[144,128]{1,0:T(8,128)S(1)} %join.3.a_ref), channel_id=1, source_target_pairs={{0,2},{1,3},{2,0},{3,1},{4,6},{5,7},{6,4},{7,5},{8,10},{9,11},{10,... | collective-permute-start | bytes 221192 | tf_op jit(solution)/shard_map/ppermute | solution.py:427
  71.5 4.9 %collective-permute-start.18 = (f32[144,128]{1,0:T(8,128)S(1)}, f32[144,128]{1,0:T(8,128)S(1)}, u32[]{:S(2)}, u32[]{:S(2)}) collective-permute-start(f32[144,128]{1,0:T(8,128)S(1)} %join.3.a_ref), channel_id=1, source_target_pairs={{0,4},{1,5},{2,6},{3,7},{4,0},{5,1},{6,2},{7,3},{8,12},{9,13},{10,... | collective-permute-start | bytes 221192 | tf_op jit(solution)/shard_map/ppermute | solution.py:427
  73.9 5.2 %collective-permute-start.19 = (f32[144,128]{1,0:T(8,128)S(1)}, f32[144,128]{1,0:T(8,128)S(1)}, u32[]{:S(2)}, u32[]{:S(2)}) collective-permute-start(f32[144,128]{1,0:T(8,128)S(1)} %join.3.a_ref), channel_id=1, source_target_pairs={{0,6},{1,7},{2,4},{3,5},{4,2},{5,3},{6,0},{7,1},{8,14},{9,15},{10,... | collective-permute-start | bytes 221192 | tf_op jit(solution)/shard_map/ppermute | solution.py:427
  79.6 3.0 %collective-permute-start.20 = (f32[128,128]{1,0:T(8,128)S(1)}, f32[128,128]{1,0:T(8,128)S(1)}, u32[]{:S(2)}, u32[]{:S(2)}) collective-permute-start(f32[128,128]{1,0:T(8,128)S(1)} %get-tuple-element.32.mine_ref), channel_id=1, source_target_pairs={{0,1},{1,0},{2,3},{3,2},{4,5},{5,4},{6,7},{7,6},{8,9},{9,8},{10,11... | collective-permute-start | bytes 196616 | tf_op jit(solution)/shard_map/ppermute | solution.py:427
  (5 other events, 19.1 us)

commit v9 on v8

--- a/solution.py
+++ b/solution.py
@@ -29,10 +29,10 @@
 
 
 def prepare_kernel(
-    slots, step, values_hbm, scales_hbm, ids_hbm, cents_hbm, q_ref, squares_ref, out_ref,
+    slots, step, values_hbm, scales_hbm, ids_hbm, cents_hbm, q_ref, squares_ref, out_ref, cent_squares_ref,
     values, scales_t, ids_ref, cents_ref, onehot_ref, total_ref, sems,
 ):
-    count, _ = cents_hbm.shape
+    count, width = cents_hbm.shape
     groups, rows = ids_ref.shape
     small = (
         pltpu.make_async_copy(ids_hbm, ids_ref, sems.at[0]),
@@ -95,6 +95,14 @@
             total_ref[...] = part
         else:
             out_ref[...] = part.astype(bf16)
+        block = cents_ref[j]
+        total = None
+        for b in range(width // 128):
+            wide = block[:, 128 * b : 128 * b + 128].astype(f32)
+            total = wide * wide if total is None else total + wide * wide
+        cent_squares_ref[step * j : step * j + step, :] = jnp.broadcast_to(
+            jnp.sum(total, axis=1, keepdims=True), (step, 128)
+        )
 
 
 def prepare(values, scales, ids, cents, slots):
@@ -109,9 +117,10 @@
             pltpu.VMEM((rows, width), bf16),
             pltpu.VMEM((1, rows), f32),
             pltpu.VMEM((groups * slots, width), bf16),
+            pltpu.VMEM((count, 128), f32),
         ),
         in_specs=[HBM] * 4,
-        out_specs=(VM, VM, VM),
+        out_specs=(VM, VM, VM, VM),
         scratch_shapes=[
             pltpu.VMEM(values.shape, bf16),
             pltpu.VMEM(scales.shape, bf16),
@@ -186,86 +195,63 @@
     )(ids, on_chip(fetched), on_chip(q))
 
 
-def nearest_kernel(step, ahead, blocks, mode, *refs):
+def nearest_kernel(step, ahead, blocks, load, *refs):
     x_refs, refs = refs[:blocks], refs[blocks:]
-    if mode == "first":
-        cents_hbm, out_ref, squares_ref, head_ref, tail_ref, sems = refs
-    elif mode == "keep":
-        cents_hbm, squares_ref, head_ref, out_ref, tail_ref, sems = refs
+    if load:
+        squares_ref, cents_hbm, out_ref, cents_ref, sems = refs
     else:
-        squares_ref, head_ref, tail_ref, out_ref = refs
+        squares_ref, cents_ref, out_ref = refs
     half = step // 2
-    kept = head_ref.shape[0]
-    parts = kept + tail_ref.shape[0]
-
-    def place(i):
-        return head_ref.at[i] if i < kept else tail_ref.at[i - kept]
-
-    copies = {}
-    if mode != "again":
-        for i in range(0 if mode == "first" else kept, parts):
-            copies[i] = pltpu.make_async_copy(
-                cents_hbm.at[pl.ds(half * i, half), :], place(i), sems.at[i]
-            )
-    waiting = list(copies)
-    for i in waiting[:ahead]:
-        copies[i].start()
-    waiting = waiting[ahead:]
-    best = [None] * (blocks // 2)
-    for i in range(0, parts, 2):
-        for k in (i, i + 1):
-            if k in copies:
+    parts = cents_ref.shape[0]
+    copies = [
+        pltpu.make_async_copy(cents_hbm.at[pl.ds(half * i, half), :], cents_ref.at[i], sems.at[i])
+        for i in range(parts if load else 0)
+    ]
+    for copy in copies[:ahead]:
+        copy.start()
+    for first in range(0, blocks, 4):
+        pairs = [(x_refs[j], x_refs[j + 1]) for j in range(first, min(first + 4, blocks), 2)]
+        best = [None] * len(pairs)
+        for i in range(0, parts, 2):
+            for k in (i, i + 1) if load and first == 0 else ():
                 copies[k].wait()
-                if waiting:
-                    copies[waiting.pop(0)].start()
-        block = jnp.concatenate([place(i)[...], place(i + 1)[...]], axis=0)
-        at = slice(step // 2 * i, step // 2 * i + step)
-        if mode != "first":
-            squares = squares_ref[at, :]
-        else:
-            total = None
-            for b in range(block.shape[1] // 128):
-                wide = block[:, 128 * b : 128 * b + 128].astype(f32)
-                total = wide * wide if total is None else total + wide * wide
-            squares = jnp.broadcast_to(jnp.sum(total, axis=1, keepdims=True), (step, 128))
-            squares_ref[at, :] = squares
-        squares = jnp.concatenate([squares, squares], axis=1)
-        for j in range(len(best)):
-            x = jnp.concatenate([x_refs[2 * j][...], x_refs[2 * j + 1][...]], axis=0)
-            cross = lax.dot_general(block, x, (((1,), (1,)), ((), ())), preferred_element_type=f32)
-            low = jnp.min(squares - 2.0 * cross, axis=0, keepdims=True)
-            best[j] = low if best[j] is None else jnp.minimum(best[j], low)
-    for j, low in enumerate(best):
-        for k in range(2):
-            out_ref[2 * j + k : 2 * j + k + 1, :] = low[:, 128 * k : 128 * k + 128]
-
-
-def nearest(xs, cents, squares=None, head=None, tail=None):
+                if k + ahead < parts:
+                    copies[k + ahead].start()
+            block = jnp.concatenate([cents_ref[i], cents_ref[i + 1]], axis=0)
+            squares = squares_ref[half * i : half * i + step, :]
+            squares = jnp.concatenate([squares, squares], axis=1)
+            for j, pair in enumerate(pairs):
+                x = jnp.concatenate([ref[...] for ref in pair], axis=0)
+                cross = lax.dot_general(block, x, (((1,), (1,)), ((), ())), preferred_element_type=f32)
+                low = jnp.min(squares - 2.0 * cross, axis=0, keepdims=True)
+                best[j] = low if best[j] is None else jnp.minimum(best[j], low)
+        for j, low in enumerate(best):
+            for k in range(2):
+                row = first + 2 * j + k
+                out_ref[row : row + 1, :] = low[:, 128 * k : 128 * k + 128]
+
+
+def nearest(xs, squares, cents, kept, keep):
     count, width = cents.shape
     rows = sum(x.shape[0] for x in xs)
     step = 512
-    parts = 2 * count // step
-    mode = "first" if squares is None else "keep" if tail is None else "again"
-    out = pltpu.VMEM((rows // 128, 128), f32)
-    first, rest = (pltpu.VMEM((n, step // 2, width), bf16) for n in (2, parts - 2))
-    sems = pltpu.SemaphoreType.DMA((parts,))
-    far, near, outs, scratch = {
-        "first": ([cents], [], [out, pltpu.VMEM((count, 128), f32), first], [rest, sems]),
-        "keep": ([cents], [squares, head], [out, rest], [sems]),
-        "again": ([], [squares, head, tail], [out], []),
-    }[mode]
-    return pl.pallas_call(
-        functools.partial(nearest_kernel, step, 3, len(xs), mode),
+    load = kept is None
+    held = pltpu.VMEM((2 * count // step, step // 2, width), bf16)
+    sems = pltpu.SemaphoreType.DMA((2 * count // step,))
+    outs = [pltpu.VMEM((rows // 128, 128), f32)] + [held] * keep
+    result = pl.pallas_call(
+        functools.partial(nearest_kernel, step, 3, len(xs), load),
         out_shape=tuple(outs),
-        in_specs=[VM] * len(xs) + [HBM] * len(far) + [VM] * len(near),
+        in_specs=[VM] * (len(xs) + 1) + [HBM if load else VM],
         out_specs=tuple([VM] * len(outs)),
-        scratch_shapes=scratch,
+        scratch_shapes=([] if keep else [held]) * load + [sems] * load,
         cost_estimate=pl.CostEstimate(
             flops=2 * rows * count * width, bytes_accessed=count * width * 2 + rows * width * 2, transcendentals=0
         ),
         compiler_params=LIMIT,
         name="nearest",
-    )(*[on_chip(x) for x in xs], *[off_chip(x) for x in far], *[on_chip(x) for x in near])
+    )(*[on_chip(x) for x in xs], on_chip(squares), off_chip(cents) if load else on_chip(kept))
+    return result[0], result[1] if keep else kept
 
 
 def halves_of(x):
@@ -434,7 +420,7 @@
     peers = coarse_ids.shape[0]
     slots = 16
 
-    q, row_squares, sent = prepare(emb_values, emb_scales, coarse_ids, centroids, slots)
+    q, row_squares, sent, cent_squares = prepare(emb_values, emb_scales, coarse_ids, centroids, slots)
 
     core = 1
 
@@ -452,11 +438,10 @@
         blocks[d ^ core] = swap(blocks[d], core)
 
     orders = ((0, 1, 8, 9), (2, 3, 6, 7, 10, 11, 14, 15), (4, 12), (5, 13))
-    lows, kept = [], []
-    for order in orders:
-        low, *more = nearest([blocks[d] for d in order], centroids, *kept)
+    lows, kept = [], None
+    for k, order in enumerate(orders):
+        low, kept = nearest([blocks[d] for d in order], cent_squares, centroids, kept, k == 1)
         lows.append(low)
-        kept += more
     where = {d: (k, j) for k, order in enumerate(orders) for j, d in enumerate(order)}
 
     coded = residuals(coarse_ids, fetched, q, count, slots, sub_width)

time: 83.9 us -> 88.5 us (1.055)
  local copies, waits for them, and re-layouts: 1.66 us -> 4.97 us
  Pallas kernels: 21.9 us -> 23.6 us
    unnamed x12 -> x20, local copies, waits for them, and re-layouts: 1.66 us -> 4.97 us
    pallas_call x4, Pallas kernels: 14.3 us -> 15.7 us  [nearest(): pl.pallas_call(functools.partial(nearest_kernel, step, 3, len(xs), load),...]
where the time goes in v9:
time: 88.5 us; the launch traced here: 88 us
  starting transfers between devices  39.5 us (45%)
  Pallas kernels  23.6 us (27%)
  waiting for transfers between devices  19 us (21%)
  local copies, waits for them, and re-layouts  4.97 us (6%)
    ppermute x21, starting transfers between devices, swap(): return lax.ppermute(x, 'cent', [(i, i ^ offset) for i in range(16)])  22.3 us
    ppermute x21, waiting for transfers between devices, swap(): return lax.ppermute(x, 'cent', [(i, i ^ offset) for i in range(16)])  19 us
    pallas_call x4, Pallas kernels, nearest(): pl.pallas_call(functools.partial(nearest_kernel, step, 3, len(xs), load),...  15.7 us
    all_to_all x1, starting transfers between devices, step(): coded = lax.all_to_all(coded, 'rows', 0, 0)  9.87 us
    all_to_all x1, starting transfers between devices, step(): fetched = lax.all_to_all(sent.reshape(peers, slots, width), 'cent', 0, 0)  7.34 us
    unnamed x20, local copies, waits for them, and re-layouts  4.97 us
    pallas_call x1, Pallas kernels, prepare(): pl.pallas_call(functools.partial(prepare_kernel, slots, step), out_shape=...  4.27 us
  transfers between devices with their start and end apart: 23, of which 7 were waited for; matrix products, arithmetic and copies ran while one was open for 0% of the time, Pallas kernels for 19%

profile of v9, /device:TPU:1, one launch (start us, length us, event | category | flops | bytes accessed | tf_op | source)
XLA Modules:
  0.0 88.0 jit_solution(3674744359001480789)
XLA Ops:
  0.6 4.3 %prepare.1 = (bf16[128,1024]{1,0:T(8,128)(2,1)S(1)}, f32[1,128]{1,0:T(1,128)S(1)}, bf16[256,1024]{1,0:T(8,128)(2,1)}, f32[2048,128]{1,0:T(8,128)S(1)}) custom-call(bf16[128,1024]{1,0:T(8,128)(2,1)} %values_hbm.1, bf16[8,128]{1,0:T(8,128)(2,1)} %bitcast.15, s32[16,128]{1,0:T(8,128)} %ids_ref.1, bf16[2048,1024]{1,0:T(8,128)(2,1)} %refs_9_.1), custom_call_target="tpu_custom_call" | custom-call | flops 1073741824 | bytes 4194304 | tf_op jit(solution)/shard_map/prepare/pallas_call | solution.py:114
  4.9 7.3 %all-to-all-start = ((bf16[16,16,1024]{2,1,0:T(8,128)(2,1)}), bf16[16,16,1024]{2,1,0:T(8,128)(2,1)S(1)}, u32[]{:S(2)}, u32[]{:S(2)}) async-start(bf16[16,16,1024]{2,1,0:T(8,128)(2,1)} %bitcast.1), calls=%async_computation | async-start | bytes 1048576 | tf_op jit(solution)/shard_map/all_to_all | solution.py:430
  12.3 1.4 %collective-permute-start.1 = (bf16[128,1024]{1,0:T(8,128)(2,1)S(1)}, bf16[128,1024]{1,0:T(8,128)(2,1)S(1)}, u32[]{:S(2)}, u32[]{:S(2)}) collective-permute-start(bf16[128,1024]{1,0:T(8,128)(2,1)S(1)} %get-tuple-element.19.q_ref.refs_0_), channel_id=1, source_target_pairs={{0,8},{1,9},{2,10},{3,11},{4,12},{5,13},{6,14},{7,15},{8,0},{9,1},... | collective-permute-start | bytes 786440 | tf_op jit(solution)/shard_map/ppermute | solution.py:413
  13.6 1.2 %collective-permute-start.3 = (bf16[128,1024]{1,0:T(8,128)(2,1)S(1)}, bf16[128,1024]{1,0:T(8,128)(2,1)S(1)}, u32[]{:S(2)}, u32[]{:S(2)}) collective-permute-start(bf16[128,1024]{1,0:T(8,128)(2,1)S(1)} %get-tuple-element.19.q_ref.refs_0_), channel_id=1, source_target_pairs={{0,2},{1,3},{2,0},{3,1},{4,6},{5,7},{6,4},{7,5},{8,10},{9,11},{10,... | collective-permute-start | bytes 786440 | tf_op jit(solution)/shard_map/ppermute | solution.py:413
  14.8 1.0 %collective-permute-start = (bf16[128,1024]{1,0:T(8,128)(2,1)S(1)}, bf16[128,1024]{1,0:T(8,128)(2,1)S(1)}, u32[]{:S(2)}, u32[]{:S(2)}) collective-permute-start(bf16[128,1024]{1,0:T(8,128)(2,1)S(1)} %get-tuple-element.19.q_ref.refs_0_), channel_id=1, source_target_pairs={{0,1},{1,0},{2,3},{3,2},{4,5},{5,4},{6,7},{7,6},{8,9},{9,8},{10,11... | collective-permute-start | bytes 786440 | tf_op jit(solution)/shard_map/ppermute | solution.py:413
  15.8 1.8 %collective-permute-start.5 = (bf16[128,1024]{1,0:T(8,128)(2,1)S(1)}, bf16[128,1024]{1,0:T(8,128)(2,1)S(1)}, u32[]{:S(2)}, u32[]{:S(2)}) collective-permute-start(bf16[128,1024]{1,0:T(8,128)(2,1)S(1)} %get-tuple-element.19.q_ref.refs_0_), channel_id=1, source_target_pairs={{0,6},{1,7},{2,4},{3,5},{4,2},{5,3},{6,0},{7,1},{8,14},{9,15},{10,... | collective-permute-start | bytes 786440 | tf_op jit(solution)/shard_map/ppermute | solution.py:413
  17.5 8.2 %collective-permute-done.1.refs_2_ = bf16[128,1024]{1,0:T(8,128)(2,1)S(1)} collective-permute-done((bf16[128,1024]{1,0:T(8,128)(2,1)S(1)}, bf16[128,1024]{1,0:T(8,128)(2,1)S(1)}, u32[]{:S(2)}, u32[]{:S(2)}) %collective-permute-start.1) | collective-permute-done | bytes 262176 | tf_op jit(solution)/shard_map/ppermute | solution.py:413
  25.7 1.0 %collective-permute-start.2 = (bf16[128,1024]{1,0:T(8,128)(2,1)S(1)}, bf16[128,1024]{1,0:T(8,128)(2,1)S(1)}, u32[]{:S(2)}, u32[]{:S(2)}) collective-permute-start(bf16[128,1024]{1,0:T(8,128)(2,1)S(1)} %collective-permute-done.1.refs_2_), channel_id=1, source_target_pairs={{0,1},{1,0},{2,3},{3,2},{4,5},{5,4},{6,7},{7,6},{8,9},{9,8},{10,11... | collective-permute-start | bytes 786440 | tf_op jit(solution)/shard_map/ppermute | solution.py:413
  26.7 1.2 %collective-permute-start.7 = (bf16[128,1024]{1,0:T(8,128)(2,1)S(1)}, bf16[128,1024]{1,0:T(8,128)(2,1)S(1)}, u32[]{:S(2)}, u32[]{:S(2)}) collective-permute-start(bf16[128,1024]{1,0:T(8,128)(2,1)S(1)} %collective-permute-done.1.refs_2_), channel_id=1, source_target_pairs={{0,2},{1,3},{2,0},{3,1},{4,6},{5,7},{6,4},{7,5},{8,10},{9,11},{10,... | collective-permute-start | bytes 786440 | tf_op jit(solution)/shard_map/ppermute | solution.py:413
  28.9 1.8 %collective-permute-start.9 = (bf16[128,1024]{1,0:T(8,128)(2,1)S(1)}, bf16[128,1024]{1,0:T(8,128)(2,1)}, u32[]{:S(2)}, u32[]{:S(2)}) collective-permute-start(bf16[128,1024]{1,0:T(8,128)(2,1)S(1)} %collective-permute-done.1.refs_2_), channel_id=1, source_target_pairs={{0,6},{1,7},{2,4},{3,5},{4,2},{5,3},{6,0},{7,1},{8,14},{9,15},{10,... | collective-permute-start | bytes 786440 | tf_op jit(solution)/shard_map/ppermute | solution.py:413
  32.9 1.8 %collective-permute-done.7.refs_4_ = bf16[128,1024]{1,0:T(8,128)(2,1)S(1)} collective-permute-done((bf16[128,1024]{1,0:T(8,128)(2,1)S(1)}, bf16[128,1024]{1,0:T(8,128)(2,1)S(1)}, u32[]{:S(2)}, u32[]{:S(2)}) %collective-permute-start.7) | collective-permute-done | bytes 262176 | tf_op jit(solution)/shard_map/ppermute | solution.py:413
  34.7 2.4 %collective-permute-start.12 = (bf16[128,1024]{1,0:T(8,128)(2,1)S(1)}, bf16[128,1024]{1,0:T(8,128)(2,1)S(1)}, u32[]{:S(2)}, u32[]{:S(2)}) collective-permute-start(bf16[128,1024]{1,0:T(8,128)(2,1)S(1)} %collective-permute-done.7.refs_4_), channel_id=1, source_target_pairs={{0,6},{1,7},{2,4},{3,5},{4,2},{5,3},{6,0},{7,1},{8,14},{9,15},{10,... | collective-permute-start | bytes 786440 | tf_op jit(solution)/shard_map/ppermute | solution.py:413
  37.1 1.5 %collective-permute-start.8 = (bf16[128,1024]{1,0:T(8,128)(2,1)S(1)}, bf16[128,1024]{1,0:T(8,128)(2,1)}, u32[]{:S(2)}, u32[]{:S(2)}) collective-permute-start(bf16[128,1024]{1,0:T(8,128)(2,1)S(1)} %collective-permute-done.7.refs_4_), channel_id=1, source_target_pairs={{0,1},{1,0},{2,3},{3,2},{4,5},{5,4},{6,7},{7,6},{8,9},{9,8},{10,11... | collective-permute-start | bytes 786440 | tf_op jit(solution)/shard_map/ppermute | solution.py:413
  38.9 1.3 %residuals.1 = s32[16,40,128]{2,1,0:T(8,128)} custom-call(s32[16,128]{1,0:T(8,128)S(1)} %copy-done.1, bf16[256,1024]{1,0:T(8,128)(2,1)S(1)} %bitcast.13, bf16[128,1024]{1,0:T(8,128)(2,1)S(1)} %get-tuple-element.19.q_ref.refs_0_), custom_call_target="tpu_custom_call" | custom-call | flops 67108864 | bytes 1310720 | tf_op jit(solution)/shard_map/residuals/pallas_call | solution.py:185
  40.2 9.9 %all-to-all-start.1 = ((s32[16,40,128]{2,1,0:T(8,128)}), s32[16,40,128]{2,1,0:T(8,128)S(1)}, u32[]{:S(2)}, u32[]{:S(2)}) async-start(s32[16,40,128]{2,1,0:T(8,128)} %residuals.1), calls=%async_computation.1 | async-start | bytes 655360 | tf_op jit(solution)/shard_map/all_to_all | solution.py:448
  52.9 4.8 %nearest.4.refs_0_ = f32[4,128]{1,0:T(4,128)S(1)} custom-call(bf16[128,1024]{1,0:T(8,128)(2,1)S(1)} %get-tuple-element.19.q_ref.refs_0_, bf16[128,1024]{1,0:T(8,128)(2,1)S(1)} %copy-done.6, bf16[128,1024]{1,0:T(8,128)(2,1)S(1)} %copy-done.4, bf16[128,1024]{1,0:T(8,128)(2,1)S(1)} %copy-done.8, f32[2048,128]{1,0:T(8,128)S(1)} %get-tuple-element.20.refs_4_.refs_8_.refs_2_, ...), custom_call_target="tpu_custom_call" | custom-call | flops 2147483648 | bytes 5242880 | tf_op jit(solution)/shard_map/nearest/pallas_call | solution.py:242
  58.5 8.3 %nearest.5 = (f32[8,128]{1,0:T(8,128)S(1)}, bf16[8,256,1024]{2,1,0:T(8,128)(2,1)S(1)}) custom-call(bf16[128,1024]{1,0:T(8,128)(2,1)S(1)} %collective-permute-done.3.refs_0_, bf16[128,1024]{1,0:T(8,128)(2,1)S(1)} %collective-permute-done.4.refs_1_, bf16[128,1024]{1,0:T(8,128)(2,1)S(1)} %collective-permute-done.5.refs_2_, ...), custom_call_target="tpu_custom_call" | custom-call | flops 4294967296 | bytes 6291456 | tf_op jit(solution)/shard_map/nearest/pallas_call | solution.py:242
  66.8 1.3 %nearest.6.refs_2_ = f32[2,128]{1,0:T(2,128)S(1)} custom-call(bf16[128,1024]{1,0:T(8,128)(2,1)S(1)} %collective-permute-done.11.refs_0_, bf16[128,1024]{1,0:T(8,128)(2,1)S(1)} %collective-permute-done.12.refs_1_, f32[2048,128]{1,0:T(8,128)S(1)} %get-tuple-element.20.refs_4_.refs_8_.refs_2_, bf16[8,256,1024]{2,1,0:T(8,128)(2,1)S(1)} %get-tuple-element.22.refs_3_), custom_call_target="tpu_custom_call" | custom-call | flops 1073741824 | bytes 4718592 | tf_op jit(solution)/shard_map/nearest/pallas_call | solution.py:242
  68.1 1.3 %nearest.7.refs_3_ = f32[2,128]{1,0:T(2,128)S(1)} custom-call(bf16[128,1024]{1,0:T(8,128)(2,1)S(1)} %collective-permute-done.13.refs_0_, bf16[128,1024]{1,0:T(8,128)(2,1)S(1)} %collective-permute-done.14.refs_1_, f32[2048,128]{1,0:T(8,128)S(1)} %get-tuple-element.20.refs_4_.refs_8_.refs_2_, bf16[8,256,1024]{2,1,0:T(8,128)(2,1)S(1)} %get-tuple-element.22.refs_3_), custom_call_target="tpu_custom_call" | custom-call | flops 1073741824 | bytes 4718592 | tf_op jit(solution)/shard_map/nearest/pallas_call | solution.py:242
  72.1 2.9 %collective-permute-done.16.b_ref = f32[144,128]{1,0:T(8,128)S(1)} collective-permute-done((f32[144,128]{1,0:T(8,128)S(1)}, f32[144,128]{1,0:T(8,128)S(1)}, u32[]{:S(2)}, u32[]{:S(2)}) %collective-permute-start.16) | collective-permute-done | bytes 73760 | tf_op jit(solution)/shard_map/ppermute | solution.py:413
  75.1 3.2 %collective-permute-start.18 = (f32[144,128]{1,0:T(8,128)S(1)}, f32[144,128]{1,0:T(8,128)S(1)}, u32[]{:S(2)}, u32[]{:S(2)}) collective-permute-start(f32[144,128]{1,0:T(8,128)S(1)} %join.3.a_ref), channel_id=1, source_target_pairs={{0,4},{1,5},{2,6},{3,7},{4,0},{5,1},{6,2},{7,3},{8,12},{9,13},{10,... | collective-permute-start | bytes 221192 | tf_op jit(solution)/shard_map/ppermute | solution.py:413
  79.0 1.9 %collective-permute-done.18.c_ref = f32[144,128]{1,0:T(8,128)S(1)} collective-permute-done((f32[144,128]{1,0:T(8,128)S(1)}, f32[144,128]{1,0:T(8,128)S(1)}, u32[]{:S(2)}, u32[]{:S(2)}) %collective-permute-start.18) | collective-permute-done | bytes 73760 | tf_op jit(solution)/shard_map/ppermute | solution.py:413
  80.9 2.4 %collective-permute-done.19.d_ref = f32[144,128]{1,0:T(8,128)S(1)} collective-permute-done((f32[144,128]{1,0:T(8,128)S(1)}, f32[144,128]{1,0:T(8,128)S(1)}, u32[]{:S(2)}, u32[]{:S(2)}) %collective-permute-start.19) | collective-permute-done | bytes 73760 | tf_op jit(solution)/shard_map/ppermute | solution.py:413
  83.8 2.3 %collective-permute-start.20 = (f32[128,128]{1,0:T(8,128)S(1)}, f32[128,128]{1,0:T(8,128)S(1)}, u32[]{:S(2)}, u32[]{:S(2)}) collective-permute-start(f32[128,128]{1,0:T(8,128)S(1)} %get-tuple-element.28.mine_ref), channel_id=1, source_target_pairs={{0,1},{1,0},{2,3},{3,2},{4,5},{5,4},{6,7},{7,6},{8,9},{9,8},{10,11... | collective-permute-start | bytes 196616 | tf_op jit(solution)/shard_map/ppermute | solution.py:413
  (53 shorter events, 12.8 us)
Async XLA Ops:
  0.6 38.3 %copy-start.1 = (s32[16,128]{1,0:T(8,128)S(1)}, s32[16,128]{1,0:T(8,128)}, u32[]{:S(2)}) copy-start(s32[16,128]{1,0:T(8,128)} %ids_ref.1) | copy-start | bytes 24580
  4.9 34.0 %all-to-all-start = ((bf16[16,16,1024]{2,1,0:T(8,128)(2,1)}), bf16[16,16,1024]{2,1,0:T(8,128)(2,1)S(1)}, u32[]{:S(2)}, u32[]{:S(2)}) async-start(bf16[16,16,1024]{2,1,0:T(8,128)(2,1)} %bitcast.1), calls=%async_computation | async-start | bytes 1048576 | tf_op jit(solution)/shard_map/all_to_all | solution.py:430
  12.3 13.5 %collective-permute-start.1 = (bf16[128,1024]{1,0:T(8,128)(2,1)S(1)}, bf16[128,1024]{1,0:T(8,128)(2,1)S(1)}, u32[]{:S(2)}, u32[]{:S(2)}) collective-permute-start(bf16[128,1024]{1,0:T(8,128)(2,1)S(1)} %get-tuple-element.19.q_ref.refs_0_), channel_id=1, source_target_pairs={{0,8},{1,9},{2,10},{3,11},{4,12},{5,13},{6,14},{7,15},{8,0},{9,1},... | collective-permute-start | bytes 786440 | tf_op jit(solution)/shard_map/ppermute | solution.py:413
  13.6 14.3 %collective-permute-start.3 = (bf16[128,1024]{1,0:T(8,128)(2,1)S(1)}, bf16[128,1024]{1,0:T(8,128)(2,1)S(1)}, u32[]{:S(2)}, u32[]{:S(2)}) collective-permute-start(bf16[128,1024]{1,0:T(8,128)(2,1)S(1)} %get-tuple-element.19.q_ref.refs_0_), channel_id=1, source_target_pairs={{0,2},{1,3},{2,0},{3,1},{4,6},{5,7},{6,4},{7,5},{8,10},{9,11},{10,... | collective-permute-start | bytes 786440 | tf_op jit(solution)/shard_map/ppermute | solution.py:413
  14.8 13.4 %collective-permute-start = (bf16[128,1024]{1,0:T(8,128)(2,1)S(1)}, bf16[128,1024]{1,0:T(8,128)(2,1)S(1)}, u32[]{:S(2)}, u32[]{:S(2)}) collective-permute-start(bf16[128,1024]{1,0:T(8,128)(2,1)S(1)} %get-tuple-element.19.q_ref.refs_0_), channel_id=1, source_target_pairs={{0,1},{1,0},{2,3},{3,2},{4,5},{5,4},{6,7},{7,6},{8,9},{9,8},{10,11... | collective-permute-start | bytes 786440 | tf_op jit(solution)/shard_map/ppermute | solution.py:413
  15.8 15.6 %collective-permute-start.5 = (bf16[128,1024]{1,0:T(8,128)(2,1)S(1)}, bf16[128,1024]{1,0:T(8,128)(2,1)S(1)}, u32[]{:S(2)}, u32[]{:S(2)}) collective-permute-start(bf16[128,1024]{1,0:T(8,128)(2,1)S(1)} %get-tuple-element.19.q_ref.refs_0_), channel_id=1, source_target_pairs={{0,6},{1,7},{2,4},{3,5},{4,2},{5,3},{6,0},{7,1},{8,14},{9,15},{10,... | collective-permute-start | bytes 786440 | tf_op jit(solution)/shard_map/ppermute | solution.py:413
  25.7 6.1 %collective-permute-start.2 = (bf16[128,1024]{1,0:T(8,128)(2,1)S(1)}, bf16[128,1024]{1,0:T(8,128)(2,1)S(1)}, u32[]{:S(2)}, u32[]{:S(2)}) collective-permute-start(bf16[128,1024]{1,0:T(8,128)(2,1)S(1)} %collective-permute-done.1.refs_2_), channel_id=1, source_target_pairs={{0,1},{1,0},{2,3},{3,2},{4,5},{5,4},{6,7},{7,6},{8,9},{9,8},{10,11... | collective-permute-start | bytes 786440 | tf_op jit(solution)/shard_map/ppermute | solution.py:413
  26.7 8.0 %collective-permute-start.7 = (bf16[128,1024]{1,0:T(8,128)(2,1)S(1)}, bf16[128,1024]{1,0:T(8,128)(2,1)S(1)}, u32[]{:S(2)}, u32[]{:S(2)}) collective-permute-start(bf16[128,1024]{1,0:T(8,128)(2,1)S(1)} %collective-permute-done.1.refs_2_), channel_id=1, source_target_pairs={{0,2},{1,3},{2,0},{3,1},{4,6},{5,7},{6,4},{7,5},{8,10},{9,11},{10,... | collective-permute-start | bytes 786440 | tf_op jit(solution)/shard_map/ppermute | solution.py:413
  27.9 9.2 %collective-permute-start.4 = (bf16[128,1024]{1,0:T(8,128)(2,1)S(1)}, bf16[128,1024]{1,0:T(8,128)(2,1)S(1)}, u32[]{:S(2)}, u32[]{:S(2)}) collective-permute-start(bf16[128,1024]{1,0:T(8,128)(2,1)S(1)} %collective-permute-done.3.refs_0_), channel_id=1, source_target_pairs={{0,1},{1,0},{2,3},{3,2},{4,5},{5,4},{6,7},{7,6},{8,9},{9,8},{10,11... | collective-permute-start | bytes 786440 | tf_op jit(solution)/shard_map/ppermute | solution.py:413
  28.9 9.7 %collective-permute-start.9 = (bf16[128,1024]{1,0:T(8,128)(2,1)S(1)}, bf16[128,1024]{1,0:T(8,128)(2,1)}, u32[]{:S(2)}, u32[]{:S(2)}) collective-permute-start(bf16[128,1024]{1,0:T(8,128)(2,1)S(1)} %collective-permute-done.1.refs_2_), channel_id=1, source_target_pairs={{0,6},{1,7},{2,4},{3,5},{4,2},{5,3},{6,0},{7,1},{8,14},{9,15},{10,... | collective-permute-start | bytes 786440 | tf_op jit(solution)/shard_map/ppermute | solution.py:413
  31.4 27.1 %collective-permute-start.6 = (bf16[128,1024]{1,0:T(8,128)(2,1)S(1)}, bf16[128,1024]{1,0:T(8,128)(2,1)}, u32[]{:S(2)}, u32[]{:S(2)}) collective-permute-start(bf16[128,1024]{1,0:T(8,128)(2,1)S(1)} %collective-permute-done.5.refs_2_), channel_id=1, source_target_pairs={{0,1},{1,0},{2,3},{3,2},{4,5},{5,4},{6,7},{7,6},{8,9},{9,8},{10,11... | collective-permute-start | bytes 786440 | tf_op jit(solution)/shard_map/ppermute | solution.py:413
  32.6 25.2 %collective-permute-start.11 = (bf16[128,1024]{1,0:T(8,128)(2,1)S(1)}, bf16[128,1024]{1,0:T(8,128)(2,1)S(1)}, u32[]{:S(2)}, u32[]{:S(2)}) collective-permute-start(bf16[128,1024]{1,0:T(8,128)(2,1)S(1)} %collective-permute-done.5.refs_2_), channel_id=1, source_target_pairs={{0,2},{1,3},{2,0},{3,1},{4,6},{5,7},{6,4},{7,5},{8,10},{9,11},{10,... | collective-permute-start | bytes 786440 | tf_op jit(solution)/shard_map/ppermute | solution.py:413
  34.7 23.7 %collective-permute-start.12 = (bf16[128,1024]{1,0:T(8,128)(2,1)S(1)}, bf16[128,1024]{1,0:T(8,128)(2,1)S(1)}, u32[]{:S(2)}, u32[]{:S(2)}) collective-permute-start(bf16[128,1024]{1,0:T(8,128)(2,1)S(1)} %collective-permute-done.7.refs_4_), channel_id=1, source_target_pairs={{0,6},{1,7},{2,4},{3,5},{4,2},{5,3},{6,0},{7,1},{8,14},{9,15},{10,... | collective-permute-start | bytes 786440 | tf_op jit(solution)/shard_map/ppermute | solution.py:413
  37.1 21.4 %collective-permute-start.8 = (bf16[128,1024]{1,0:T(8,128)(2,1)S(1)}, bf16[128,1024]{1,0:T(8,128)(2,1)}, u32[]{:S(2)}, u32[]{:S(2)}) collective-permute-start(bf16[128,1024]{1,0:T(8,128)(2,1)S(1)} %collective-permute-done.7.refs_4_), channel_id=1, source_target_pairs={{0,1},{1,0},{2,3},{3,2},{4,5},{5,4},{6,7},{7,6},{8,9},{9,8},{10,11... | collective-permute-start | bytes 786440 | tf_op jit(solution)/shard_map/ppermute | solution.py:413
  38.6 19.9 %collective-permute-start.10 = (bf16[128,1024]{1,0:T(8,128)(2,1)}, bf16[128,1024]{1,0:T(8,128)(2,1)}, u32[]{:S(2)}, u32[]{:S(2)}) collective-permute-start(bf16[128,1024]{1,0:T(8,128)(2,1)} %collective-permute-done.9.refs_6_), channel_id=1, source_target_pairs={{0,1},{1,0},{2,3},{3,2},{4,5},{5,4},{6,7},{7,6},{8,9},{9,8},{10,11... | collective-permute-start | bytes 786440 | tf_op jit(solution)/shard_map/ppermute | solution.py:413
  40.2 29.2 %all-to-all-start.1 = ((s32[16,40,128]{2,1,0:T(8,128)}), s32[16,40,128]{2,1,0:T(8,128)S(1)}, u32[]{:S(2)}, u32[]{:S(2)}) async-start(s32[16,40,128]{2,1,0:T(8,128)} %residuals.1), calls=%async_computation.1 | async-start | bytes 655360 | tf_op jit(solution)/shard_map/all_to_all | solution.py:448
  57.8 10.3 %collective-permute-start.13 = (bf16[128,1024]{1,0:T(8,128)(2,1)S(1)}, bf16[128,1024]{1,0:T(8,128)(2,1)S(1)}, u32[]{:S(2)}, u32[]{:S(2)}) collective-permute-start(bf16[128,1024]{1,0:T(8,128)(2,1)S(1)} %collective-permute-done.11.refs_0_), channel_id=1, source_target_pairs={{0,1},{1,0},{2,3},{3,2},{4,5},{5,4},{6,7},{7,6},{8,9},{9,8},{10,11... | collective-permute-start | bytes 786440 | tf_op jit(solution)/shard_map/ppermute | solution.py:413
  58.4 9.8 %collective-permute-start.14 = (bf16[128,1024]{1,0:T(8,128)(2,1)S(1)}, bf16[128,1024]{1,0:T(8,128)(2,1)S(1)}, u32[]{:S(2)}, u32[]{:S(2)}) collective-permute-start(bf16[128,1024]{1,0:T(8,128)(2,1)S(1)} %collective-permute-done.12.refs_1_), channel_id=1, source_target_pairs={{0,1},{1,0},{2,3},{3,2},{4,5},{5,4},{6,7},{7,6},{8,9},{9,8},{10,11... | collective-permute-start | bytes 786440 | tf_op jit(solution)/shard_map/ppermute | solution.py:413
  70.3 1.4 %collective-permute-start.15 = (f32[144,128]{1,0:T(8,128)S(1)}, f32[144,128]{1,0:T(8,128)S(1)}, u32[]{:S(2)}, u32[]{:S(2)}) collective-permute-start(f32[144,128]{1,0:T(8,128)S(1)} %get-tuple-element.24), channel_id=1, source_target_pairs={{0,1},{1,0},{2,3},{3,2},{4,5},{5,4},{6,7},{7,6},{8,9},{9,8},{10,11... | collective-permute-start | bytes 221192 | tf_op jit(solution)/shard_map/ppermute | solution.py:413
  71.7 3.3 %collective-permute-start.16 = (f32[144,128]{1,0:T(8,128)S(1)}, f32[144,128]{1,0:T(8,128)S(1)}, u32[]{:S(2)}, u32[]{:S(2)}) collective-permute-start(f32[144,128]{1,0:T(8,128)S(1)} %join.2.a_ref), channel_id=1, source_target_pairs={{0,8},{1,9},{2,10},{3,11},{4,12},{5,13},{6,14},{7,15},{8,0},{9,1},... | collective-permute-start | bytes 221192 | tf_op jit(solution)/shard_map/ppermute | solution.py:413
  75.0 3.9 %collective-permute-start.17 = (f32[144,128]{1,0:T(8,128)S(1)}, f32[144,128]{1,0:T(8,128)S(1)}, u32[]{:S(2)}, u32[]{:S(2)}) collective-permute-start(f32[144,128]{1,0:T(8,128)S(1)} %join.3.a_ref), channel_id=1, source_target_pairs={{0,2},{1,3},{2,0},{3,1},{4,6},{5,7},{6,4},{7,5},{8,10},{9,11},{10,... | collective-permute-start | bytes 221192 | tf_op jit(solution)/shard_map/ppermute | solution.py:413
  75.1 5.7 %collective-permute-start.18 = (f32[144,128]{1,0:T(8,128)S(1)}, f32[144,128]{1,0:T(8,128)S(1)}, u32[]{:S(2)}, u32[]{:S(2)}) collective-permute-start(f32[144,128]{1,0:T(8,128)S(1)} %join.3.a_ref), channel_id=1, source_target_pairs={{0,4},{1,5},{2,6},{3,7},{4,0},{5,1},{6,2},{7,3},{8,12},{9,13},{10,... | collective-permute-start | bytes 221192 | tf_op jit(solution)/shard_map/ppermute | solution.py:413
  78.3 4.9 %collective-permute-start.19 = (f32[144,128]{1,0:T(8,128)S(1)}, f32[144,128]{1,0:T(8,128)S(1)}, u32[]{:S(2)}, u32[]{:S(2)}) collective-permute-start(f32[144,128]{1,0:T(8,128)S(1)} %join.3.a_ref), channel_id=1, source_target_pairs={{0,6},{1,7},{2,4},{3,5},{4,2},{5,3},{6,0},{7,1},{8,14},{9,15},{10,... | collective-permute-start | bytes 221192 | tf_op jit(solution)/shard_map/ppermute | solution.py:413
  83.8 3.2 %collective-permute-start.20 = (f32[128,128]{1,0:T(8,128)S(1)}, f32[128,128]{1,0:T(8,128)S(1)}, u32[]{:S(2)}, u32[]{:S(2)}) collective-permute-start(f32[128,128]{1,0:T(8,128)S(1)} %get-tuple-element.28.mine_ref), channel_id=1, source_target_pairs={{0,1},{1,0},{2,3},{3,2},{4,5},{5,4},{6,7},{7,6},{8,9},{9,8},{10,11... | collective-permute-start | bytes 196616 | tf_op jit(solution)/shard_map/ppermute | solution.py:413
  (9 other events, 22.9 us)

commit v10 on v9

--- a/solution.py
+++ b/solution.py
@@ -195,7 +195,7 @@
     )(ids, on_chip(fetched), on_chip(q))
 
 
-def nearest_kernel(step, ahead, blocks, load, *refs):
+def nearest_kernel(step, blocks, load, *refs):
     x_refs, refs = refs[:blocks], refs[blocks:]
     if load:
         squares_ref, cents_hbm, out_ref, cents_ref, sems = refs
@@ -207,7 +207,7 @@
         pltpu.make_async_copy(cents_hbm.at[pl.ds(half * i, half), :], cents_ref.at[i], sems.at[i])
         for i in range(parts if load else 0)
     ]
-    for copy in copies[:ahead]:
+    for copy in copies:
         copy.start()
     for first in range(0, blocks, 4):
         pairs = [(x_refs[j], x_refs[j + 1]) for j in range(first, min(first + 4, blocks), 2)]
@@ -215,8 +215,6 @@
         for i in range(0, parts, 2):
             for k in (i, i + 1) if load and first == 0 else ():
                 copies[k].wait()
-                if k + ahead < parts:
-                    copies[k + ahead].start()
             block = jnp.concatenate([cents_ref[i], cents_ref[i + 1]], axis=0)
             squares = squares_ref[half * i : half * i + step, :]
             squares = jnp.concatenate([squares, squares], axis=1)
@@ -240,7 +238,7 @@
     sems = pltpu.SemaphoreType.DMA((2 * count // step,))
     outs = [pltpu.VMEM((rows // 128, 128), f32)] + [held] * keep
     result = pl.pallas_call(
-        functools.partial(nearest_kernel, step, 3, len(xs), load),
+        functools.partial(nearest_kernel, step, len(xs), load),
         out_shape=tuple(outs),
         in_specs=[VM] * (len(xs) + 1) + [HBM if load else VM],
         out_specs=tuple([VM] * len(outs)),

time: 88.5 us -> 87.2 us (0.985)
  Pallas kernels: 23.6 us -> 22.5 us
    pallas_call x4, Pallas kernels: 15.7 us -> 14.6 us  [nearest(): pl.pallas_call(functools.partial(nearest_kernel, step, len(xs), load), ou...]
  transfers between devices with their start and end apart: 23 -> 23, of which waited for: 7 -> 7; matrix products, arithmetic and copies ran while one was open for 0% -> 0% of each run, Pallas kernels for 19% -> 18%
where the time goes in v10:
time: 87.2 us; the launch traced here: 86.8 us
  starting transfers between devices  39.5 us (45%)
  Pallas kernels  22.5 us (26%)
  waiting for transfers between devices  19 us (22%)
  local copies, waits for them, and re-layouts  4.97 us (6%)
    ppermute x21, starting transfers between devices, swap(): return lax.ppermute(x, 'cent', [(i, i ^ offset) for i in range(16)])  22.3 us
    ppermute x21, waiting for transfers between devices, swap(): return lax.ppermute(x, 'cent', [(i, i ^ offset) for i in range(16)])  19 us
    pallas_call x4, Pallas kernels, nearest(): pl.pallas_call(functools.partial(nearest_kernel, step, len(xs), load), ou...  14.6 us
    all_to_all x1, starting transfers between devices, step(): coded = lax.all_to_all(coded, 'rows', 0, 0)  9.87 us
    all_to_all x1, starting transfers between devices, step(): fetched = lax.all_to_all(sent.reshape(peers, slots, width), 'cent', 0, 0)  7.34 us
    unnamed x20, local copies, waits for them, and re-layouts  4.97 us
    pallas_call x1, Pallas kernels, prepare(): pl.pallas_call(functools.partial(prepare_kernel, slots, step), out_shape=...  4.27 us
  transfers between devices with their start and end apart: 23, of which 7 were waited for; matrix products, arithmetic and copies ran while one was open for 0% of the time, Pallas kernels for 18%

profile of v10, /device:TPU:1, one launch (start us, length us, event | category | flops | bytes accessed | tf_op | source)
XLA Modules:
  0.0 86.8 jit_solution(5445543181366570440)
XLA Ops:
  0.6 4.3 %prepare.1 = (bf16[128,1024]{1,0:T(8,128)(2,1)S(1)}, f32[1,128]{1,0:T(1,128)S(1)}, bf16[256,1024]{1,0:T(8,128)(2,1)}, f32[2048,128]{1,0:T(8,128)S(1)}) custom-call(bf16[128,1024]{1,0:T(8,128)(2,1)} %values_hbm.1, bf16[8,128]{1,0:T(8,128)(2,1)} %bitcast.15, s32[16,128]{1,0:T(8,128)} %ids_ref.1, bf16[2048,1024]{1,0:T(8,128)(2,1)} %refs_9_.1), custom_call_target="tpu_custom_call" | custom-call | flops 1073741824 | bytes 4194304 | tf_op jit(solution)/shard_map/prepare/pallas_call | solution.py:114
  4.9 7.3 %all-to-all-start = ((bf16[16,16,1024]{2,1,0:T(8,128)(2,1)}), bf16[16,16,1024]{2,1,0:T(8,128)(2,1)S(1)}, u32[]{:S(2)}, u32[]{:S(2)}) async-start(bf16[16,16,1024]{2,1,0:T(8,128)(2,1)} %bitcast.1), calls=%async_computation | async-start | bytes 1048576 | tf_op jit(solution)/shard_map/all_to_all | solution.py:428
  12.3 1.4 %collective-permute-start.1 = (bf16[128,1024]{1,0:T(8,128)(2,1)S(1)}, bf16[128,1024]{1,0:T(8,128)(2,1)S(1)}, u32[]{:S(2)}, u32[]{:S(2)}) collective-permute-start(bf16[128,1024]{1,0:T(8,128)(2,1)S(1)} %get-tuple-element.19.q_ref.refs_0_), channel_id=1, source_target_pairs={{0,8},{1,9},{2,10},{3,11},{4,12},{5,13},{6,14},{7,15},{8,0},{9,1},... | collective-permute-start | bytes 786440 | tf_op jit(solution)/shard_map/ppermute | solution.py:411
  13.6 1.2 %collective-permute-start.3 = (bf16[128,1024]{1,0:T(8,128)(2,1)S(1)}, bf16[128,1024]{1,0:T(8,128)(2,1)S(1)}, u32[]{:S(2)}, u32[]{:S(2)}) collective-permute-start(bf16[128,1024]{1,0:T(8,128)(2,1)S(1)} %get-tuple-element.19.q_ref.refs_0_), channel_id=1, source_target_pairs={{0,2},{1,3},{2,0},{3,1},{4,6},{5,7},{6,4},{7,5},{8,10},{9,11},{10,... | collective-permute-start | bytes 786440 | tf_op jit(solution)/shard_map/ppermute | solution.py:411
  14.8 1.0 %collective-permute-start = (bf16[128,1024]{1,0:T(8,128)(2,1)S(1)}, bf16[128,1024]{1,0:T(8,128)(2,1)S(1)}, u32[]{:S(2)}, u32[]{:S(2)}) collective-permute-start(bf16[128,1024]{1,0:T(8,128)(2,1)S(1)} %get-tuple-element.19.q_ref.refs_0_), channel_id=1, source_target_pairs={{0,1},{1,0},{2,3},{3,2},{4,5},{5,4},{6,7},{7,6},{8,9},{9,8},{10,11... | collective-permute-start | bytes 786440 | tf_op jit(solution)/shard_map/ppermute | solution.py:411
  15.8 1.8 %collective-permute-start.5 = (bf16[128,1024]{1,0:T(8,128)(2,1)S(1)}, bf16[128,1024]{1,0:T(8,128)(2,1)S(1)}, u32[]{:S(2)}, u32[]{:S(2)}) collective-permute-start(bf16[128,1024]{1,0:T(8,128)(2,1)S(1)} %get-tuple-element.19.q_ref.refs_0_), channel_id=1, source_target_pairs={{0,6},{1,7},{2,4},{3,5},{4,2},{5,3},{6,0},{7,1},{8,14},{9,15},{10,... | collective-permute-start | bytes 786440 | tf_op jit(solution)/shard_map/ppermute | solution.py:411
  17.5 8.2 %collective-permute-done.1.refs_2_ = bf16[128,1024]{1,0:T(8,128)(2,1)S(1)} collective-permute-done((bf16[128,1024]{1,0:T(8,128)(2,1)S(1)}, bf16[128,1024]{1,0:T(8,128)(2,1)S(1)}, u32[]{:S(2)}, u32[]{:S(2)}) %collective-permute-start.1) | collective-permute-done | bytes 262176 | tf_op jit(solution)/shard_map/ppermute | solution.py:411
  25.7 1.0 %collective-permute-start.2 = (bf16[128,1024]{1,0:T(8,128)(2,1)S(1)}, bf16[128,1024]{1,0:T(8,128)(2,1)S(1)}, u32[]{:S(2)}, u32[]{:S(2)}) collective-permute-start(bf16[128,1024]{1,0:T(8,128)(2,1)S(1)} %collective-permute-done.1.refs_2_), channel_id=1, source_target_pairs={{0,1},{1,0},{2,3},{3,2},{4,5},{5,4},{6,7},{7,6},{8,9},{9,8},{10,11... | collective-permute-start | bytes 786440 | tf_op jit(solution)/shard_map/ppermute | solution.py:411
  26.7 1.2 %collective-permute-start.7 = (bf16[128,1024]{1,0:T(8,128)(2,1)S(1)}, bf16[128,1024]{1,0:T(8,128)(2,1)S(1)}, u32[]{:S(2)}, u32[]{:S(2)}) collective-permute-start(bf16[128,1024]{1,0:T(8,128)(2,1)S(1)} %collective-permute-done.1.refs_2_), channel_id=1, source_target_pairs={{0,2},{1,3},{2,0},{3,1},{4,6},{5,7},{6,4},{7,5},{8,10},{9,11},{10,... | collective-permute-start | bytes 786440 | tf_op jit(solution)/shard_map/ppermute | solution.py:411
  28.9 1.8 %collective-permute-start.9 = (bf16[128,1024]{1,0:T(8,128)(2,1)S(1)}, bf16[128,1024]{1,0:T(8,128)(2,1)}, u32[]{:S(2)}, u32[]{:S(2)}) collective-permute-start(bf16[128,1024]{1,0:T(8,128)(2,1)S(1)} %collective-permute-done.1.refs_2_), channel_id=1, source_target_pairs={{0,6},{1,7},{2,4},{3,5},{4,2},{5,3},{6,0},{7,1},{8,14},{9,15},{10,... | collective-permute-start | bytes 786440 | tf_op jit(solution)/shard_map/ppermute | solution.py:411
  32.9 1.8 %collective-permute-done.7.refs_4_ = bf16[128,1024]{1,0:T(8,128)(2,1)S(1)} collective-permute-done((bf16[128,1024]{1,0:T(8,128)(2,1)S(1)}, bf16[128,1024]{1,0:T(8,128)(2,1)S(1)}, u32[]{:S(2)}, u32[]{:S(2)}) %collective-permute-start.7) | collective-permute-done | bytes 262176 | tf_op jit(solution)/shard_map/ppermute | solution.py:411
  34.7 2.4 %collective-permute-start.12 = (bf16[128,1024]{1,0:T(8,128)(2,1)S(1)}, bf16[128,1024]{1,0:T(8,128)(2,1)S(1)}, u32[]{:S(2)}, u32[]{:S(2)}) collective-permute-start(bf16[128,1024]{1,0:T(8,128)(2,1)S(1)} %collective-permute-done.7.refs_4_), channel_id=1, source_target_pairs={{0,6},{1,7},{2,4},{3,5},{4,2},{5,3},{6,0},{7,1},{8,14},{9,15},{10,... | collective-permute-start | bytes 786440 | tf_op jit(solution)/shard_map/ppermute | solution.py:411
  37.1 1.5 %collective-permute-start.8 = (bf16[128,1024]{1,0:T(8,128)(2,1)S(1)}, bf16[128,1024]{1,0:T(8,128)(2,1)}, u32[]{:S(2)}, u32[]{:S(2)}) collective-permute-start(bf16[128,1024]{1,0:T(8,128)(2,1)S(1)} %collective-permute-done.7.refs_4_), channel_id=1, source_target_pairs={{0,1},{1,0},{2,3},{3,2},{4,5},{5,4},{6,7},{7,6},{8,9},{9,8},{10,11... | collective-permute-start | bytes 786440 | tf_op jit(solution)/shard_map/ppermute | solution.py:411
  38.9 1.3 %residuals.1 = s32[16,40,128]{2,1,0:T(8,128)} custom-call(s32[16,128]{1,0:T(8,128)S(1)} %copy-done.1, bf16[256,1024]{1,0:T(8,128)(2,1)S(1)} %bitcast.13, bf16[128,1024]{1,0:T(8,128)(2,1)S(1)} %get-tuple-element.19.q_ref.refs_0_), custom_call_target="tpu_custom_call" | custom-call | flops 67108864 | bytes 1310720 | tf_op jit(solution)/shard_map/residuals/pallas_call | solution.py:185
  40.2 9.9 %all-to-all-start.1 = ((s32[16,40,128]{2,1,0:T(8,128)}), s32[16,40,128]{2,1,0:T(8,128)S(1)}, u32[]{:S(2)}, u32[]{:S(2)}) async-start(s32[16,40,128]{2,1,0:T(8,128)} %residuals.1), calls=%async_computation.1 | async-start | bytes 655360 | tf_op jit(solution)/shard_map/all_to_all | solution.py:446
  52.9 4.3 %nearest.4.refs_0_ = f32[4,128]{1,0:T(4,128)S(1)} custom-call(bf16[128,1024]{1,0:T(8,128)(2,1)S(1)} %get-tuple-element.19.q_ref.refs_0_, bf16[128,1024]{1,0:T(8,128)(2,1)S(1)} %copy-done.6, bf16[128,1024]{1,0:T(8,128)(2,1)S(1)} %copy-done.4, bf16[128,1024]{1,0:T(8,128)(2,1)S(1)} %copy-done.8, f32[2048,128]{1,0:T(8,128)S(1)} %get-tuple-element.20.refs_4_.refs_8_.refs_2_, ...), custom_call_target="tpu_custom_call" | custom-call | flops 2147483648 | bytes 5242880 | tf_op jit(solution)/shard_map/nearest/pallas_call | solution.py:240
  57.9 7.7 %nearest.5 = (f32[8,128]{1,0:T(8,128)S(1)}, bf16[8,256,1024]{2,1,0:T(8,128)(2,1)S(1)}) custom-call(bf16[128,1024]{1,0:T(8,128)(2,1)S(1)} %collective-permute-done.3.refs_0_, bf16[128,1024]{1,0:T(8,128)(2,1)S(1)} %collective-permute-done.4.refs_1_, bf16[128,1024]{1,0:T(8,128)(2,1)S(1)} %collective-permute-done.5.refs_2_, ...), custom_call_target="tpu_custom_call" | custom-call | flops 4294967296 | bytes 6291456 | tf_op jit(solution)/shard_map/nearest/pallas_call | solution.py:240
  65.6 1.3 %nearest.6.refs_2_ = f32[2,128]{1,0:T(2,128)S(1)} custom-call(bf16[128,1024]{1,0:T(8,128)(2,1)S(1)} %collective-permute-done.11.refs_0_, bf16[128,1024]{1,0:T(8,128)(2,1)S(1)} %collective-permute-done.12.refs_1_, f32[2048,128]{1,0:T(8,128)S(1)} %get-tuple-element.20.refs_4_.refs_8_.refs_2_, bf16[8,256,1024]{2,1,0:T(8,128)(2,1)S(1)} %get-tuple-element.22.refs_3_), custom_call_target="tpu_custom_call" | custom-call | flops 1073741824 | bytes 4718592 | tf_op jit(solution)/shard_map/nearest/pallas_call | solution.py:240
  67.0 1.3 %nearest.7.refs_3_ = f32[2,128]{1,0:T(2,128)S(1)} custom-call(bf16[128,1024]{1,0:T(8,128)(2,1)S(1)} %collective-permute-done.13.refs_0_, bf16[128,1024]{1,0:T(8,128)(2,1)S(1)} %collective-permute-done.14.refs_1_, f32[2048,128]{1,0:T(8,128)S(1)} %get-tuple-element.20.refs_4_.refs_8_.refs_2_, bf16[8,256,1024]{2,1,0:T(8,128)(2,1)S(1)} %get-tuple-element.22.refs_3_), custom_call_target="tpu_custom_call" | custom-call | flops 1073741824 | bytes 4718592 | tf_op jit(solution)/shard_map/nearest/pallas_call | solution.py:240
  71.0 2.9 %collective-permute-done.16.b_ref = f32[144,128]{1,0:T(8,128)S(1)} collective-permute-done((f32[144,128]{1,0:T(8,128)S(1)}, f32[144,128]{1,0:T(8,128)S(1)}, u32[]{:S(2)}, u32[]{:S(2)}) %collective-permute-start.16) | collective-permute-done | bytes 73760 | tf_op jit(solution)/shard_map/ppermute | solution.py:411
  74.0 3.2 %collective-permute-start.18 = (f32[144,128]{1,0:T(8,128)S(1)}, f32[144,128]{1,0:T(8,128)S(1)}, u32[]{:S(2)}, u32[]{:S(2)}) collective-permute-start(f32[144,128]{1,0:T(8,128)S(1)} %join.3.a_ref), channel_id=1, source_target_pairs={{0,4},{1,5},{2,6},{3,7},{4,0},{5,1},{6,2},{7,3},{8,12},{9,13},{10,... | collective-permute-start | bytes 221192 | tf_op jit(solution)/shard_map/ppermute | solution.py:411
  77.9 1.9 %collective-permute-done.18.c_ref = f32[144,128]{1,0:T(8,128)S(1)} collective-permute-done((f32[144,128]{1,0:T(8,128)S(1)}, f32[144,128]{1,0:T(8,128)S(1)}, u32[]{:S(2)}, u32[]{:S(2)}) %collective-permute-start.18) | collective-permute-done | bytes 73760 | tf_op jit(solution)/shard_map/ppermute | solution.py:411
  79.7 2.4 %collective-permute-done.19.d_ref = f32[144,128]{1,0:T(8,128)S(1)} collective-permute-done((f32[144,128]{1,0:T(8,128)S(1)}, f32[144,128]{1,0:T(8,128)S(1)}, u32[]{:S(2)}, u32[]{:S(2)}) %collective-permute-start.19) | collective-permute-done | bytes 73760 | tf_op jit(solution)/shard_map/ppermute | solution.py:411
  82.7 2.3 %collective-permute-start.20 = (f32[128,128]{1,0:T(8,128)S(1)}, f32[128,128]{1,0:T(8,128)S(1)}, u32[]{:S(2)}, u32[]{:S(2)}) collective-permute-start(f32[128,128]{1,0:T(8,128)S(1)} %get-tuple-element.28.mine_ref), channel_id=1, source_target_pairs={{0,1},{1,0},{2,3},{3,2},{4,5},{5,4},{6,7},{7,6},{8,9},{9,8},{10,11... | collective-permute-start | bytes 196616 | tf_op jit(solution)/shard_map/ppermute | solution.py:411
  (53 shorter events, 12.8 us)
Async XLA Ops:
  0.6 38.3 %copy-start.1 = (s32[16,128]{1,0:T(8,128)S(1)}, s32[16,128]{1,0:T(8,128)}, u32[]{:S(2)}) copy-start(s32[16,128]{1,0:T(8,128)} %ids_ref.1) | copy-start | bytes 24580
  4.9 34.0 %all-to-all-start = ((bf16[16,16,1024]{2,1,0:T(8,128)(2,1)}), bf16[16,16,1024]{2,1,0:T(8,128)(2,1)S(1)}, u32[]{:S(2)}, u32[]{:S(2)}) async-start(bf16[16,16,1024]{2,1,0:T(8,128)(2,1)} %bitcast.1), calls=%async_computation | async-start | bytes 1048576 | tf_op jit(solution)/shard_map/all_to_all | solution.py:428
  12.3 13.5 %collective-permute-start.1 = (bf16[128,1024]{1,0:T(8,128)(2,1)S(1)}, bf16[128,1024]{1,0:T(8,128)(2,1)S(1)}, u32[]{:S(2)}, u32[]{:S(2)}) collective-permute-start(bf16[128,1024]{1,0:T(8,128)(2,1)S(1)} %get-tuple-element.19.q_ref.refs_0_), channel_id=1, source_target_pairs={{0,8},{1,9},{2,10},{3,11},{4,12},{5,13},{6,14},{7,15},{8,0},{9,1},... | collective-permute-start | bytes 786440 | tf_op jit(solution)/shard_map/ppermute | solution.py:411
  13.6 14.3 %collective-permute-start.3 = (bf16[128,1024]{1,0:T(8,128)(2,1)S(1)}, bf16[128,1024]{1,0:T(8,128)(2,1)S(1)}, u32[]{:S(2)}, u32[]{:S(2)}) collective-permute-start(bf16[128,1024]{1,0:T(8,128)(2,1)S(1)} %get-tuple-element.19.q_ref.refs_0_), channel_id=1, source_target_pairs={{0,2},{1,3},{2,0},{3,1},{4,6},{5,7},{6,4},{7,5},{8,10},{9,11},{10,... | collective-permute-start | bytes 786440 | tf_op jit(solution)/shard_map/ppermute | solution.py:411
  14.8 13.4 %collective-permute-start = (bf16[128,1024]{1,0:T(8,128)(2,1)S(1)}, bf16[128,1024]{1,0:T(8,128)(2,1)S(1)}, u32[]{:S(2)}, u32[]{:S(2)}) collective-permute-start(bf16[128,1024]{1,0:T(8,128)(2,1)S(1)} %get-tuple-element.19.q_ref.refs_0_), channel_id=1, source_target_pairs={{0,1},{1,0},{2,3},{3,2},{4,5},{5,4},{6,7},{7,6},{8,9},{9,8},{10,11... | collective-permute-start | bytes 786440 | tf_op jit(solution)/shard_map/ppermute | solution.py:411
  15.8 15.6 %collective-permute-start.5 = (bf16[128,1024]{1,0:T(8,128)(2,1)S(1)}, bf16[128,1024]{1,0:T(8,128)(2,1)S(1)}, u32[]{:S(2)}, u32[]{:S(2)}) collective-permute-start(bf16[128,1024]{1,0:T(8,128)(2,1)S(1)} %get-tuple-element.19.q_ref.refs_0_), channel_id=1, source_target_pairs={{0,6},{1,7},{2,4},{3,5},{4,2},{5,3},{6,0},{7,1},{8,14},{9,15},{10,... | collective-permute-start | bytes 786440 | tf_op jit(solution)/shard_map/ppermute | solution.py:411
  25.7 6.1 %collective-permute-start.2 = (bf16[128,1024]{1,0:T(8,128)(2,1)S(1)}, bf16[128,1024]{1,0:T(8,128)(2,1)S(1)}, u32[]{:S(2)}, u32[]{:S(2)}) collective-permute-start(bf16[128,1024]{1,0:T(8,128)(2,1)S(1)} %collective-permute-done.1.refs_2_), channel_id=1, source_target_pairs={{0,1},{1,0},{2,3},{3,2},{4,5},{5,4},{6,7},{7,6},{8,9},{9,8},{10,11... | collective-permute-start | bytes 786440 | tf_op jit(solution)/shard_map/ppermute | solution.py:411
  26.7 8.0 %collective-permute-start.7 = (bf16[128,1024]{1,0:T(8,128)(2,1)S(1)}, bf16[128,1024]{1,0:T(8,128)(2,1)S(1)}, u32[]{:S(2)}, u32[]{:S(2)}) collective-permute-start(bf16[128,1024]{1,0:T(8,128)(2,1)S(1)} %collective-permute-done.1.refs_2_), channel_id=1, source_target_pairs={{0,2},{1,3},{2,0},{3,1},{4,6},{5,7},{6,4},{7,5},{8,10},{9,11},{10,... | collective-permute-start | bytes 786440 | tf_op jit(solution)/shard_map/ppermute | solution.py:411
  27.9 9.2 %collective-permute-start.4 = (bf16[128,1024]{1,0:T(8,128)(2,1)S(1)}, bf16[128,1024]{1,0:T(8,128)(2,1)S(1)}, u32[]{:S(2)}, u32[]{:S(2)}) collective-permute-start(bf16[128,1024]{1,0:T(8,128)(2,1)S(1)} %collective-permute-done.3.refs_0_), channel_id=1, source_target_pairs={{0,1},{1,0},{2,3},{3,2},{4,5},{5,4},{6,7},{7,6},{8,9},{9,8},{10,11... | collective-permute-start | bytes 786440 | tf_op jit(solution)/shard_map/ppermute | solution.py:411
  28.9 9.7 %collective-permute-start.9 = (bf16[128,1024]{1,0:T(8,128)(2,1)S(1)}, bf16[128,1024]{1,0:T(8,128)(2,1)}, u32[]{:S(2)}, u32[]{:S(2)}) collective-permute-start(bf16[128,1024]{1,0:T(8,128)(2,1)S(1)} %collective-permute-done.1.refs_2_), channel_id=1, source_target_pairs={{0,6},{1,7},{2,4},{3,5},{4,2},{5,3},{6,0},{7,1},{8,14},{9,15},{10,... | collective-permute-start | bytes 786440 | tf_op jit(solution)/shard_map/ppermute | solution.py:411
  31.4 26.5 %collective-permute-start.6 = (bf16[128,1024]{1,0:T(8,128)(2,1)S(1)}, bf16[128,1024]{1,0:T(8,128)(2,1)}, u32[]{:S(2)}, u32[]{:S(2)}) collective-permute-start(bf16[128,1024]{1,0:T(8,128)(2,1)S(1)} %collective-permute-done.5.refs_2_), channel_id=1, source_target_pairs={{0,1},{1,0},{2,3},{3,2},{4,5},{5,4},{6,7},{7,6},{8,9},{9,8},{10,11... | collective-permute-start | bytes 786440 | tf_op jit(solution)/shard_map/ppermute | solution.py:411
  32.6 24.7 %collective-permute-start.11 = (bf16[128,1024]{1,0:T(8,128)(2,1)S(1)}, bf16[128,1024]{1,0:T(8,128)(2,1)S(1)}, u32[]{:S(2)}, u32[]{:S(2)}) collective-permute-start(bf16[128,1024]{1,0:T(8,128)(2,1)S(1)} %collective-permute-done.5.refs_2_), channel_id=1, source_target_pairs={{0,2},{1,3},{2,0},{3,1},{4,6},{5,7},{6,4},{7,5},{8,10},{9,11},{10,... | collective-permute-start | bytes 786440 | tf_op jit(solution)/shard_map/ppermute | solution.py:411
  34.7 23.1 %collective-permute-start.12 = (bf16[128,1024]{1,0:T(8,128)(2,1)S(1)}, bf16[128,1024]{1,0:T(8,128)(2,1)S(1)}, u32[]{:S(2)}, u32[]{:S(2)}) collective-permute-start(bf16[128,1024]{1,0:T(8,128)(2,1)S(1)} %collective-permute-done.7.refs_4_), channel_id=1, source_target_pairs={{0,6},{1,7},{2,4},{3,5},{4,2},{5,3},{6,0},{7,1},{8,14},{9,15},{10,... | collective-permute-start | bytes 786440 | tf_op jit(solution)/shard_map/ppermute | solution.py:411
  37.1 20.9 %collective-permute-start.8 = (bf16[128,1024]{1,0:T(8,128)(2,1)S(1)}, bf16[128,1024]{1,0:T(8,128)(2,1)}, u32[]{:S(2)}, u32[]{:S(2)}) collective-permute-start(bf16[128,1024]{1,0:T(8,128)(2,1)S(1)} %collective-permute-done.7.refs_4_), channel_id=1, source_target_pairs={{0,1},{1,0},{2,3},{3,2},{4,5},{5,4},{6,7},{7,6},{8,9},{9,8},{10,11... | collective-permute-start | bytes 786440 | tf_op jit(solution)/shard_map/ppermute | solution.py:411
  38.6 19.4 %collective-permute-start.10 = (bf16[128,1024]{1,0:T(8,128)(2,1)}, bf16[128,1024]{1,0:T(8,128)(2,1)}, u32[]{:S(2)}, u32[]{:S(2)}) collective-permute-start(bf16[128,1024]{1,0:T(8,128)(2,1)} %collective-permute-done.9.refs_6_), channel_id=1, source_target_pairs={{0,1},{1,0},{2,3},{3,2},{4,5},{5,4},{6,7},{7,6},{8,9},{9,8},{10,11... | collective-permute-start | bytes 786440 | tf_op jit(solution)/shard_map/ppermute | solution.py:411
  40.2 28.1 %all-to-all-start.1 = ((s32[16,40,128]{2,1,0:T(8,128)}), s32[16,40,128]{2,1,0:T(8,128)S(1)}, u32[]{:S(2)}, u32[]{:S(2)}) async-start(s32[16,40,128]{2,1,0:T(8,128)} %residuals.1), calls=%async_computation.1 | async-start | bytes 655360 | tf_op jit(solution)/shard_map/all_to_all | solution.py:446
  57.2 9.7 %collective-permute-start.13 = (bf16[128,1024]{1,0:T(8,128)(2,1)S(1)}, bf16[128,1024]{1,0:T(8,128)(2,1)S(1)}, u32[]{:S(2)}, u32[]{:S(2)}) collective-permute-start(bf16[128,1024]{1,0:T(8,128)(2,1)S(1)} %collective-permute-done.11.refs_0_), channel_id=1, source_target_pairs={{0,1},{1,0},{2,3},{3,2},{4,5},{5,4},{6,7},{7,6},{8,9},{9,8},{10,11... | collective-permute-start | bytes 786440 | tf_op jit(solution)/shard_map/ppermute | solution.py:411
  57.8 9.2 %collective-permute-start.14 = (bf16[128,1024]{1,0:T(8,128)(2,1)S(1)}, bf16[128,1024]{1,0:T(8,128)(2,1)S(1)}, u32[]{:S(2)}, u32[]{:S(2)}) collective-permute-start(bf16[128,1024]{1,0:T(8,128)(2,1)S(1)} %collective-permute-done.12.refs_1_), channel_id=1, source_target_pairs={{0,1},{1,0},{2,3},{3,2},{4,5},{5,4},{6,7},{7,6},{8,9},{9,8},{10,11... | collective-permute-start | bytes 786440 | tf_op jit(solution)/shard_map/ppermute | solution.py:411
  69.2 1.4 %collective-permute-start.15 = (f32[144,128]{1,0:T(8,128)S(1)}, f32[144,128]{1,0:T(8,128)S(1)}, u32[]{:S(2)}, u32[]{:S(2)}) collective-permute-start(f32[144,128]{1,0:T(8,128)S(1)} %get-tuple-element.24), channel_id=1, source_target_pairs={{0,1},{1,0},{2,3},{3,2},{4,5},{5,4},{6,7},{7,6},{8,9},{9,8},{10,11... | collective-permute-start | bytes 221192 | tf_op jit(solution)/shard_map/ppermute | solution.py:411
  70.6 3.3 %collective-permute-start.16 = (f32[144,128]{1,0:T(8,128)S(1)}, f32[144,128]{1,0:T(8,128)S(1)}, u32[]{:S(2)}, u32[]{:S(2)}) collective-permute-start(f32[144,128]{1,0:T(8,128)S(1)} %join.2.a_ref), channel_id=1, source_target_pairs={{0,8},{1,9},{2,10},{3,11},{4,12},{5,13},{6,14},{7,15},{8,0},{9,1},... | collective-permute-start | bytes 221192 | tf_op jit(solution)/shard_map/ppermute | solution.py:411
  73.9 3.9 %collective-permute-start.17 = (f32[144,128]{1,0:T(8,128)S(1)}, f32[144,128]{1,0:T(8,128)S(1)}, u32[]{:S(2)}, u32[]{:S(2)}) collective-permute-start(f32[144,128]{1,0:T(8,128)S(1)} %join.3.a_ref), channel_id=1, source_target_pairs={{0,2},{1,3},{2,0},{3,1},{4,6},{5,7},{6,4},{7,5},{8,10},{9,11},{10,... | collective-permute-start | bytes 221192 | tf_op jit(solution)/shard_map/ppermute | solution.py:411
  74.0 5.7 %collective-permute-start.18 = (f32[144,128]{1,0:T(8,128)S(1)}, f32[144,128]{1,0:T(8,128)S(1)}, u32[]{:S(2)}, u32[]{:S(2)}) collective-permute-start(f32[144,128]{1,0:T(8,128)S(1)} %join.3.a_ref), channel_id=1, source_target_pairs={{0,4},{1,5},{2,6},{3,7},{4,0},{5,1},{6,2},{7,3},{8,12},{9,13},{10,... | collective-permute-start | bytes 221192 | tf_op jit(solution)/shard_map/ppermute | solution.py:411
  77.2 4.9 %collective-permute-start.19 = (f32[144,128]{1,0:T(8,128)S(1)}, f32[144,128]{1,0:T(8,128)S(1)}, u32[]{:S(2)}, u32[]{:S(2)}) collective-permute-start(f32[144,128]{1,0:T(8,128)S(1)} %join.3.a_ref), channel_id=1, source_target_pairs={{0,6},{1,7},{2,4},{3,5},{4,2},{5,3},{6,0},{7,1},{8,14},{9,15},{10,... | collective-permute-start | bytes 221192 | tf_op jit(solution)/shard_map/ppermute | solution.py:411
  82.7 3.2 %collective-permute-start.20 = (f32[128,128]{1,0:T(8,128)S(1)}, f32[128,128]{1,0:T(8,128)S(1)}, u32[]{:S(2)}, u32[]{:S(2)}) collective-permute-start(f32[128,128]{1,0:T(8,128)S(1)} %get-tuple-element.28.mine_ref), channel_id=1, source_target_pairs={{0,1},{1,0},{2,3},{3,2},{4,5},{5,4},{6,7},{7,6},{8,9},{9,8},{10,11... | collective-permute-start | bytes 196616 | tf_op jit(solution)/shard_map/ppermute | solution.py:411
  (9 other events, 22.9 us)
